TPU v7x, 32 devices: a whole 2x2x4 slice. The times are simulated.
32 devices in a mesh: seq: 2 (over core), narrow: 4 (over y, x), wide: 4 (over z).
Axes of the slice: x: 2, y: 2, z: 4, core: 2. Of those that a mesh axis runs over, the one named last changes fastest.
Arguments:
- tokens: bfloat16 [8192, 2048], P('seq', 'narrow'), may hold values from -6 to 6
- attn_gain: float32 [2048], P('narrow'), may hold values from 0.5 to 1.5
- w_query: bfloat16 [2048, 2048], P('narrow', 'wide'), may hold values from -0.125 to 0.125
- w_key: bfloat16 [2048, 512], P('narrow', 'wide'), may hold values from -0.125 to 0.125
- w_value: bfloat16 [2048, 512], P('narrow', 'wide'), may hold values from -0.125 to 0.125
- w_out: bfloat16 [2048, 2048], P('wide', 'narrow'), may hold values from -2 to 2
- ffn_gain: float32 [2048], P('narrow'), may hold values from 0.5 to 1.5
- w_gate: bfloat16 [2048, 8192], P('narrow', 'wide'), may hold values from -0.125 to 0.125
- w_up: bfloat16 [2048, 8192], P('narrow', 'wide'), may hold values from -0.125 to 0.125
- w_down: bfloat16 [8192, 2048], P('wide', 'narrow'), may hold values from -0.0625 to 0.0625
- segment_ids: int32 [8192], replicated, may hold values from 0 to 2, as said below
- token_mask: int32 [8192], replicated, may hold values from 0 to 1, as said below
- out_grad: bfloat16 [8192, 2048], P('seq', 'narrow'), may hold values from -6 to 6
Outputs:
- result: bfloat16 [8192, 2048], P('seq', 'narrow')
- input_grad: float32 [8192, 2048], P('seq', 'narrow')
- grad_attn_gain: float32 [2048], P('narrow')
- grad_w_query: float32 [2048, 2048], P('narrow', 'wide')
- grad_w_key: float32 [2048, 512], P('narrow', 'wide')
- grad_w_value: float32 [2048, 512], P('narrow', 'wide')
- grad_w_out: float32 [2048, 2048], P('wide', 'narrow')
- grad_ffn_gain: float32 [2048], P('narrow')
- grad_w_gate: float32 [2048, 8192], P('narrow', 'wide')
- grad_w_up: float32 [2048, 8192], P('narrow', 'wide')
- grad_w_down: float32 [8192, 2048], P('wide', 'narrow')
Inputs may be any that keep to these rules, and one draw needn't show every extreme that they name: `segment_ids`: the pack holds three sequences in order, ids 0, 1, 2, never falling: the first and the last hold 2 to 256 positions each, the middle one all the rest. `token_mask`: padding is the last positions of each sequence: 1 to 255 of the middle one; of the first and the last, one or more and fewer than the sequence's length; the first position of each sequence is a real token.
All inputs are finite; a program needn't handle non-finite values.
Results may differ from a plain program's by a relative error of at most 0.018.
Values may be sent and summed in bfloat16 or wider, within the bound.
A program may use at most 384 MiB of HBM per device.

v0:
```python
import jax
import jax.numpy as jnp
from jax import lax
from jax.sharding import PartitionSpec as P

D = 2048
HD = 64


EPS = 1e-05
THETA = 500000.0
NEG = -1e30


def positions(segment_ids):
    token_index = jnp.arange(segment_ids.shape[0], dtype=jnp.int32)
    seg_first = jnp.concatenate([jnp.ones((1,), dtype=bool), segment_ids[1:] != segment_ids[:-1]])
    seg_start = lax.cummax(jnp.where(seg_first, token_index, jnp.zeros_like(token_index)), axis=0)
    return token_index - seg_start


def rotation(token_pos):
    half_dim = HD // 2
    frequency = THETA ** (-2.0 * jnp.arange(half_dim, dtype=jnp.float32) / HD)
    angles = token_pos.astype(jnp.float32)[:, None] * frequency[None, :]
    cosine_table = jnp.concatenate([jnp.cos(angles), jnp.cos(angles)], axis=1)
    sine_table = jnp.concatenate([jnp.sin(angles), jnp.sin(angles)], axis=1)
    return (cosine_table, sine_table)


def rotate(vectors, cosine_table, sine_table, turn_sign):
    half_dim = HD // 2
    turned = jnp.concatenate([-vectors[..., half_dim:], vectors[..., :half_dim]], axis=-1)
    return vectors * cosine_table[:, None, :] + turn_sign * turned * sine_table[:, None, :]


def narrow_total(values):
    return lax.psum(values, "narrow")


def wide_total(values):
    return lax.psum(values, "wide")


def gather_rows(values):
    return lax.all_gather(values, "narrow", axis=0, tiled=True)


def rms_norm(values):
    squares = narrow_total(jnp.sum(values * values, axis=1))
    row_scale = lax.rsqrt(squares / D + EPS)
    return (values * row_scale[:, None], row_scale)


def norm_back(grad_h, normed, row_scale, gain_vec):
    grad_normed = grad_h * gain_vec[None, :]
    inner_sum = narrow_total(jnp.sum(grad_normed * normed, axis=1))
    grad_input = row_scale[:, None] * (grad_normed - normed * (inner_sum / D)[:, None])
    return (grad_input, jnp.sum(grad_h * normed, axis=0))


def sum_rows(left_side, weight, product_kind):

    def term_rows():
        if product_kind == "flip":
            return lax.dot_general(
                left_side, weight, (((1,), (1,)), ((), ())), preferred_element_type=jnp.float32
            )
        return jnp.dot(left_side, weight, preferred_element_type=jnp.float32)

    return lax.psum_scatter(term_rows(), "narrow", scatter_dimension=0, tiled=True)


def back_rows(grad_rows, weight, inputs):
    shard_piece = lax.all_gather(grad_rows, "narrow", axis=0, tiled=True)
    product = lax.dot_general(
        shard_piece, weight, (((1,), (1,)), ((), ())), preferred_element_type=jnp.float32
    )
    weight_grad = lax.dot_general(
        inputs, shard_piece, (((0,), (0,)), ((), ())), preferred_element_type=jnp.float32
    )
    return (product, weight_grad)


def body(
    tokens,
    attn_gain,
    w_query,
    w_key,
    w_value,
    w_out,
    ffn_gain,
    w_gate,
    w_up,
    w_down,
    segment_ids,
    token_mask,
    out_grad,
):
    narrow_count = lax.axis_size("narrow")
    tok_count = tokens.shape[0]
    quarter = tok_count // narrow_count
    total_tokens = segment_ids.shape[0]
    seq_index = lax.axis_index("seq")
    narrow_index = lax.axis_index("narrow")
    q_width = w_query.shape[1]
    kv_width = w_key.shape[1]
    q_heads = q_width // HD
    kv_heads = kv_width // HD
    group_size = q_heads // kv_heads
    ff_width = w_gate.shape[1]
    score_scale = HD ** (-0.5)
    cosine_all, sine_all = rotation(positions(segment_ids))
    own_first = seq_index * tok_count + narrow_index * quarter
    own_index = own_first + jnp.arange(quarter, dtype=jnp.int32)
    cosine_table = lax.dynamic_slice_in_dim(cosine_all, own_first, quarter, 0)
    sine_table = lax.dynamic_slice_in_dim(sine_all, own_first, quarter, 0)
    own_segment = lax.dynamic_slice_in_dim(segment_ids, own_first, quarter, 0)
    key_index = jnp.arange(total_tokens, dtype=jnp.int32)
    allowed = (
        (own_segment[:, None] == segment_ids[None, :])
        & (key_index[None, :] <= own_index[:, None])
        & (token_mask[None, :] == 1)
    )
    row_valid = lax.dynamic_slice_in_dim(token_mask, seq_index * tok_count, tok_count, 0)
    grad_low = jnp.where(row_valid[:, None] == 1, out_grad, jnp.zeros_like(out_grad))
    grad_float = grad_low.astype(jnp.float32)
    x_float = tokens.astype(jnp.float32)
    normed_one, scale_one = rms_norm(x_float)
    h_one = (normed_one * attn_gain[None, :]).astype(jnp.bfloat16)
    w_qkv = jnp.concatenate([w_query, w_key, w_value], axis=1)
    qkv_lin = sum_rows(h_one, w_qkv, "plain")
    query_rot = rotate(
        qkv_lin[:, :q_width].reshape(quarter, q_heads, HD), cosine_table, sine_table, 1.0
    ).astype(jnp.bfloat16)
    key_rot = rotate(
        qkv_lin[:, q_width : q_width + kv_width].reshape(quarter, kv_heads, HD),
        cosine_table,
        sine_table,
        1.0,
    ).astype(jnp.bfloat16)
    value_low = qkv_lin[:, q_width + kv_width :].astype(jnp.bfloat16)
    kv_local = jnp.concatenate([key_rot.reshape(quarter, kv_width), value_low], axis=1)
    kv_all = lax.all_gather(kv_local, ("seq", "narrow"), axis=0, tiled=True)
    keys_all = kv_all[:, :kv_width].reshape(total_tokens, kv_heads, HD)
    values_all = kv_all[:, kv_width:].reshape(total_tokens, kv_heads, HD)
    query_heads = jnp.transpose(query_rot, (1, 0, 2))
    head_ids = jnp.arange(q_heads, dtype=jnp.int32)

    def head_scores(query_one, head_id):
        kv_id = head_id // group_size
        key_one = lax.dynamic_index_in_dim(keys_all, kv_id, 1, keepdims=False)
        value_one = lax.dynamic_index_in_dim(values_all, kv_id, 1, keepdims=False)
        scores = (
            lax.dot_general(
                query_one, key_one, (((1,), (1,)), ((), ())), preferred_element_type=jnp.float32
            )
            * score_scale
        )
        return (jnp.where(allowed, scores, NEG), key_one, value_one)

    def head_forward(packed):
        query_one, head_id = packed
        scores, key_one, value_one = head_scores(query_one, head_id)
        row_top = jnp.max(scores, axis=1, keepdims=True)
        log_total = row_top + jnp.log(jnp.sum(jnp.exp(scores - row_top), axis=1, keepdims=True))
        prob_low = jnp.exp(scores - log_total).astype(jnp.bfloat16)
        return (jnp.dot(prob_low, value_one, preferred_element_type=jnp.float32), log_total[:, 0])

    head_out, log_totals = lax.map(head_forward, (query_heads, head_ids))
    attn_heads = jnp.transpose(head_out, (1, 0, 2)).reshape(quarter, q_width).astype(jnp.bfloat16)
    attn_all = gather_rows(attn_heads)
    middle = x_float + wide_total(jnp.dot(attn_all, w_out, preferred_element_type=jnp.float32))
    normed_two, scale_two = rms_norm(middle)
    h_two = (normed_two * ffn_gain[None, :]).astype(jnp.bfloat16)
    w_gate_up = jnp.concatenate([w_gate, w_up], axis=1)
    gate_up = sum_rows(h_two, w_gate_up, "plain")
    gate_lin = gate_up[:, :ff_width]
    up_lin = gate_up[:, ff_width:]
    gate_sig = jax.nn.sigmoid(gate_lin)
    act_low = (gate_lin * gate_sig * up_lin).astype(jnp.bfloat16)
    act_all = gather_rows(act_low)
    down_sum = wide_total(jnp.dot(act_all, w_down, preferred_element_type=jnp.float32))
    result = (middle + down_sum).astype(jnp.bfloat16)
    grad_w_down = lax.dot_general(
        act_all, grad_low, (((0,), (0,)), ((), ())), preferred_element_type=jnp.float32
    )
    act_grad = sum_rows(grad_low, w_down, "flip")
    gate_grad = act_grad * up_lin * gate_sig * (1.0 + gate_lin * (1.0 - gate_sig))
    up_grad = act_grad * gate_lin * gate_sig
    gate_up_grad = jnp.concatenate([gate_grad, up_grad], axis=1).astype(jnp.bfloat16)
    middle_part, grad_gate_up = back_rows(gate_up_grad, w_gate_up, h_two)
    middle_norm_grad, grad_ffn_gain = norm_back(
        wide_total(middle_part), normed_two, scale_two, ffn_gain
    )
    middle_grad = grad_float + middle_norm_grad
    attn_grad_low = middle_grad.astype(jnp.bfloat16)
    grad_w_out = lax.dot_general(
        attn_all, attn_grad_low, (((0,), (0,)), ((), ())), preferred_element_type=jnp.float32
    )
    heads_grad = sum_rows(attn_grad_low, w_out, "flip").astype(jnp.bfloat16)
    heads_grad_split = jnp.transpose(heads_grad.reshape(quarter, q_heads, HD), (1, 0, 2))

    def head_backward(packed):
        query_one, grad_one, log_total, head_id = packed
        scores, key_one, value_one = head_scores(query_one, head_id)
        attn_prob = jnp.exp(scores - log_total[:, None])
        prob_low = attn_prob.astype(jnp.bfloat16)
        prob_grad = lax.dot_general(
            grad_one, value_one, (((1,), (1,)), ((), ())), preferred_element_type=jnp.float32
        )
        inner_sum = jnp.sum(attn_prob * prob_grad, axis=1, keepdims=True)
        score_grad = (attn_prob * (prob_grad - inner_sum)).astype(jnp.bfloat16)
        query_grad = jnp.dot(score_grad, key_one, preferred_element_type=jnp.float32) * score_scale
        key_grad = (
            lax.dot_general(
                score_grad, query_one, (((0,), (0,)), ((), ())), preferred_element_type=jnp.float32
            )
            * score_scale
        )
        value_grad = lax.dot_general(
            prob_low, grad_one, (((0,), (0,)), ((), ())), preferred_element_type=jnp.float32
        )
        return (query_grad, key_grad, value_grad)

    query_grads, key_grads, value_grads = lax.map(
        head_backward, (query_heads, heads_grad_split, log_totals, head_ids)
    )
    key_sum = jnp.sum(key_grads.reshape(kv_heads, group_size, total_tokens, HD), axis=1)
    value_sum = jnp.sum(value_grads.reshape(kv_heads, group_size, total_tokens, HD), axis=1)
    kv_grad_all = jnp.concatenate(
        [
            jnp.transpose(key_sum, (1, 0, 2)).reshape(total_tokens, kv_width),
            jnp.transpose(value_sum, (1, 0, 2)).reshape(total_tokens, kv_width),
        ],
        axis=1,
    )
    kv_grad = lax.psum_scatter(
        kv_grad_all.astype(jnp.bfloat16), ("seq", "narrow"), scatter_dimension=0, tiled=True
    ).astype(jnp.float32)
    query_back = rotate(
        jnp.transpose(query_grads, (1, 0, 2)), cosine_table, sine_table, -1.0
    ).reshape(quarter, q_width)
    key_back = rotate(
        kv_grad[:, :kv_width].reshape(quarter, kv_heads, HD), cosine_table, sine_table, -1.0
    ).reshape(quarter, kv_width)
    qkv_grad = jnp.concatenate([query_back, key_back, kv_grad[:, kv_width:]], axis=1).astype(
        jnp.bfloat16
    )
    first_part, grad_qkv = back_rows(qkv_grad, w_qkv, h_one)
    input_part, grad_attn_gain = norm_back(wide_total(first_part), normed_one, scale_one, attn_gain)
    input_grad = middle_grad + input_part
    summed = (
        lax.psum(grad_attn_gain.astype(jnp.bfloat16), "seq").astype(jnp.float32),
        lax.psum(grad_qkv.astype(jnp.bfloat16), "seq").astype(jnp.float32),
        lax.psum(grad_w_out.astype(jnp.bfloat16), "seq").astype(jnp.float32),
        lax.psum(grad_ffn_gain.astype(jnp.bfloat16), "seq").astype(jnp.float32),
        lax.psum(grad_gate_up.astype(jnp.bfloat16), "seq").astype(jnp.float32),
        lax.psum(grad_w_down.astype(jnp.bfloat16), "seq").astype(jnp.float32),
    )
    qkv_total = summed[1]
    gate_up_total = summed[4]
    return (
        result,
        input_grad,
        summed[0],
        qkv_total[:, :q_width],
        qkv_total[:, q_width : q_width + kv_width],
        qkv_total[:, q_width + kv_width :],
        summed[2],
        summed[3],
        gate_up_total[:, :ff_width],
        gate_up_total[:, ff_width:],
        summed[5],
    )


def solution(mesh):
    return jax.shard_map(
        body,
        mesh=mesh,
        in_specs=(
            P("seq", "narrow"),
            P("narrow"),
            P("narrow", "wide"),
            P("narrow", "wide"),
            P("narrow", "wide"),
            P("wide", "narrow"),
            P("narrow"),
            P("narrow", "wide"),
            P("narrow", "wide"),
            P("wide", "narrow"),
            P(),
            P(),
            P("seq", "narrow"),
        ),
        out_specs=(
            P("seq", "narrow"),
            P("seq", "narrow"),
            P("narrow"),
            P("narrow", "wide"),
            P("narrow", "wide"),
            P("narrow", "wide"),
            P("wide", "narrow"),
            P("narrow"),
            P("narrow", "wide"),
            P("narrow", "wide"),
            P("wide", "narrow"),
        ),
        check_vma=False,
    )
```

profile of v0, /device:TPU:0, one launch (start us, length us, event | category | flops | bytes accessed | tf_op | source)
XLA Modules:
  0.0 4983.6 jit_solution(15209267365387991906)
XLA Ops:
  10.5 17.5 psum.98
  51.3 111.1 %reduce-scatter.5.cloned.1.call-done = f32[1024,768]{1,0:T(8,128)} async-done(((f32[4096,768]{1,0:T(8,128)}), f32[1024,768]{1,0:T(8,128)}) %reduce-scatter.5.cloned.1.call-update) | async-done | bytes 3145744 | tf_op jit(solution)/shard_map/reduce_scatter | solution.py:71
  182.3 22.7 all-gather.6.cloned.1.call-done
  217.7 410.5 %while.34 = (s32[]{:T(128)}, bf16[8,1024,64]{1,2,0:T(8,128)(2,1)S(1)}, f32[8,1024]{1,0:T(8,128)}, bf16[8,1024,64]{2,1,0:T(8,128)(2,1)}, s32[8]{0:T(128)S(1)}, /*...) while((s32[]{:T(128)}, ...), condition=%wide.region_8.9_spmd.clone.clone, body=%wide.region_5.8_spmd.clone.sunk.clone | while | flops 2239757312 | bytes 111760208 | solution.py:170
  220.9 19.6 fusion.142
  272.2 19.6 fusion.142
  323.5 19.6 fusion.142
  374.8 19.6 fusion.142
  426.1 19.6 fusion.142
  477.4 19.6 fusion.142
  528.7 19.6 fusion.142
  580.0 19.6 fusion.142
  629.6 52.4 %all-gather.8.cloned.1.call-done = bf16[4096,512]{0,1:T(8,128)(2,1)} async-done(((bf16[1024,512]{0,1:T(8,128)(2,1)}), bf16[4096,512]{0,1:T(8,128)(2,1)}) %all-gather.8.cloned.1.call-update) | async-done | bytes 4194320 | tf_op jit(solution)/shard_map/all_gather | solution.py:46
  690.3 17.7 fusion.82
  714.4 266.7 %all-reduce.10.cloned.1.call-done = f32[4096,512]{1,0:T(8,128)} async-done(((f32[4096,512]{1,0:T(8,128)}), f32[4096,512]{1,0:T(8,128)}) %all-reduce.10.cloned.1.call-update) | async-done | bytes 8388624 | tf_op jit(solution)/shard_map/psum | solution.py:42
  990.3 16.6 psum.100
  1006.9 34.1 fusion.83
  1042.9 229.3 %reduce-scatter.7.cloned.1.call-done = f32[1024,2048]{1,0:T(8,128)} async-done(((f32[4096,2048]{1,0:T(8,128)}), f32[1024,2048]{1,0:T(8,128)}) %reduce-scatter.7.cloned.1.call-update) | async-done | bytes 8388624 | tf_op jit(solution)/shard_map/reduce_scatter | solution.py:71
  1272.2 1120.8 %all-reduce.14.cloned.1.call-done = f32[4096,4096]{1,0:T(8,128)} async-done(((f32[4096,4096]{1,0:T(8,128)}), f32[4096,4096]{1,0:T(8,128)}) %all-reduce.14.cloned.1.call-update) | async-done | bytes 67108880
  2415.0 298.5 %all-gather.12.cloned.1.call-done = bf16[4096,4096]{1,0:T(8,128)(2,1)} async-done(((bf16[1024,4096]{1,0:T(8,128)(2,1)}), bf16[4096,4096]{1,0:T(8,128)(2,1)}) %all-gather.12.cloned.1.call-update) | async-done | bytes 33554448 | tf_op jit(solution)/shard_map/all_gather | solution.py:75
  2713.5 25.0 fusion.91
  2738.6 290.9 %all-reduce.12.cloned.1.call-done = f32[4096,512]{1,0:T(8,128)} async-done(((f32[4096,512]{1,0:T(8,128)}), f32[4096,512]{1,0:T(8,128)}) %all-reduce.12.cloned.1.call-update) | async-done | bytes 8388624 | tf_op jit(solution)/shard_map/psum | solution.py:42
  3037.0 16.0 psum.103
  3071.1 83.6 %reduce-scatter.9.cloned.1.call-done = f32[1024,512]{1,0:T(8,128)} async-done(((f32[4096,512]{1,0:T(8,128)}), f32[1024,512]{1,0:T(8,128)}) %reduce-scatter.9.cloned.1.call-update) | async-done | bytes 2097168 | tf_op jit(solution)/shard_map/reduce_scatter | solution.py:71
  3159.0 861.1 %while.35 = (s32[]{:T(128)}, f32[8,1024,64]{1,2,0:T(8,128)}, f32[8,8192,64]{1,2,0:T(8,128)}, f32[8,8192,64]{1,2,0:T(8,128)}, bf16[8,1024,64]{2,1,0:T(8,128)(2,1)...) while((s32[]{:T(128)}, f32[8,1024,64]{1,2,0:T(8,128)}, ...), condition=%wide.region_21.22_spmd.clone.clone, body=%wide.region_19.21_spmd.clone.sunk.clone | while | flops 5478349824 | bytes 344006528 | solution.py:226
  3178.0 28.8 multiply_reduce_fusion.6
  3206.8 27.5 multiply_convert_fusion.9
  3285.6 28.7 multiply_reduce_fusion.6
  3314.3 27.5 multiply_convert_fusion.9
  3393.1 28.7 multiply_reduce_fusion.6
  3421.8 27.5 multiply_convert_fusion.9
  3500.6 28.7 multiply_reduce_fusion.6
  3529.4 27.5 multiply_convert_fusion.9
  3574.7 15.0 fusion.155
  3608.2 28.7 multiply_reduce_fusion.6
  3637.0 27.5 multiply_convert_fusion.9
  3715.8 28.7 multiply_reduce_fusion.6
  3744.5 27.5 multiply_convert_fusion.9
  3823.3 28.7 multiply_reduce_fusion.6
  3852.1 27.5 multiply_convert_fusion.9
  3930.9 28.7 multiply_reduce_fusion.6
  3959.7 27.5 multiply_convert_fusion.9
  4039.5 46.7 reduce-scatter.11.cloned.1.call-done
  4090.9 155.2 %all-gather.10.cloned.1.call-done = bf16[4096,2048]{1,0:T(8,128)(2,1)} async-done(((bf16[1024,2048]{1,0:T(8,128)(2,1)}), bf16[4096,2048]{1,0:T(8,128)(2,1)}) %all-gather.10.cloned.1.call-update) | async-done | bytes 16777232 | tf_op jit(solution)/shard_map/all_gather | solution.py:46
  4261.0 25.4 convolution_convert_fusion
  4289.5 29.1 all-gather.14.cloned.1.call-done
  4375.6 554.8 %all-reduce.16.cloned.1.call-done = (f32[4096,512]{1,0:T(8,128)}, f32[4096,512]{1,0:T(8,128)}) async-done(((f32[4096,512]{1,0:T(8,128)}, f32[4096,512]{1,0:T(8,128)}), (f32[4096,512]{1,0:T(8,128)}, f32[4096,512]{1,0:T(8,128)})) %all-reduce.16.cloned.1.call-update) | async-done | bytes 16777232 | tf_op jit(solution)/shard_map/psum | solution.py:42
  4939.9 16.0 psum.105
  (335 shorter events, 874.0 us)
Async XLA Ops:
  7.2 683.1 %copy-start = (bf16[2048,512]{1,0:T(8,128)(2,1)S(1)}, bf16[2048,512]{1,0:T(8,128)(2,1)}, u32[]{:S(2)}) copy-start(bf16[2048,512]{1,0:T(8,128)(2,1)} %param.26) | copy-start | bytes 6291460
  7.2 155.2 %reduce-scatter.5.cloned.1.call-start = ((), (), s32[]{:S(2)}) async-start(), calls=%async_computation.4 | async-start | bytes 15728640 | tf_op jit(solution)/shard_map/reduce_scatter | solution.py:71
  42.1 162.9 %all-gather.6.cloned.1.call-start = ((), (), s32[]{:S(2)}) async-start(), calls=%async_computation.5 | async-start | bytes 4718592 | tf_op jit(solution)/shard_map/all_gather | solution.py:144
  43.7 124.9 %copy-start.21 = (s32[8192]{0:T(1024)S(1)}, s32[8192]{0:T(1024)}, u32[]{:S(2)}) copy-start(s32[8192]{0:T(1024)} %param.28) | copy-start | bytes 98308
  47.4 129.0 %copy-start.7 = (f32[1024,64]{0,1:T(8,128)}, f32[1024,64]{0,1:T(8,128)S(1)}, u32[]{:S(2)}) copy-start(f32[1024,64]{0,1:T(8,128)S(1)} %fusion.80) | copy-start | bytes 786436
  168.2 513.9 %all-gather.8.cloned.1.call-start = ((), (), s32[]{:S(2)}) async-start(), calls=%async_computation.6 | async-start | bytes 5242880 | tf_op jit(solution)/shard_map/all_gather | solution.py:46
  343.0 13.8 copy-start.3
  497.0 13.8 copy-start.3
  628.2 62.0 %copy-start.27 = (pred[8192]{0:T(1024)(128)(4,1)}, pred[8192]{0:T(1024)(128)(4,1)S(1)}, u32[]{:S(2)}) copy-start(pred[8192]{0:T(1024)(128)(4,1)S(1)} %get-tuple-element.864) | copy-start | bytes 24580
  628.2 62.0 %copy-start.31 = (s32[1024]{0:T(1024)}, s32[1024]{0:T(1024)S(1)}, u32[]{:S(2)}) copy-start(s32[1024]{0:T(1024)S(1)} %get-tuple-element.865) | copy-start | bytes 12292
  628.2 62.0 %copy-start.33 = (s32[1024]{0:T(1024)}, s32[1024]{0:T(1024)S(1)}, u32[]{:S(2)}) copy-start(s32[1024]{0:T(1024)S(1)} %get-tuple-element.866) | copy-start | bytes 12292
  629.1 61.1 %copy-start.22 = (s32[8192]{0:T(1024)S(1)}, s32[8192]{0:T(1024)}, u32[]{:S(2)}) copy-start(s32[8192]{0:T(1024)} %param.28) | copy-start | bytes 98308
  629.2 351.9 %all-reduce.10.cloned.1.call-start = ((), (), s32[]{:S(2)}) async-start(), calls=%async_computation.7 | async-start | bytes 16777216 | tf_op jit(solution)/shard_map/psum | solution.py:42
  690.2 582.0 %reduce-scatter.7.cloned.1.call-start = ((), (), s32[]{:S(2)}) async-start(), calls=%async_computation.9 | async-start | bytes 41943040 | tf_op jit(solution)/shard_map/reduce_scatter | solution.py:71
  690.2 2362.8 %copy-start.23 = (pred[4096]{0:T(1024)(128)(4,1)}, pred[4096]{0:T(1024)(128)(4,1)S(1)}, u32[]{:S(2)}) copy-start(pred[4096]{0:T(1024)(128)(4,1)S(1)} %dynamic-slice_compare_fusion) | copy-start | bytes 12292
  708.0 1684.9 %all-reduce.14.cloned.1.call-start = ((), (), s32[]{:S(2)}) async-start(), calls=%async_computation.15 | async-start | bytes 134217728
  714.4 292.4 %copy-start.25 = (f32[512]{0:T(512)S(1)}, f32[512]{0:T(512)}, u32[]{:S(2)}) copy-start(f32[512]{0:T(512)} %param.23) | copy-start | bytes 6148
  1006.9 2046.2 %copy-start.19 = (f32[4096]{0:T(1024)}, f32[4096]{0:T(1024)S(1)}, u32[]{:S(2)}) copy-start(f32[4096]{0:T(1024)S(1)} %add_rsqrt_fusion) | copy-start | bytes 49156
  1041.0 1672.5 %all-gather.12.cloned.1.call-start = ((), (), s32[]{:S(2)}) async-start(), calls=%async_computation.10 | async-start | bytes 41943040 | tf_op jit(solution)/shard_map/all_gather | solution.py:75
  2414.8 614.8 %all-reduce.12.cloned.1.call-start = ((), (), s32[]{:S(2)}) async-start(), calls=%async_computation.11 | async-start | bytes 16777216 | tf_op jit(solution)/shard_map/psum | solution.py:42
  2738.6 416.2 %reduce-scatter.9.cloned.1.call-start = ((), (), s32[]{:S(2)}) async-start(), calls=%async_computation.12 | async-start | bytes 10485760 | tf_op jit(solution)/shard_map/reduce_scatter | solution.py:71
  3071.0 88.0 %copy-start.16 = (s32[8192]{0:T(1024)S(1)}, s32[8192]{0:T(1024)}, u32[]{:S(2)}) copy-start(s32[8192]{0:T(1024)} %param.27) | copy-start | bytes 98308
  3071.0 88.0 %copy-start.28 = (pred[8192]{0:T(1024)(128)(4,1)S(1)}, pred[8192]{0:T(1024)(128)(4,1)}, u32[]{:S(2)}) copy-start(pred[8192]{0:T(1024)(128)(4,1)} %copy-done.27) | copy-start | bytes 24580
  3071.0 88.0 %copy-start.32 = (s32[1024]{0:T(1024)S(1)}, s32[1024]{0:T(1024)}, u32[]{:S(2)}) copy-start(s32[1024]{0:T(1024)} %copy-done.31) | copy-start | bytes 12292
  3071.0 88.0 %copy-start.34 = (s32[1024]{0:T(1024)S(1)}, s32[1024]{0:T(1024)}, u32[]{:S(2)}) copy-start(s32[1024]{0:T(1024)} %copy-done.33) | copy-start | bytes 12292
  3071.0 1015.2 %reduce-scatter.11.cloned.1.call-start = ((), (), s32[]{:S(2)}) async-start(), calls=%async_computation.13 | async-start | bytes 4718592 | tf_op jit(solution)/shard_map/reduce_scatter | solution.py:238
  3162.7 15.4 copy-start.4
  3270.2 15.4 copy-start.4
  3377.7 15.4 copy-start.4
  3485.3 15.4 copy-start.4
  3592.9 15.4 copy-start.4
  3700.4 15.4 copy-start.4
  3808.0 15.4 copy-start.4
  3915.6 15.4 copy-start.4
  4034.8 211.3 %all-gather.10.cloned.1.call-start = ((), (), s32[]{:S(2)}) async-start(), calls=%async_computation.8 | async-start | bytes 20971520 | tf_op jit(solution)/shard_map/all_gather | solution.py:46
  4035.5 283.1 %all-gather.14.cloned.1.call-start = ((), (), s32[]{:S(2)}) async-start(), calls=%async_computation.14 | async-start | bytes 7864320 | tf_op jit(solution)/shard_map/all_gather | solution.py:75
  4037.3 208.8 %copy-start.24 = (pred[4096]{0:T(1024)(128)(4,1)S(1)}, pred[4096]{0:T(1024)(128)(4,1)}, u32[]{:S(2)}) copy-start(pred[4096]{0:T(1024)(128)(4,1)} %copy-done.23) | copy-start | bytes 12292
  4090.8 170.2 %copy-start.20 = (f32[4096]{0:T(1024)S(1)}, f32[4096]{0:T(1024)}, u32[]{:S(2)}) copy-start(f32[4096]{0:T(1024)} %copy-done.19) | copy-start | bytes 49156
  4090.8 170.2 %copy-start.26 = (f32[512]{0:T(512)S(1)}, f32[512]{0:T(512)}, u32[]{:S(2)}) copy-start(f32[512]{0:T(512)} %param.23) | copy-start | bytes 6148
  4090.8 271.9 %all-reduce.18.cloned.1.call-start = ((), (), s32[]{:S(2)}) async-start(), calls=%async_computation.17 | async-start | bytes 15204352 | tf_op jit(solution)/shard_map/psum | solution.py:255
  4246.1 40.2 slice-start
  4261.0 25.4 slice-start.1
  4261.0 25.4 copy-start.9
  4286.4 32.2 copy-start.18
  4286.4 32.2 copy-start.29
  4327.7 14.7 copy-start.14
  4327.7 602.7 %all-reduce.16.cloned.1.call-start = ((), (), s32[]{:S(2)}) async-start(), calls=%async_computation.16 | async-start | bytes 33554432 | tf_op jit(solution)/shard_map/psum | solution.py:42
  4375.6 560.7 %copy-start.30 = (bf16[512]{0:T(512)(128)(2,1)S(1)}, bf16[512]{0:T(512)(128)(2,1)}, u32[]{:S(2)}) copy-start(bf16[512]{0:T(512)(128)(2,1)} %get-tuple-element.396) | copy-start | bytes 3076
  (32 other events, 308.6 us)
Sparse Core Ops, SparseCore 0:
  42.2 120.1 reduce-scatter.4
  168.3 36.6 all-gather.5
  629.3 52.7 all-gather.7
  690.2 290.8 all-reduce.9
  984.0 288.1 reduce-scatter.6
  1275.9 1116.9 all-reduce.13
  2414.9 298.5 all-gather.11
  2738.7 290.8 all-reduce.11
  3071.1 83.5 reduce-scatter.8
  4034.9 51.2 reduce-scatter.10
  4088.7 157.4 all-gather.9
  4248.4 70.1 all-gather.13
  4327.8 34.8 all-reduce.17
  4366.0 564.4 all-reduce.15
where the time goes:
time: 4990 us; the launch traced here: 4980 us
  waiting for transfers between devices  3270 us (66%)
  matrix products  1040 us (21%)
  other arithmetic  454 us (9%)
  local copies, waits for them, and re-layouts  90.9 us (2%)
  blocking collectives  68.5 us (1%)
    unnamed x15, waiting for transfers between devices  1120 us
    psum x3, waiting for transfers between devices, wide_total(): return lax.psum(values, 'wide')  1110 us
    reduce_scatter x3, waiting for transfers between devices, sum_rows(): lax.psum_scatter(term_rows(), 'narrow', scatter_dimension=0, tiled=True)  424 us
    dot_general x16, matrix products, head_scores(): lax.dot_general(query_one, key_one, (((1,), (1,)), ((), ())), preferred_e...  386 us
    all_gather x2, waiting for transfers between devices, back_rows(): shard_piece = lax.all_gather(grad_rows, 'narrow', axis=0, tiled=True)  328 us
    convert_element_type x8, other arithmetic, head_backward(): score_grad = (attn_prob * (prob_grad - inner_sum)).astype(jnp.bfloat16)  220 us
    all_gather x2, waiting for transfers between devices, gather_rows(): return lax.all_gather(values, 'narrow', axis=0, tiled=True)  208 us
    dot_general x8, matrix products, head_backward(): lax.dot_general(prob_low, grad_one, (((0,), (0,)), ((), ())), preferred_e...  119 us
  transfers between devices with their start and end apart: 14, of which 14 were waited for; matrix products, arithmetic and copies ran while one was open for 4% of the time, Pallas kernels for 0%

commit v1 on v0

v1 whole, which is shorter than its diff:
```python
import functools

import jax
import jax.numpy as jnp
from jax import lax
from jax.experimental import pallas as pl
from jax.experimental.pallas import tpu as pltpu
from jax.sharding import PartitionSpec as P

HD = 64
EPS = 1e-05
THETA = 500000.0
NEG = -1e30
SN = ("seq", "narrow")
NS = ("narrow", "seq")
BF = jnp.bfloat16
F32 = jnp.float32
NT = (((1,), (1,)), ((), ()))
TN = (((0,), (0,)), ((), ()))


def pieces_of(value):
    first = value.astype(BF).astype(F32)
    second = (value - first).astype(BF).astype(F32)
    third = (value - first - second).astype(BF).astype(F32)
    return first, second, third


def qkv_kernel(qw, x_ref, gain_ref, w_ref, cos_ref, sin_ref, h_ref, q_ref, kv_ref):
    x = x_ref[...].astype(F32)
    mean = jnp.mean(x * x, axis=1, keepdims=True)
    h = (x * lax.rsqrt(mean + EPS) * gain_ref[...]).astype(BF)
    h_ref[...] = h
    t = jnp.dot(h, w_ref[...], preferred_element_type=F32)
    width = t.shape[1]
    lane = lax.broadcasted_iota(jnp.int32, t.shape, 1)
    turned = jnp.where(
        lane % HD < HD // 2, -pltpu.roll(t, width - HD // 2, 1), pltpu.roll(t, HD // 2, 1)
    )
    copies = width // 128
    cos = jnp.concatenate([cos_ref[...]] * copies, axis=1)
    sin = jnp.concatenate([sin_ref[...]] * copies, axis=1)
    plain = (lane >= qw) & (lane % 128 >= HD)
    out = jnp.where(plain, t, t * cos + turned * sin)
    q_ref[...] = (out[:, :qw] * (HD ** -0.5)).astype(BF)
    kv_ref[...] = out[:, qw:].astype(BF)


def qkv_call(x, gain, w, cos, sin, qw):
    rows, d = x.shape
    width = w.shape[1]
    bm = min(256, rows)
    return pl.pallas_call(
        functools.partial(qkv_kernel, qw),
        grid=(rows // bm,),
        in_specs=[
            pl.BlockSpec((bm, d), lambda r: (r, 0)),
            pl.BlockSpec((1, d), lambda r: (0, 0)),
            pl.BlockSpec((d, width), lambda r: (0, 0)),
            pl.BlockSpec((bm, 128), lambda r: (r, 0)),
            pl.BlockSpec((bm, 128), lambda r: (r, 0)),
        ],
        out_specs=[
            pl.BlockSpec((bm, d), lambda r: (r, 0)),
            pl.BlockSpec((bm, qw), lambda r: (r, 0)),
            pl.BlockSpec((bm, width - qw), lambda r: (r, 0)),
        ],
        out_shape=[
            jax.ShapeDtypeStruct((rows, d), BF),
            jax.ShapeDtypeStruct((rows, qw), BF),
            jax.ShapeDtypeStruct((rows, width - qw), BF),
        ],
        cost_estimate=pl.CostEstimate(
            flops=2 * rows * d * width, bytes_accessed=4 * rows * d + 2 * d * width, transcendentals=rows
        ),
        compiler_params=pltpu.CompilerParams(vmem_limit_bytes=40 << 20),
        name="norm_qkv",
    )(x, gain, w, cos, sin)


class Plan:
    def __init__(self, total, group, wide):
        self.total, self.group, self.wide = total, group, wide
        self.chunk = total // (2 * group)
        self.cw = self.chunk // wide
        self.rows = 2 * self.chunk


def build_keys(plan, kv_ref, kf_ref, kx, vx):
    cw = plan.cw
    lane = lax.broadcasted_iota(jnp.int32, (cw, 128), 1)
    ones = jnp.where(lane < 3, 1.0, 0.0).astype(BF)

    def fill(c, carry):
        late = c >= plan.group
        owner = jnp.where(late, 2 * plan.group - 1 - c, c)
        for w in range(plan.wide):
            src = pl.multiple_of(owner * plan.rows + w * 2 * cw + jnp.where(late, cw, 0), cw)
            dst = pl.multiple_of(c * plan.chunk + w * cw, cw)
            kv = kv_ref[pl.ds(src, cw), :]
            kx[pl.ds(dst, cw), :] = jnp.where(lane < HD, kv, kf_ref[pl.ds(dst, cw), :])
            vx[pl.ds(dst, cw), :] = jnp.where(lane < HD, ones, kv)
        return carry

    lax.fori_loop(0, 2 * plan.group, fill, 0)


def split_heads(block, heads, low):
    tiles = []
    for h in range(heads):
        tile = block[:, (h // 2) * 128 : (h // 2 + 1) * 128]
        if (h % 2 == 0) != low:
            tile = pltpu.roll(tile, HD, 1)
        tiles.append(tile)
    return tiles


def join_heads(tiles, low):
    rows = tiles[0].shape[0]
    lane = lax.broadcasted_iota(jnp.int32, (rows, 128), 1)
    pairs = []
    for h in range(0, len(tiles), 2):
        first, second = tiles[h], tiles[h + 1]
        if low:
            second = pltpu.roll(second, HD, 1)
        else:
            first = pltpu.roll(first, HD, 1)
        pairs.append(jnp.where(lane < HD, first, second))
    return jnp.concatenate(pairs, axis=1)


def block_place(plan, s_ref):
    block = pl.program_id(1)
    w, late = block // 2, block % 2 == 1
    c = jnp.where(late, 2 * plan.group - 1 - s_ref[0], s_ref[0])
    return w, c


def forward_kernel(plan, heads, s_ref, q_ref, kv_ref, kf_ref, o_ref, qe_ref, kx, vx):
    cw, chunk = plan.cw, plan.chunk

    @pl.when(pl.program_id(1) == 0)
    def _():
        build_keys(plan, kv_ref, kf_ref, kx, vx)

    w, c = block_place(plan, s_ref)
    lane = lax.broadcasted_iota(jnp.int32, (cw, 128), 1)
    token = c * chunk + w * cw + lax.broadcasted_iota(jnp.int32, (cw, 128), 0)
    segment = (token >= s_ref[1]).astype(jnp.int32) + (token >= s_ref[2]).astype(jnp.int32)
    mark = jnp.where(lane == HD + segment, 1.0, 0.0)
    tiles = split_heads(q_ref[...].astype(F32), heads, True)
    q32 = jnp.concatenate([jnp.where(lane < HD, t, mark) for t in tiles], axis=0)
    q = q32.astype(BF)
    rows = heads * cw

    def step(j, carry, diagonal=False):
        top, acc = carry
        at = pl.ds(pl.multiple_of(j * chunk, chunk), chunk)
        s = lax.dot_general(q, kx[at, :], NT, preferred_element_type=F32)
        if diagonal:
            row = lax.broadcasted_iota(jnp.int32, (rows, chunk), 0) % cw + w * cw
            col = lax.broadcasted_iota(jnp.int32, (rows, chunk), 1)
            s = jnp.where(col <= row, s, NEG)
        new = jnp.maximum(top, jnp.max(s, axis=1, keepdims=True))
        p = jnp.exp(s - new).astype(BF)
        acc = acc * jnp.exp(top - new) + jnp.dot(p, vx[at, :], preferred_element_type=F32)
        return new, acc

    start = (jnp.full((rows, 1), NEG, F32), jnp.zeros((rows, 128), F32))
    carry = lax.fori_loop(0, c, step, start)
    top, acc = step(c, carry, True)
    total = acc[:, 0:1]
    out = acc / total
    o_ref[...] = join_heads([out[h * cw : (h + 1) * cw] for h in range(heads)], False).astype(BF)
    first, second, third = pieces_of(-(top + jnp.log(total)))
    wide_lane = lax.broadcasted_iota(jnp.int32, (rows, 128), 1)
    qe = jnp.where(wide_lane == HD + 3, first, q32)
    qe = jnp.where(wide_lane == HD + 4, second, qe)
    qe = jnp.where(wide_lane == HD + 5, third, qe)
    qe_ref[0, 0] = qe.astype(BF)


def forward_call(plan, scalars, q, kv, kf, kv_heads, heads):
    rows = plan.rows
    blocks = rows // plan.cw
    total = plan.total
    pairs = kv_heads * heads * total * rows // 2
    return pl.pallas_call(
        functools.partial(forward_kernel, plan, heads),
        grid_spec=pltpu.PrefetchScalarGridSpec(
            num_scalar_prefetch=1,
            grid=(kv_heads, blocks),
            in_specs=[
                pl.BlockSpec((plan.cw, heads * HD), lambda g, b, s: (b, g)),
                pl.BlockSpec((total, 128), lambda g, b, s: (0, g)),
                pl.BlockSpec((total, 128), lambda g, b, s: (0, 0)),
            ],
            out_specs=[
                pl.BlockSpec((plan.cw, heads * HD), lambda g, b, s: (b, g)),
                pl.BlockSpec((1, 1, heads * plan.cw, 128), lambda g, b, s: (g, b, 0, 0)),
            ],
            scratch_shapes=[pltpu.VMEM((total, 128), BF), pltpu.VMEM((total, 128), BF)],
        ),
        out_shape=[
            jax.ShapeDtypeStruct(q.shape, BF),
            jax.ShapeDtypeStruct((kv_heads, blocks, heads * plan.cw, 128), BF),
        ],
        cost_estimate=pl.CostEstimate(
            flops=8 * pairs * HD, bytes_accessed=8 * total * 128, transcendentals=pairs
        ),
        compiler_params=pltpu.CompilerParams(vmem_limit_bytes=48 << 20),
        name="attention_forward",
    )(scalars, q, kv, kf)


def backward_kernel(
    plan, heads, s_ref, qe_ref, kv_ref, kf_ref, o_ref, do_ref, dq_ref, dkv_ref, kx, vx, total
):
    cw, chunk = plan.cw, plan.chunk

    @pl.when(pl.program_id(1) == 0)
    def _():
        build_keys(plan, kv_ref, kf_ref, kx, vx)
        total[...] = jnp.zeros_like(total)

    w, c = block_place(plan, s_ref)
    rows = heads * cw
    lane = lax.broadcasted_iota(jnp.int32, (cw, 128), 1)
    o = split_heads(o_ref[...].astype(F32), heads, False)
    do = split_heads(do_ref[...].astype(F32), heads, False)
    marked = []
    for one, grad in zip(o, do):
        clean = jnp.where(lane >= HD, grad, 0.0)
        first, second, third = pieces_of(-jnp.sum(one * clean, axis=1, keepdims=True))
        tile = jnp.where(lane == 0, first, clean)
        tile = jnp.where(lane == 1, second, tile)
        marked.append(jnp.where(lane == 2, third, tile))
    dox32 = jnp.concatenate(marked, axis=0)
    wide_lane = lax.broadcasted_iota(jnp.int32, (rows, 128), 1)
    dox = dox32.astype(BF)
    do_clean = jnp.where(wide_lane >= HD, dox32, 0.0).astype(BF)
    q = qe_ref[0, 0]
    q_clean = jnp.where(wide_lane < HD, q.astype(F32), 0.0).astype(BF)

    def step(j, dq, diagonal=False):
        at = pl.ds(pl.multiple_of(j * chunk, chunk), chunk)
        key = kx[at, :]
        s = lax.dot_general(key, q, NT, preferred_element_type=F32)
        if diagonal:
            row = lax.broadcasted_iota(jnp.int32, (chunk, rows), 1) % cw + w * cw
            col = lax.broadcasted_iota(jnp.int32, (chunk, rows), 0)
            s = jnp.where(col <= row, s, NEG)
        p = jnp.exp(s)
        dp = lax.dot_general(vx[at, :], dox, NT, preferred_element_type=F32)
        ds = (p * dp).astype(BF)
        total[at, :] += jnp.dot(ds, q_clean, preferred_element_type=F32) + jnp.dot(
            p.astype(BF), do_clean, preferred_element_type=F32
        )
        return dq + lax.dot_general(ds, key, TN, preferred_element_type=F32)

    dq = lax.fori_loop(0, c, step, jnp.zeros((rows, 128), F32))
    dq = step(c, dq, True) * (HD ** -0.5)
    dq_ref[...] = join_heads([dq[h * cw : (h + 1) * cw] for h in range(heads)], True)

    @pl.when(pl.program_id(1) == pl.num_programs(1) - 1)
    def _():
        def put(c, carry):
            late = c >= plan.group
            owner = jnp.where(late, 2 * plan.group - 1 - c, c)
            for w in range(plan.wide):
                dst = pl.multiple_of(owner * plan.rows + w * 2 * cw + jnp.where(late, cw, 0), cw)
                src = pl.multiple_of(c * chunk + w * cw, cw)
                dkv_ref[pl.ds(dst, cw), :] = total[pl.ds(src, cw), :].astype(BF)
            return carry

        lax.fori_loop(0, 2 * plan.group, put, 0)


def backward_call(plan, scalars, qe, kv, kf, o, do, kv_heads, heads):
    rows = plan.rows
    blocks = rows // plan.cw
    total = plan.total
    pairs = kv_heads * heads * total * rows // 2
    return pl.pallas_call(
        functools.partial(backward_kernel, plan, heads),
        grid_spec=pltpu.PrefetchScalarGridSpec(
            num_scalar_prefetch=1,
            grid=(kv_heads, blocks),
            in_specs=[
                pl.BlockSpec((1, 1, heads * plan.cw, 128), lambda g, b, s: (g, b, 0, 0)),
                pl.BlockSpec((total, 128), lambda g, b, s: (0, g)),
                pl.BlockSpec((total, 128), lambda g, b, s: (0, 0)),
                pl.BlockSpec((plan.cw, heads * HD), lambda g, b, s: (b, g)),
                pl.BlockSpec((plan.cw, heads * HD), lambda g, b, s: (b, g)),
            ],
            out_specs=[
                pl.BlockSpec((plan.cw, heads * HD), lambda g, b, s: (b, g)),
                pl.BlockSpec((total, 128), lambda g, b, s: (0, g)),
            ],
            scratch_shapes=[
                pltpu.VMEM((total, 128), BF),
                pltpu.VMEM((total, 128), BF),
                pltpu.VMEM((total, 128), F32),
            ],
        ),
        out_shape=[
            jax.ShapeDtypeStruct(o.shape, F32),
            jax.ShapeDtypeStruct((total, kv_heads * 128), BF),
        ],
        cost_estimate=pl.CostEstimate(
            flops=20 * pairs * HD, bytes_accessed=8 * total * 128, transcendentals=pairs
        ),
        compiler_params=pltpu.CompilerParams(vmem_limit_bytes=56 << 20),
        name="attention_backward",
    )(scalars, qe, kv, kf, o, do)


def half_of(weight, seq_index, seq_count):
    part = weight.shape[0] // seq_count
    return lax.dynamic_slice_in_dim(weight, seq_index * part, part, 0)


def body(
    tokens, attn_gain, w_query, w_key, w_value, w_out, ffn_gain, w_gate, w_up, w_down,
    segment_ids, token_mask, out_grad,
):
    seq_count = lax.axis_size("seq")
    narrow = lax.axis_size("narrow")
    wide = lax.axis_size("wide")
    group = seq_count * narrow
    seq_index = lax.axis_index("seq")
    narrow_index = lax.axis_index("narrow")
    wide_index = lax.axis_index("wide")
    index = seq_index * narrow + narrow_index
    total = segment_ids.shape[0]
    plan = Plan(total, group, wide)
    chunk, cw, rows = plan.chunk, plan.cw, plan.rows
    own = rows // wide
    d_part = tokens.shape[1]
    d = d_part * narrow
    qw = w_query.shape[1]
    kw = w_key.shape[1]
    kv_heads = kw // HD
    heads = qw // kw
    ff = w_gate.shape[1]

    start_one = jnp.sum((segment_ids < 1).astype(jnp.int32))
    start_two = jnp.sum((segment_ids < 2).astype(jnp.int32))
    scalars = jnp.stack([index, start_one, start_two]).astype(jnp.int32)

    def to_rows(values):
        parts = values.reshape(group, chunk, d_part)
        parts = jnp.where(seq_index == 1, parts[::-1], parts)
        got = lax.all_to_all(parts, SN, 0, 0, tiled=True)
        got = got.reshape(2, narrow, wide, cw, d_part)
        return jnp.transpose(got, (2, 0, 3, 1, 4)).reshape(rows, d)

    def from_rows(values):
        parts = values.astype(BF).reshape(2, cw, narrow, d_part)
        parts = jnp.transpose(parts, (0, 2, 1, 3)).reshape(group, cw, d_part)
        got = lax.all_to_all(parts, SN, 0, 0, tiled=True)
        every = lax.all_gather(got, "wide", axis=0)
        every = jnp.where(seq_index == 1, every[:, ::-1], every)
        return jnp.transpose(every, (1, 0, 2, 3)).reshape(group * chunk, d_part)

    def gather_weight(weight):
        return lax.all_gather(half_of(weight, seq_index, seq_count), NS, axis=0, tiled=True)

    def scatter_grad(grad):
        mine = lax.psum_scatter(grad.astype(BF), NS, scatter_dimension=0, tiled=True)
        return lax.all_gather(mine, "seq", axis=0, tiled=True).astype(F32)

    def wide_scatter(values):
        return lax.psum_scatter(values.astype(BF), "wide", scatter_dimension=0, tiled=True).astype(F32)

    def wide_gather(values):
        return lax.all_gather(values, "wide", axis=0, tiled=True)

    def own_rows(values):
        return lax.dynamic_slice_in_dim(values, wide_index * own, own, 0)

    x_rows = to_rows(tokens)
    w_kv = jnp.concatenate(
        [w_key.reshape(d_part, kv_heads, 1, HD), w_value.reshape(d_part, kv_heads, 1, HD)], axis=2
    ).reshape(d_part, 2 * kw)
    w_qkv = gather_weight(jnp.concatenate([w_query, w_kv], axis=1))
    gains = lax.all_gather(jnp.stack([attn_gain, ffn_gain]), "narrow", axis=1, tiled=True)
    gain_one, gain_two = gains[0:1], gains[1:2]

    row = jnp.arange(rows, dtype=jnp.int32)
    row_chunk = jnp.where((row // cw) % 2 == 1, 2 * group - 1 - index, index)
    row_token = row_chunk * chunk + (row // (2 * cw)) * cw + row % cw
    row_start = jnp.where(row_token >= start_two, start_two, jnp.where(row_token >= start_one, start_one, 0))
    row_pos = (row_token - row_start).astype(F32)
    frequency = THETA ** (-2.0 * jnp.arange(HD // 2, dtype=F32) / HD)
    angles = row_pos[:, None] * jnp.tile(frequency, 4)[None, :]
    cos, sin = jnp.cos(angles), jnp.sin(angles)

    h_one, q, kv = qkv_call(x_rows, gain_one, w_qkv, cos, sin, qw)
    kv_all = lax.all_gather(kv, SN, axis=0, tiled=True)

    lane = jnp.arange(128, dtype=jnp.int32)[None, :]
    closed = (segment_ids[:, None] != lane - HD) | (token_mask[:, None] != 1)
    kf = jnp.where((lane >= HD) & (lane < HD + 3) & closed, NEG, 0.0)
    kf = jnp.where((lane >= HD + 3) & (lane < HD + 6), 1.0, kf).astype(BF)

    o, qe = forward_call(plan, scalars, q, kv_all, kf, kv_heads, heads)

    w_o = gather_weight(w_out).reshape(narrow, qw, d_part)
    w_gu = gather_weight(jnp.concatenate([w_gate, w_up], axis=1))
    w_dn = gather_weight(w_down).reshape(narrow, ff, d_part)

    def times_split(left, weight):
        out = lax.dot_general(left, weight, (((1,), (1,)), ((), ())), preferred_element_type=F32)
        return out.reshape(left.shape[0], d)

    def times_split_back(left, weight):
        left = left.reshape(left.shape[0], narrow, d_part)
        return lax.dot_general(left, weight, (((1, 2), (0, 2)), ((), ())), preferred_element_type=F32)

    x_own = own_rows(x_rows).astype(F32)
    x2 = x_own + wide_scatter(times_split(o, w_o))
    r2 = lax.rsqrt(jnp.mean(x2 * x2, axis=1, keepdims=True) + EPS)
    z2 = x2 * r2
    h_two = wide_gather((z2 * gain_two).astype(BF))
    gate = jnp.dot(h_two, w_gu[:, :ff], preferred_element_type=F32)
    up = jnp.dot(h_two, w_gu[:, ff:], preferred_element_type=F32)
    sig = jax.nn.sigmoid(gate)
    act = (gate * sig * up).astype(BF)
    result = from_rows(x2 + wide_scatter(times_split(act, w_dn)))

    row_valid = lax.dynamic_slice_in_dim(token_mask, seq_index * (group * chunk), group * chunk, 0)
    g_rows = to_rows(jnp.where(row_valid[:, None] == 1, out_grad, jnp.zeros_like(out_grad)))
    d_act = times_split_back(g_rows, w_dn)
    d_gate = d_act * up * sig * (1.0 + gate * (1.0 - sig))
    d_up = d_act * gate * sig
    dgu = jnp.concatenate([d_gate, d_up], axis=1).astype(BF)
    dh2 = wide_scatter(lax.dot_general(dgu, w_gu, NT, preferred_element_type=F32))
    grad_gain_two = jnp.sum(dh2 * z2, axis=0)
    dz2 = dh2 * gain_two
    dx2 = own_rows(g_rows).astype(F32) + r2 * (dz2 - z2 * jnp.mean(dz2 * z2, axis=1, keepdims=True))
    db = wide_gather(dx2.astype(BF))
    do = times_split_back(db, w_o).astype(BF)
    dq, dkv = backward_call(plan, scalars, qe, kv_all, kf, o, do, kv_heads, heads)
    dkv = lax.psum_scatter(dkv, SN, scatter_dimension=0, tiled=True).astype(F32)

    def turn_back(values):
        left, right = jnp.roll(values, -(HD // 2), 1), jnp.roll(values, HD // 2, 1)
        lanes = jnp.arange(values.shape[1])[None, :]
        turned = jnp.where(lanes % HD < HD // 2, -left, right)
        copies = values.shape[1] // 128
        return values * jnp.tile(cos, (1, copies)) - turned * jnp.tile(sin, (1, copies))

    is_value = (jnp.arange(2 * kw) % 128 >= HD)[None, :]
    dqkv = jnp.concatenate([turn_back(dq), jnp.where(is_value, dkv, turn_back(dkv))], axis=1).astype(BF)
    dh1 = wide_scatter(lax.dot_general(dqkv, w_qkv, NT, preferred_element_type=F32))
    r1 = lax.rsqrt(jnp.mean(x_own * x_own, axis=1, keepdims=True) + EPS)
    z1 = x_own * r1
    grad_gain_one = jnp.sum(dh1 * z1, axis=0)
    dz1 = dh1 * gain_one
    dx = dx2 + r1 * (dz1 - z1 * jnp.mean(dz1 * z1, axis=1, keepdims=True))
    input_grad = from_rows(dx).astype(F32)

    def tn(left, right):
        return lax.dot_general(left, right, TN, preferred_element_type=F32)

    grad_gu = scatter_grad(tn(h_two, dgu))
    grad_dn = scatter_grad(
        jnp.transpose(tn(act, g_rows).astype(BF).reshape(ff, narrow, d_part), (1, 0, 2)).reshape(narrow * ff, d_part)
    )
    grad_o = scatter_grad(
        jnp.transpose(tn(o, db).astype(BF).reshape(qw, narrow, d_part), (1, 0, 2)).reshape(narrow * qw, d_part)
    )
    grad_qkv = scatter_grad(tn(h_one, dqkv))
    gain_grads = lax.psum(jnp.stack([grad_gain_one, grad_gain_two]), ("seq", "narrow", "wide"))
    gain_grads = lax.dynamic_slice_in_dim(gain_grads, narrow_index * d_part, d_part, 1)
    grad_kv = grad_qkv[:, qw:].reshape(d_part, kv_heads, 2, HD)
    return (
        result,
        input_grad,
        gain_grads[0],
        grad_qkv[:, :qw],
        grad_kv[:, :, 0].reshape(d_part, kw),
        grad_kv[:, :, 1].reshape(d_part, kw),
        grad_o,
        gain_grads[1],
        grad_gu[:, :ff],
        grad_gu[:, ff:],
        grad_dn,
    )


def solution(mesh):
    width_in, width_out = P("narrow", "wide"), P("wide", "narrow")
    acts = P("seq", "narrow")
    return jax.shard_map(
        body,
        mesh=mesh,
        in_specs=(
            acts, P("narrow"), width_in, width_in, width_in, width_out, P("narrow"),
            width_in, width_in, width_out, P(), P(), acts,
        ),
        out_specs=(
            acts, acts, P("narrow"), width_in, width_in, width_in, width_out, P("narrow"),
            width_in, width_in, width_out,
        ),
        check_vma=False,
    )
```

time: 4990 us -> 1680 us (0.34)
  waiting for transfers between devices: 3270 us -> 871 us
  matrix products: 1040 us -> 158 us
  other arithmetic: 454 us -> 63 us
  Pallas kernels: 0 us -> 231 us
  blocking collectives: 68.5 us -> 226 us
    psum x4 -> x0, waiting for transfers between devices: 1120 us -> none  [the longest x3 1110 us: wide_total(): return lax.psum(values, 'wide')]
    unnamed x15 -> x20, waiting for transfers between devices: 1120 us -> 0.33 us
    dot_general x68 -> x12, matrix products: 1040 us -> 158 us  [the longest x4 53.6 us: tn(): return lax.dot_general(left, right, TN, preferred_element_type=F32)]
    pallas_call x0 -> x3, Pallas kernels: none -> 231 us  [the longest x1 131 us: backward_call(): pl.pallas_call(functools.partial(backward_kernel, plan, heads), grid_spec...]
    convert_element_type x16 -> x8, other arithmetic: 241 us -> 27.9 us  [the longest x2 5.3 us: scatter_grad(): return lax.all_gather(mine, 'seq', axis=0, tiled=True).astype(F32)]
    all_gather x5 -> x11, waiting for transfers between devices: 558 us -> 381 us  [the longest x2 148 us: wide_gather(): return lax.all_gather(values, 'wide', axis=0, tiled=True)]
    reduce_sum x13 -> x4, other arithmetic: 148 us -> 8.21 us  [the longest x1 3.24 us: body(): grad_gain_two = jnp.sum(dh2 * z2, axis=0)]
    all_to_all x0 -> x3, blocking collectives: none -> 119 us  [the longest x1 79.7 us: to_rows(): got = lax.all_to_all(parts, SN, 0, 0, tiled=True)]
  transfers between devices with their start and end apart: 14 -> 21, of which waited for: 14 -> 14; matrix products, arithmetic and copies ran while one was open for 4% -> 13% of each run, Pallas kernels for 0% -> 0%
where the time goes in v1:
time: 1680 us; the launch traced here: 1670 us
  waiting for transfers between devices  871 us (52%)
  Pallas kernels  231 us (14%)
  blocking collectives  226 us (13%)
  matrix products  158 us (9%)
  local copies, waits for them, and re-layouts  99 us (6%)
  other arithmetic  63 us (4%)
    reduce_scatter x4, waiting for transfers between devices, wide_scatter(): lax.psum_scatter(values.astype(BF), 'wide', scatter_dimension=0, tiled=True)  301 us
    reduce_scatter x4, waiting for transfers between devices, scatter_grad(): lax.psum_scatter(grad.astype(BF), NS, scatter_dimension=0, tiled=True)  188 us
    all_gather x2, waiting for transfers between devices, wide_gather(): return lax.all_gather(values, 'wide', axis=0, tiled=True)  148 us
    pallas_call x1, Pallas kernels, backward_call(): pl.pallas_call(functools.partial(backward_kernel, plan, heads), grid_spec...  131 us
    all_gather x2, waiting for transfers between devices, from_rows(): every = lax.all_gather(got, 'wide', axis=0)  116 us
    pallas_call x1, Pallas kernels, forward_call(): pl.pallas_call(functools.partial(forward_kernel, plan, heads), grid_spec=...  93.2 us
    all_gather x4, waiting for transfers between devices, gather_weight(): lax.all_gather(half_of(weight, seq_index, seq_count), NS, axis=0, tiled=T...  91 us
    all_to_all x1, blocking collectives, to_rows(): got = lax.all_to_all(parts, SN, 0, 0, tiled=True)  79.7 us
  transfers between devices with their start and end apart: 21, of which 14 were waited for; matrix products, arithmetic and copies ran while one was open for 13% of the time, Pallas kernels for 0%

profile of v1, /device:TPU:0, one launch (start us, length us, event | category | flops | bytes accessed | tf_op | source)
XLA Modules:
  0.0 1670.2 jit_solution(14339795208442636923)
XLA Ops:
  11.4 6.7 reverse_select_fusion.3
  18.1 5.3 all-to-all-start
  24.4 61.0 %all_gather.48 = f32[2,2048]{1,0:T(2,128)S(1)} all-gather(f32[2,512]{1,0:T(2,128)S(1)} %pad_maximum_fusion.10), channel_id=1, replica_groups=mesh['seq'=2,'narrow'=4,'wide'=4] {'narrow'}, dimensions={1}, use_global_device_ids=true | all-gather | bytes 20480 | tf_op jit(solution)/shard_map/all_gather | solution.py:387
  89.3 5.4 copy.66
  102.4 6.4 norm_qkv.1
  114.3 4.6 select_convert_fusion.kf_ref
  118.8 4.2 copy.71
  123.0 25.9 %all-gather.16.cloned.1.call-done.kv_ref = bf16[8192,256]{1,0:T(8,128)(2,1)} async-done(((bf16[1024,256]{1,0:T(8,128)(2,1)}), bf16[8192,256]{1,0:T(8,128)(2,1)}) %all-gather.16.cloned.1.call-update) | async-done | bytes 4194320 | tf_op jit(solution)/shard_map/all_gather | solution.py:400
  150.1 93.2 %attention_forward.1 = (bf16[1024,512]{1,0:T(8,128)(2,1)S(1)}, bf16[2,8,512,128]{3,2,1,0:T(8,128)(2,1)S(1)}) custom-call(s32[3]{0:T(128)S(1)} %pad_add_fusion.s_ref, bf16[1024,512]{1,0:T(8,128)(2,1)S(1)} %copy-done.11, bf16[8192,256]{1,0:T(8,128)(2,1)} %all-gather.16.cloned.1.call-done.kv_ref, bf16[8192,128]{1,0:T(8,128)(2,1)} %select_convert_fusion.kf_ref), custom_call_target="tpu_custom_call" | custom-call | flops 17179869184 | bytes 8388608 | tf_op jit(solution)/shard_map/attention_forward/pallas_call | solution.py:188
  245.7 4.4 convolution_convert_fusion.3
  251.3 76.2 %reduce-scatter.10.cloned.1.call-done = bf16[256,2048]{1,0:T(8,128)(2,1)} async-done(((bf16[1024,2048]{1,0:T(8,128)(2,1)}), bf16[256,2048]{1,0:T(8,128)(2,1)}) %reduce-scatter.10.cloned.1.call-update) | async-done | bytes 1048592 | tf_op jit(solution)/shard_map/reduce_scatter | solution.py:374
  339.0 79.7 %all_to_all.20 = bf16[8,512,512]{2,1,0:T(8,128)(2,1)S(1)} all-to-all(bf16[8,512,512]{2,1,0:T(8,128)(2,1)S(1)} %reverse_select_fusion.1), channel_id=1, replica_groups=mesh['seq'=2,'narrow'=4,'wide'=4] {'seq','narrow'}, dimensions={0} | all-to-all | bytes 8388608 | tf_op jit(solution)/shard_map/all_to_all | solution.py:354
  423.3 14.5 fusion.76
  437.8 67.2 %all-gather.20.cloned.1.call-done = bf16[1024,2048]{1,0:T(8,128)(2,1)} async-done(((bf16[256,2048]{1,0:T(8,128)(2,1)}), bf16[1024,2048]{1,0:T(8,128)(2,1)}) %all-gather.20.cloned.1.call-update) | async-done | bytes 4194320 | tf_op jit(solution)/shard_map/all_gather | solution.py:377
  505.0 91.0 %all-gather.22.cloned.1.call-done = bf16[2048,4096]{1,0:T(8,128)(2,1)} async-done(((bf16[256,4096]{1,0:T(8,128)(2,1)}), bf16[2048,4096]{1,0:T(8,128)(2,1)}) %all-gather.22.cloned.1.call-update) | async-done | bytes 16777232 | tf_op jit(solution)/shard_map/all_gather | solution.py:367
  596.0 14.4 fusion.2
  610.5 21.7 %fusion.6 = (bf16[1024,2048]{1,0:T(8,128)(2,1)}, bf16[1024,2048]{1,0:T(8,128)(2,1)}, bf16[1024,2048]{1,0:T(8,128)(2,1)}) fusion(f32[1024,2048,1]{1,0,2:T(8,128)} %fusion.76, f32[1024,2048]{1,0:T(8,128)} %fusion.2, bf16[1024,2048]{1,0:T(8,128)(2,1)} %all-gather.20.cloned.1.call-done, bf16[2048,4096]{1,0:T(8,128)(2,1)} %all-gather.22.cloned.1.call-done), kind=kOutput, calls=%fused_computation.10 | convolution fusion | flops 8623489024 | bytes 41943040 | tf_op jit(solution)/shard_map/dot_general | solution.py:427
  632.1 24.0 %fusion.14 = bf16[1024,2048]{1,0:T(8,128)(2,1)} fusion(bf16[2048,4096]{1,0:T(8,128)(2,1)} %all-gather.22.cloned.1.call-done, bf16[1024,2048]{1,0:T(8,128)(2,1)} %get-tuple-element.66, bf16[1024,2048]{1,0:T(8,128)(2,1)} %get-tuple-element.65), kind=kOutput, calls=%fused_computation.30 | convolution fusion | flops 17198743552 | bytes 29360128 | tf_op jit(solution)/shard_map/dot_general | solution.py:438
  656.2 5.4 copy.75
  665.1 68.0 %reduce-scatter.14.cloned.1.call-done = bf16[256,2048]{1,0:T(8,128)(2,1)} async-done(((bf16[1024,2048]{1,0:T(8,128)(2,1)}), bf16[256,2048]{1,0:T(8,128)(2,1)}) %reduce-scatter.14.cloned.1.call-update) | async-done | bytes 1048592 | tf_op jit(solution)/shard_map/reduce_scatter | solution.py:374
  740.4 81.2 %all-gather.26.cloned.1.call-done = bf16[1024,2048]{1,0:T(8,128)(2,1)} async-done(((bf16[256,2048]{1,0:T(8,128)(2,1)}), bf16[1024,2048]{1,0:T(8,128)(2,1)}) %all-gather.26.cloned.1.call-update) | async-done | bytes 4194320 | tf_op jit(solution)/shard_map/all_gather | solution.py:377
  821.6 6.2 bitcast_convert_fusion.do_ref
  827.8 131.1 %attention_backward.1 = (f32[1024,512]{1,0:T(8,128)}, bf16[8192,256]{1,0:T(8,128)(2,1)}) custom-call(s32[3]{0:T(128)} %copy-done.4, bf16[2,8,512,128]{3,2,1,0:T(8,128)(2,1)} %copy-done.12, bf16[8192,256]{1,0:T(8,128)(2,1)} %all-gather.16.cloned.1.call-done.kv_ref, bf16[8192,128]{1,0:T(8,128)(2,1)} %select_convert_fusion.kf_ref, bf16[1024,512]{1,0:T(8,128)(2,1)} %copy-done.8, ...), custom_call_target="tpu_custom_call" | custom-call | flops 42949672960 | bytes 8388608 | tf_op jit(solution)/shard_map/attention_backward/pallas_call | solution.py:284
  959.0 14.0 convolution_convert_fusion.1
  972.9 11.5 copy.82
  984.9 25.4 %convolution_convert_fusion = bf16[2048,4096]{1,0:T(8,128)(2,1)} fusion(bf16[1024,2048]{1,0:T(8,128)(2,1)} %all-gather.20.cloned.1.call-done, bf16[1024,2048]{1,0:T(8,128)(2,1)} %get-tuple-element.66, bf16[1024,2048]{1,0:T(8,128)(2,1)} %get-tuple-element.65), kind=kOutput, calls=%fused_computation | convolution fusion | flops 17205035008 | bytes 29360128 | tf_op jit(solution)/shard_map/dot_general | solution.py:465
  1022.1 5.0 convolution_convert_fusion.4
  1027.2 11.5 copy.72
  1038.7 13.9 convolution_convert_fusion.2
  1052.6 31.6 %reduce-scatter.26.cloned.1.call-done = bf16[1024,512]{1,0:T(8,128)(2,1)} async-done(((bf16[8192,512]{1,0:T(8,128)(2,1)}), bf16[1024,512]{1,0:T(8,128)(2,1)}) %reduce-scatter.26.cloned.1.call-update) | async-done | bytes 1048592 | tf_op jit(solution)/shard_map/reduce_scatter | solution.py:370
  1084.6 5.9 convolution_convert_fusion.6
  1095.8 8.4 convolution_convert_fusion.5
  1104.3 99.4 %reduce-scatter.24.cloned.1.call-done = bf16[256,4096]{1,0:T(8,128)(2,1)} async-done(((bf16[2048,4096]{1,0:T(8,128)(2,1)}), bf16[256,4096]{1,0:T(8,128)(2,1)}) %reduce-scatter.24.cloned.1.call-update) | async-done | bytes 2097168 | tf_op jit(solution)/shard_map/reduce_scatter | solution.py:370
  1203.8 79.5 %reduce-scatter.18.cloned.1.call-done = bf16[256,2048]{1,0:T(8,128)(2,1)} async-done(((bf16[1024,2048]{1,0:T(8,128)(2,1)}), bf16[256,2048]{1,0:T(8,128)(2,1)}) %reduce-scatter.18.cloned.1.call-update) | async-done | bytes 1048592 | tf_op jit(solution)/shard_map/reduce_scatter | solution.py:374
  1285.7 77.8 %reduce-scatter.12.cloned.1.call-done = bf16[256,2048]{1,0:T(8,128)(2,1)} async-done(((bf16[1024,2048]{1,0:T(8,128)(2,1)}), bf16[256,2048]{1,0:T(8,128)(2,1)}) %reduce-scatter.12.cloned.1.call-update) | async-done | bytes 1048592 | tf_op jit(solution)/shard_map/reduce_scatter | solution.py:374
  1363.5 4.9 fusion.23
  1370.5 18.6 %all_to_all.21 = bf16[8,128,512]{2,1,0:T(8,128)(2,1)} all-to-all(bf16[8,128,512]{2,1,0:T(8,128)(2,1)S(1)} %bitcast.156), channel_id=1, replica_groups=mesh['seq'=2,'narrow'=4,'wide'=4] {'seq','narrow'}, dimensions={0} | all-to-all | bytes 2097152 | tf_op jit(solution)/shard_map/all_to_all | solution.py:361
  1390.1 21.0 %all_to_all.22 = bf16[8,128,512]{2,1,0:T(8,128)(2,1)} all-to-all(bf16[8,128,512]{2,1,0:T(8,128)(2,1)S(1)} %bitcast.157), channel_id=1, replica_groups=mesh['seq'=2,'narrow'=4,'wide'=4] {'seq','narrow'}, dimensions={0} | all-to-all | bytes 2097152 | tf_op jit(solution)/shard_map/all_to_all | solution.py:361
  1411.2 4.2 convert_element_type.133
  1415.4 9.8 reduce-scatter.22.cloned.1.call-done
  1428.6 47.0 %reduce-scatter.20.cloned.1.call-done = bf16[256,768]{1,0:T(8,128)(2,1)} async-done(((bf16[2048,768]{1,0:T(8,128)(2,1)}), bf16[256,768]{1,0:T(8,128)(2,1)}) %reduce-scatter.20.cloned.1.call-update) | async-done | bytes 393232 | tf_op jit(solution)/shard_map/reduce_scatter | solution.py:370
  1481.5 40.9 %psum.7 = f32[2,2048]{1,0:T(2,128)S(1)} all-reduce(f32[2,2048]{1,0:T(2,128)S(1)} %pad_maximum_fusion.9), channel_id=1, replica_groups=mesh['seq'=2,'narrow'=4,'wide'=4] {'seq','narrow','wide'}, use_global_device_ids=true, to_apply=%region_13.14 | all-reduce | flops 4096 | bytes 32768 | tf_op jit(solution)/shard_map/psum | solution.py:475
  1523.1 6.7 fusion.68
  1529.8 44.8 %all-gather.34.cloned.1.call-done = bf16[32,128,512]{2,1,0:T(8,128)(2,1)} async-done(((bf16[8,128,512]{2,1,0:T(8,128)(2,1)}), bf16[32,128,512]{2,1,0:T(8,128)(2,1)}) %all-gather.34.cloned.1.call-update) | async-done | bytes 4194320 | tf_op jit(solution)/shard_map/all_gather | solution.py:362
  1574.6 5.1 convert_bitcast_fusion
  1579.7 4.6 copy.79
  1584.3 70.9 %all-gather.32.cloned.1.call-done = bf16[32,128,512]{2,1,0:T(8,128)(2,1)} async-done(((bf16[8,128,512]{2,1,0:T(8,128)(2,1)}), bf16[32,128,512]{2,1,0:T(8,128)(2,1)}) %all-gather.32.cloned.1.call-update) | async-done | bytes 4194320 | tf_op jit(solution)/shard_map/all_gather | solution.py:362
  1655.2 5.1 fusion.10
  (187 shorter events, 89.6 us)
Async XLA Ops:
  7.2 243.0 %copy-start = (bf16[2048,512]{1,0:T(8,128)(2,1)S(1)}, bf16[2048,512]{1,0:T(8,128)(2,1)}, u32[]{:S(2)}) copy-start(bf16[2048,512]{1,0:T(8,128)(2,1)} %param.22) | copy-start | bytes 6291460
  7.2 90.9 %all-gather.14.cloned.1.call-start = ((), (), s32[]{:S(2)}) async-start(), calls=%async_computation.13 | async-start | bytes 3538944 | tf_op jit(solution)/shard_map/all_gather | solution.py:367
  18.1 5.4 copy-start.27
  18.1 6.3 copy-start.35
  18.1 6.3 copy-start.36
  18.1 67.3 %copy-start.26 = (s32[8192]{0:T(1024)S(1)}, s32[8192]{0:T(1024)}, u32[]{:S(2)}) copy-start(s32[8192]{0:T(1024)} %param.23) | copy-start | bytes 98308
  18.1 71.2 %all-to-all-start = ((bf16[8,512,512]{2,1,0:T(8,128)(2,1)}), bf16[8,512,512]{2,1,0:T(8,128)(2,1)}, u32[]{:S(2)}, u32[]{:S(2)}) async-start(bf16[8,512,512]{2,1,0:T(8,128)(2,1)} %reverse_select_fusion.3), calls=%async_computation | async-start | bytes 8388608 | tf_op jit(solution)/shard_map/all_to_all | solution.py:354
  23.4 95.4 %all-gather.18.cloned.1.call-start = ((), (), s32[]{:S(2)}) async-start(), calls=%async_computation.15 | async-start | bytes 2359296 | tf_op jit(solution)/shard_map/all_gather | solution.py:367
  24.2 124.6 %all-gather.16.cloned.1.call-start = ((), (), s32[]{:S(2)}) async-start(), calls=%async_computation.14 | async-start | bytes 4718592 | tf_op jit(solution)/shard_map/all_gather | solution.py:400
  89.3 647.0 %copy-start.24 = (f32[1,2048]{1,0:T(1,128)}, f32[1,2048]{1,0:T(1,128)S(1)}, u32[]{:S(2)}) copy-start(f32[1,2048]{1,0:T(1,128)S(1)} %get-tuple-element.84) | copy-start | bytes 24580
  98.1 2.4 copy-start.2
  102.4 11.8 copy-start.28
  112.6 214.8 %reduce-scatter.10.cloned.1.call-start = ((), (), s32[]{:S(2)}) async-start(), calls=%async_computation.16 | async-start | bytes 5242880 | tf_op jit(solution)/shard_map/reduce_scatter | solution.py:374
  114.2 129.1 %copy-start.4 = (s32[3]{0:T(128)}, s32[3]{0:T(128)S(1)}, u32[]{:S(2)}) copy-start(s32[3]{0:T(128)S(1)} %pad_add_fusion.s_ref) | copy-start | bytes 40
  150.1 95.6 %copy-start.20 = (bf16[4,512,512]{2,1,0:T(8,128)(2,1)S(1)}, bf16[4,512,512]{2,1,0:T(8,128)(2,1)}, u32[]{:S(2)}) copy-start(bf16[4,512,512]{2,1,0:T(8,128)(2,1)} %copy.71) | copy-start | bytes 6291460
  250.1 173.2 %all-gather.24.cloned.1.call-start = ((), (), s32[]{:S(2)}) async-start(), calls=%async_computation.19 | async-start | bytes 9437184 | tf_op jit(solution)/shard_map/all_gather | solution.py:367
  251.2 81.2 %copy-start.19 = (bf16[512,2048]{1,0:T(8,128)(2,1)S(1)}, bf16[512,2048]{1,0:T(8,128)(2,1)}, u32[]{:S(2)}) copy-start(bf16[512,2048]{1,0:T(8,128)(2,1)} %param.20) | copy-start | bytes 6291460
  251.2 253.8 %all-gather.20.cloned.1.call-start = ((), (), s32[]{:S(2)}) async-start(), calls=%async_computation.17 | async-start | bytes 5242880 | tf_op jit(solution)/shard_map/all_gather | solution.py:377
  329.4 406.9 %copy-start.30 = (f32[256]{0:T(256)}, f32[256]{0:T(256)S(1)}, u32[]{:S(2)}) copy-start(f32[256]{0:T(256)S(1)} %add_rsqrt_fusion.1) | copy-start | bytes 3076
  332.3 263.7 %all-gather.22.cloned.1.call-start = ((), (), s32[]{:S(2)}) async-start(), calls=%async_computation.18 | async-start | bytes 18874368 | tf_op jit(solution)/shard_map/all_gather | solution.py:367
  335.2 397.9 %reduce-scatter.14.cloned.1.call-start = ((), (), s32[]{:S(2)}) async-start(), calls=%async_computation.21 | async-start | bytes 5242880 | tf_op jit(solution)/shard_map/reduce_scatter | solution.py:374
  418.7 2.1 copy-start.13
  656.1 165.4 %all-gather.26.cloned.1.call-start = ((), (), s32[]{:S(2)}) async-start(), calls=%async_computation.22 | async-start | bytes 5242880 | tf_op jit(solution)/shard_map/all_gather | solution.py:377
  661.6 71.4 %copy-start.14 = (bf16[256,2048]{1,0:T(8,128)(2,1)S(1)}, bf16[256,2048]{1,0:T(8,128)(2,1)}, u32[]{:S(2)}) copy-start(bf16[256,2048]{1,0:T(8,128)(2,1)} %reduce-scatter.10.cloned.1.call-done) | copy-start | bytes 3145732
  736.3 91.5 %copy-start.32 = (f32[256]{0:T(256)}, f32[256]{0:T(256)S(1)}, u32[]{:S(2)}) copy-start(f32[256]{0:T(256)S(1)} %broadcast_multiply_fusion.1) | copy-start | bytes 3076
  740.1 275.9 %reduce-scatter.16.cloned.1.call-start = ((), (), s32[]{:S(2)}) async-start(), calls=%async_computation.23 | async-start | bytes 4718592 | tf_op jit(solution)/shard_map/reduce_scatter | solution.py:445
  958.9 125.4 %reduce-scatter.26.cloned.1.call-start = ((), (), s32[]{:S(2)}) async-start(), calls=%async_computation.29 | async-start | bytes 9437184 | tf_op jit(solution)/shard_map/reduce_scatter | solution.py:370
  984.5 219.2 %reduce-scatter.24.cloned.1.call-start = ((), (), s32[]{:S(2)}) async-start(), calls=%async_computation.27 | async-start | bytes 18874368 | tf_op jit(solution)/shard_map/reduce_scatter | solution.py:370
  1010.3 273.0 %reduce-scatter.18.cloned.1.call-start = ((), (), s32[]{:S(2)}) async-start(), calls=%async_computation.24 | async-start | bytes 5242880 | tf_op jit(solution)/shard_map/reduce_scatter | solution.py:374
  1017.2 2.4 copy-start.17
  1019.3 2.2 copy-start.6
  1019.3 2.9 copy-start.21
  1027.2 336.3 %reduce-scatter.12.cloned.1.call-start = ((), (), s32[]{:S(2)}) async-start(), calls=%async_computation.20 | async-start | bytes 5242880 | tf_op jit(solution)/shard_map/reduce_scatter | solution.py:374
  1052.6 32.0 %copy-start.9 = (bf16[1024,512]{1,0:T(8,128)(2,1)S(1)}, bf16[1024,512]{1,0:T(8,128)(2,1)}, u32[]{:S(2)}) copy-start(bf16[1024,512]{1,0:T(8,128)(2,1)} %copy-done.8) | copy-start | bytes 3145732
  1052.6 358.6 %all-gather.30.cloned.1.call-start = ((), (), s32[]{:S(2)}) async-start(), calls=%async_computation.30 | async-start | bytes 3145728 | tf_op jit(solution)/shard_map/all_gather | solution.py:371
  1084.3 340.8 %reduce-scatter.22.cloned.1.call-start = ((), (), s32[]{:S(2)}) async-start(), calls=%async_computation.26 | async-start | bytes 2359296 | tf_op jit(solution)/shard_map/reduce_scatter | solution.py:370
  1095.7 379.9 %reduce-scatter.20.cloned.1.call-start = ((), (), s32[]{:S(2)}) async-start(), calls=%async_computation.25 | async-start | bytes 3538944 | tf_op jit(solution)/shard_map/reduce_scatter | solution.py:370
  1104.2 99.6 %copy-start.34 = (f32[256]{0:T(256)S(1)}, f32[256]{0:T(256)}, u32[]{:S(2)}) copy-start(f32[256]{0:T(256)} %get-tuple-element.62) | copy-start | bytes 3076
  1104.2 259.3 %copy-start.15 = (bf16[256,2048]{1,0:T(8,128)(2,1)S(1)}, bf16[256,2048]{1,0:T(8,128)(2,1)}, u32[]{:S(2)}) copy-start(bf16[256,2048]{1,0:T(8,128)(2,1)} %reduce-scatter.10.cloned.1.call-done) | copy-start | bytes 3145732
  1104.2 259.3 %copy-start.18 = (bf16[256,2048]{1,0:T(8,128)(2,1)S(1)}, bf16[256,2048]{1,0:T(8,128)(2,1)}, u32[]{:S(2)}) copy-start(bf16[256,2048]{1,0:T(8,128)(2,1)} %reduce-scatter.14.cloned.1.call-done) | copy-start | bytes 3145732
  1104.2 259.3 %copy-start.25 = (f32[1,2048]{1,0:T(1,128)S(1)}, f32[1,2048]{1,0:T(1,128)}, u32[]{:S(2)}) copy-start(f32[1,2048]{1,0:T(1,128)} %copy-done.24) | copy-start | bytes 24580
  1104.2 259.3 %copy-start.31 = (f32[256]{0:T(256)S(1)}, f32[256]{0:T(256)}, u32[]{:S(2)}) copy-start(f32[256]{0:T(256)} %copy-done.30) | copy-start | bytes 3076
  1104.2 259.3 %copy-start.33 = (f32[256]{0:T(256)S(1)}, f32[256]{0:T(256)}, u32[]{:S(2)}) copy-start(f32[256]{0:T(256)} %copy-done.32) | copy-start | bytes 3076
  1104.2 418.8 %all-gather.28.cloned.1.call-start = ((), (), s32[]{:S(2)}) async-start(), calls=%async_computation.28 | async-start | bytes 6291456 | tf_op jit(solution)/shard_map/all_gather | solution.py:371
  1203.7 370.9 %all-gather.34.cloned.1.call-start = ((), (), s32[]{:S(2)}) async-start(), calls=%async_computation.32 | async-start | bytes 5242880 | tf_op jit(solution)/shard_map/all_gather | solution.py:362
  1389.0 266.2 %all-gather.32.cloned.1.call-start = ((), (), s32[]{:S(2)}) async-start(), calls=%async_computation.31 | async-start | bytes 5242880 | tf_op jit(solution)/shard_map/all_gather | solution.py:362
  1427.5 54.0 %copy-start.29 = (f32[2048]{0:T(1024)S(1)}, f32[2048]{0:T(1024)}, u32[]{:S(2)}) copy-start(f32[2048]{0:T(1024)} %get-tuple-element.58) | copy-start | bytes 24580
  1655.2 7.6 copy-start.1
  (10 other events, 13.4 us)
Sparse Core Ops, SparseCore 0:
  11.5 68.2 all-gather.13
  82.3 26.9 all-gather.17
  112.7 36.1 all-gather.15
  250.2 77.1 reduce-scatter.9
  329.9 92.1 all-gather.23
  424.2 80.7 all-gather.19
  507.6 88.3 all-gather.21
  656.3 76.7 reduce-scatter.13
  740.3 81.2 all-gather.25
  959.0 50.0 reduce-scatter.15
  1013.0 71.2 reduce-scatter.25
  1087.7 115.9 reduce-scatter.23
  1206.6 76.7 reduce-scatter.17
  1286.2 77.2 reduce-scatter.11
  1364.9 11.2 all-gather.29
  1379.9 45.2 reduce-scatter.21
  1429.3 46.2 reduce-scatter.19
  1477.0 13.6 all-gather.27
  1492.3 82.2 all-gather.33
  1576.0 79.1 all-gather.31

commit v2 on v1

v2 whole, which is shorter than its diff:
```python
import functools

import jax
import jax.numpy as jnp
from jax import lax
from jax.experimental import pallas as pl
from jax.experimental.pallas import tpu as pltpu
from jax.sharding import PartitionSpec as P

HD = 64
EPS = 1e-05
THETA = 500000.0
NEG = -1e30
SN = ("seq", "narrow")
NS = ("narrow", "seq")
BF = jnp.bfloat16
F32 = jnp.float32
NT = (((1,), (1,)), ((), ()))
TN = (((0,), (0,)), ((), ()))


def pieces_of(value):
    first = value.astype(BF).astype(F32)
    second = (value - first).astype(BF).astype(F32)
    third = (value - first - second).astype(BF).astype(F32)
    return first, second, third


class Plan:
    def __init__(self, total, group, wide):
        self.total, self.group, self.wide = total, group, wide
        self.chunk = total // (2 * group)
        self.cw = self.chunk // wide
        self.rows = 2 * self.chunk
        self.own = 2 * self.cw


def block_of(plan, s_ref, r):
    return lax.rem(s_ref[3] + r, plan.wide)


def near_of(plan, z, p):
    side = jnp.minimum(z, plan.wide - 1 - z)
    both = jnp.where(lax.rem(p, 2) == 1, z + (p + 1) // 2, z - p // 2)
    one = jnp.where(z <= plan.wide - 1 - z, z + p - side, z - p + side)
    return jnp.where(p <= 2 * side, both, one)


def turn(values, sign):
    width = values.shape[1]
    lane = lax.broadcasted_iota(jnp.int32, values.shape, 1)
    left, right = pltpu.roll(values, width - HD // 2, 1), pltpu.roll(values, HD // 2, 1)
    return jnp.where(lane % HD < HD // 2, -sign * left, sign * right)


def widen(table, width):
    return jnp.concatenate([table] * (width // 128), axis=1) if width > 128 else table


def qkv_kernel(plan, qw, s_ref, x_ref, gain_ref, w_ref, cos_ref, sin_ref, h_ref, q_ref, kv_ref, own_ref, x_scr):
    narrow = plan.group // 2
    part = x_ref.shape[3]
    for half in range(2):
        for n in range(narrow):
            x_scr[half * plan.cw : (half + 1) * plan.cw, n * part : (n + 1) * part] = x_ref[
                s_ref[0] ^ (half * narrow + n), 0
            ]
    low = x_scr[...]

    @pl.when(pl.program_id(0) == 0)
    def _():
        own_ref[...] = low

    x = low.astype(F32)
    mean = jnp.mean(x * x, axis=1, keepdims=True)
    h = (x * lax.rsqrt(mean + EPS) * gain_ref[...]).astype(BF)
    h_ref[...] = h
    t = jnp.dot(h, w_ref[...], preferred_element_type=F32)
    width = t.shape[1]
    lane = lax.broadcasted_iota(jnp.int32, t.shape, 1)
    plain = (lane >= qw) & (lane % 128 >= HD)
    out = jnp.where(plain, t, t * widen(cos_ref[...], width) + turn(t, 1.0) * widen(sin_ref[...], width))
    q_ref[...] = (out[:, :qw] * (HD ** -0.5)).astype(BF)
    kv_ref[...] = out[:, qw:].astype(BF)


def qkv_call(plan, scalars, x, gain, w, cos, sin, qw):
    part = x.shape[3]
    d = part * plan.group // 2
    width = w.shape[1]
    rows, bm = plan.rows, plan.own
    return pl.pallas_call(
        functools.partial(qkv_kernel, plan, qw),
        grid_spec=pltpu.PrefetchScalarGridSpec(
            num_scalar_prefetch=1,
            grid=(plan.wide,),
            in_specs=[
                pl.BlockSpec((plan.group, 1, plan.cw, part), lambda r, s: (0, block_of(plan, s, r), 0, 0)),
                pl.BlockSpec((1, d), lambda r, s: (0, 0)),
                pl.BlockSpec((d, width), lambda r, s: (0, 0)),
                pl.BlockSpec((bm, 128), lambda r, s: (r, 0)),
                pl.BlockSpec((bm, 128), lambda r, s: (r, 0)),
            ],
            out_specs=[
                pl.BlockSpec((bm, d), lambda r, s: (r, 0)),
                pl.BlockSpec((bm, qw), lambda r, s: (r, 0)),
                pl.BlockSpec((bm, width - qw), lambda r, s: (r, 0)),
                pl.BlockSpec((bm, d), lambda r, s: (0, 0)),
            ],
            scratch_shapes=[pltpu.VMEM((bm, d), BF)],
        ),
        out_shape=[
            jax.ShapeDtypeStruct((rows, d), BF),
            jax.ShapeDtypeStruct((rows, qw), BF),
            jax.ShapeDtypeStruct((rows, width - qw), BF),
            jax.ShapeDtypeStruct((bm, d), BF),
        ],
        cost_estimate=pl.CostEstimate(
            flops=2 * rows * d * width, bytes_accessed=4 * rows * d + 2 * d * width, transcendentals=rows
        ),
        compiler_params=pltpu.CompilerParams(vmem_limit_bytes=40 << 20),
        name="norm_qkv",
    )(scalars, x, gain, w, cos, sin)


def keys_kernel(plan, s_ref, kv_ref, kf_ref, kx_ref, vx_ref):
    cw, group = plan.cw, plan.group
    lane = lax.broadcasted_iota(jnp.int32, (cw, 128), 1)
    ones = jnp.where(lane < 3, 1.0, 0.0).astype(BF)

    @pl.loop(0, 2 * group)
    def _(c):
        late = c >= group
        owner = jnp.where(late, 2 * group - 1 - c, c)
        for r in range(plan.wide):
            at = pl.ds(pl.multiple_of(c * plan.chunk + block_of(plan, s_ref, r) * cw, cw), cw)
            kv = kv_ref[s_ref[0] ^ owner, r, jnp.where(late, 1, 0)]
            kx_ref[0, at, :] = jnp.where(lane < HD, kv, kf_ref[at, :])
            vx_ref[0, at, :] = jnp.where(lane < HD, ones, kv)


def keys_call(plan, scalars, kv, kf, kv_heads):
    group, total = plan.group, plan.total
    kv = kv.reshape(group, plan.wide, 2, plan.cw, kv_heads * 128)
    out = pl.BlockSpec((1, total, 128), lambda g, s: (g, 0, 0))
    return pl.pallas_call(
        functools.partial(keys_kernel, plan),
        grid_spec=pltpu.PrefetchScalarGridSpec(
            num_scalar_prefetch=1,
            grid=(kv_heads,),
            in_specs=[
                pl.BlockSpec((group, plan.wide, 2, plan.cw, 128), lambda g, s: (0, 0, 0, 0, g)),
                pl.BlockSpec((total, 128), lambda g, s: (0, 0)),
            ],
            out_specs=[out, out],
        ),
        out_shape=[jax.ShapeDtypeStruct((kv_heads, total, 128), BF)] * 2,
        cost_estimate=pl.CostEstimate(
            flops=kv_heads * total * 128, bytes_accessed=8 * kv_heads * total * 128, transcendentals=0
        ),
        compiler_params=pltpu.CompilerParams(vmem_limit_bytes=40 << 20),
        name="keys",
    )(scalars, kv, kf)


def split_heads(block, heads, low):
    tiles = []
    for h in range(heads):
        tile = block[:, (h // 2) * 128 : (h // 2 + 1) * 128]
        if (h % 2 == 0) != low:
            tile = pltpu.roll(tile, HD, 1)
        tiles.append(tile)
    return tiles


def join_heads(tiles, low):
    rows = tiles[0].shape[0]
    lane = lax.broadcasted_iota(jnp.int32, (rows, 128), 1)
    pairs = []
    for h in range(0, len(tiles), 2):
        first, second = tiles[h], tiles[h + 1]
        if low:
            second = pltpu.roll(second, HD, 1)
        else:
            first = pltpu.roll(first, HD, 1)
        pairs.append(jnp.where(lane < HD, first, second))
    return jnp.concatenate(pairs, axis=1)


def chunk_of(plan, s_ref, half):
    return jnp.where(half == 1, 2 * plan.group - 1 - s_ref[0], s_ref[0])


def forward_kernel(plan, heads, r, s_ref, q_ref, kx, vx, o_ref, qe_ref):
    cw, chunk = plan.cw, plan.chunk
    w, c = block_of(plan, s_ref, r), chunk_of(plan, s_ref, pl.program_id(1))
    lane = lax.broadcasted_iota(jnp.int32, (cw, 128), 1)
    token = c * chunk + w * cw + lax.broadcasted_iota(jnp.int32, (cw, 128), 0)
    segment = (token >= s_ref[1]).astype(jnp.int32) + (token >= s_ref[2]).astype(jnp.int32)
    mark = jnp.where(lane == HD + segment, 1.0, 0.0)
    tiles = split_heads(q_ref[...].astype(F32), heads, True)
    q32 = jnp.concatenate([jnp.where(lane < HD, t, mark) for t in tiles], axis=0)
    q = q32.astype(BF)
    rows = heads * cw

    def step(j, carry, diagonal=False):
        top, acc = carry
        at = pl.ds(pl.multiple_of(j * chunk, chunk), chunk)
        s = lax.dot_general(q, kx[0, at, :], NT, preferred_element_type=F32)
        if diagonal:
            row = lax.broadcasted_iota(jnp.int32, (rows, chunk), 0) % cw + w * cw
            col = lax.broadcasted_iota(jnp.int32, (rows, chunk), 1)
            s = jnp.where(col <= row, s, NEG)
        new = jnp.maximum(top, jnp.max(s, axis=1, keepdims=True))
        p = jnp.exp(s - new).astype(BF)
        acc = acc * jnp.exp(top - new) + jnp.dot(p, vx[0, at, :], preferred_element_type=F32)
        return new, acc

    start = (jnp.full((rows, 1), NEG, F32), jnp.zeros((rows, 128), F32))
    carry = lax.fori_loop(0, c, step, start)
    top, acc = step(c, carry, True)
    total = acc[:, 0:1]
    out = acc / total
    o_ref[...] = join_heads([out[h * cw : (h + 1) * cw] for h in range(heads)], False).astype(BF)
    first, second, third = pieces_of(-(top + jnp.log(total)))
    wide_lane = lax.broadcasted_iota(jnp.int32, (rows, 128), 1)
    qe = jnp.where(wide_lane == HD + 3, first, q32)
    qe = jnp.where(wide_lane == HD + 4, second, qe)
    qe = jnp.where(wide_lane == HD + 5, third, qe)
    qe_ref[0, 0] = qe.astype(BF)


def forward_call(plan, scalars, q, kx, vx, kv_heads, heads, r):
    total, cw = plan.total, plan.cw
    pairs = kv_heads * heads * total * plan.own // 2
    keys = pl.BlockSpec((1, total, 128), lambda g, b, s: (g, 0, 0))
    return pl.pallas_call(
        functools.partial(forward_kernel, plan, heads, r),
        grid_spec=pltpu.PrefetchScalarGridSpec(
            num_scalar_prefetch=1,
            grid=(kv_heads, 2),
            in_specs=[pl.BlockSpec((cw, heads * HD), lambda g, b, s: (2 * r + b, g)), keys, keys],
            out_specs=[
                pl.BlockSpec((cw, heads * HD), lambda g, b, s: (b, g)),
                pl.BlockSpec((1, 1, heads * cw, 128), lambda g, b, s: (g, b, 0, 0)),
            ],
        ),
        out_shape=[
            jax.ShapeDtypeStruct((plan.own, q.shape[1]), BF),
            jax.ShapeDtypeStruct((kv_heads, 2, heads * cw, 128), BF),
        ],
        cost_estimate=pl.CostEstimate(
            flops=16 * pairs * HD, bytes_accessed=8 * total * 128, transcendentals=pairs
        ),
        compiler_params=pltpu.CompilerParams(vmem_limit_bytes=48 << 20),
        name="attention_forward",
    )(scalars, q, kx, vx)


def backward_kernel(plan, heads, r, first_call, s_ref, qe_ref, kx, vx, o_ref, do_ref, cos_ref, sin_ref, *refs):
    dq_ref, total = refs[-2:]
    cw, chunk = plan.cw, plan.chunk
    half = pl.program_id(0)

    @pl.when(half == 0)
    def _():
        total[...] = jnp.zeros_like(total) if first_call else refs[0][...]

    w, c = block_of(plan, s_ref, r), chunk_of(plan, s_ref, half)
    rows = heads * cw
    lane = lax.broadcasted_iota(jnp.int32, (cw, 128), 1)
    o = split_heads(o_ref[...].astype(F32), heads, False)
    do = split_heads(do_ref[...].astype(F32), heads, False)
    marked = []
    for one, grad in zip(o, do):
        clean = jnp.where(lane >= HD, grad, 0.0)
        first, second, third = pieces_of(-jnp.sum(one * clean, axis=1, keepdims=True))
        tile = jnp.where(lane == 0, first, clean)
        tile = jnp.where(lane == 1, second, tile)
        marked.append(jnp.where(lane == 2, third, tile))
    dox32 = jnp.concatenate(marked, axis=0)
    wide_lane = lax.broadcasted_iota(jnp.int32, (rows, 128), 1)
    dox = dox32.astype(BF)
    do_clean = jnp.where(wide_lane >= HD, dox32, 0.0).astype(BF)
    q = qe_ref[0, 0]
    q_clean = jnp.where(wide_lane < HD, q.astype(F32), 0.0).astype(BF)

    def step(j, dq, diagonal=False):
        at = pl.ds(pl.multiple_of(j * chunk, chunk), chunk)
        key = kx[0, at, :]
        s = lax.dot_general(key, q, NT, preferred_element_type=F32)
        if diagonal:
            row = lax.broadcasted_iota(jnp.int32, (chunk, rows), 1) % cw + w * cw
            col = lax.broadcasted_iota(jnp.int32, (chunk, rows), 0)
            s = jnp.where(col <= row, s, NEG)
        p = jnp.exp(s)
        dp = lax.dot_general(vx[0, at, :], dox, NT, preferred_element_type=F32)
        ds = (p * dp).astype(BF)
        total[at, :] += jnp.dot(ds, q_clean, preferred_element_type=F32) + jnp.dot(
            p.astype(BF), do_clean, preferred_element_type=F32
        )
        return dq + lax.dot_general(ds, key, TN, preferred_element_type=F32)

    dq = lax.fori_loop(0, c, step, jnp.zeros((rows, 128), F32))
    dq = step(c, dq, True) * (HD ** -0.5)
    dq = join_heads([dq[h * cw : (h + 1) * cw] for h in range(heads)], True)
    width = dq.shape[1]
    dq = dq * widen(cos_ref[...], width) + turn(dq, -1.0) * widen(sin_ref[...], width)
    dq_ref[...] = dq.astype(BF)


def backward_call(plan, scalars, qe, kx, vx, o, do, cos, sin, heads, r, g, before):
    total, cw = plan.total, plan.cw
    pairs = heads * total * plan.own // 2
    once = pl.Buffered(1)
    keys = pl.BlockSpec((1, total, 128), lambda b, s: (g, 0, 0), pipeline_mode=once)
    some = pl.BlockSpec((cw, heads * HD), lambda b, s: (b, g))
    table = pl.BlockSpec((cw, 128), lambda b, s: (2 * r + b, 0))
    sums = pl.BlockSpec((total, 128), lambda b, s: (0, 0), pipeline_mode=once)
    operands = [scalars, qe, kx, vx, o, do, cos, sin]
    in_specs = [
        pl.BlockSpec((1, 1, heads * cw, 128), lambda b, s: (g, b, 0, 0)),
        keys, keys, some, some, table, table,
    ]
    aliases = {}
    if before is not None:
        operands.append(before)
        in_specs.append(sums)
        aliases = {8: 1}
    return pl.pallas_call(
        functools.partial(backward_kernel, plan, heads, r, before is None),
        grid_spec=pltpu.PrefetchScalarGridSpec(
            num_scalar_prefetch=1,
            grid=(2,),
            in_specs=in_specs,
            out_specs=[pl.BlockSpec((cw, heads * HD), lambda b, s: (b, 0)), sums],
        ),
        out_shape=[
            jax.ShapeDtypeStruct((plan.own, heads * HD), BF),
            jax.ShapeDtypeStruct((total, 128), F32),
        ],
        input_output_aliases=aliases,
        cost_estimate=pl.CostEstimate(
            flops=36 * pairs * HD, bytes_accessed=12 * total * 128, transcendentals=pairs
        ),
        compiler_params=pltpu.CompilerParams(vmem_limit_bytes=56 << 20),
        name="attention_backward",
    )(*operands)


def rows_kernel(plan, s_ref, x_ref, out_ref):
    narrow = plan.group // 2
    part = x_ref.shape[3]
    for half in range(2):
        for n in range(narrow):
            out_ref[half * plan.cw : (half + 1) * plan.cw, n * part : (n + 1) * part] = x_ref[
                s_ref[0] ^ (half * narrow + n), 0
            ]


def rows_call(plan, scalars, x):
    part = x.shape[3]
    d = part * plan.group // 2
    return pl.pallas_call(
        functools.partial(rows_kernel, plan),
        grid_spec=pltpu.PrefetchScalarGridSpec(
            num_scalar_prefetch=1,
            grid=(plan.wide,),
            in_specs=[
                pl.BlockSpec((plan.group, 1, plan.cw, part), lambda p, s: (0, near_of(plan, s[3], p), 0, 0))
            ],
            out_specs=pl.BlockSpec((plan.own, d), lambda p, s: (p, 0)),
        ),
        out_shape=jax.ShapeDtypeStruct((plan.rows, d), x.dtype),
        cost_estimate=pl.CostEstimate(flops=x.size, bytes_accessed=4 * x.size, transcendentals=0),
        compiler_params=pltpu.CompilerParams(vmem_limit_bytes=40 << 20),
        name="rows",
    )(scalars, x)


MESH = pl.DeviceIdType.MESH


def greet(partners):
    barrier = pltpu.get_barrier_semaphore()
    for partner in partners:
        pl.semaphore_signal(barrier, inc=1, device_id=partner, device_id_type=MESH)
    pl.semaphore_wait(barrier, len(partners))


def along_wide(plan, r):
    return {"wide": lax.rem(lax.axis_index("wide") + r + plan.wide, plan.wide)}


def push(src, dst, send, recv, device):
    return pltpu.make_async_remote_copy(
        src_ref=src, dst_ref=dst, send_sem=send, recv_sem=recv, device_id=device, device_id_type=MESH
    )


def ffn_kernel(
    plan, x2_ref, gain_ref, g_ref, wg_ref, wu_ref, wd_ref,
    act_ref, dg_ref, du_ref, h_out, dn_ref, dx_ref, gain_out,
    h_buf, in_buf, out_buf, dn_acc, dh_acc, own_dh, own_g, ag_send, ag_recv, rs_send, rs_recv,
):
    wide, narrow = plan.wide, plan.group // 2
    own, d = x2_ref.shape
    part = d // narrow
    piece, step = pl.program_id(0), pl.program_id(1)
    last = pl.num_programs(1) - 1
    tall = min(32, own)

    z = lax.axis_index("wide")
    owner = near_of(plan, z, piece)

    def share(p):
        return push(h_buf.at[z], h_buf.at[z], ag_send.at[p], ag_recv.at[z], {"wide": near_of(plan, z, p)})

    def give(device):
        return push(out_buf.at[device], in_buf.at[z], rs_send.at[device], rs_recv.at[z], {"wide": device})

    @pl.when((piece == 0) & (step == 0))
    def _():
        greet([along_wide(plan, r) for r in range(1, wide)])

        @pl.loop(0, own // tall)
        def _(b):
            at = pl.ds(pl.multiple_of(b * tall, tall), tall)
            x2 = x2_ref[at, :]
            scale = lax.rsqrt(jnp.mean(x2 * x2, axis=1, keepdims=True) + EPS)
            h_buf[z, at, :] = (x2 * scale * gain_ref[...]).astype(BF)

        share(1).start()
        if wide > 2:
            share(2).start()
        own_g[...] = g_ref[...]

    for p in range(3, wide):
        @pl.when((piece == min(p - 3, wide - 1)) & (step == last))
        def _():
            share(p).start()

    @pl.when((piece > 0) & (step == 0))
    def _():
        push(h_buf.at[z], h_buf.at[owner], ag_send.at[0], ag_recv.at[owner], {"wide": owner}).wait_recv()

    @pl.when(step == 0)
    def _():
        h_out[...] = h_buf[owner]

    h = h_buf[owner]
    wg, wu = wg_ref[...], wu_ref[...]
    gate = jnp.dot(h, wg, preferred_element_type=F32)
    up = jnp.dot(h, wu, preferred_element_type=F32)
    d_act = jnp.zeros_like(gate)
    for n in range(narrow):
        d_act += lax.dot_general(
            g_ref[:, n * part : (n + 1) * part], wd_ref[n], NT, preferred_element_type=F32
        )
    sig = jax.nn.sigmoid(gate)
    silu = gate * sig
    act = (silu * up).astype(BF)
    dg = (d_act * up * sig * (1.0 + gate * (1.0 - sig))).astype(BF)
    du = (d_act * silu).astype(BF)
    act_ref[...] = act
    dg_ref[...] = dg
    du_ref[...] = du
    dh = lax.dot_general(dg, wg, NT, preferred_element_type=F32) + lax.dot_general(
        du, wu, NT, preferred_element_type=F32
    )

    @pl.when(step == 0)
    def _():
        dh_acc[...] = dh

    @pl.when(step > 0)
    def _():
        dh_acc[...] += dh

    for n in range(narrow):
        at = slice(n * part, (n + 1) * part)
        down = jnp.dot(act, wd_ref[n], preferred_element_type=F32)

        @pl.when(step == 0)
        def _():
            dn_acc[:, at] = down

        @pl.when(step > 0)
        def _():
            dn_acc[:, at] += down

    @pl.when(step == last)
    def _():
        dn_ref[0] = dn_acc[...].astype(BF)

    @pl.when((step == last) & (piece == 0))
    def _():
        own_dh[...] = dh_acc[...]

    @pl.when((step == last) & (piece > 0))
    def _():
        out_buf[owner] = dh_acc[...].astype(BF)
        give(owner).start()

    @pl.when((step == last) & (piece == wide - 1))
    def _():
        for p in range(1, wide):
            other = near_of(plan, z, p)
            push(out_buf.at[z], in_buf.at[other], rs_send.at[z], rs_recv.at[other], {"wide": other}).wait_recv()
        gain_out[...] = jnp.zeros_like(gain_out)

        @pl.loop(0, own // tall)
        def _(b):
            at = pl.ds(pl.multiple_of(b * tall, tall), tall)
            dh2 = own_dh[at, :]
            for p in range(1, wide):
                dh2 = dh2 + in_buf[near_of(plan, z, p), at, :].astype(F32)
            x2 = x2_ref[at, :]
            scale = lax.rsqrt(jnp.mean(x2 * x2, axis=1, keepdims=True) + EPS)
            z2 = x2 * scale
            gain_out[...] += jnp.sum(dh2 * z2, axis=0, keepdims=True)
            dz2 = dh2 * gain_ref[...]
            inner = jnp.mean(dz2 * z2, axis=1, keepdims=True)
            dx_ref[at, :] = own_g[at, :].astype(F32) + scale * (dz2 - z2 * inner)

        for p in range(1, wide):
            share(p).wait_send()
            give(near_of(plan, z, p)).wait_send()


def ffn_call(plan, x2, gain, g_rows, w_gu, w_dn):
    own, d = x2.shape
    wide, rows = plan.wide, plan.rows
    narrow, ff, part = w_dn.shape
    tile = min(512, ff)
    tiles = ff // tile
    fixed = lambda shape: pl.BlockSpec(shape, lambda p, f: (0,) * len(shape), pipeline_mode=pl.Buffered(1))
    tall = pl.BlockSpec((own, tile), lambda p, f: (p, f))
    hidden = jax.ShapeDtypeStruct((rows, ff), BF)
    buffer = pltpu.VMEM((wide, own, d), BF)
    sems = pltpu.SemaphoreType.DMA((wide,))
    return pl.pallas_call(
        functools.partial(ffn_kernel, plan),
        grid=(wide, tiles),
        in_specs=[
            fixed((own, d)),
            fixed((1, d)),
            pl.BlockSpec((own, d), lambda p, f: (p, 0)),
            pl.BlockSpec((d, tile), lambda p, f: (0, f)),
            pl.BlockSpec((d, tile), lambda p, f: (0, tiles + f)),
            pl.BlockSpec((narrow, tile, part), lambda p, f: (0, f, 0)),
        ],
        out_specs=[
            tall, tall, tall,
            pl.BlockSpec((own, d), lambda p, f: (p, 0)),
            pl.BlockSpec((1, own, d), lambda p, f: (p, 0, 0)),
            fixed((own, d)),
            fixed((1, d)),
        ],
        out_shape=[
            hidden, hidden, hidden,
            jax.ShapeDtypeStruct((rows, d), BF),
            jax.ShapeDtypeStruct((wide, own, d), BF),
            jax.ShapeDtypeStruct((own, d), F32),
            jax.ShapeDtypeStruct((1, d), F32),
        ],
        scratch_shapes=[
            buffer, buffer, buffer,
            pltpu.VMEM((own, d), F32), pltpu.VMEM((own, d), F32), pltpu.VMEM((own, d), F32),
            pltpu.VMEM((own, d), BF),
            sems, sems, sems, sems,
        ],
        cost_estimate=pl.CostEstimate(
            flops=16 * rows * d * ff, bytes_accessed=6 * d * ff + 12 * rows * d, transcendentals=rows * ff
        ),
        compiler_params=pltpu.CompilerParams(
            vmem_limit_bytes=58 << 20, collective_id=1, has_side_effects=True
        ),
        name="feed_forward",
    )(x2, gain, g_rows, w_gu, w_gu, w_dn)


def tail_kernel(
    plan, kv_heads, *refs
):
    sums_ref = refs[:kv_heads]
    (
        dh_ref, term_ref, gain2_ref, dx2_ref, x_ref, gain_ref, wkv_ref, cos_ref, sin_ref,
        dkv_ref, got_ref, gain_out,
        swap_out, swap_in, low, near_in, mine, head_in, dh_acc, dx_low, every, term_in,
        gain_part, gain_in, gain_sum, gain_all,
        swap_sem, near_send, near_recv, head_send, head_recv, part_send, part_recv,
        right_send, right_recv, left_send, left_recv, own_sem, term_sem,
        gain_send, gain_recv, gain2_send, gain2_recv,
    ) = refs[kv_heads:]
    group, wide, chunk, cw, own = plan.group, plan.wide, plan.chunk, plan.cw, plan.own
    narrow = group // 2
    part = dx_low.shape[1] // narrow
    seq, me, z = lax.axis_index("seq"), lax.axis_index("narrow"), lax.axis_index("wide")
    index = seq * narrow + me

    def member(k):
        other = lax.rem(index + k + group, group)
        return {"seq": other // narrow, "narrow": lax.rem(other, narrow)}

    sibling = {"seq": 1 - seq}
    greet([member(k) for k in range(1, group)] + [along_wide(plan, r) for r in range(1, wide)])

    def place(owner_seq, half, n):
        quarter = owner_seq if half == 0 else 3 - owner_seq
        return (quarter * narrow + (n if half == 0 else narrow - 1 - n)) * chunk

    @pl.loop(0, narrow)
    def _(n):
        for g in range(kv_heads):
            for half in range(2):
                at = pl.ds(pl.multiple_of(place(1 - seq, half, n), chunk), chunk)
                swap_out[n, g, half] = sums_ref[g][at, :].astype(BF)

    swap = push(swap_out, swap_in, swap_sem.at[0], swap_sem.at[1], sibling)
    swap.start()
    term = push(term_ref, term_in, term_sem.at[0], term_sem.at[1], along_wide(plan, -1))
    term.start()
    swap.wait_recv()

    @pl.loop(0, narrow)
    def _(n):
        for g in range(kv_heads):
            for half in range(2):
                at = pl.ds(pl.multiple_of(place(seq, half, n), chunk), chunk)
                low[n, g, half] = (sums_ref[g][at, :] + swap_in[n, g, half].astype(F32)).astype(BF)

    def near(k):
        other = lax.rem(me + k, narrow)
        return push(low.at[other], near_in.at[k], near_send.at[k], near_recv.at[k], {"narrow": other})

    for k in range(1, narrow):
        near(k).start()
    for k in range(1, narrow):
        near(k).wait_recv()

    lane = lax.broadcasted_iota(jnp.int32, (cw, 128), 1)
    for r in range(wide):
        block = lax.rem(z + r, wide)
        at = pl.ds(pl.multiple_of(block * cw, cw), cw)
        for half in range(2):
            rows = slice((2 * r + half) * cw, (2 * r + half + 1) * cw)
            for g in range(kv_heads):
                total = low[me, g, half, at, :].astype(F32)
                for k in range(1, narrow):
                    total = total + near_in[k, g, half, at, :].astype(F32)
                back = total * cos_ref[rows, :] + turn(total, -1.0) * sin_ref[rows, :]
                value = jnp.where(lane < HD, back, total).astype(BF)
                mine[r, half * cw : (half + 1) * cw, g * 128 : (g + 1) * 128] = value
                dkv_ref[rows, g * 128 : (g + 1) * 128] = value

    def heads_to(r):
        return push(mine.at[r], head_in.at[r], head_send.at[r], head_recv.at[r], along_wide(plan, r))

    for r in range(1, wide):
        heads_to(r).start()
    head_in[0] = mine[0]
    tile = min(512, part)
    for r in range(wide):
        if r > 0:
            heads_to(r).wait_recv()

        @pl.loop(0, dh_acc.shape[1] // tile)
        def _(b):
            at = pl.ds(pl.multiple_of(b * tile, tile), tile)
            more = lax.dot_general(head_in[r], wkv_ref[r, at, :], NT, preferred_element_type=F32)
            dh_acc[:, at] = (dh_ref[:, at] if r == 0 else dh_acc[:, at]) + more

    term.wait_recv()
    gain_part[0:1, :] = jnp.zeros_like(gain2_ref[...])
    gain_part[1:2, :] = gain2_ref[...]
    tall = min(32, own)

    @pl.loop(0, own // tall)
    def _(b):
        at = pl.ds(pl.multiple_of(b * tall, tall), tall)
        dh1 = dh_acc[at, :] + term_in[at, :].astype(F32)
        x = x_ref[at, :].astype(F32)
        scale = lax.rsqrt(jnp.mean(x * x, axis=1, keepdims=True) + EPS)
        z1 = x * scale
        gain_part[0:1, :] += jnp.sum(dh1 * z1, axis=0, keepdims=True)
        dz1 = dh1 * gain_ref[...]
        inner = jnp.mean(dz1 * z1, axis=1, keepdims=True)
        dx_low[at, :] = (dx2_ref[at, :] + scale * (dz1 - z1 * inner)).astype(BF)

    def slab(other):
        rows = pl.ds(pl.multiple_of((other // narrow) * cw, cw), cw)
        return dx_low.at[rows, pl.ds(pl.multiple_of(lax.rem(other, narrow) * part, part), part)]

    def parts_to(k):
        other = lax.rem(index + k, group)
        return push(slab(other), every.at[0, index], part_send.at[k], part_recv.at[k], member(k))

    def parts_from(k):
        other = lax.rem(index - k + group, group)
        return push(slab(index), every.at[0, other], part_send.at[k], part_recv.at[k], member(k))

    def columns(other):
        return gain_part.at[:, pl.ds(pl.multiple_of(lax.rem(other, narrow) * part, part), part)]

    def gain_to(k):
        other = lax.rem(index + k, group)
        return push(columns(other), gain_in.at[k], gain_send.at[k], gain_recv.at[k], member(k))

    for k in range(1, group):
        parts_to(k).start()
    for k in range(1, group):
        gain_to(k).start()
    stay = pltpu.make_async_copy(slab(index), every.at[0, index], own_sem)
    stay.start()
    stay.wait()
    for k in range(1, group):
        parts_from(k).wait_recv()
    for k in range(1, group):
        gain_to(k).wait_recv()
    gain = gain_part[:, pl.ds(pl.multiple_of(me * part, part), part)]
    for k in range(1, group):
        gain = gain + gain_in[k]
    gain_sum[...] = gain

    def gain_on(r):
        return push(gain_sum, gain_all.at[r], gain2_send.at[r], gain2_recv.at[r], along_wide(plan, r))

    for r in range(1, wide):
        gain_on(r).start()

    def to_right(h):
        return push(
            every.at[(wide - h) % wide], every.at[wide - 1 - h], right_send.at[h], right_recv.at[h], along_wide(plan, 1)
        )

    def to_left(h):
        return push(every.at[h], every.at[h + 1], left_send.at[h], left_recv.at[h], along_wide(plan, -1))

    for h in range(wide - 1):
        @pl.when((z <= wide - 2) & (z >= h))
        def _():
            to_right(h).start()

        @pl.when((z >= 1) & (z + h <= wide - 1))
        def _():
            to_left(h).start()

        @pl.when(z >= h + 1)
        def _():
            to_right(h).wait_recv()

        @pl.when(z + h + 1 <= wide - 1)
        def _():
            to_left(h).wait_recv()

    for h in range(wide - 1):
        @pl.when((z <= wide - 2) & (z >= h))
        def _():
            to_right(h).wait_send()

        @pl.when((z >= 1) & (z + h <= wide - 1))
        def _():
            to_left(h).wait_send()

    got_ref[...] = every[...]
    gain = gain_sum[...]
    for r in range(1, wide):
        gain_on(r).wait_recv()
        gain = gain + gain_all[r]
    gain_out[...] = gain
    for r in range(1, wide):
        gain_on(r).wait_send()
    for k in range(1, group):
        gain_to(k).wait_send()
    term.wait_send()
    swap.wait_send()
    for k in range(1, narrow):
        near(k).wait_send()
    for r in range(1, wide):
        heads_to(r).wait_send()
    for k in range(1, group):
        parts_to(k).wait_send()


def tail_call(plan, sums, dh, term, gain2, dx2, x, gain, w_kv, cos, sin):
    kv_heads = len(sums)
    own, d = dh.shape
    group, wide, chunk, cw = plan.group, plan.wide, plan.chunk, plan.cw
    narrow = group // 2
    part = d // narrow
    dma = pltpu.SemaphoreType.DMA
    quarter = pltpu.VMEM((narrow, kv_heads, 2, chunk, 128), BF)
    whole = pl.BlockSpec(memory_space=pltpu.VMEM)
    return pl.pallas_call(
        functools.partial(tail_kernel, plan, kv_heads),
        in_specs=[whole] * (kv_heads + 9),
        out_specs=[whole] * 3,
        out_shape=[
            jax.ShapeDtypeStruct((plan.rows, kv_heads * 128), BF),
            jax.ShapeDtypeStruct((wide, group, cw, part), BF),
            jax.ShapeDtypeStruct((2, part), F32),
        ],
        scratch_shapes=[
            quarter, quarter, quarter, quarter,
            pltpu.VMEM((wide, own, kv_heads * 128), BF),
            pltpu.VMEM((wide, own, kv_heads * 128), BF),
            pltpu.VMEM((own, d), F32),
            pltpu.VMEM((own, d), BF),
            pltpu.VMEM((wide, group, cw, part), BF),
            pltpu.VMEM((own, d), BF),
            pltpu.VMEM((2, d), F32),
            pltpu.VMEM((group, 2, part), F32),
            pltpu.VMEM((2, part), F32),
            pltpu.VMEM((wide, 2, part), F32),
            dma((2,)), dma((narrow,)), dma((narrow,)), dma((wide,)), dma((wide,)), dma((group,)), dma((group,)),
            dma((wide,)), dma((wide,)), dma((wide,)), dma((wide,)), dma(()), dma((2,)),
            dma((group,)), dma((group,)), dma((wide,)), dma((wide,)),
        ],
        cost_estimate=pl.CostEstimate(
            flops=200 * own * d * wide * kv_heads * 128,
            bytes_accessed=4 * kv_heads * plan.total * 128,
            transcendentals=0,
        ),
        compiler_params=pltpu.CompilerParams(
            vmem_limit_bytes=58 << 20, collective_id=2, has_side_effects=True
        ),
        name="input_gradient",
    )(*sums, dh, term, gain2, dx2, x, gain, w_kv, cos, sin)


def assemble_kernel(plan, crossed, s_ref, in_ref, out_ref):
    group = plan.group
    for l in range(group):
        owner = jnp.where(s_ref[0] >= group // 2, group - 1 - l, l)
        out_ref[l, 0] = in_ref[0, s_ref[0] ^ owner if crossed else owner].astype(out_ref.dtype)


def assemble_call(plan, scalars, values, dtype, crossed):
    wide, group, cw, part = values.shape
    out = pl.pallas_call(
        functools.partial(assemble_kernel, plan, crossed),
        grid_spec=pltpu.PrefetchScalarGridSpec(
            num_scalar_prefetch=1,
            grid=(wide,),
            in_specs=[pl.BlockSpec((1, group, cw, part), lambda r, s: (r, 0, 0, 0))],
            out_specs=[pl.BlockSpec((group, 1, cw, part), lambda r, s: (0, block_of(plan, s, r), 0, 0))],
        ),
        out_shape=[jax.ShapeDtypeStruct((group, wide, cw, part), dtype)],
        cost_estimate=pl.CostEstimate(flops=values.size, bytes_accessed=6 * values.size, transcendentals=0),
        compiler_params=pltpu.CompilerParams(vmem_limit_bytes=40 << 20),
        name="assemble",
    )(scalars, values)[0]
    return out.reshape(group * wide * cw, part)


def half_of(weight, seq_index, seq_count):
    part = weight.shape[0] // seq_count
    return lax.dynamic_slice_in_dim(weight, seq_index * part, part, 0)


def body(
    tokens, attn_gain, w_query, w_key, w_value, w_out, ffn_gain, w_gate, w_up, w_down,
    segment_ids, token_mask, out_grad,
):
    seq_count = lax.axis_size("seq")
    narrow = lax.axis_size("narrow")
    wide = lax.axis_size("wide")
    group = seq_count * narrow
    seq_index = lax.axis_index("seq")
    narrow_index = lax.axis_index("narrow")
    wide_index = lax.axis_index("wide")
    index = seq_index * narrow + narrow_index
    total = segment_ids.shape[0]
    plan = Plan(total, group, wide)
    chunk, cw, rows, own = plan.chunk, plan.cw, plan.rows, plan.own
    d_part = tokens.shape[1]
    d = d_part * narrow
    qw = w_query.shape[1]
    kw = w_key.shape[1]
    kv_heads = kw // HD
    heads = qw // kw
    ff = w_gate.shape[1]
    pieces = range(wide)

    start_one = jnp.sum((segment_ids < 1).astype(jnp.int32))
    start_two = jnp.sum((segment_ids < 2).astype(jnp.int32))
    scalars = jnp.stack([index, start_one, start_two, wide_index]).astype(jnp.int32)

    def swap(values, axes, k, size):
        return values if k == 0 else lax.ppermute(values, axes, [(a, a ^ k) for a in range(size)])

    def exchange(parts):
        sent = [lax.dynamic_index_in_dim(parts, index ^ k, 0, keepdims=False) for k in range(group)]
        return jnp.stack([swap(part, SN, k, group) for k, part in enumerate(sent)])

    def to_rows(values):
        parts = values.reshape(group, wide, cw, d_part)
        return exchange(jnp.where(seq_index == 1, parts[::-1], parts))

    def send(values, r):
        return values if r == 0 else lax.ppermute(values, "wide", [(a, (a + r) % wide) for a in pieces])

    def fetch(values, r):
        return send(values, (wide - r) % wide)

    def wide_total(parts):
        out = parts[0]
        for r in range(1, len(parts)):
            out = out + send(parts[r].astype(BF), r).astype(F32)
        return out

    def from_rows(values, dtype):
        parts = values.astype(BF).reshape(2, cw, narrow, d_part)
        parts = jnp.transpose(parts, (0, 2, 1, 3)).reshape(group, cw, d_part)
        got = exchange(parts)
        return assemble_call(plan, scalars, jnp.stack([fetch(got, r) for r in pieces]), dtype, True)

    def gather_weight(weight):
        return lax.all_gather(half_of(weight, seq_index, seq_count), NS, axis=0, tiled=True)

    def scatter_grad(grad):
        mine = lax.psum_scatter(grad.astype(BF), NS, scatter_dimension=0, tiled=True)
        return lax.all_gather(mine, "seq", axis=0, tiled=True).astype(F32)

    def after(values, *others):
        return lax.optimization_barrier((values, *others))[0]

    x_parts = to_rows(tokens)
    w_kv = jnp.concatenate(
        [w_key.reshape(d_part, kv_heads, 1, HD), w_value.reshape(d_part, kv_heads, 1, HD)], axis=2
    ).reshape(d_part, 2 * kw)
    w_qkv = gather_weight(jnp.concatenate([w_query, w_kv], axis=1))
    gains = jnp.stack([attn_gain, ffn_gain])
    gains = jnp.stack([swap(gains, "narrow", k, narrow) for k in range(narrow)])
    order = narrow_index ^ jnp.arange(narrow)
    gains = jnp.sum(jnp.where((order[:, None] == jnp.arange(narrow)[None, :])[:, :, None, None], gains[None], 0.0), axis=1)
    gains = jnp.transpose(gains, (1, 0, 2)).reshape(2, d)
    gain_one, gain_two = gains[0:1], gains[1:2]

    row = jnp.arange(rows, dtype=jnp.int32)
    row_chunk = jnp.where((row // cw) % 2 == 1, 2 * group - 1 - index, index)
    row_block = (row // own + wide_index) % wide
    row_token = row_chunk * chunk + row_block * cw + row % cw
    row_start = jnp.where(row_token >= start_two, start_two, jnp.where(row_token >= start_one, start_one, 0))
    row_pos = (row_token - row_start).astype(F32)
    frequency = THETA ** (-2.0 * jnp.arange(HD // 2, dtype=F32) / HD)
    angles = row_pos[:, None] * jnp.tile(frequency, 4)[None, :]
    cos, sin = jnp.cos(angles), jnp.sin(angles)

    h_one, q, kv, x_low = qkv_call(plan, scalars, x_parts, gain_one, w_qkv, cos, sin, qw)
    near = [swap(kv, "narrow", k, narrow) for k in range(narrow)]
    far = [swap(part, "seq", 1, seq_count) for part in near]
    kv_all = jnp.concatenate(near + far, axis=0)

    lane = jnp.arange(128, dtype=jnp.int32)[None, :]
    closed = (segment_ids[:, None] != lane - HD) | (token_mask[:, None] != 1)
    kf = jnp.where((lane >= HD) & (lane < HD + 3) & closed, NEG, 0.0)
    kf = jnp.where((lane >= HD + 3) & (lane < HD + 6), 1.0, kf).astype(BF)
    kx, vx = keys_call(plan, scalars, kv_all, kf, kv_heads)

    w_o = jnp.transpose(gather_weight(after(w_out, x_parts)).reshape(narrow, qw, d_part), (1, 0, 2)).reshape(qw, d)
    w_gu = gather_weight(after(jnp.concatenate([w_gate, w_up], axis=1), x_parts))
    w_dn = gather_weight(after(w_down, x_parts)).reshape(narrow, ff, d_part)
    row_valid = lax.dynamic_slice_in_dim(token_mask, seq_index * (group * chunk), group * chunk, 0)
    g_low = jnp.where(row_valid[:, None] == 1, out_grad, jnp.zeros_like(out_grad))
    g_parts = to_rows(after(g_low, kv_all))
    g_rows = rows_call(plan, scalars, g_parts)

    far_first = sorted(pieces, key=lambda r: (r == 0, -min(r, wide - r)))
    near_first = sorted(pieces, key=lambda r: min(r, wide - r))
    o, qe, attn = [None] * wide, [None] * wide, [None] * wide
    for r in far_first:
        o[r], qe[r] = forward_call(plan, scalars, q, kx, vx, kv_heads, heads, r)
        attn[r] = jnp.dot(o[r], w_o, preferred_element_type=F32)
    x_own = x_low.astype(F32)
    x2 = x_own + wide_total(attn)

    act, d_gate, d_up, h_all, down, dx2, grad_gain_two = ffn_call(plan, x2, gain_two, g_rows, w_gu, w_dn)

    db_own = dx2.astype(BF)
    db = [fetch(db_own, r) for r in pieces]
    sums = [None] * kv_heads
    dq, terms = [None] * wide, [None] * wide
    w_q = w_qkv[:, :qw]
    w_k = w_qkv[:, qw:]
    for r in pieces:
        do = lax.dot_general(db[r], w_o, NT, preferred_element_type=F32).astype(BF)
        parts = []
        for g in range(kv_heads):
            part, sums[g] = backward_call(
                plan, scalars, qe[r], kx, vx, o[r], do, cos, sin, heads, r, g, sums[g]
            )
            parts.append(part)
        dq[r] = jnp.concatenate(parts, axis=1)
        terms[r] = lax.dot_general(dq[r], w_q, NT, preferred_element_type=F32)
    dh1 = wide_total(terms[:-1])

    down = after(down, *db)
    slot = [jnp.argmax(near_of(plan, wide_index, jnp.arange(wide)) == (wide_index + r) % wide) for r in pieces]
    down = [lax.dynamic_index_in_dim(down, slot[r], 0, keepdims=False) for r in pieces]
    result = from_rows(x2 + wide_total([down[0].astype(F32)] + down[1:]), BF)

    w_k_all = jnp.stack([send(w_k, r) for r in pieces])
    sums[0] = after(sums[0], result)
    dkv, got, gain_grads = tail_call(
        plan, sums, dh1, terms[-1].astype(BF), grad_gain_two, dx2, x_low, gain_one, w_k_all, cos, sin
    )
    input_grad = assemble_call(plan, scalars, got, F32, False)

    def tn(left, right):
        return lax.dot_general(left, right, TN, preferred_element_type=F32).astype(BF)

    def tn_split(left, right):
        return jnp.concatenate([tn(left, right[:, n * d_part : (n + 1) * d_part]) for n in range(narrow)], axis=0)

    grad_gu = scatter_grad(jnp.concatenate([tn(h_all, d_gate), tn(h_all, d_up)], axis=1))
    grad_dn = scatter_grad(tn_split(act, g_rows))
    grad_o = scatter_grad(tn_split(jnp.concatenate(o, axis=0), jnp.concatenate(db, axis=0)))
    grad_qkv = scatter_grad(tn(h_one, jnp.concatenate([jnp.concatenate(dq, axis=0), dkv], axis=1)))
    grad_kv = grad_qkv[:, qw:].reshape(d_part, kv_heads, 2, HD)
    return (
        result,
        input_grad,
        gain_grads[0],
        grad_qkv[:, :qw],
        grad_kv[:, :, 0].reshape(d_part, kw),
        grad_kv[:, :, 1].reshape(d_part, kw),
        grad_o,
        gain_grads[1],
        grad_gu[:, :ff],
        grad_gu[:, ff:],
        grad_dn,
    )


def solution(mesh):
    width_in, width_out = P("narrow", "wide"), P("wide", "narrow")
    acts = P("seq", "narrow")
    return jax.shard_map(
        body,
        mesh=mesh,
        in_specs=(
            acts, P("narrow"), width_in, width_in, width_in, width_out, P("narrow"),
            width_in, width_in, width_out, P(), P(), acts,
        ),
        out_specs=(
            acts, acts, P("narrow"), width_in, width_in, width_in, width_out, P("narrow"),
            width_in, width_in, width_out,
        ),
        check_vma=False,
    )
```

time: 1680 us -> 1340 us (0.80)
  waiting for transfers between devices: 871 us -> 343 us
  Pallas kernels: 231 us -> 652 us
  blocking collectives: 226 us -> 5.09 us
  matrix products: 158 us -> 69.5 us
  starting transfers between devices: 7.35 us -> 91.9 us
    pallas_call x3 -> x19, Pallas kernels: 231 us -> 652 us  [the longest x1 214 us: ffn_call(): pl.pallas_call(functools.partial(ffn_kernel, plan), grid=(wide, tiles), i...]
    reduce_scatter x5 -> x0, waiting for transfers between devices: 301 us -> none  [the longest x4 301 us: wide_scatter(): lax.psum_scatter(values.astype(BF), 'wide', scatter_dimension=0, tiled=True)]
    ppermute x0 -> x48, waiting for transfers between devices: none -> 291 us  [the longest x17 178 us: send(): lax.ppermute(values, 'wide', [(a, (a + r) % wide) for a in pieces])]
    all_gather x5 -> x0, waiting for transfers between devices: 290 us -> none  [the longest x2 148 us: wide_gather(): return lax.all_gather(values, 'wide', axis=0, tiled=True)]
    reduce_scatter x4, waiting for transfers between devices: 188 us -> 32.4 us  [scatter_grad(): lax.psum_scatter(grad.astype(BF), NS, scatter_dimension=0, tiled=True)]
    all_to_all x3 -> x0, blocking collectives: 119 us -> none  [the longest x1 79.7 us: to_rows(): got = lax.all_to_all(parts, SN, 0, 0, tiled=True)]
    ppermute x0 -> x48, starting transfers between devices: none -> 91.5 us  [the longest x17 66.5 us: send(): lax.ppermute(values, 'wide', [(a, (a + r) % wide) for a in pieces])]
    all_gather x4, waiting for transfers between devices: 91 us -> 0.01 us  [gather_weight(): lax.all_gather(half_of(weight, seq_index, seq_count), NS, axis=0, tiled=T...]
  transfers between devices with their start and end apart: 21 -> 58, of which waited for: 14 -> 21; matrix products, arithmetic and copies ran while one was open for 13% -> 12% of each run, Pallas kernels for 0% -> 33%
where the time goes in v2:
time: 1340 us; the launch traced here: 1330 us
  Pallas kernels  652 us (49%)
  waiting for transfers between devices  343 us (26%)
  local copies, waits for them, and re-layouts  93.5 us (7%)
  starting transfers between devices  91.9 us (7%)
  matrix products  69.5 us (5%)
  other arithmetic  56.4 us (4%)
  between operations  23 us (2%)
    pallas_call x1, Pallas kernels, ffn_call(): pl.pallas_call(functools.partial(ffn_kernel, plan), grid=(wide, tiles), i...  214 us
    ppermute x17, waiting for transfers between devices, send(): lax.ppermute(values, 'wide', [(a, (a + r) % wide) for a in pieces])  178 us
    pallas_call x8, Pallas kernels, backward_call(): pl.pallas_call(functools.partial(backward_kernel, plan, heads, r, before...  175 us
    pallas_call x1, Pallas kernels, tail_call(): pl.pallas_call(functools.partial(tail_kernel, plan, kv_heads), in_specs=[...  144 us
    ppermute x31, waiting for transfers between devices, swap(): lax.ppermute(values, axes, [(a, a ^ k) for a in range(size)])  113 us
    pallas_call x4, Pallas kernels, forward_call(): pl.pallas_call(functools.partial(forward_kernel, plan, heads, r), grid_sp...  96.9 us
    ppermute x17, starting transfers between devices, send(): lax.ppermute(values, 'wide', [(a, (a + r) % wide) for a in pieces])  66.5 us
    unnamed x162, local copies, waits for them, and re-layouts  60.2 us
  transfers between devices with their start and end apart: 58, of which 21 were waited for; matrix products, arithmetic and copies ran while one was open for 12% of the time, Pallas kernels for 33%

profile of v2, /device:TPU:0, one launch (start us, length us, event | category | flops | bytes accessed | tf_op | source)
XLA Modules:
  0.0 1334.4 jit_solution(37479296139922425)
XLA Ops:
  11.5 5.0 reverse_select_fusion.1
  23.6 13.4 %collective-permute-done = bf16[4,128,512]{2,1,0:T(8,128)(2,1)S(1)} collective-permute-done((bf16[4,128,512]{2,1,0:T(8,128)(2,1)S(1)}, bf16[4,128,512]{2,1,0:T(8,128)(2,1)S(1)}, u32[]{:S(2)}, u32[]{:S(2)}) %collective-permute-start) | collective-permute-done | bytes 524320 | tf_op jit(solution)/shard_map/ppermute | solution.py:891
  37.0 12.3 collective-permute-done.1
  49.3 8.4 collective-permute-done.2
  57.8 9.7 collective-permute-done.4
  67.5 12.1 collective-permute-done.5
  106.2 9.6 norm_qkv.1
  128.8 15.1 %collective-permute-done.10 = bf16[1024,256]{1,0:T(8,128)(2,1)} collective-permute-done((bf16[1024,256]{1,0:T(8,128)(2,1)}, bf16[1024,256]{1,0:T(8,128)(2,1)}, u32[]{:S(2)}, u32[]{:S(2)}) %collective-permute-start.10) | collective-permute-done | bytes 524320 | tf_op jit(solution)/shard_map/ppermute | solution.py:891
  146.7 9.1 collective-permute-done.12
  167.8 4.3 keys.1
  178.3 24.1 %attention_forward.5 = (bf16[256,512]{1,0:T(8,128)(2,1)S(1)}, bf16[2,2,512,128]{3,2,1,0:T(8,128)(2,1)S(1)}) custom-call(s32[4]{0:T(128)S(1)} %pad_add_fusion.s_ref, bf16[1024,512]{1,0:T(8,128)(2,1)S(1)} %copy-done.22, bf16[2,8192,128]{2,1,0:T(8,128)(2,1)S(1)} %copy-done.18, bf16[2,8192,128]{2,1,0:T(8,128)(2,1)} %copy-done.19), custom_call_target="tpu_custom_call" | custom-call | flops 8589934592 | bytes 8388608 | tf_op jit(solution)/shard_map/attention_forward/pallas_call | solution.py:237
  203.9 24.1 %attention_forward.4 = (bf16[256,512]{1,0:T(8,128)(2,1)S(1)}, bf16[2,2,512,128]{3,2,1,0:T(8,128)(2,1)S(1)}) custom-call(s32[4]{0:T(128)S(1)} %pad_add_fusion.s_ref, bf16[1024,512]{1,0:T(8,128)(2,1)S(1)} %copy-done.22, bf16[2,8192,128]{2,1,0:T(8,128)(2,1)S(1)} %copy-done.18, bf16[2,8192,128]{2,1,0:T(8,128)(2,1)} %copy-done.19), custom_call_target="tpu_custom_call" | custom-call | flops 8589934592 | bytes 8388608 | tf_op jit(solution)/shard_map/attention_forward/pallas_call | solution.py:237
  228.9 24.1 %attention_forward.6 = (bf16[256,512]{1,0:T(8,128)(2,1)S(1)}, bf16[2,2,512,128]{3,2,1,0:T(8,128)(2,1)S(1)}) custom-call(s32[4]{0:T(128)S(1)} %pad_add_fusion.s_ref, bf16[1024,512]{1,0:T(8,128)(2,1)S(1)} %copy-done.22, bf16[2,8192,128]{2,1,0:T(8,128)(2,1)S(1)} %copy-done.18, bf16[2,8192,128]{2,1,0:T(8,128)(2,1)} %copy-done.19), custom_call_target="tpu_custom_call" | custom-call | flops 8589934592 | bytes 8388608 | tf_op jit(solution)/shard_map/attention_forward/pallas_call | solution.py:237
  253.7 24.6 %attention_forward.7 = (bf16[256,512]{1,0:T(8,128)(2,1)S(1)}, bf16[2,2,512,128]{3,2,1,0:T(8,128)(2,1)S(1)}) custom-call(s32[4]{0:T(128)S(1)} %pad_add_fusion.s_ref, bf16[1024,512]{1,0:T(8,128)(2,1)S(1)} %copy-done.22, bf16[2,8192,128]{2,1,0:T(8,128)(2,1)S(1)} %copy-done.18, bf16[2,8192,128]{2,1,0:T(8,128)(2,1)} %copy-done.19), custom_call_target="tpu_custom_call" | custom-call | flops 8589934592 | bytes 8388608 | tf_op jit(solution)/shard_map/attention_forward/pallas_call | solution.py:237
  293.4 23.3 %collective-permute-done.25 = bf16[4,128,512]{2,1,0:T(8,128)(2,1)S(1)} collective-permute-done((bf16[4,128,512]{2,1,0:T(8,128)(2,1)S(1)}, bf16[4,128,512]{2,1,0:T(8,128)(2,1)S(1)}, u32[]{:S(2)}, u32[]{:S(2)}) %collective-permute-start.25) | collective-permute-done | bytes 524320 | tf_op jit(solution)/shard_map/ppermute | solution.py:891
  320.1 35.2 %collective-permute-done.18 = bf16[256,2048]{1,0:T(8,128)(2,1)S(1)} collective-permute-done((bf16[256,2048]{1,0:T(8,128)(2,1)S(1)}, bf16[256,2048]{1,0:T(8,128)(2,1)S(1)}, u32[]{:S(2)}, u32[]{:S(2)}) %collective-permute-start.18) | collective-permute-done | bytes 1048608 | tf_op jit(solution)/shard_map/ppermute | solution.py:902
  357.9 214.4 %feed_forward.1 = (bf16[1024,2048]{1,0:T(8,128)(2,1)}, bf16[1024,2048]{1,0:T(8,128)(2,1)}, bf16[1024,2048]{1,0:T(8,128)(2,1)}, bf16[1024,2048]{1,0:T(8,128)(2,1)...) custom-call(f32[256,2048]{1,0:T(8,128)} %add_add_fusion.x2_ref, f32[1,2048]{1,0:T(1,128)} %bitcast.193, ...), custom_call_target="tpu_custom_call" | custom-call | flops 68719476736 | bytes 50331648 | tf_op jit(solution)/shard_map/feed_forward/pallas_call | solution.py:542
  572.3 4.7 convolution_convert_fusion.3
  588.5 12.3 convolution_convert_fusion.1
  600.9 9.7 convolution_convert_fusion
  610.6 7.5 pad_maximum_fusion
  638.4 11.4 collective-permute-done.45
  649.8 43.1 %collective-permute-done.46 = bf16[2048,256]{1,0:T(8,128)(2,1)} collective-permute-done((bf16[2048,256]{1,0:T(8,128)(2,1)}, bf16[2048,256]{1,0:T(8,128)(2,1)}, u32[]{:S(2)}, u32[]{:S(2)}) %collective-permute-start.46) | collective-permute-done | bytes 1048608 | tf_op jit(solution)/shard_map/ppermute | solution.py:902
  697.1 19.6 %collective-permute-start.27 = (bf16[256,2048]{1,0:T(8,128)(2,1)S(1)}, bf16[256,2048]{1,0:T(8,128)(2,1)}, u32[]{:S(2)}, u32[]{:S(2)}) collective-permute-start(bf16[256,2048]{1,0:T(8,128)(2,1)S(1)} %convert_element_type.141), channel_id=1, source_target_pairs={{0,3},{1,0},{2,1},{3,2},{4,7},{5,4},{6,5},{7,6},{8,11},{9,8},{10,9... | collective-permute-start | bytes 3145736 | tf_op jit(solution)/shard_map/ppermute | solution.py:902
  716.6 4.3 collective-permute-start.28
  722.3 21.2 %attention_backward.8 = (bf16[256,256]{1,0:T(8,128)(2,1)}, f32[8192,128]{1,0:T(8,128)}) custom-call(s32[4]{0:T(128)} %copy-done.14, bf16[2,2,512,128]{3,2,1,0:T(8,128)(2,1)} %copy-done.26, bf16[2,8192,128]{2,1,0:T(8,128)(2,1)} %copy-done.17, bf16[2,8192,128]{2,1,0:T(8,128)(2,1)} %copy-done.19, bf16[256,512]{1,0:T(8,128)(2,1)} %copy-done.8, ...), custom_call_target="tpu_custom_call" | custom-call | flops 9663676416 | bytes 12582912 | tf_op jit(solution)/shard_map/attention_backward/pallas_call | solution.py:330
  744.5 20.8 %attention_backward.12 = (bf16[256,256]{1,0:T(8,128)(2,1)}, f32[8192,128]{1,0:T(8,128)}) custom-call(s32[4]{0:T(128)} %copy-done.14, bf16[2,2,512,128]{3,2,1,0:T(8,128)(2,1)} %copy-done.26, bf16[2,8192,128]{2,1,0:T(8,128)(2,1)} %copy-done.17, bf16[2,8192,128]{2,1,0:T(8,128)(2,1)} %copy-done.19, bf16[256,512]{1,0:T(8,128)(2,1)} %copy-done.8, ...), custom_call_target="tpu_custom_call" | custom-call | flops 9663676416 | bytes 12582912 | tf_op jit(solution)/shard_map/attention_backward/pallas_call | solution.py:330
  768.8 22.1 %attention_backward.9 = (bf16[256,256]{1,0:T(8,128)(2,1)}, f32[8192,128]{1,0:T(8,128)}) custom-call(s32[4]{0:T(128)} %copy-done.14, bf16[2,2,512,128]{3,2,1,0:T(8,128)(2,1)} %copy-done.25, bf16[2,8192,128]{2,1,0:T(8,128)(2,1)} %copy-done.17, bf16[2,8192,128]{2,1,0:T(8,128)(2,1)} %copy-done.19, ...), custom_call_target="tpu_custom_call", output_to_operand_aliasing={{1}: (8, {})} | custom-call | flops 9663676416 | bytes 12582912 | tf_op jit(solution)/shard_map/attention_backward/pallas_call | solution.py:330
  791.9 22.0 %attention_backward.13 = (bf16[256,256]{1,0:T(8,128)(2,1)}, f32[8192,128]{1,0:T(8,128)}) custom-call(s32[4]{0:T(128)} %copy-done.14, bf16[2,2,512,128]{3,2,1,0:T(8,128)(2,1)} %copy-done.25, bf16[2,8192,128]{2,1,0:T(8,128)(2,1)} %copy-done.17, bf16[2,8192,128]{2,1,0:T(8,128)(2,1)} %copy-done.19, ...), custom_call_target="tpu_custom_call", output_to_operand_aliasing={{1}: (8, {})} | custom-call | flops 9663676416 | bytes 12582912 | tf_op jit(solution)/shard_map/attention_backward/pallas_call | solution.py:330
  816.6 24.3 %collective-permute-start.43 = (bf16[256,2048]{1,0:T(8,128)(2,1)}, bf16[256,2048]{1,0:T(8,128)(2,1)}, u32[]{:S(2)}, u32[]{:S(2)}) collective-permute-start(bf16[256,2048]{1,0:T(8,128)(2,1)} %convolution_convert_fusion.9), channel_id=1, source_target_pairs={{0,1},{1,2},{2,3},{3,0},{4,5},{5,6},{6,7},{7,4},{8,9},{9,10},{10,1... | collective-permute-start | bytes 3145736 | tf_op jit(solution)/shard_map/ppermute | solution.py:902
  861.6 22.0 %attention_backward.14 = (bf16[256,256]{1,0:T(8,128)(2,1)}, f32[8192,128]{1,0:T(8,128)}) custom-call(s32[4]{0:T(128)} %copy-done.14, bf16[2,2,512,128]{3,2,1,0:T(8,128)(2,1)} %copy-done.24, bf16[2,8192,128]{2,1,0:T(8,128)(2,1)} %copy-done.17, bf16[2,8192,128]{2,1,0:T(8,128)(2,1)} %copy-done.19, ...), custom_call_target="tpu_custom_call", output_to_operand_aliasing={{1}: (8, {})} | custom-call | flops 9663676416 | bytes 12582912 | tf_op jit(solution)/shard_map/attention_backward/pallas_call | solution.py:330
  883.6 22.0 %attention_backward.10 = (bf16[256,256]{1,0:T(8,128)(2,1)}, f32[8192,128]{1,0:T(8,128)}) custom-call(s32[4]{0:T(128)} %copy-done.14, bf16[2,2,512,128]{3,2,1,0:T(8,128)(2,1)} %copy-done.24, bf16[2,8192,128]{2,1,0:T(8,128)(2,1)} %copy-done.17, bf16[2,8192,128]{2,1,0:T(8,128)(2,1)} %copy-done.19, ...), custom_call_target="tpu_custom_call", output_to_operand_aliasing={{1}: (8, {})} | custom-call | flops 9663676416 | bytes 12582912 | tf_op jit(solution)/shard_map/attention_backward/pallas_call | solution.py:330
  905.6 22.1 %attention_backward.15 = (bf16[256,256]{1,0:T(8,128)(2,1)}, f32[8192,128]{1,0:T(8,128)}) custom-call(s32[4]{0:T(128)} %copy-done.14, bf16[2,2,512,128]{3,2,1,0:T(8,128)(2,1)} %copy-done.23, bf16[2,8192,128]{2,1,0:T(8,128)(2,1)} %copy-done.17, bf16[2,8192,128]{2,1,0:T(8,128)(2,1)} %copy-done.19, ...), custom_call_target="tpu_custom_call", output_to_operand_aliasing={{1}: (8, {})} | custom-call | flops 9663676416 | bytes 12582912 | tf_op jit(solution)/shard_map/attention_backward/pallas_call | solution.py:330
  927.8 22.4 %attention_backward.11 = (bf16[256,256]{1,0:T(8,128)(2,1)}, f32[8192,128]{1,0:T(8,128)}) custom-call(s32[4]{0:T(128)} %copy-done.14, bf16[2,2,512,128]{3,2,1,0:T(8,128)(2,1)} %copy-done.23, bf16[2,8192,128]{2,1,0:T(8,128)(2,1)} %copy-done.17, bf16[2,8192,128]{2,1,0:T(8,128)(2,1)} %copy-done.19, ...), custom_call_target="tpu_custom_call", output_to_operand_aliasing={{1}: (8, {})} | custom-call | flops 9663676416 | bytes 12582912 | tf_op jit(solution)/shard_map/attention_backward/pallas_call | solution.py:330
  967.3 4.2 collective-permute-done.34
  988.7 9.6 collective-permute-done.44
  1001.9 12.0 collective-permute-done.40
  1014.0 66.4 %collective-permute-done.41 = bf16[8,128,512]{2,1,0:T(8,128)(2,1)} collective-permute-done((bf16[8,128,512]{2,1,0:T(8,128)(2,1)}, bf16[8,128,512]{2,1,0:T(8,128)(2,1)}, u32[]{:S(2)}, u32[]{:S(2)}) %collective-permute-start.41) | collective-permute-done | bytes 1048608 | tf_op jit(solution)/shard_map/ppermute | solution.py:902
  1086.1 143.8 %input_gradient.1 = (bf16[1024,256]{1,0:T(8,128)(2,1)}, bf16[4,8,128,512]{3,2,1,0:T(8,128)(2,1)}, f32[2,512]{1,0:T(2,128)}) custom-call(f32[8192,128]{1,0:T(8,128)} %get-tuple-element.89.refs_0_, f32[8192,128]{1,0:T(8,128)} %get-tuple-element.93.refs_1_, f32[256,2048]{1,0:T(8,128)} %convert_add_fusion.1.refs_2_, ...), custom_call_target="tpu_custom_call" | custom-call | flops 107374182400 | bytes 8388608 | tf_op jit(solution)/shard_map/input_gradient/pallas_call | solution.py:795
  1229.9 7.5 convolution_convert_fusion.2
  1241.0 4.2 assemble.3
  1249.4 32.3 %reduce-scatter.5.cloned.1.call-done = bf16[256,768]{1,0:T(8,128)(2,1)} async-done(((bf16[2048,768]{1,0:T(8,128)(2,1)}), bf16[256,768]{1,0:T(8,128)(2,1)}) %reduce-scatter.5.cloned.1.call-update) | async-done | bytes 393232 | tf_op jit(solution)/shard_map/reduce_scatter | solution.py:923
  1287.4 6.6 all-gather.17.cloned.1.call-done
  1294.0 4.2 convert_element_type.171
  1298.2 11.4 all-gather.15.cloned.1.call-done
  1309.6 6.8 fusion.48
  1316.4 5.3 copy.68
  1321.8 5.5 copy.69
  (354 shorter events, 211.1 us)
Async XLA Ops:
  7.2 95.1 %all-gather.7.cloned.1.call-start = ((), (), s32[]{:S(2)}) async-start(), calls=%async_computation.4 | async-start | bytes 3538944 | tf_op jit(solution)/shard_map/all_gather | solution.py:920
  11.4 113.3 %all-gather.9.cloned.1.call-start = ((), (), s32[]{:S(2)}) async-start(), calls=%async_computation.5 | async-start | bytes 2359296 | tf_op jit(solution)/shard_map/all_gather | solution.py:920
  17.0 20.0 %collective-permute-start = (bf16[4,128,512]{2,1,0:T(8,128)(2,1)S(1)}, bf16[4,128,512]{2,1,0:T(8,128)(2,1)S(1)}, u32[]{:S(2)}, u32[]{:S(2)}) collective-permute-start(bf16[4,128,512]{2,1,0:T(8,128)(2,1)S(1)} %get-tuple-element.176), channel_id=1, source_target_pairs={{0,4},{4,0},{8,12},{12,8},{16,20},{20,16},{24,28},{28,24},{1,5},{5... | collective-permute-start | bytes 1572872 | tf_op jit(solution)/shard_map/ppermute | solution.py:891
  20.0 29.3 %collective-permute-start.1 = (bf16[4,128,512]{2,1,0:T(8,128)(2,1)S(1)}, bf16[4,128,512]{2,1,0:T(8,128)(2,1)S(1)}, u32[]{:S(2)}, u32[]{:S(2)}) collective-permute-start(bf16[4,128,512]{2,1,0:T(8,128)(2,1)S(1)} %get-tuple-element.175), channel_id=1, source_target_pairs={{0,8},{4,12},{8,0},{12,4},{16,24},{20,28},{24,16},{28,20},{1,9},{5... | collective-permute-start | bytes 1572872 | tf_op jit(solution)/shard_map/ppermute | solution.py:891
  21.5 36.2 %collective-permute-start.2 = (bf16[4,128,512]{2,1,0:T(8,128)(2,1)S(1)}, bf16[4,128,512]{2,1,0:T(8,128)(2,1)S(1)}, u32[]{:S(2)}, u32[]{:S(2)}) collective-permute-start(bf16[4,128,512]{2,1,0:T(8,128)(2,1)S(1)} %get-tuple-element.174), channel_id=1, source_target_pairs={{0,12},{4,8},{8,4},{12,0},{16,28},{20,24},{24,20},{28,16},{1,13},{... | collective-permute-start | bytes 1572872 | tf_op jit(solution)/shard_map/ppermute | solution.py:891
  21.5 36.2 %collective-permute-start.3 = (bf16[4,128,512]{2,1,0:T(8,128)(2,1)S(1)}, bf16[4,128,512]{2,1,0:T(8,128)(2,1)S(1)}, u32[]{:S(2)}, u32[]{:S(2)}) collective-permute-start(bf16[4,128,512]{2,1,0:T(8,128)(2,1)S(1)} %get-tuple-element.173), channel_id=1, source_target_pairs={{0,16},{4,20},{8,24},{12,28},{16,0},{20,4},{24,8},{28,12},{1,17},{... | collective-permute-start | bytes 1572872 | tf_op jit(solution)/shard_map/ppermute | solution.py:891
  21.5 45.9 %collective-permute-start.4 = (bf16[4,128,512]{2,1,0:T(8,128)(2,1)S(1)}, bf16[4,128,512]{2,1,0:T(8,128)(2,1)S(1)}, u32[]{:S(2)}, u32[]{:S(2)}) collective-permute-start(bf16[4,128,512]{2,1,0:T(8,128)(2,1)S(1)} %get-tuple-element.172), channel_id=1, source_target_pairs={{0,20},{4,16},{8,28},{12,24},{16,4},{20,0},{24,12},{28,8},{1,21},{... | collective-permute-start | bytes 1572872 | tf_op jit(solution)/shard_map/ppermute | solution.py:891
  36.9 42.7 %collective-permute-start.5 = (bf16[4,128,512]{2,1,0:T(8,128)(2,1)S(1)}, bf16[4,128,512]{2,1,0:T(8,128)(2,1)S(1)}, u32[]{:S(2)}, u32[]{:S(2)}) collective-permute-start(bf16[4,128,512]{2,1,0:T(8,128)(2,1)S(1)} %get-tuple-element.171), channel_id=1, source_target_pairs={{0,24},{4,28},{8,16},{12,20},{16,8},{20,12},{24,0},{28,4},{1,25},{... | collective-permute-start | bytes 1572872 | tf_op jit(solution)/shard_map/ppermute | solution.py:891
  49.3 30.4 %collective-permute-start.6 = (bf16[4,128,512]{2,1,0:T(8,128)(2,1)S(1)}, bf16[4,128,512]{2,1,0:T(8,128)(2,1)S(1)}, u32[]{:S(2)}, u32[]{:S(2)}) collective-permute-start(bf16[4,128,512]{2,1,0:T(8,128)(2,1)S(1)} %get-tuple-element.170), channel_id=1, source_target_pairs={{0,28},{4,24},{8,20},{12,16},{16,12},{20,8},{24,4},{28,0},{1,29},{... | collective-permute-start | bytes 1572872 | tf_op jit(solution)/shard_map/ppermute | solution.py:891
  82.5 275.4 %all-gather.13.cloned.1.call-start = ((), (), s32[]{:S(2)}) async-start(), calls=%async_computation.7 | async-start | bytes 9437184 | tf_op jit(solution)/shard_map/all_gather | solution.py:920
  83.6 274.3 %all-gather.11.cloned.1.call-start = ((), (), s32[]{:S(2)}) async-start(), calls=%async_computation.6 | async-start | bytes 18874368 | tf_op jit(solution)/shard_map/all_gather | solution.py:920
  88.0 1149.5 %reduce-scatter.11.cloned.1.call-start = ((), (), s32[]{:S(2)}) async-start(), calls=%async_computation.12 | async-start | bytes 9437184 | tf_op jit(solution)/shard_map/reduce_scatter | solution.py:923
  88.1 13.3 collective-permute-start.7
  118.8 25.1 %collective-permute-start.10 = (bf16[1024,256]{1,0:T(8,128)(2,1)}, bf16[1024,256]{1,0:T(8,128)(2,1)}, u32[]{:S(2)}, u32[]{:S(2)}) collective-permute-start(bf16[1024,256]{1,0:T(8,128)(2,1)} %get-tuple-element.63), channel_id=1, source_target_pairs={{0,4},{4,0},{8,12},{12,8},{1,5},{5,1},{9,13},{13,9},{2,6},{6,2},{1... | collective-permute-start | bytes 1572872 | tf_op jit(solution)/shard_map/ppermute | solution.py:891
  119.2 26.2 %collective-permute-start.11 = (bf16[1024,256]{1,0:T(8,128)(2,1)}, bf16[1024,256]{1,0:T(8,128)(2,1)}, u32[]{:S(2)}, u32[]{:S(2)}) collective-permute-start(bf16[1024,256]{1,0:T(8,128)(2,1)} %get-tuple-element.63), channel_id=1, source_target_pairs={{0,8},{4,12},{8,0},{12,4},{1,9},{5,13},{9,1},{13,5},{2,10},{6,14},... | collective-permute-start | bytes 1572872 | tf_op jit(solution)/shard_map/ppermute | solution.py:891
  121.0 34.8 %collective-permute-start.12 = (bf16[1024,256]{1,0:T(8,128)(2,1)}, bf16[1024,256]{1,0:T(8,128)(2,1)}, u32[]{:S(2)}, u32[]{:S(2)}) collective-permute-start(bf16[1024,256]{1,0:T(8,128)(2,1)} %get-tuple-element.63), channel_id=1, source_target_pairs={{0,12},{4,8},{8,4},{12,0},{1,13},{5,9},{9,5},{13,1},{2,14},{6,10},... | collective-permute-start | bytes 1572872 | tf_op jit(solution)/shard_map/ppermute | solution.py:891
  122.3 35.6 %collective-permute-start.13 = (bf16[1024,256]{1,0:T(8,128)(2,1)}, bf16[1024,256]{1,0:T(8,128)(2,1)}, u32[]{:S(2)}, u32[]{:S(2)}) collective-permute-start(bf16[1024,256]{1,0:T(8,128)(2,1)} %get-tuple-element.63), channel_id=1, source_target_pairs={{0,16},{16,0},{1,17},{17,1},{2,18},{18,2},{3,19},{19,3},{4,20},{20... | collective-permute-start | bytes 1572872 | tf_op jit(solution)/shard_map/ppermute | solution.py:891
  143.9 15.1 %collective-permute-start.14 = (bf16[1024,256]{1,0:T(8,128)(2,1)}, bf16[1024,256]{1,0:T(8,128)(2,1)S(1)}, u32[]{:S(2)}, u32[]{:S(2)}) collective-permute-start(bf16[1024,256]{1,0:T(8,128)(2,1)} %collective-permute-done.10), channel_id=1, source_target_pairs={{0,16},{16,0},{1,17},{17,1},{2,18},{18,2},{3,19},{19,3},{4,20},{20... | collective-permute-start | bytes 1572872 | tf_op jit(solution)/shard_map/ppermute | solution.py:891
  145.5 13.6 %collective-permute-start.15 = (bf16[1024,256]{1,0:T(8,128)(2,1)}, bf16[1024,256]{1,0:T(8,128)(2,1)S(1)}, u32[]{:S(2)}, u32[]{:S(2)}) collective-permute-start(bf16[1024,256]{1,0:T(8,128)(2,1)} %collective-permute-done.11), channel_id=1, source_target_pairs={{0,16},{16,0},{1,17},{17,1},{2,18},{18,2},{3,19},{19,3},{4,20},{20... | collective-permute-start | bytes 1572872 | tf_op jit(solution)/shard_map/ppermute | solution.py:891
  163.3 116.6 %collective-permute-start.20 = (bf16[4,128,512]{2,1,0:T(8,128)(2,1)}, bf16[4,128,512]{2,1,0:T(8,128)(2,1)}, u32[]{:S(2)}, u32[]{:S(2)}) collective-permute-start(bf16[4,128,512]{2,1,0:T(8,128)(2,1)} %get-tuple-element.168), channel_id=1, source_target_pairs={{0,4},{4,0},{8,12},{12,8},{16,20},{20,16},{24,28},{28,24},{1,5},{5... | collective-permute-start | bytes 1572872 | tf_op jit(solution)/shard_map/ppermute | solution.py:891
  163.6 119.3 %collective-permute-start.21 = (bf16[4,128,512]{2,1,0:T(8,128)(2,1)}, bf16[4,128,512]{2,1,0:T(8,128)(2,1)}, u32[]{:S(2)}, u32[]{:S(2)}) collective-permute-start(bf16[4,128,512]{2,1,0:T(8,128)(2,1)} %get-tuple-element.167), channel_id=1, source_target_pairs={{0,8},{4,12},{8,0},{12,4},{16,24},{20,28},{24,16},{28,20},{1,9},{5... | collective-permute-start | bytes 1572872 | tf_op jit(solution)/shard_map/ppermute | solution.py:891
  165.6 120.1 %collective-permute-start.22 = (bf16[4,128,512]{2,1,0:T(8,128)(2,1)}, bf16[4,128,512]{2,1,0:T(8,128)(2,1)}, u32[]{:S(2)}, u32[]{:S(2)}) collective-permute-start(bf16[4,128,512]{2,1,0:T(8,128)(2,1)} %get-tuple-element.166), channel_id=1, source_target_pairs={{0,12},{4,8},{8,4},{12,0},{16,28},{20,24},{24,20},{28,16},{1,13},{... | collective-permute-start | bytes 1572872 | tf_op jit(solution)/shard_map/ppermute | solution.py:891
  167.1 121.5 %collective-permute-start.23 = (bf16[4,128,512]{2,1,0:T(8,128)(2,1)}, bf16[4,128,512]{2,1,0:T(8,128)(2,1)}, u32[]{:S(2)}, u32[]{:S(2)}) collective-permute-start(bf16[4,128,512]{2,1,0:T(8,128)(2,1)} %get-tuple-element.165), channel_id=1, source_target_pairs={{0,16},{4,20},{8,24},{12,28},{16,0},{20,4},{24,8},{28,12},{1,17},{... | collective-permute-start | bytes 1572872 | tf_op jit(solution)/shard_map/ppermute | solution.py:891
  167.1 123.8 %collective-permute-start.24 = (bf16[4,128,512]{2,1,0:T(8,128)(2,1)}, bf16[4,128,512]{2,1,0:T(8,128)(2,1)}, u32[]{:S(2)}, u32[]{:S(2)}) collective-permute-start(bf16[4,128,512]{2,1,0:T(8,128)(2,1)} %get-tuple-element.164), channel_id=1, source_target_pairs={{0,20},{4,16},{8,28},{12,24},{16,4},{20,0},{24,12},{28,8},{1,21},{... | collective-permute-start | bytes 1572872 | tf_op jit(solution)/shard_map/ppermute | solution.py:891
  279.9 36.7 %collective-permute-start.25 = (bf16[4,128,512]{2,1,0:T(8,128)(2,1)S(1)}, bf16[4,128,512]{2,1,0:T(8,128)(2,1)S(1)}, u32[]{:S(2)}, u32[]{:S(2)}) collective-permute-start(bf16[4,128,512]{2,1,0:T(8,128)(2,1)S(1)} %copy-done.41), channel_id=1, source_target_pairs={{0,24},{4,28},{8,16},{12,20},{16,8},{20,12},{24,0},{28,4},{1,25},{... | collective-permute-start | bytes 1572872 | tf_op jit(solution)/shard_map/ppermute | solution.py:891
  283.0 37.2 %collective-permute-start.17 = (bf16[256,2048]{1,0:T(8,128)(2,1)S(1)}, bf16[256,2048]{1,0:T(8,128)(2,1)S(1)}, u32[]{:S(2)}, u32[]{:S(2)}) collective-permute-start(bf16[256,2048]{1,0:T(8,128)(2,1)S(1)} %convolution_convert_fusion.12), channel_id=1, source_target_pairs={{0,1},{1,2},{2,3},{3,0},{4,5},{5,6},{6,7},{7,4},{8,9},{9,10},{10,1... | collective-permute-start | bytes 3145736 | tf_op jit(solution)/shard_map/ppermute | solution.py:902
  285.7 69.6 %collective-permute-start.18 = (bf16[256,2048]{1,0:T(8,128)(2,1)S(1)}, bf16[256,2048]{1,0:T(8,128)(2,1)S(1)}, u32[]{:S(2)}, u32[]{:S(2)}) collective-permute-start(bf16[256,2048]{1,0:T(8,128)(2,1)S(1)} %convolution_convert_fusion.11), channel_id=1, source_target_pairs={{0,2},{1,3},{2,0},{3,1},{4,6},{5,7},{6,4},{7,5},{8,10},{9,11},{10,... | collective-permute-start | bytes 3145736 | tf_op jit(solution)/shard_map/ppermute | solution.py:902
  288.6 66.7 %collective-permute-start.19 = (bf16[256,2048]{1,0:T(8,128)(2,1)S(1)}, bf16[256,2048]{1,0:T(8,128)(2,1)S(1)}, u32[]{:S(2)}, u32[]{:S(2)}) collective-permute-start(bf16[256,2048]{1,0:T(8,128)(2,1)S(1)} %convolution_convert_fusion.10), channel_id=1, source_target_pairs={{0,3},{1,0},{2,1},{3,2},{4,7},{5,4},{6,5},{7,6},{8,11},{9,8},{10,9... | collective-permute-start | bytes 3145736 | tf_op jit(solution)/shard_map/ppermute | solution.py:902
  290.9 25.8 %collective-permute-start.26 = (bf16[4,128,512]{2,1,0:T(8,128)(2,1)S(1)}, bf16[4,128,512]{2,1,0:T(8,128)(2,1)S(1)}, u32[]{:S(2)}, u32[]{:S(2)}) collective-permute-start(bf16[4,128,512]{2,1,0:T(8,128)(2,1)S(1)} %copy-done.40), channel_id=1, source_target_pairs={{0,28},{4,24},{8,20},{12,16},{16,12},{20,8},{24,4},{28,0},{1,29},{... | collective-permute-start | bytes 1572872 | tf_op jit(solution)/shard_map/ppermute | solution.py:891
  588.5 649.8 %reduce-scatter.9.cloned.1.call-start = ((), (), s32[]{:S(2)}) async-start(), calls=%async_computation.10 | async-start | bytes 18874368 | tf_op jit(solution)/shard_map/reduce_scatter | solution.py:923
  618.1 627.7 %reduce-scatter.7.cloned.1.call-start = ((), (), s32[]{:S(2)}) async-start(), calls=%async_computation.9 | async-start | bytes 2359296 | tf_op jit(solution)/shard_map/reduce_scatter | solution.py:923
  621.5 28.3 %collective-permute-start.45 = (bf16[2048,256]{1,0:T(8,128)(2,1)}, bf16[2048,256]{1,0:T(8,128)(2,1)}, u32[]{:S(2)}, u32[]{:S(2)}) collective-permute-start(bf16[2048,256]{1,0:T(8,128)(2,1)} %get-tuple-element.179), channel_id=1, source_target_pairs={{0,1},{1,2},{2,3},{3,0},{4,5},{5,6},{6,7},{7,4},{8,9},{9,10},{10,1... | collective-permute-start | bytes 3145736 | tf_op jit(solution)/shard_map/ppermute | solution.py:902
  621.5 71.4 %collective-permute-start.46 = (bf16[2048,256]{1,0:T(8,128)(2,1)}, bf16[2048,256]{1,0:T(8,128)(2,1)}, u32[]{:S(2)}, u32[]{:S(2)}) collective-permute-start(bf16[2048,256]{1,0:T(8,128)(2,1)} %get-tuple-element.179), channel_id=1, source_target_pairs={{0,2},{1,3},{2,0},{3,1},{4,6},{5,7},{6,4},{7,5},{8,10},{9,11},{10,... | collective-permute-start | bytes 3145736 | tf_op jit(solution)/shard_map/ppermute | solution.py:902
  623.4 69.5 %collective-permute-start.47 = (bf16[2048,256]{1,0:T(8,128)(2,1)}, bf16[2048,256]{1,0:T(8,128)(2,1)}, u32[]{:S(2)}, u32[]{:S(2)}) collective-permute-start(bf16[2048,256]{1,0:T(8,128)(2,1)} %get-tuple-element.179), channel_id=1, source_target_pairs={{0,3},{1,0},{2,1},{3,2},{4,7},{5,4},{6,5},{7,6},{8,11},{9,8},{10,9... | collective-permute-start | bytes 3145736 | tf_op jit(solution)/shard_map/ppermute | solution.py:902
  697.1 69.1 %collective-permute-start.27 = (bf16[256,2048]{1,0:T(8,128)(2,1)S(1)}, bf16[256,2048]{1,0:T(8,128)(2,1)}, u32[]{:S(2)}, u32[]{:S(2)}) collective-permute-start(bf16[256,2048]{1,0:T(8,128)(2,1)S(1)} %convert_element_type.141), channel_id=1, source_target_pairs={{0,3},{1,0},{2,1},{3,2},{4,7},{5,4},{6,5},{7,6},{8,11},{9,8},{10,9... | collective-permute-start | bytes 3145736 | tf_op jit(solution)/shard_map/ppermute | solution.py:902
  716.6 124.2 %collective-permute-start.28 = (bf16[256,2048]{1,0:T(8,128)(2,1)S(1)}, bf16[256,2048]{1,0:T(8,128)(2,1)S(1)}, u32[]{:S(2)}, u32[]{:S(2)}) collective-permute-start(bf16[256,2048]{1,0:T(8,128)(2,1)S(1)} %convert_element_type.141), channel_id=1, source_target_pairs={{0,2},{1,3},{2,0},{3,1},{4,6},{5,7},{6,4},{7,5},{8,10},{9,11},{10,... | collective-permute-start | bytes 3145736 | tf_op jit(solution)/shard_map/ppermute | solution.py:902
  720.9 120.0 %collective-permute-start.29 = (bf16[256,2048]{1,0:T(8,128)(2,1)S(1)}, bf16[256,2048]{1,0:T(8,128)(2,1)}, u32[]{:S(2)}, u32[]{:S(2)}) collective-permute-start(bf16[256,2048]{1,0:T(8,128)(2,1)S(1)} %convert_element_type.141), channel_id=1, source_target_pairs={{0,1},{1,2},{2,3},{3,0},{4,5},{5,6},{6,7},{7,4},{8,9},{9,10},{10,1... | collective-permute-start | bytes 3145736 | tf_op jit(solution)/shard_map/ppermute | solution.py:902
  816.6 172.1 %collective-permute-start.43 = (bf16[256,2048]{1,0:T(8,128)(2,1)}, bf16[256,2048]{1,0:T(8,128)(2,1)}, u32[]{:S(2)}, u32[]{:S(2)}) collective-permute-start(bf16[256,2048]{1,0:T(8,128)(2,1)} %convolution_convert_fusion.9), channel_id=1, source_target_pairs={{0,1},{1,2},{2,3},{3,0},{4,5},{5,6},{6,7},{7,4},{8,9},{9,10},{10,1... | collective-permute-start | bytes 3145736 | tf_op jit(solution)/shard_map/ppermute | solution.py:902
  845.5 104.6 %collective-permute-start.30 = (bf16[256,2048]{1,0:T(8,128)(2,1)}, bf16[256,2048]{1,0:T(8,128)(2,1)}, u32[]{:S(2)}, u32[]{:S(2)}) collective-permute-start(bf16[256,2048]{1,0:T(8,128)(2,1)} %get-tuple-element.159), channel_id=1, source_target_pairs={{0,1},{1,2},{2,3},{3,0},{4,5},{5,6},{6,7},{7,4},{8,9},{9,10},{10,1... | collective-permute-start | bytes 3145736 | tf_op jit(solution)/shard_map/ppermute | solution.py:902
  845.5 104.6 %collective-permute-start.31 = (bf16[256,2048]{1,0:T(8,128)(2,1)}, bf16[256,2048]{1,0:T(8,128)(2,1)}, u32[]{:S(2)}, u32[]{:S(2)}) collective-permute-start(bf16[256,2048]{1,0:T(8,128)(2,1)} %get-tuple-element.161), channel_id=1, source_target_pairs={{0,2},{1,3},{2,0},{3,1},{4,6},{5,7},{6,4},{7,5},{8,10},{9,11},{10,... | collective-permute-start | bytes 3145736 | tf_op jit(solution)/shard_map/ppermute | solution.py:902
  845.6 104.6 %collective-permute-start.32 = (bf16[256,2048]{1,0:T(8,128)(2,1)S(1)}, bf16[256,2048]{1,0:T(8,128)(2,1)}, u32[]{:S(2)}, u32[]{:S(2)}) collective-permute-start(bf16[256,2048]{1,0:T(8,128)(2,1)S(1)} %get-tuple-element.160), channel_id=1, source_target_pairs={{0,3},{1,0},{2,1},{3,2},{4,7},{5,4},{6,5},{7,6},{8,11},{9,8},{10,9... | collective-permute-start | bytes 3145736 | tf_op jit(solution)/shard_map/ppermute | solution.py:902
  963.2 35.2 %collective-permute-start.44 = (bf16[256,2048]{1,0:T(8,128)(2,1)}, bf16[256,2048]{1,0:T(8,128)(2,1)}, u32[]{:S(2)}, u32[]{:S(2)}) collective-permute-start(bf16[256,2048]{1,0:T(8,128)(2,1)} %convolution_convert_fusion.8), channel_id=1, source_target_pairs={{0,2},{1,3},{2,0},{3,1},{4,6},{5,7},{6,4},{7,5},{8,10},{9,11},{10,... | collective-permute-start | bytes 3145736 | tf_op jit(solution)/shard_map/ppermute | solution.py:902
  981.6 32.4 %collective-permute-start.40 = (bf16[8,128,512]{2,1,0:T(8,128)(2,1)}, bf16[8,128,512]{2,1,0:T(8,128)(2,1)}, u32[]{:S(2)}, u32[]{:S(2)}) collective-permute-start(bf16[8,128,512]{2,1,0:T(8,128)(2,1)} %bitcast_dynamic-update-slice_fusion.14), channel_id=1, source_target_pairs={{0,3},{1,0},{2,1},{3,2},{4,7},{5,4},{6,5},{7,6},{8,11},{9,8},{10,9... | collective-permute-start | bytes 3145736 | tf_op jit(solution)/shard_map/ppermute | solution.py:902
  982.6 97.8 %collective-permute-start.41 = (bf16[8,128,512]{2,1,0:T(8,128)(2,1)}, bf16[8,128,512]{2,1,0:T(8,128)(2,1)}, u32[]{:S(2)}, u32[]{:S(2)}) collective-permute-start(bf16[8,128,512]{2,1,0:T(8,128)(2,1)} %bitcast_dynamic-update-slice_fusion.14), channel_id=1, source_target_pairs={{0,2},{1,3},{2,0},{3,1},{4,6},{5,7},{6,4},{7,5},{8,10},{9,11},{10,... | collective-permute-start | bytes 3145736 | tf_op jit(solution)/shard_map/ppermute | solution.py:902
  982.6 97.8 %collective-permute-start.42 = (bf16[8,128,512]{2,1,0:T(8,128)(2,1)}, bf16[8,128,512]{2,1,0:T(8,128)(2,1)}, u32[]{:S(2)}, u32[]{:S(2)}) collective-permute-start(bf16[8,128,512]{2,1,0:T(8,128)(2,1)} %bitcast_dynamic-update-slice_fusion.14), channel_id=1, source_target_pairs={{0,1},{1,2},{2,3},{3,0},{4,5},{5,6},{6,7},{7,4},{8,9},{9,10},{10,1... | collective-permute-start | bytes 3145736 | tf_op jit(solution)/shard_map/ppermute | solution.py:902
  986.0 295.8 %reduce-scatter.5.cloned.1.call-start = ((), (), s32[]{:S(2)}) async-start(), calls=%async_computation.8 | async-start | bytes 3538944 | tf_op jit(solution)/shard_map/reduce_scatter | solution.py:923
  1237.4 56.5 %all-gather.17.cloned.1.call-start = ((), (), s32[]{:S(2)}) async-start(), calls=%async_computation.13 | async-start | bytes 3145728 | tf_op jit(solution)/shard_map/all_gather | solution.py:924
  1238.2 71.4 %all-gather.15.cloned.1.call-start = ((), (), s32[]{:S(2)}) async-start(), calls=%async_computation.11 | async-start | bytes 6291456 | tf_op jit(solution)/shard_map/all_gather | solution.py:924
  (72 other events, 2218.7 us)
Sparse Core Ops, SparseCore 0:
  11.5 55.7 all-gather.6
  82.6 28.2 all-gather.8
  113.4 93.9 all-gather.12
  209.7 112.7 all-gather.10
  588.6 70.7 reduce-scatter.10
  663.2 115.9 reduce-scatter.8
  986.1 40.3 reduce-scatter.6
  1237.6 44.1 reduce-scatter.4
  1283.4 10.5 all-gather.16
  1295.4 14.1 all-gather.14

commit v3 on v2

--- a/solution.py
+++ b/solution.py
@@ -257,97 +257,6 @@
     )(scalars, q, kx, vx)
 
 
-def backward_kernel(plan, heads, r, first_call, s_ref, qe_ref, kx, vx, o_ref, do_ref, cos_ref, sin_ref, *refs):
-    dq_ref, total = refs[-2:]
-    cw, chunk = plan.cw, plan.chunk
-    half = pl.program_id(0)
-
-    @pl.when(half == 0)
-    def _():
-        total[...] = jnp.zeros_like(total) if first_call else refs[0][...]
-
-    w, c = block_of(plan, s_ref, r), chunk_of(plan, s_ref, half)
-    rows = heads * cw
-    lane = lax.broadcasted_iota(jnp.int32, (cw, 128), 1)
-    o = split_heads(o_ref[...].astype(F32), heads, False)
-    do = split_heads(do_ref[...].astype(F32), heads, False)
-    marked = []
-    for one, grad in zip(o, do):
-        clean = jnp.where(lane >= HD, grad, 0.0)
-        first, second, third = pieces_of(-jnp.sum(one * clean, axis=1, keepdims=True))
-        tile = jnp.where(lane == 0, first, clean)
-        tile = jnp.where(lane == 1, second, tile)
-        marked.append(jnp.where(lane == 2, third, tile))
-    dox32 = jnp.concatenate(marked, axis=0)
-    wide_lane = lax.broadcasted_iota(jnp.int32, (rows, 128), 1)
-    dox = dox32.astype(BF)
-    do_clean = jnp.where(wide_lane >= HD, dox32, 0.0).astype(BF)
-    q = qe_ref[0, 0]
-    q_clean = jnp.where(wide_lane < HD, q.astype(F32), 0.0).astype(BF)
-
-    def step(j, dq, diagonal=False):
-        at = pl.ds(pl.multiple_of(j * chunk, chunk), chunk)
-        key = kx[0, at, :]
-        s = lax.dot_general(key, q, NT, preferred_element_type=F32)
-        if diagonal:
-            row = lax.broadcasted_iota(jnp.int32, (chunk, rows), 1) % cw + w * cw
-            col = lax.broadcasted_iota(jnp.int32, (chunk, rows), 0)
-            s = jnp.where(col <= row, s, NEG)
-        p = jnp.exp(s)
-        dp = lax.dot_general(vx[0, at, :], dox, NT, preferred_element_type=F32)
-        ds = (p * dp).astype(BF)
-        total[at, :] += jnp.dot(ds, q_clean, preferred_element_type=F32) + jnp.dot(
-            p.astype(BF), do_clean, preferred_element_type=F32
-        )
-        return dq + lax.dot_general(ds, key, TN, preferred_element_type=F32)
-
-    dq = lax.fori_loop(0, c, step, jnp.zeros((rows, 128), F32))
-    dq = step(c, dq, True) * (HD ** -0.5)
-    dq = join_heads([dq[h * cw : (h + 1) * cw] for h in range(heads)], True)
-    width = dq.shape[1]
-    dq = dq * widen(cos_ref[...], width) + turn(dq, -1.0) * widen(sin_ref[...], width)
-    dq_ref[...] = dq.astype(BF)
-
-
-def backward_call(plan, scalars, qe, kx, vx, o, do, cos, sin, heads, r, g, before):
-    total, cw = plan.total, plan.cw
-    pairs = heads * total * plan.own // 2
-    once = pl.Buffered(1)
-    keys = pl.BlockSpec((1, total, 128), lambda b, s: (g, 0, 0), pipeline_mode=once)
-    some = pl.BlockSpec((cw, heads * HD), lambda b, s: (b, g))
-    table = pl.BlockSpec((cw, 128), lambda b, s: (2 * r + b, 0))
-    sums = pl.BlockSpec((total, 128), lambda b, s: (0, 0), pipeline_mode=once)
-    operands = [scalars, qe, kx, vx, o, do, cos, sin]
-    in_specs = [
-        pl.BlockSpec((1, 1, heads * cw, 128), lambda b, s: (g, b, 0, 0)),
-        keys, keys, some, some, table, table,
-    ]
-    aliases = {}
-    if before is not None:
-        operands.append(before)
-        in_specs.append(sums)
-        aliases = {8: 1}
-    return pl.pallas_call(
-        functools.partial(backward_kernel, plan, heads, r, before is None),
-        grid_spec=pltpu.PrefetchScalarGridSpec(
-            num_scalar_prefetch=1,
-            grid=(2,),
-            in_specs=in_specs,
-            out_specs=[pl.BlockSpec((cw, heads * HD), lambda b, s: (b, 0)), sums],
-        ),
-        out_shape=[
-            jax.ShapeDtypeStruct((plan.own, heads * HD), BF),
-            jax.ShapeDtypeStruct((total, 128), F32),
-        ],
-        input_output_aliases=aliases,
-        cost_estimate=pl.CostEstimate(
-            flops=36 * pairs * HD, bytes_accessed=12 * total * 128, transcendentals=pairs
-        ),
-        compiler_params=pltpu.CompilerParams(vmem_limit_bytes=56 << 20),
-        name="attention_backward",
-    )(*operands)
-
-
 def rows_kernel(plan, s_ref, x_ref, out_ref):
     narrow = plan.group // 2
     part = x_ref.shape[3]
@@ -398,10 +307,45 @@
     )
 
 
+class Chain:
+    def __init__(self, plan, buf, sems):
+        self.wide, self.buf, self.sems = plan.wide, buf, sems
+        self.z = lax.axis_index("wide")
+
+    def copy(self, slot, h, way):
+        send, recv = (self.sems[0], self.sems[1]) if way > 0 else (self.sems[2], self.sems[3])
+        return push(self.buf.at[slot], self.buf.at[slot], send.at[h], recv.at[h], {"wide": self.z + way})
+
+    def sends(self, h, way):
+        z, last = self.z, self.wide - 1
+        return (z >= h - 1) & (z < last) if way > 0 else (z + h - 1 <= last) & (z > 0)
+
+    def go(self, h):
+        for way in (1, -1):
+            @pl.when(self.sends(h, way))
+            def _():
+                self.copy(self.z - way * (h - 1), h, way).start()
+
+    def arrive(self, h):
+        for way in (1, -1):
+            @pl.when(self.z >= h if way > 0 else self.z + h <= self.wide - 1)
+            def _():
+                slot = self.z - way * h
+                send, recv = (self.sems[0], self.sems[1]) if way > 0 else (self.sems[2], self.sems[3])
+                push(self.buf.at[slot], self.buf.at[slot], send.at[h], recv.at[h], {"wide": slot}).wait_recv()
+
+    def finish(self):
+        for h in range(1, self.wide):
+            for way in (1, -1):
+                @pl.when(self.sends(h, way))
+                def _():
+                    self.copy(self.z - way * (h - 1), h, way).wait_send()
+
+
 def ffn_kernel(
     plan, x2_ref, gain_ref, g_ref, wg_ref, wu_ref, wd_ref,
     act_ref, dg_ref, du_ref, h_out, dn_ref, dx_ref, gain_out,
-    h_buf, in_buf, out_buf, dn_acc, dh_acc, own_dh, own_g, ag_send, ag_recv, rs_send, rs_recv,
+    h_buf, in_buf, out_buf, dn_acc, dh_acc, own_dh, own_g, rs_send, rs_recv, *chain_sems
 ):
     wide, narrow = plan.wide, plan.group // 2
     own, d = x2_ref.shape
@@ -413,8 +357,7 @@
     z = lax.axis_index("wide")
     owner = near_of(plan, z, piece)
 
-    def share(p):
-        return push(h_buf.at[z], h_buf.at[z], ag_send.at[p], ag_recv.at[z], {"wide": near_of(plan, z, p)})
+    chain = Chain(plan, h_buf, chain_sems)
 
     def give(device):
         return push(out_buf.at[device], in_buf.at[z], rs_send.at[device], rs_recv.at[z], {"wide": device})
@@ -430,19 +373,15 @@
             scale = lax.rsqrt(jnp.mean(x2 * x2, axis=1, keepdims=True) + EPS)
             h_buf[z, at, :] = (x2 * scale * gain_ref[...]).astype(BF)
 
-        share(1).start()
-        if wide > 2:
-            share(2).start()
+        chain.go(1)
         own_g[...] = g_ref[...]
 
-    for p in range(3, wide):
-        @pl.when((piece == min(p - 3, wide - 1)) & (step == last))
+    for h in range(1, wide):
+        @pl.when((piece == h) & (step == 0))
         def _():
-            share(p).start()
-
-    @pl.when((piece > 0) & (step == 0))
-    def _():
-        push(h_buf.at[z], h_buf.at[owner], ag_send.at[0], ag_recv.at[owner], {"wide": owner}).wait_recv()
+            chain.arrive(h)
+            if h + 1 < wide:
+                chain.go(h + 1)
 
     @pl.when(step == 0)
     def _():
@@ -523,8 +462,8 @@
             inner = jnp.mean(dz2 * z2, axis=1, keepdims=True)
             dx_ref[at, :] = own_g[at, :].astype(F32) + scale * (dz2 - z2 * inner)
 
+        chain.finish()
         for p in range(1, wide):
-            share(p).wait_send()
             give(near_of(plan, z, p)).wait_send()
 
 
@@ -568,7 +507,7 @@
             buffer, buffer, buffer,
             pltpu.VMEM((own, d), F32), pltpu.VMEM((own, d), F32), pltpu.VMEM((own, d), F32),
             pltpu.VMEM((own, d), BF),
-            sems, sems, sems, sems,
+            sems, sems, sems, sems, sems, sems,
         ],
         cost_estimate=pl.CostEstimate(
             flops=16 * rows * d * ff, bytes_accessed=6 * d * ff + 12 * rows * d, transcendentals=rows * ff
@@ -580,55 +519,268 @@
     )(x2, gain, g_rows, w_gu, w_gu, w_dn)
 
 
+def backward_kernel(
+    plan, kv_heads, heads, dx2_ref, qe_ref, kx, vx, o_ref, wo_ref, wq_ref, cos_ref, sin_ref, dn_ref,
+    dq_ref, sums, dh_ref, db_out, dn_got,
+    db_buf, in_buf, out_buf, term_acc, rs_send, rs_recv, dn_send, dn_recv, out_sem, *chain_sems
+):
+    wide, cw, chunk, own = plan.wide, plan.cw, plan.chunk, plan.own
+    rows = heads * cw
+    width = heads * HD
+    z = lax.axis_index("wide")
+    index = lax.axis_index("seq") * lax.axis_size("narrow") + lax.axis_index("narrow")
+    unit, g = pl.program_id(0), pl.program_id(1)
+    last_unit, last_g = 2 * wide - 1, kv_heads - 1
+    place = jnp.where(unit == 0, 0, jnp.where(unit == last_unit, 1, unit + 1))
+    piece, half = place // 2, lax.rem(place, 2)
+    w = near_of(plan, z, piece)
+    r = lax.rem(w - z + wide, wide)
+    c = jnp.where(half == 1, 2 * plan.group - 1 - index, index)
+    chain = Chain(plan, db_buf, chain_sems)
+    low_rows = pl.ds(pl.multiple_of(half * cw, cw), cw)
+
+    def give(device):
+        return push(out_buf.at[device], in_buf.at[z], rs_send.at[device], rs_recv.at[z], {"wide": device})
+
+    def give_down(p):
+        device = near_of(plan, z, p)
+        slot = lax.rem(z - device + wide, wide)
+        return push(dn_ref.at[p], dn_got.at[slot], dn_send.at[p], dn_recv.at[slot], {"wide": device})
+
+    def keep(p):
+        device = near_of(plan, z, p)
+        slot = lax.rem(device - z + wide, wide)
+        return pltpu.make_async_copy(db_buf.at[device], db_out.at[slot], out_sem.at[p])
+
+    @pl.when((unit == 0) & (g == 0))
+    def _():
+        db_buf[z] = dx2_ref[...].astype(BF)
+        greet([along_wide(plan, k) for k in range(1, wide)])
+        chain.go(1)
+        keep(0).start()
+
+        @pl.loop(0, kv_heads * plan.total // chunk)
+        def _(b):
+            at = pl.ds(pl.multiple_of(lax.rem(b, plan.total // chunk) * chunk, chunk), chunk)
+            sums[b // (plan.total // chunk), at, :] = jnp.zeros((chunk, 128), F32)
+
+    for h in range(1, wide):
+        @pl.when((unit == 2 * h - 1) & (g == 0))
+        def _():
+            chain.arrive(h)
+            if h + 1 < wide:
+                chain.go(h + 1)
+
+        @pl.when((unit == 2 * h - 2) & (g == last_g))
+        def _():
+            give_down(h).start()
+
+        @pl.when((unit == 2 * h - 1) & (g == last_g))
+        def _():
+            keep(h).start()
+
+    lane = lax.broadcasted_iota(jnp.int32, (cw, 128), 1)
+    columns = pl.ds(pl.multiple_of(g * width, width), width)
+    grad = lax.dot_general(db_buf[w, low_rows, :], wo_ref[g], NT, preferred_element_type=F32)
+    do = split_heads(grad.astype(BF).astype(F32), heads, False)
+    o = split_heads(o_ref[r, low_rows, columns].astype(F32), heads, False)
+    marked = []
+    for one, other in zip(o, do):
+        clean = jnp.where(lane >= HD, other, 0.0)
+        first, second, third = pieces_of(-jnp.sum(one * clean, axis=1, keepdims=True))
+        tile = jnp.where(lane == 0, first, clean)
+        tile = jnp.where(lane == 1, second, tile)
+        marked.append(jnp.where(lane == 2, third, tile))
+    dox32 = jnp.concatenate(marked, axis=0)
+    wide_lane = lax.broadcasted_iota(jnp.int32, (rows, 128), 1)
+    dox = dox32.astype(BF)
+    do_clean = jnp.where(wide_lane >= HD, dox32, 0.0).astype(BF)
+    q = qe_ref[r, g, half]
+    q_clean = jnp.where(wide_lane < HD, q.astype(F32), 0.0).astype(BF)
+
+    def step(j, dq, diagonal=False):
+        at = pl.ds(pl.multiple_of(j * chunk, chunk), chunk)
+        key = kx[g, at, :]
+        s = lax.dot_general(key, q, NT, preferred_element_type=F32)
+        if diagonal:
+            row = lax.broadcasted_iota(jnp.int32, (chunk, rows), 1) % cw + w * cw
+            col = lax.broadcasted_iota(jnp.int32, (chunk, rows), 0)
+            s = jnp.where(col <= row, s, NEG)
+        p = jnp.exp(s)
+        dp = lax.dot_general(vx[g, at, :], dox, NT, preferred_element_type=F32)
+        ds = (p * dp).astype(BF)
+        sums[g, at, :] += jnp.dot(ds, q_clean, preferred_element_type=F32) + jnp.dot(
+            p.astype(BF), do_clean, preferred_element_type=F32
+        )
+        return dq + lax.dot_general(ds, key, TN, preferred_element_type=F32)
+
+    dq = lax.fori_loop(0, c, step, jnp.zeros((rows, 128), F32))
+    dq = step(c, dq, True) * (HD ** -0.5)
+    dq = join_heads([dq[h * cw : (h + 1) * cw] for h in range(heads)], True)
+    at = pl.ds(pl.multiple_of(r * own + half * cw, cw), cw)
+    dq = dq * widen(cos_ref[at, :], width) + turn(dq, -1.0) * widen(sin_ref[at, :], width)
+    dq = dq.astype(BF)
+    dq_ref[at, columns] = dq
+
+    term = lax.dot_general(dq, wq_ref[:, columns], NT, preferred_element_type=F32)
+
+    @pl.when(g == 0)
+    def _():
+        term_acc[...] = term
+
+    @pl.when(g > 0)
+    def _():
+        term_acc[...] += term
+
+    @pl.when((g == last_g) & (piece == 0))
+    def _():
+        dh_ref[low_rows, :] = term_acc[...]
+
+    @pl.when((g == last_g) & (piece > 0))
+    def _():
+        out_buf[w, low_rows, :] = term_acc[...].astype(BF)
+
+    @pl.when((g == last_g) & (piece > 0) & (half == 1))
+    def _():
+        give(w).start()
+
+    @pl.when((unit == last_unit) & (g == last_g))
+    def _():
+        for p in range(1, wide):
+            other = near_of(plan, z, p)
+            push(out_buf.at[z], in_buf.at[other], rs_send.at[z], rs_recv.at[other], {"wide": other}).wait_recv()
+        tall = min(32, own)
+
+        @pl.loop(0, own // tall)
+        def _(b):
+            at = pl.ds(pl.multiple_of(b * tall, tall), tall)
+            total = dh_ref[at, :]
+            for p in range(1, wide):
+                total = total + in_buf[near_of(plan, z, p), at, :].astype(F32)
+            dh_ref[at, :] = total
+
+        chain.finish()
+        for p in range(wide):
+            keep(p).wait()
+        for p in range(1, wide):
+            other = near_of(plan, z, p)
+            slot = lax.rem(other - z + wide, wide)
+            push(dn_ref.at[p], dn_got.at[slot], dn_send.at[p], dn_recv.at[slot], {"wide": other}).wait_recv()
+            give(other).wait_send()
+            give_down(p).wait_send()
+
+
+def backward_call(plan, dx2, qe, kx, vx, o, w_o, w_q, cos, sin, down, heads):
+    kv_heads, total, _ = kx.shape
+    own, d = dx2.shape
+    wide, rows, cw = plan.wide, plan.rows, plan.cw
+    qw = w_q.shape[1]
+    pairs = kv_heads * heads * total * rows // 2
+    fixed = lambda a: pl.BlockSpec(a.shape, lambda u, g: (0,) * a.ndim, pipeline_mode=pl.Buffered(1))
+    hbm = pl.BlockSpec(memory_space=pl.ANY)
+    given = [dx2, qe, kx, vx, o, w_o.reshape(kv_heads, heads * HD, d), w_q, cos, sin]
+    outs = [
+        jax.ShapeDtypeStruct((rows, qw), BF),
+        jax.ShapeDtypeStruct((kv_heads, total, 128), F32),
+        jax.ShapeDtypeStruct((own, d), F32),
+    ]
+    pieces = jax.ShapeDtypeStruct((wide, own, d), BF)
+    buffer = pltpu.VMEM((wide, own, d), BF)
+    sems = pltpu.SemaphoreType.DMA((wide,))
+    return pl.pallas_call(
+        functools.partial(backward_kernel, plan, kv_heads, heads),
+        grid=(2 * wide, kv_heads),
+        in_specs=[fixed(a) for a in given] + [hbm],
+        out_specs=[fixed(a) for a in outs] + [hbm, hbm],
+        out_shape=outs + [pieces, pieces],
+        scratch_shapes=[buffer, buffer, buffer, pltpu.VMEM((cw, d), F32)] + [sems] * 9,
+        cost_estimate=pl.CostEstimate(
+            flops=36 * pairs * HD, bytes_accessed=12 * kv_heads * total * 128, transcendentals=pairs
+        ),
+        compiler_params=pltpu.CompilerParams(
+            vmem_limit_bytes=60 << 20, collective_id=3, has_side_effects=True
+        ),
+        name="attention_backward",
+    )(*given, down)
+
+
 def tail_kernel(
-    plan, kv_heads, *refs
+    plan, kv_heads, sums_ref, h_ref, res_ref, dh_ref, gain2_ref, dx2_ref, x_ref, gain_ref, wkv_ref,
+    cos_ref, sin_ref, res_out, got_out, gain_out, kv_out,
+    swap_out, swap_in, low, near_in, dkv, head_in, dh_acc, dx_low, every, results,
+    gain_part, gain_in, gain_sum, gain_all, kv_part, kv_in,
+    swap_sem, near_send, near_recv, head_send, head_recv, part_send, part_recv,
+    res_send, res_recv, gain_send, gain_recv, gain2_send, gain2_recv, kv_send, kv_recv, own_sem, *chain_sems
 ):
-    sums_ref = refs[:kv_heads]
-    (
-        dh_ref, term_ref, gain2_ref, dx2_ref, x_ref, gain_ref, wkv_ref, cos_ref, sin_ref,
-        dkv_ref, got_ref, gain_out,
-        swap_out, swap_in, low, near_in, mine, head_in, dh_acc, dx_low, every, term_in,
-        gain_part, gain_in, gain_sum, gain_all,
-        swap_sem, near_send, near_recv, head_send, head_recv, part_send, part_recv,
-        right_send, right_recv, left_send, left_recv, own_sem, term_sem,
-        gain_send, gain_recv, gain2_send, gain2_recv,
-    ) = refs[kv_heads:]
     group, wide, chunk, cw, own = plan.group, plan.wide, plan.chunk, plan.cw, plan.own
     narrow = group // 2
     part = dx_low.shape[1] // narrow
     seq, me, z = lax.axis_index("seq"), lax.axis_index("narrow"), lax.axis_index("wide")
     index = seq * narrow + me
+    res_chain = Chain(plan, results, chain_sems[:4])
+    dx_chain = Chain(plan, every, chain_sems[4:])
+
+    def device(k):
+        return lax.rem(index + k + group, group)
 
     def member(k):
-        other = lax.rem(index + k + group, group)
-        return {"seq": other // narrow, "narrow": lax.rem(other, narrow)}
-
-    sibling = {"seq": 1 - seq}
+        return {"seq": device(k) // narrow, "narrow": lax.rem(device(k), narrow)}
+
     greet([member(k) for k in range(1, group)] + [along_wide(plan, r) for r in range(1, wide)])
+
+    def slab(ref, other):
+        rows = pl.ds(pl.multiple_of((other // narrow) * cw, cw), cw)
+        return ref.at[rows, pl.ds(pl.multiple_of(lax.rem(other, narrow) * part, part), part)]
+
+    class Parts:
+        def __init__(self, ref, slots, send, recv, stay):
+            self.ref, self.slots, self.send, self.recv = ref, slots, send, recv
+            self.stay = pltpu.make_async_copy(slab(ref, index), slots.at[z, index], stay)
+
+        def to(self, k):
+            return push(slab(self.ref, device(k)), self.slots.at[z, index], self.send.at[k], self.recv.at[k], member(k))
+
+        def start(self):
+            for k in range(1, group):
+                self.to(k).start()
+            self.stay.start()
+
+        def wait(self):
+            self.stay.wait()
+            for k in range(1, group):
+                other = device(-k)
+                push(
+                    slab(self.ref, index), self.slots.at[z, other], self.send.at[k], self.recv.at[k], member(k)
+                ).wait_recv()
+
+        def sent(self):
+            for k in range(1, group):
+                self.to(k).wait_send()
 
     def place(owner_seq, half, n):
         quarter = owner_seq if half == 0 else 3 - owner_seq
-        return (quarter * narrow + (n if half == 0 else narrow - 1 - n)) * chunk
+        return pl.ds(
+            pl.multiple_of((quarter * narrow + (n if half == 0 else narrow - 1 - n)) * chunk, chunk), chunk
+        )
 
     @pl.loop(0, narrow)
     def _(n):
         for g in range(kv_heads):
             for half in range(2):
-                at = pl.ds(pl.multiple_of(place(1 - seq, half, n), chunk), chunk)
-                swap_out[n, g, half] = sums_ref[g][at, :].astype(BF)
-
-    swap = push(swap_out, swap_in, swap_sem.at[0], swap_sem.at[1], sibling)
+                swap_out[n, g, half] = sums_ref[g, place(1 - seq, half, n), :].astype(BF)
+
+    swap = push(swap_out, swap_in, swap_sem.at[0], swap_sem.at[1], {"seq": 1 - seq})
     swap.start()
-    term = push(term_ref, term_in, term_sem.at[0], term_sem.at[1], along_wide(plan, -1))
-    term.start()
+    res_parts = Parts(res_ref, results, res_send, res_recv, own_sem.at[0])
+    res_parts.start()
     swap.wait_recv()
 
     @pl.loop(0, narrow)
     def _(n):
         for g in range(kv_heads):
             for half in range(2):
-                at = pl.ds(pl.multiple_of(place(seq, half, n), chunk), chunk)
-                low[n, g, half] = (sums_ref[g][at, :] + swap_in[n, g, half].astype(F32)).astype(BF)
+                total = sums_ref[g, place(seq, half, n), :] + swap_in[n, g, half].astype(F32)
+                low[n, g, half] = total.astype(BF)
 
     def near(k):
         other = lax.rem(me + k, narrow)
@@ -636,13 +788,14 @@
 
     for k in range(1, narrow):
         near(k).start()
+    res_parts.wait()
+    res_chain.go(1)
     for k in range(1, narrow):
         near(k).wait_recv()
 
     lane = lax.broadcasted_iota(jnp.int32, (cw, 128), 1)
     for r in range(wide):
-        block = lax.rem(z + r, wide)
-        at = pl.ds(pl.multiple_of(block * cw, cw), cw)
+        at = pl.ds(pl.multiple_of(lax.rem(z + r, wide) * cw, cw), cw)
         for half in range(2):
             rows = slice((2 * r + half) * cw, (2 * r + half + 1) * cw)
             for g in range(kv_heads):
@@ -650,28 +803,41 @@
                 for k in range(1, narrow):
                     total = total + near_in[k, g, half, at, :].astype(F32)
                 back = total * cos_ref[rows, :] + turn(total, -1.0) * sin_ref[rows, :]
-                value = jnp.where(lane < HD, back, total).astype(BF)
-                mine[r, half * cw : (half + 1) * cw, g * 128 : (g + 1) * 128] = value
-                dkv_ref[rows, g * 128 : (g + 1) * 128] = value
+                dkv[rows, g * 128 : (g + 1) * 128] = jnp.where(lane < HD, back, total).astype(BF)
 
     def heads_to(r):
-        return push(mine.at[r], head_in.at[r], head_send.at[r], head_recv.at[r], along_wide(plan, r))
+        mine = dkv.at[pl.ds(r * own, own)]
+        return push(mine, head_in.at[r], head_send.at[r], head_recv.at[r], along_wide(plan, r))
 
     for r in range(1, wide):
         heads_to(r).start()
-    head_in[0] = mine[0]
+
+    for n in range(narrow):
+        columns = slice(n * part, (n + 1) * part)
+        kv_part[n] = lax.dot_general(dkv[...], h_ref[:, columns], TN, preferred_element_type=F32).astype(BF)
+
+    def kv_to(k):
+        return push(kv_part.at[lax.rem(device(k), narrow)], kv_in.at[k], kv_send.at[k], kv_recv.at[k], member(k))
+
+    for k in range(1, group):
+        kv_to(k).start()
+    if wide > 1:
+        res_chain.arrive(1)
+    if wide > 2:
+        res_chain.go(2)
+
     tile = min(512, part)
     for r in range(wide):
         if r > 0:
             heads_to(r).wait_recv()
+        mine = dkv[0:own] if r == 0 else head_in[r]
 
         @pl.loop(0, dh_acc.shape[1] // tile)
         def _(b):
             at = pl.ds(pl.multiple_of(b * tile, tile), tile)
-            more = lax.dot_general(head_in[r], wkv_ref[r, at, :], NT, preferred_element_type=F32)
+            more = lax.dot_general(mine, wkv_ref[r, at, :], NT, preferred_element_type=F32)
             dh_acc[:, at] = (dh_ref[:, at] if r == 0 else dh_acc[:, at]) + more
 
-    term.wait_recv()
     gain_part[0:1, :] = jnp.zeros_like(gain2_ref[...])
     gain_part[1:2, :] = gain2_ref[...]
     tall = min(32, own)
@@ -679,7 +845,7 @@
     @pl.loop(0, own // tall)
     def _(b):
         at = pl.ds(pl.multiple_of(b * tall, tall), tall)
-        dh1 = dh_acc[at, :] + term_in[at, :].astype(F32)
+        dh1 = dh_acc[at, :]
         x = x_ref[at, :].astype(F32)
         scale = lax.rsqrt(jnp.mean(x * x, axis=1, keepdims=True) + EPS)
         z1 = x * scale
@@ -688,38 +854,25 @@
         inner = jnp.mean(dz1 * z1, axis=1, keepdims=True)
         dx_low[at, :] = (dx2_ref[at, :] + scale * (dz1 - z1 * inner)).astype(BF)
 
-    def slab(other):
-        rows = pl.ds(pl.multiple_of((other // narrow) * cw, cw), cw)
-        return dx_low.at[rows, pl.ds(pl.multiple_of(lax.rem(other, narrow) * part, part), part)]
-
-    def parts_to(k):
-        other = lax.rem(index + k, group)
-        return push(slab(other), every.at[0, index], part_send.at[k], part_recv.at[k], member(k))
-
-    def parts_from(k):
-        other = lax.rem(index - k + group, group)
-        return push(slab(index), every.at[0, other], part_send.at[k], part_recv.at[k], member(k))
-
-    def columns(other):
-        return gain_part.at[:, pl.ds(pl.multiple_of(lax.rem(other, narrow) * part, part), part)]
+    dx_parts = Parts(dx_low, every, part_send, part_recv, own_sem.at[1])
+    dx_parts.start()
 
     def gain_to(k):
-        other = lax.rem(index + k, group)
-        return push(columns(other), gain_in.at[k], gain_send.at[k], gain_recv.at[k], member(k))
-
-    for k in range(1, group):
-        parts_to(k).start()
+        columns = pl.ds(pl.multiple_of(lax.rem(device(k), narrow) * part, part), part)
+        return push(gain_part.at[:, columns], gain_in.at[k], gain_send.at[k], gain_recv.at[k], member(k))
+
     for k in range(1, group):
         gain_to(k).start()
-    stay = pltpu.make_async_copy(slab(index), every.at[0, index], own_sem)
-    stay.start()
-    stay.wait()
-    for k in range(1, group):
-        parts_from(k).wait_recv()
+    for h in range(2, wide):
+        res_chain.arrive(h)
+        if h + 1 < wide:
+            res_chain.go(h + 1)
+    dx_parts.wait()
+    dx_chain.go(1)
+
+    gain = gain_part[:, pl.ds(pl.multiple_of(me * part, part), part)]
     for k in range(1, group):
         gain_to(k).wait_recv()
-    gain = gain_part[:, pl.ds(pl.multiple_of(me * part, part), part)]
-    for k in range(1, group):
         gain = gain + gain_in[k]
     gain_sum[...] = gain
 
@@ -728,123 +881,109 @@
 
     for r in range(1, wide):
         gain_on(r).start()
-
-    def to_right(h):
-        return push(
-            every.at[(wide - h) % wide], every.at[wide - 1 - h], right_send.at[h], right_recv.at[h], along_wide(plan, 1)
-        )
-
-    def to_left(h):
-        return push(every.at[h], every.at[h + 1], left_send.at[h], left_recv.at[h], along_wide(plan, -1))
-
-    for h in range(wide - 1):
-        @pl.when((z <= wide - 2) & (z >= h))
-        def _():
-            to_right(h).start()
-
-        @pl.when((z >= 1) & (z + h <= wide - 1))
-        def _():
-            to_left(h).start()
-
-        @pl.when(z >= h + 1)
-        def _():
-            to_right(h).wait_recv()
-
-        @pl.when(z + h + 1 <= wide - 1)
-        def _():
-            to_left(h).wait_recv()
-
-    for h in range(wide - 1):
-        @pl.when((z <= wide - 2) & (z >= h))
-        def _():
-            to_right(h).wait_send()
-
-        @pl.when((z >= 1) & (z + h <= wide - 1))
-        def _():
-            to_left(h).wait_send()
-
-    got_ref[...] = every[...]
+    for k in range(1, group):
+        kv_to(k).wait_recv()
+    res_keep = pltpu.make_async_copy(results, res_out, own_sem.at[2])
+    res_keep.start()
+    kv_out[...] = kv_part[me].astype(F32)
+    for k in range(1, group):
+        kv_out[...] += kv_in[k].astype(F32)
     gain = gain_sum[...]
     for r in range(1, wide):
         gain_on(r).wait_recv()
         gain = gain + gain_all[r]
     gain_out[...] = gain
-    for r in range(1, wide):
-        gain_on(r).wait_send()
-    for k in range(1, group):
-        gain_to(k).wait_send()
-    term.wait_send()
+    for h in range(1, wide):
+        dx_chain.arrive(h)
+        if h + 1 < wide:
+            dx_chain.go(h + 1)
+    got_keep = pltpu.make_async_copy(every, got_out, own_sem.at[3])
+    got_keep.start()
+
+    res_chain.finish()
+    dx_chain.finish()
     swap.wait_send()
     for k in range(1, narrow):
         near(k).wait_send()
     for r in range(1, wide):
         heads_to(r).wait_send()
+        gain_on(r).wait_send()
+    res_parts.sent()
+    dx_parts.sent()
     for k in range(1, group):
-        parts_to(k).wait_send()
-
-
-def tail_call(plan, sums, dh, term, gain2, dx2, x, gain, w_kv, cos, sin):
-    kv_heads = len(sums)
+        gain_to(k).wait_send()
+        kv_to(k).wait_send()
+    res_keep.wait()
+    got_keep.wait()
+
+
+def tail_call(plan, sums, h, res, dh, gain2, dx2, x, gain, w_kv, cos, sin):
+    kv_heads = sums.shape[0]
     own, d = dh.shape
     group, wide, chunk, cw = plan.group, plan.wide, plan.chunk, plan.cw
     narrow = group // 2
     part = d // narrow
+    kv_width = kv_heads * 128
     dma = pltpu.SemaphoreType.DMA
     quarter = pltpu.VMEM((narrow, kv_heads, 2, chunk, 128), BF)
+    slots = (wide, group, cw, part)
+    given = [sums, h, res, dh, gain2, dx2, x, gain, w_kv, cos, sin]
     whole = pl.BlockSpec(memory_space=pltpu.VMEM)
+    hbm = pl.BlockSpec(memory_space=pl.ANY)
     return pl.pallas_call(
         functools.partial(tail_kernel, plan, kv_heads),
-        in_specs=[whole] * (kv_heads + 9),
-        out_specs=[whole] * 3,
+        in_specs=[whole] * len(given),
+        out_specs=[hbm, hbm, whole, whole],
         out_shape=[
-            jax.ShapeDtypeStruct((plan.rows, kv_heads * 128), BF),
-            jax.ShapeDtypeStruct((wide, group, cw, part), BF),
+            jax.ShapeDtypeStruct(slots, BF),
+            jax.ShapeDtypeStruct(slots, BF),
             jax.ShapeDtypeStruct((2, part), F32),
+            jax.ShapeDtypeStruct((kv_width, part), F32),
         ],
         scratch_shapes=[
             quarter, quarter, quarter, quarter,
-            pltpu.VMEM((wide, own, kv_heads * 128), BF),
-            pltpu.VMEM((wide, own, kv_heads * 128), BF),
+            pltpu.VMEM((plan.rows, kv_width), BF),
+            pltpu.VMEM((wide, own, kv_width), BF),
             pltpu.VMEM((own, d), F32),
             pltpu.VMEM((own, d), BF),
-            pltpu.VMEM((wide, group, cw, part), BF),
-            pltpu.VMEM((own, d), BF),
+            pltpu.VMEM(slots, BF),
+            pltpu.VMEM(slots, BF),
             pltpu.VMEM((2, d), F32),
             pltpu.VMEM((group, 2, part), F32),
             pltpu.VMEM((2, part), F32),
             pltpu.VMEM((wide, 2, part), F32),
+            pltpu.VMEM((narrow, kv_width, part), BF),
+            pltpu.VMEM((group, kv_width, part), BF),
             dma((2,)), dma((narrow,)), dma((narrow,)), dma((wide,)), dma((wide,)), dma((group,)), dma((group,)),
-            dma((wide,)), dma((wide,)), dma((wide,)), dma((wide,)), dma(()), dma((2,)),
-            dma((group,)), dma((group,)), dma((wide,)), dma((wide,)),
-        ],
+            dma((group,)), dma((group,)), dma((group,)), dma((group,)), dma((wide,)), dma((wide,)),
+            dma((group,)), dma((group,)), dma((4,)),
+        ] + [dma((wide,))] * 8,
         cost_estimate=pl.CostEstimate(
-            flops=200 * own * d * wide * kv_heads * 128,
-            bytes_accessed=4 * kv_heads * plan.total * 128,
-            transcendentals=0,
+            flops=200 * own * d * wide * kv_width, bytes_accessed=4 * sums.size, transcendentals=0
         ),
         compiler_params=pltpu.CompilerParams(
-            vmem_limit_bytes=58 << 20, collective_id=2, has_side_effects=True
+            vmem_limit_bytes=60 << 20, collective_id=2, has_side_effects=True
         ),
         name="input_gradient",
-    )(*sums, dh, term, gain2, dx2, x, gain, w_kv, cos, sin)
-
-
-def assemble_kernel(plan, crossed, s_ref, in_ref, out_ref):
+    )(*given)
+
+
+def assemble_kernel(plan, s_ref, in_ref, out_ref):
     group = plan.group
     for l in range(group):
         owner = jnp.where(s_ref[0] >= group // 2, group - 1 - l, l)
-        out_ref[l, 0] = in_ref[0, s_ref[0] ^ owner if crossed else owner].astype(out_ref.dtype)
-
-
-def assemble_call(plan, scalars, values, dtype, crossed):
+        out_ref[l, 0] = in_ref[0, owner].astype(out_ref.dtype)
+
+
+def assemble_call(plan, scalars, values, dtype):
     wide, group, cw, part = values.shape
     out = pl.pallas_call(
-        functools.partial(assemble_kernel, plan, crossed),
+        functools.partial(assemble_kernel, plan),
         grid_spec=pltpu.PrefetchScalarGridSpec(
             num_scalar_prefetch=1,
             grid=(wide,),
-            in_specs=[pl.BlockSpec((1, group, cw, part), lambda r, s: (r, 0, 0, 0))],
-            out_specs=[pl.BlockSpec((group, 1, cw, part), lambda r, s: (0, block_of(plan, s, r), 0, 0))],
+            in_specs=[pl.BlockSpec((1, group, cw, part), lambda w, s: (w, 0, 0, 0))],
+            out_specs=[pl.BlockSpec((group, 1, cw, part), lambda w, s: (0, w, 0, 0))],
         ),
         out_shape=[jax.ShapeDtypeStruct((group, wide, cw, part), dtype)],
         cost_estimate=pl.CostEstimate(flops=values.size, bytes_accessed=6 * values.size, transcendentals=0),
@@ -901,20 +1040,11 @@
     def send(values, r):
         return values if r == 0 else lax.ppermute(values, "wide", [(a, (a + r) % wide) for a in pieces])
 
-    def fetch(values, r):
-        return send(values, (wide - r) % wide)
-
     def wide_total(parts):
         out = parts[0]
         for r in range(1, len(parts)):
             out = out + send(parts[r].astype(BF), r).astype(F32)
         return out
-
-    def from_rows(values, dtype):
-        parts = values.astype(BF).reshape(2, cw, narrow, d_part)
-        parts = jnp.transpose(parts, (0, 2, 1, 3)).reshape(group, cw, d_part)
-        got = exchange(parts)
-        return assemble_call(plan, scalars, jnp.stack([fetch(got, r) for r in pieces]), dtype, True)
 
     def gather_weight(weight):
         return lax.all_gather(half_of(weight, seq_index, seq_count), NS, axis=0, tiled=True)
@@ -968,7 +1098,6 @@
     g_rows = rows_call(plan, scalars, g_parts)
 
     far_first = sorted(pieces, key=lambda r: (r == 0, -min(r, wide - r)))
-    near_first = sorted(pieces, key=lambda r: min(r, wide - r))
     o, qe, attn = [None] * wide, [None] * wide, [None] * wide
     for r in far_first:
         o[r], qe[r] = forward_call(plan, scalars, q, kx, vx, kv_heads, heads, r)
@@ -978,35 +1107,21 @@
 
     act, d_gate, d_up, h_all, down, dx2, grad_gain_two = ffn_call(plan, x2, gain_two, g_rows, w_gu, w_dn)
 
-    db_own = dx2.astype(BF)
-    db = [fetch(db_own, r) for r in pieces]
-    sums = [None] * kv_heads
-    dq, terms = [None] * wide, [None] * wide
-    w_q = w_qkv[:, :qw]
-    w_k = w_qkv[:, qw:]
-    for r in pieces:
-        do = lax.dot_general(db[r], w_o, NT, preferred_element_type=F32).astype(BF)
-        parts = []
-        for g in range(kv_heads):
-            part, sums[g] = backward_call(
-                plan, scalars, qe[r], kx, vx, o[r], do, cos, sin, heads, r, g, sums[g]
-            )
-            parts.append(part)
-        dq[r] = jnp.concatenate(parts, axis=1)
-        terms[r] = lax.dot_general(dq[r], w_q, NT, preferred_element_type=F32)
-    dh1 = wide_total(terms[:-1])
-
-    down = after(down, *db)
-    slot = [jnp.argmax(near_of(plan, wide_index, jnp.arange(wide)) == (wide_index + r) % wide) for r in pieces]
-    down = [lax.dynamic_index_in_dim(down, slot[r], 0, keepdims=False) for r in pieces]
-    result = from_rows(x2 + wide_total([down[0].astype(F32)] + down[1:]), BF)
-
-    w_k_all = jnp.stack([send(w_k, r) for r in pieces])
-    sums[0] = after(sums[0], result)
-    dkv, got, gain_grads = tail_call(
-        plan, sums, dh1, terms[-1].astype(BF), grad_gain_two, dx2, x_low, gain_one, w_k_all, cos, sin
+    o = jnp.stack(o)
+    w_q, w_kv = w_qkv[:, :qw], w_qkv[:, qw:]
+    dq, sums, dh1, db, down_in = backward_call(
+        plan, dx2, jnp.stack(qe), kx, vx, o, w_o, w_q, cos, sin, down, heads
     )
-    input_grad = assemble_call(plan, scalars, got, F32, False)
+    result = x2 + down[0].astype(F32)
+    for r in range(1, wide):
+        result = result + down_in[r].astype(F32)
+
+    w_kv = jnp.stack([send(w_kv, r) for r in pieces])
+    result, input_grad, gain_grads, grad_kv = tail_call(
+        plan, sums, h_one, result.astype(BF), dh1, grad_gain_two, dx2, x_low, gain_one, w_kv, cos, sin
+    )
+    result = assemble_call(plan, scalars, result, BF)
+    input_grad = assemble_call(plan, scalars, input_grad, F32)
 
     def tn(left, right):
         return lax.dot_general(left, right, TN, preferred_element_type=F32).astype(BF)
@@ -1016,14 +1131,14 @@
 
     grad_gu = scatter_grad(jnp.concatenate([tn(h_all, d_gate), tn(h_all, d_up)], axis=1))
     grad_dn = scatter_grad(tn_split(act, g_rows))
-    grad_o = scatter_grad(tn_split(jnp.concatenate(o, axis=0), jnp.concatenate(db, axis=0)))
-    grad_qkv = scatter_grad(tn(h_one, jnp.concatenate([jnp.concatenate(dq, axis=0), dkv], axis=1)))
-    grad_kv = grad_qkv[:, qw:].reshape(d_part, kv_heads, 2, HD)
+    grad_o = scatter_grad(tn_split(o.reshape(rows, qw), db.reshape(rows, d)))
+    grad_q = scatter_grad(tn(h_one, dq))
+    grad_kv = jnp.transpose(grad_kv.reshape(kv_heads, 2, HD, d_part), (3, 0, 1, 2))
     return (
         result,
         input_grad,
         gain_grads[0],
-        grad_qkv[:, :qw],
+        grad_q,
         grad_kv[:, :, 0].reshape(d_part, kw),
         grad_kv[:, :, 1].reshape(d_part, kw),
         grad_o,

time: 1340 us -> 1200 us (0.90)
  waiting for transfers between devices: 343 us -> 172 us
  Pallas kernels: 652 us -> 785 us
  starting transfers between devices: 91.9 us -> 38.7 us
  matrix products: 69.5 us -> 51.4 us
  local copies, waits for them, and re-layouts: 93.5 us -> 79.6 us
    ppermute x17 -> x6, waiting for transfers between devices: 178 us -> 69.9 us  [send(): lax.ppermute(values, 'wide', [(a, (a + r) % wide) for a in pieces])]
    pallas_call x10 -> x3, Pallas kernels: 182 us -> 278 us  [the longest x1 271 us: backward_call(): pl.pallas_call(functools.partial(backward_kernel, plan, kv_heads, heads),...]
    ppermute x17 -> x6, starting transfers between devices: 66.5 us -> 17.7 us  [send(): lax.ppermute(values, 'wide', [(a, (a + r) % wide) for a in pieces])]
    pallas_call x1, Pallas kernels: 144 us -> 190 us  [tail_call(): pl.pallas_call(functools.partial(tail_kernel, plan, kv_heads), in_specs=[...]
    reduce_scatter x4, waiting for transfers between devices: 32.4 us -> 0.02 us  [scatter_grad(): lax.psum_scatter(grad.astype(BF), NS, scatter_dimension=0, tiled=True)]
    all_gather x2, waiting for transfers between devices: 18 us -> 0.01 us  [scatter_grad(): return lax.all_gather(mine, 'seq', axis=0, tiled=True).astype(F32)]
    dot_general x8 -> x0, matrix products: 16.8 us -> none  [the longest x4 8.78 us: body(): terms[r] = lax.dot_general(dq[r], w_q, NT, preferred_element_type=F32)]
    ppermute x31 -> x24, waiting for transfers between devices: 113 us -> 101 us  [swap(): lax.ppermute(values, axes, [(a, a ^ k) for a in range(size)])]
  transfers between devices with their start and end apart: 58 -> 40, of which waited for: 21 -> 12; matrix products, arithmetic and copies ran while one was open for 12% -> 10% of each run, Pallas kernels for 33% -> 48%
where the time goes in v3:
time: 1200 us
  Pallas kernels  785 us (65%)
  waiting for transfers between devices  172 us (14%)
  local copies, waits for them, and re-layouts  79.6 us (7%)
  matrix products  51.4 us (4%)
  other arithmetic  50.2 us (4%)
  starting transfers between devices  38.7 us (3%)
  between operations  15.5 us (1%)
    pallas_call x1, Pallas kernels, backward_call(): pl.pallas_call(functools.partial(backward_kernel, plan, kv_heads, heads),...  271 us
    pallas_call x1, Pallas kernels, ffn_call(): pl.pallas_call(functools.partial(ffn_kernel, plan), grid=(wide, tiles), i...  205 us
    pallas_call x1, Pallas kernels, tail_call(): pl.pallas_call(functools.partial(tail_kernel, plan, kv_heads), in_specs=[...  190 us
    ppermute x24, waiting for transfers between devices, swap(): lax.ppermute(values, axes, [(a, a ^ k) for a in range(size)])  101 us
    pallas_call x4, Pallas kernels, forward_call(): pl.pallas_call(functools.partial(forward_kernel, plan, heads, r), grid_sp...  96.5 us
    ppermute x6, waiting for transfers between devices, send(): lax.ppermute(values, 'wide', [(a, (a + r) % wide) for a in pieces])  69.9 us
    unnamed x132, local copies, waits for them, and re-layouts  54.4 us
    dot_general x11, matrix products, tn(): lax.dot_general(left, right, TN, preferred_element_type=F32).astype(BF)  46.7 us
  transfers between devices with their start and end apart: 40, of which 12 were waited for; matrix products, arithmetic and copies ran while one was open for 10% of the time, Pallas kernels for 48%

profile of v3, /device:TPU:0, one launch (start us, length us, event | category | flops | bytes accessed | tf_op | source)
XLA Modules:
  0.0 1197.2 jit_solution(14695733955437496197)
XLA Ops:
  11.5 5.0 reverse_select_fusion.1
  17.0 3.0 collective-permute-start
  23.6 13.4 %collective-permute-done = bf16[4,128,512]{2,1,0:T(8,128)(2,1)S(1)} collective-permute-done((bf16[4,128,512]{2,1,0:T(8,128)(2,1)S(1)}, bf16[4,128,512]{2,1,0:T(8,128)(2,1)S(1)}, u32[]{:S(2)}, u32[]{:S(2)}) %collective-permute-start) | collective-permute-done | bytes 524320 | tf_op jit(solution)/shard_map/ppermute | solution.py:1030
  37.0 12.3 %collective-permute-done.1 = bf16[4,128,512]{2,1,0:T(8,128)(2,1)S(1)} collective-permute-done((bf16[4,128,512]{2,1,0:T(8,128)(2,1)S(1)}, bf16[4,128,512]{2,1,0:T(8,128)(2,1)S(1)}, u32[]{:S(2)}, u32[]{:S(2)}) %collective-permute-start.1) | collective-permute-done | bytes 524320 | tf_op jit(solution)/shard_map/ppermute | solution.py:1030
  49.3 8.4 collective-permute-done.2
  57.8 9.7 collective-permute-done.4
  67.5 12.1 %collective-permute-done.5 = bf16[4,128,512]{2,1,0:T(8,128)(2,1)S(1)} collective-permute-done((bf16[4,128,512]{2,1,0:T(8,128)(2,1)S(1)}, bf16[4,128,512]{2,1,0:T(8,128)(2,1)S(1)}, u32[]{:S(2)}, u32[]{:S(2)}) %collective-permute-start.5) | collective-permute-done | bytes 524320 | tf_op jit(solution)/shard_map/ppermute | solution.py:1030
  83.7 2.7 pad_maximum_fusion.2
  94.0 3.1 multiply_sine_fusion
  97.1 2.8 select_convert_fusion.kf_ref
  106.1 9.5 norm_qkv.1
  124.5 3.2 copy.59
  131.0 12.5 %collective-permute-done.10 = bf16[1024,256]{1,0:T(8,128)(2,1)} collective-permute-done((bf16[1024,256]{1,0:T(8,128)(2,1)}, bf16[1024,256]{1,0:T(8,128)(2,1)}, u32[]{:S(2)}, u32[]{:S(2)}) %collective-permute-start.10) | collective-permute-done | bytes 524320 | tf_op jit(solution)/shard_map/ppermute | solution.py:1030
  146.2 9.4 collective-permute-done.12
  167.5 4.3 keys.1
  178.0 24.2 %attention_forward.5 = (bf16[256,512]{1,0:T(8,128)(2,1)S(1)}, bf16[2,2,512,128]{3,2,1,0:T(8,128)(2,1)S(1)}) custom-call(s32[4]{0:T(128)S(1)} %pad_add_fusion.s_ref, bf16[1024,512]{1,0:T(8,128)(2,1)S(1)} %copy-done.31, bf16[2,8192,128]{2,1,0:T(8,128)(2,1)S(1)} %copy-done.27, bf16[2,8192,128]{2,1,0:T(8,128)(2,1)} %copy-done.28), custom_call_target="tpu_custom_call" | custom-call | flops 8589934592 | bytes 8388608 | tf_op jit(solution)/shard_map/attention_forward/pallas_call | solution.py:237
  204.4 24.0 %attention_forward.4 = (bf16[256,512]{1,0:T(8,128)(2,1)S(1)}, bf16[2,2,512,128]{3,2,1,0:T(8,128)(2,1)S(1)}) custom-call(s32[4]{0:T(128)S(1)} %pad_add_fusion.s_ref, bf16[1024,512]{1,0:T(8,128)(2,1)S(1)} %copy-done.31, bf16[2,8192,128]{2,1,0:T(8,128)(2,1)S(1)} %copy-done.27, bf16[2,8192,128]{2,1,0:T(8,128)(2,1)} %copy-done.28), custom_call_target="tpu_custom_call" | custom-call | flops 8589934592 | bytes 8388608 | tf_op jit(solution)/shard_map/attention_forward/pallas_call | solution.py:237
  229.2 24.3 %attention_forward.6 = (bf16[256,512]{1,0:T(8,128)(2,1)S(1)}, bf16[2,2,512,128]{3,2,1,0:T(8,128)(2,1)S(1)}) custom-call(s32[4]{0:T(128)S(1)} %pad_add_fusion.s_ref, bf16[1024,512]{1,0:T(8,128)(2,1)S(1)} %copy-done.31, bf16[2,8192,128]{2,1,0:T(8,128)(2,1)S(1)} %copy-done.27, bf16[2,8192,128]{2,1,0:T(8,128)(2,1)} %copy-done.28), custom_call_target="tpu_custom_call" | custom-call | flops 8589934592 | bytes 8388608 | tf_op jit(solution)/shard_map/attention_forward/pallas_call | solution.py:237
  254.3 24.1 %attention_forward.7 = (bf16[256,512]{1,0:T(8,128)(2,1)S(1)}, bf16[2,2,512,128]{3,2,1,0:T(8,128)(2,1)S(1)}) custom-call(s32[4]{0:T(128)S(1)} %pad_add_fusion.s_ref, bf16[1024,512]{1,0:T(8,128)(2,1)S(1)} %copy-done.31, bf16[2,8192,128]{2,1,0:T(8,128)(2,1)S(1)} %copy-done.27, bf16[2,8192,128]{2,1,0:T(8,128)(2,1)} %copy-done.28), custom_call_target="tpu_custom_call" | custom-call | flops 8589934592 | bytes 8388608 | tf_op jit(solution)/shard_map/attention_forward/pallas_call | solution.py:237
  284.7 3.9 collective-permute-start.18
  293.6 22.9 %collective-permute-done.25 = bf16[4,128,512]{2,1,0:T(8,128)(2,1)S(1)} collective-permute-done((bf16[4,128,512]{2,1,0:T(8,128)(2,1)S(1)}, bf16[4,128,512]{2,1,0:T(8,128)(2,1)S(1)}, u32[]{:S(2)}, u32[]{:S(2)}) %collective-permute-start.25) | collective-permute-done | bytes 524320 | tf_op jit(solution)/shard_map/ppermute | solution.py:1030
  320.0 35.2 %collective-permute-done.18 = bf16[256,2048]{1,0:T(8,128)(2,1)S(1)} collective-permute-done((bf16[256,2048]{1,0:T(8,128)(2,1)S(1)}, bf16[256,2048]{1,0:T(8,128)(2,1)S(1)}, u32[]{:S(2)}, u32[]{:S(2)}) %collective-permute-start.18) | collective-permute-done | bytes 1048608 | tf_op jit(solution)/shard_map/ppermute | solution.py:1041
  355.2 2.6 add_add_fusion.x2_ref
  357.8 204.9 %feed_forward.1 = (bf16[1024,2048]{1,0:T(8,128)(2,1)}, bf16[1024,2048]{1,0:T(8,128)(2,1)}, bf16[1024,2048]{1,0:T(8,128)(2,1)}, bf16[1024,2048]{1,0:T(8,128)(2,1)...) custom-call(f32[256,2048]{1,0:T(8,128)} %add_add_fusion.x2_ref, f32[1,2048]{1,0:T(1,128)} %bitcast.178, ...), custom_call_target="tpu_custom_call" | custom-call | flops 68719476736 | bytes 50331648 | tf_op jit(solution)/shard_map/feed_forward/pallas_call | solution.py:481
  562.8 4.7 convolution_convert_fusion.5
  567.5 2.5 convolution_convert_fusion.4
  570.0 2.5 convolution_convert_fusion.3
  572.5 2.5 convolution_convert_fusion.2
  575.0 3.9 pad_maximum_fusion.1
  579.0 12.5 %convolution_convert_fusion.1 = bf16[2048,2048]{0,1:T(8,128)(2,1)S(1)} fusion(bf16[1024,2048]{1,0:T(8,128)(2,1)} %get-tuple-element.75, bf16[1024,2048]{1,0:T(8,128)(2,1)} %get-tuple-element.76), kind=kOutput, calls=%fused_computation.3 | convolution fusion | flops 8594128896 | bytes 16777216 | tf_op jit(solution)/shard_map/dot_general | solution.py:1127
  591.5 9.7 convolution_convert_fusion
  601.2 7.7 pad_maximum_fusion
  609.0 4.9 reshape_reshape.3.wo_ref
  618.2 271.2 %attention_backward.1 = (bf16[1024,512]{1,0:T(8,128)(2,1)}, f32[2,8192,128]{2,1,0:T(8,128)}, f32[256,2048]{1,0:T(8,128)}, bf16[4,256,2048]{2,1,0:T(8,128)(2,1)}, bf16[4,256,2048]{2,1,0:T(8,128)(2,1)}) custom-call(f32[256,2048]{1,0:T(8,128)} %get-tuple-element.58.dx2_ref, bf16[4,2,2,512,128]{4,3,2,1,0:T(8,128)(2,1)} %pad_maximum_fusion.4.qe_ref, ...), custom_call_target="tpu_custom_call" | custom-call | flops 77309411328 | bytes 25165824 | tf_op jit(solution)/shard_map/attention_backward/pallas_call | solution.py:690
  889.4 2.4 convolution_convert_fusion.13
  897.1 6.2 convolution_convert_fusion.6
  904.3 11.9 collective-permute-start.28
  916.2 12.4 %collective-permute-done.27 = bf16[2048,256]{1,0:T(8,128)(2,1)S(1)} collective-permute-done((bf16[2048,256]{1,0:T(8,128)(2,1)S(1)}, bf16[2048,256]{1,0:T(8,128)(2,1)S(1)}, u32[]{:S(2)}, u32[]{:S(2)}) %collective-permute-start.27) | collective-permute-done | bytes 1048608 | tf_op jit(solution)/shard_map/ppermute | solution.py:1041
  928.6 22.3 %collective-permute-done.28 = bf16[2048,256]{1,0:T(8,128)(2,1)S(1)} collective-permute-done((bf16[2048,256]{1,0:T(8,128)(2,1)S(1)}, bf16[2048,256]{1,0:T(8,128)(2,1)S(1)}, u32[]{:S(2)}, u32[]{:S(2)}) %collective-permute-start.28) | collective-permute-done | bytes 1048608 | tf_op jit(solution)/shard_map/ppermute | solution.py:1041
  951.0 2.7 pad_maximum_fusion.3.wkv_ref
  955.4 3.0 fusion.res_ref
  958.5 190.0 %input_gradient.1 = (bf16[4,8,128,512]{3,2,1,0:T(8,128)(2,1)}, bf16[4,8,128,512]{3,2,1,0:T(8,128)(2,1)}, f32[2,512]{1,0:T(2,128)}, f32[256,512]{1,0:T(8,128)}) custom-call(f32[2,8192,128]{2,1,0:T(8,128)} %get-tuple-element.64.sums_ref, bf16[1024,2048]{1,0:T(8,128)(2,1)} %copy-done.29, bf16[256,2048]{1,0:T(8,128)(2,1)} %fusion.res_ref, ...), custom_call_target="tpu_custom_call" | custom-call | flops 107374182400 | bytes 8388608 | tf_op jit(solution)/shard_map/input_gradient/pallas_call | solution.py:933
  1153.5 4.2 assemble.3
  1157.7 3.0 assemble.2
  1168.3 4.2 convert_element_type.143
  1172.5 6.8 fusion.27
  1179.3 5.3 copy.52
  1184.6 5.5 copy.53
  (259 shorter events, 102.4 us)
Async XLA Ops:
  7.2 75.4 %copy-start = (bf16[2048,512]{1,0:T(8,128)(2,1)S(1)}, bf16[2048,512]{1,0:T(8,128)(2,1)}, u32[]{:S(2)}) copy-start(bf16[2048,512]{1,0:T(8,128)(2,1)} %param.22) | copy-start | bytes 6291460
  7.2 94.9 %all-gather.7.cloned.1.call-start = ((), (), s32[]{:S(2)}) async-start(), calls=%async_computation.4 | async-start | bytes 3538944 | tf_op jit(solution)/shard_map/all_gather | solution.py:1050
  11.4 113.1 %all-gather.9.cloned.1.call-start = ((), (), s32[]{:S(2)}) async-start(), calls=%async_computation.5 | async-start | bytes 2359296 | tf_op jit(solution)/shard_map/all_gather | solution.py:1050
  17.0 64.8 %copy-start.43 = (bf16[512,512]{1,0:T(8,128)(2,1)S(1)}, bf16[512,512]{1,0:T(8,128)(2,1)}, u32[]{:S(2)}) copy-start(bf16[512,512]{1,0:T(8,128)(2,1)} %param.18) | copy-start | bytes 1572868
  17.0 20.0 %collective-permute-start = (bf16[4,128,512]{2,1,0:T(8,128)(2,1)S(1)}, bf16[4,128,512]{2,1,0:T(8,128)(2,1)S(1)}, u32[]{:S(2)}, u32[]{:S(2)}) collective-permute-start(bf16[4,128,512]{2,1,0:T(8,128)(2,1)S(1)} %get-tuple-element.130), channel_id=1, source_target_pairs={{0,4},{4,0},{8,12},{12,8},{16,20},{20,16},{24,28},{28,24},{1,5},{5... | collective-permute-start | bytes 1572872 | tf_op jit(solution)/shard_map/ppermute | solution.py:1030
  20.0 29.3 %collective-permute-start.1 = (bf16[4,128,512]{2,1,0:T(8,128)(2,1)S(1)}, bf16[4,128,512]{2,1,0:T(8,128)(2,1)S(1)}, u32[]{:S(2)}, u32[]{:S(2)}) collective-permute-start(bf16[4,128,512]{2,1,0:T(8,128)(2,1)S(1)} %get-tuple-element.129), channel_id=1, source_target_pairs={{0,8},{4,12},{8,0},{12,4},{16,24},{20,28},{24,16},{28,20},{1,9},{5... | collective-permute-start | bytes 1572872 | tf_op jit(solution)/shard_map/ppermute | solution.py:1030
  21.5 36.2 %collective-permute-start.2 = (bf16[4,128,512]{2,1,0:T(8,128)(2,1)S(1)}, bf16[4,128,512]{2,1,0:T(8,128)(2,1)S(1)}, u32[]{:S(2)}, u32[]{:S(2)}) collective-permute-start(bf16[4,128,512]{2,1,0:T(8,128)(2,1)S(1)} %get-tuple-element.128), channel_id=1, source_target_pairs={{0,12},{4,8},{8,4},{12,0},{16,28},{20,24},{24,20},{28,16},{1,13},{... | collective-permute-start | bytes 1572872 | tf_op jit(solution)/shard_map/ppermute | solution.py:1030
  21.5 36.2 %collective-permute-start.3 = (bf16[4,128,512]{2,1,0:T(8,128)(2,1)S(1)}, bf16[4,128,512]{2,1,0:T(8,128)(2,1)S(1)}, u32[]{:S(2)}, u32[]{:S(2)}) collective-permute-start(bf16[4,128,512]{2,1,0:T(8,128)(2,1)S(1)} %get-tuple-element.127), channel_id=1, source_target_pairs={{0,16},{4,20},{8,24},{12,28},{16,0},{20,4},{24,8},{28,12},{1,17},{... | collective-permute-start | bytes 1572872 | tf_op jit(solution)/shard_map/ppermute | solution.py:1030
  21.5 45.9 %collective-permute-start.4 = (bf16[4,128,512]{2,1,0:T(8,128)(2,1)S(1)}, bf16[4,128,512]{2,1,0:T(8,128)(2,1)S(1)}, u32[]{:S(2)}, u32[]{:S(2)}) collective-permute-start(bf16[4,128,512]{2,1,0:T(8,128)(2,1)S(1)} %get-tuple-element.126), channel_id=1, source_target_pairs={{0,20},{4,16},{8,28},{12,24},{16,4},{20,0},{24,12},{28,8},{1,21},{... | collective-permute-start | bytes 1572872 | tf_op jit(solution)/shard_map/ppermute | solution.py:1030
  36.9 42.7 %collective-permute-start.5 = (bf16[4,128,512]{2,1,0:T(8,128)(2,1)S(1)}, bf16[4,128,512]{2,1,0:T(8,128)(2,1)S(1)}, u32[]{:S(2)}, u32[]{:S(2)}) collective-permute-start(bf16[4,128,512]{2,1,0:T(8,128)(2,1)S(1)} %get-tuple-element.125), channel_id=1, source_target_pairs={{0,24},{4,28},{8,16},{12,20},{16,8},{20,12},{24,0},{28,4},{1,25},{... | collective-permute-start | bytes 1572872 | tf_op jit(solution)/shard_map/ppermute | solution.py:1030
  49.3 30.4 %collective-permute-start.6 = (bf16[4,128,512]{2,1,0:T(8,128)(2,1)S(1)}, bf16[4,128,512]{2,1,0:T(8,128)(2,1)S(1)}, u32[]{:S(2)}, u32[]{:S(2)}) collective-permute-start(bf16[4,128,512]{2,1,0:T(8,128)(2,1)S(1)} %get-tuple-element.124), channel_id=1, source_target_pairs={{0,28},{4,24},{8,20},{12,16},{16,12},{20,8},{24,4},{28,0},{1,29},{... | collective-permute-start | bytes 1572872 | tf_op jit(solution)/shard_map/ppermute | solution.py:1030
  82.5 275.3 %all-gather.13.cloned.1.call-start = ((), (), s32[]{:S(2)}) async-start(), calls=%async_computation.7 | async-start | bytes 9437184 | tf_op jit(solution)/shard_map/all_gather | solution.py:1050
  83.6 274.2 %all-gather.11.cloned.1.call-start = ((), (), s32[]{:S(2)}) async-start(), calls=%async_computation.6 | async-start | bytes 18874368 | tf_op jit(solution)/shard_map/all_gather | solution.py:1050
  88.0 815.4 %reduce-scatter.11.cloned.1.call-start = ((), (), s32[]{:S(2)}) async-start(), calls=%async_computation.12 | async-start | bytes 9437184 | tf_op jit(solution)/shard_map/reduce_scatter | solution.py:1053
  88.3 13.0 %collective-permute-start.7 = (f32[2,512]{1,0:T(2,128)S(1)}, f32[2,512]{1,0:T(2,128)S(1)}, u32[]{:S(2)}, u32[]{:S(2)}) collective-permute-start(f32[2,512]{1,0:T(2,128)S(1)} %get-tuple-element.145), channel_id=1, source_target_pairs={{0,4},{4,0},{8,12},{12,8},{1,5},{5,1},{9,13},{13,9},{2,6},{6,2},{1... | collective-permute-start | bytes 12296 | tf_op jit(solution)/shard_map/ppermute | solution.py:1030
  88.4 12.8 %collective-permute-start.8 = (f32[2,512]{1,0:T(2,128)S(1)}, f32[2,512]{1,0:T(2,128)S(1)}, u32[]{:S(2)}, u32[]{:S(2)}) collective-permute-start(f32[2,512]{1,0:T(2,128)S(1)} %get-tuple-element.145), channel_id=1, source_target_pairs={{0,8},{4,12},{8,0},{12,4},{1,9},{5,13},{9,1},{13,5},{2,10},{6,14},... | collective-permute-start | bytes 12296 | tf_op jit(solution)/shard_map/ppermute | solution.py:1030
  90.3 11.0 collective-permute-start.9
  106.1 16.0 %copy-start.37 = (bf16[4096,512]{1,0:T(8,128)(2,1)S(1)}, bf16[4096,512]{1,0:T(8,128)(2,1)}, u32[]{:S(2)}) copy-start(bf16[4096,512]{1,0:T(8,128)(2,1)} %param.25) | copy-start | bytes 12582916
  116.6 238.6 %copy-start.8 = (bf16[256,2048]{1,0:T(8,128)(2,1)}, bf16[256,2048]{1,0:T(8,128)(2,1)S(1)}, u32[]{:S(2)}) copy-start(bf16[256,2048]{1,0:T(8,128)(2,1)S(1)} %get-tuple-element.45.x_ref) | copy-start | bytes 3145732
  118.6 24.9 %collective-permute-start.10 = (bf16[1024,256]{1,0:T(8,128)(2,1)}, bf16[1024,256]{1,0:T(8,128)(2,1)}, u32[]{:S(2)}, u32[]{:S(2)}) collective-permute-start(bf16[1024,256]{1,0:T(8,128)(2,1)} %get-tuple-element.47), channel_id=1, source_target_pairs={{0,4},{4,0},{8,12},{12,8},{1,5},{5,1},{9,13},{13,9},{2,6},{6,2},{1... | collective-permute-start | bytes 1572872 | tf_op jit(solution)/shard_map/ppermute | solution.py:1030
  119.1 26.1 %collective-permute-start.11 = (bf16[1024,256]{1,0:T(8,128)(2,1)}, bf16[1024,256]{1,0:T(8,128)(2,1)}, u32[]{:S(2)}, u32[]{:S(2)}) collective-permute-start(bf16[1024,256]{1,0:T(8,128)(2,1)} %get-tuple-element.47), channel_id=1, source_target_pairs={{0,8},{4,12},{8,0},{12,4},{1,9},{5,13},{9,1},{13,5},{2,10},{6,14},... | collective-permute-start | bytes 1572872 | tf_op jit(solution)/shard_map/ppermute | solution.py:1030
  121.0 34.7 %collective-permute-start.12 = (bf16[1024,256]{1,0:T(8,128)(2,1)}, bf16[1024,256]{1,0:T(8,128)(2,1)}, u32[]{:S(2)}, u32[]{:S(2)}) collective-permute-start(bf16[1024,256]{1,0:T(8,128)(2,1)} %get-tuple-element.47), channel_id=1, source_target_pairs={{0,12},{4,8},{8,4},{12,0},{1,13},{5,9},{9,5},{13,1},{2,14},{6,10},... | collective-permute-start | bytes 1572872 | tf_op jit(solution)/shard_map/ppermute | solution.py:1030
  122.1 35.7 %collective-permute-start.13 = (bf16[1024,256]{1,0:T(8,128)(2,1)}, bf16[1024,256]{1,0:T(8,128)(2,1)}, u32[]{:S(2)}, u32[]{:S(2)}) collective-permute-start(bf16[1024,256]{1,0:T(8,128)(2,1)} %get-tuple-element.47), channel_id=1, source_target_pairs={{0,16},{16,0},{1,17},{17,1},{2,18},{18,2},{3,19},{19,3},{4,20},{20... | collective-permute-start | bytes 1572872 | tf_op jit(solution)/shard_map/ppermute | solution.py:1030
  130.9 28.1 %copy-start.34 = (bf16[4096,512]{1,0:T(8,128)(2,1)S(1)}, bf16[4096,512]{1,0:T(8,128)(2,1)}, u32[]{:S(2)}) copy-start(bf16[4096,512]{1,0:T(8,128)(2,1)} %broadcast_select_fusion) | copy-start | bytes 12582916
  143.5 15.4 %collective-permute-start.14 = (bf16[1024,256]{1,0:T(8,128)(2,1)}, bf16[1024,256]{1,0:T(8,128)(2,1)S(1)}, u32[]{:S(2)}, u32[]{:S(2)}) collective-permute-start(bf16[1024,256]{1,0:T(8,128)(2,1)} %collective-permute-done.10), channel_id=1, source_target_pairs={{0,16},{16,0},{1,17},{17,1},{2,18},{18,2},{3,19},{19,3},{4,20},{20... | collective-permute-start | bytes 1572872 | tf_op jit(solution)/shard_map/ppermute | solution.py:1030
  145.2 13.8 %collective-permute-start.15 = (bf16[1024,256]{1,0:T(8,128)(2,1)}, bf16[1024,256]{1,0:T(8,128)(2,1)S(1)}, u32[]{:S(2)}, u32[]{:S(2)}) collective-permute-start(bf16[1024,256]{1,0:T(8,128)(2,1)} %collective-permute-done.11), channel_id=1, source_target_pairs={{0,16},{16,0},{1,17},{17,1},{2,18},{18,2},{3,19},{19,3},{4,20},{20... | collective-permute-start | bytes 1572872 | tf_op jit(solution)/shard_map/ppermute | solution.py:1030
  155.6 3.4 collective-permute-start.16
  163.3 116.6 %collective-permute-start.20 = (bf16[4,128,512]{2,1,0:T(8,128)(2,1)}, bf16[4,128,512]{2,1,0:T(8,128)(2,1)}, u32[]{:S(2)}, u32[]{:S(2)}) collective-permute-start(bf16[4,128,512]{2,1,0:T(8,128)(2,1)} %get-tuple-element.122), channel_id=1, source_target_pairs={{0,4},{4,0},{8,12},{12,8},{16,20},{20,16},{24,28},{28,24},{1,5},{5... | collective-permute-start | bytes 1572872 | tf_op jit(solution)/shard_map/ppermute | solution.py:1030
  163.4 119.5 %collective-permute-start.21 = (bf16[4,128,512]{2,1,0:T(8,128)(2,1)}, bf16[4,128,512]{2,1,0:T(8,128)(2,1)}, u32[]{:S(2)}, u32[]{:S(2)}) collective-permute-start(bf16[4,128,512]{2,1,0:T(8,128)(2,1)} %get-tuple-element.121), channel_id=1, source_target_pairs={{0,8},{4,12},{8,0},{12,4},{16,24},{20,28},{24,16},{28,20},{1,9},{5... | collective-permute-start | bytes 1572872 | tf_op jit(solution)/shard_map/ppermute | solution.py:1030
  165.3 119.3 %collective-permute-start.22 = (bf16[4,128,512]{2,1,0:T(8,128)(2,1)}, bf16[4,128,512]{2,1,0:T(8,128)(2,1)}, u32[]{:S(2)}, u32[]{:S(2)}) collective-permute-start(bf16[4,128,512]{2,1,0:T(8,128)(2,1)} %get-tuple-element.120), channel_id=1, source_target_pairs={{0,12},{4,8},{8,4},{12,0},{16,28},{20,24},{24,20},{28,16},{1,13},{... | collective-permute-start | bytes 1572872 | tf_op jit(solution)/shard_map/ppermute | solution.py:1030
  166.8 121.7 %collective-permute-start.23 = (bf16[4,128,512]{2,1,0:T(8,128)(2,1)}, bf16[4,128,512]{2,1,0:T(8,128)(2,1)}, u32[]{:S(2)}, u32[]{:S(2)}) collective-permute-start(bf16[4,128,512]{2,1,0:T(8,128)(2,1)} %get-tuple-element.119), channel_id=1, source_target_pairs={{0,16},{4,20},{8,24},{12,28},{16,0},{20,4},{24,8},{28,12},{1,17},{... | collective-permute-start | bytes 1572872 | tf_op jit(solution)/shard_map/ppermute | solution.py:1030
  166.8 124.1 %collective-permute-start.24 = (bf16[4,128,512]{2,1,0:T(8,128)(2,1)}, bf16[4,128,512]{2,1,0:T(8,128)(2,1)}, u32[]{:S(2)}, u32[]{:S(2)}) collective-permute-start(bf16[4,128,512]{2,1,0:T(8,128)(2,1)} %get-tuple-element.118), channel_id=1, source_target_pairs={{0,20},{4,16},{8,28},{12,24},{16,4},{20,0},{24,12},{28,8},{1,21},{... | collective-permute-start | bytes 1572872 | tf_op jit(solution)/shard_map/ppermute | solution.py:1030
  178.0 25.7 %copy-start.32 = (bf16[64,8,4,512]{3,1,2,0:T(8,128)(2,1)S(1)}, bf16[64,8,4,512]{3,1,2,0:T(8,128)(2,1)}, u32[]{:S(2)}) copy-start(bf16[64,8,4,512]{3,1,2,0:T(8,128)(2,1)} %copy.54) | copy-start | bytes 6291460
  254.3 24.1 %copy-start.11 = (bf16[256,512]{1,0:T(8,128)(2,1)}, bf16[256,512]{1,0:T(8,128)(2,1)S(1)}, u32[]{:S(2)}) copy-start(bf16[256,512]{1,0:T(8,128)(2,1)S(1)} %get-tuple-element.53) | copy-start | bytes 786436
  279.9 36.7 %collective-permute-start.25 = (bf16[4,128,512]{2,1,0:T(8,128)(2,1)S(1)}, bf16[4,128,512]{2,1,0:T(8,128)(2,1)S(1)}, u32[]{:S(2)}, u32[]{:S(2)}) collective-permute-start(bf16[4,128,512]{2,1,0:T(8,128)(2,1)S(1)} %copy-done.41), channel_id=1, source_target_pairs={{0,24},{4,28},{8,16},{12,20},{16,8},{20,12},{24,0},{28,4},{1,25},{... | collective-permute-start | bytes 1572872 | tf_op jit(solution)/shard_map/ppermute | solution.py:1030
  282.9 37.1 %collective-permute-start.17 = (bf16[256,2048]{1,0:T(8,128)(2,1)S(1)}, bf16[256,2048]{1,0:T(8,128)(2,1)S(1)}, u32[]{:S(2)}, u32[]{:S(2)}) collective-permute-start(bf16[256,2048]{1,0:T(8,128)(2,1)S(1)} %convolution_convert_fusion.9), channel_id=1, source_target_pairs={{0,1},{1,2},{2,3},{3,0},{4,5},{5,6},{6,7},{7,4},{8,9},{9,10},{10,1... | collective-permute-start | bytes 3145736 | tf_op jit(solution)/shard_map/ppermute | solution.py:1041
  284.7 70.6 %collective-permute-start.18 = (bf16[256,2048]{1,0:T(8,128)(2,1)S(1)}, bf16[256,2048]{1,0:T(8,128)(2,1)S(1)}, u32[]{:S(2)}, u32[]{:S(2)}) collective-permute-start(bf16[256,2048]{1,0:T(8,128)(2,1)S(1)} %convolution_convert_fusion.8), channel_id=1, source_target_pairs={{0,2},{1,3},{2,0},{3,1},{4,6},{5,7},{6,4},{7,5},{8,10},{9,11},{10,... | collective-permute-start | bytes 3145736 | tf_op jit(solution)/shard_map/ppermute | solution.py:1041
  288.5 66.7 %collective-permute-start.19 = (bf16[256,2048]{1,0:T(8,128)(2,1)S(1)}, bf16[256,2048]{1,0:T(8,128)(2,1)S(1)}, u32[]{:S(2)}, u32[]{:S(2)}) collective-permute-start(bf16[256,2048]{1,0:T(8,128)(2,1)S(1)} %convolution_convert_fusion.7), channel_id=1, source_target_pairs={{0,3},{1,0},{2,1},{3,2},{4,7},{5,4},{6,5},{7,6},{8,11},{9,8},{10,9... | collective-permute-start | bytes 3145736 | tf_op jit(solution)/shard_map/ppermute | solution.py:1041
  290.9 25.8 %collective-permute-start.26 = (bf16[4,128,512]{2,1,0:T(8,128)(2,1)S(1)}, bf16[4,128,512]{2,1,0:T(8,128)(2,1)S(1)}, u32[]{:S(2)}, u32[]{:S(2)}) collective-permute-start(bf16[4,128,512]{2,1,0:T(8,128)(2,1)S(1)} %copy-done.40), channel_id=1, source_target_pairs={{0,28},{4,24},{8,20},{12,16},{16,12},{20,8},{24,4},{28,0},{1,29},{... | collective-permute-start | bytes 1572872 | tf_op jit(solution)/shard_map/ppermute | solution.py:1030
  357.8 204.9 %copy-start.3 = (bf16[1024,2048]{1,0:T(8,128)(2,1)S(1)}, bf16[1024,2048]{1,0:T(8,128)(2,1)}, u32[]{:S(2)}) copy-start(bf16[1024,2048]{1,0:T(8,128)(2,1)} %copy-done.2) | copy-start | bytes 12582916
  578.9 379.6 %reduce-scatter.9.cloned.1.call-start = ((), (), s32[]{:S(2)}) async-start(), calls=%async_computation.10 | async-start | bytes 18874368 | tf_op jit(solution)/shard_map/reduce_scatter | solution.py:1053
  609.0 552.4 %reduce-scatter.7.cloned.1.call-start = ((), (), s32[]{:S(2)}) async-start(), calls=%async_computation.9 | async-start | bytes 2359296 | tf_op jit(solution)/shard_map/reduce_scatter | solution.py:1053
  897.1 267.7 %reduce-scatter.5.cloned.1.call-start = ((), (), s32[]{:S(2)}) async-start(), calls=%async_computation.8 | async-start | bytes 2359296 | tf_op jit(solution)/shard_map/reduce_scatter | solution.py:1053
  903.3 265.0 %all-gather.17.cloned.1.call-start = ((), (), s32[]{:S(2)}) async-start(), calls=%async_computation.13 | async-start | bytes 3145728 | tf_op jit(solution)/shard_map/all_gather | solution.py:1054
  904.1 268.4 %all-gather.15.cloned.1.call-start = ((), (), s32[]{:S(2)}) async-start(), calls=%async_computation.11 | async-start | bytes 6291456 | tf_op jit(solution)/shard_map/all_gather | solution.py:1054
  904.2 24.4 %collective-permute-start.27 = (bf16[2048,256]{1,0:T(8,128)(2,1)S(1)}, bf16[2048,256]{1,0:T(8,128)(2,1)S(1)}, u32[]{:S(2)}, u32[]{:S(2)}) collective-permute-start(bf16[2048,256]{1,0:T(8,128)(2,1)S(1)} %get-tuple-element.133), channel_id=1, source_target_pairs={{0,1},{1,2},{2,3},{3,0},{4,5},{5,6},{6,7},{7,4},{8,9},{9,10},{10,1... | collective-permute-start | bytes 3145736 | tf_op jit(solution)/shard_map/ppermute | solution.py:1041
  904.3 46.6 %collective-permute-start.28 = (bf16[2048,256]{1,0:T(8,128)(2,1)S(1)}, bf16[2048,256]{1,0:T(8,128)(2,1)S(1)}, u32[]{:S(2)}, u32[]{:S(2)}) collective-permute-start(bf16[2048,256]{1,0:T(8,128)(2,1)S(1)} %get-tuple-element.133), channel_id=1, source_target_pairs={{0,2},{1,3},{2,0},{3,1},{4,6},{5,7},{6,4},{7,5},{8,10},{9,11},{10,... | collective-permute-start | bytes 3145736 | tf_op jit(solution)/shard_map/ppermute | solution.py:1041
  916.2 34.7 %collective-permute-start.29 = (bf16[2048,256]{1,0:T(8,128)(2,1)S(1)}, bf16[2048,256]{1,0:T(8,128)(2,1)S(1)}, u32[]{:S(2)}, u32[]{:S(2)}) collective-permute-start(bf16[2048,256]{1,0:T(8,128)(2,1)S(1)} %get-tuple-element.133), channel_id=1, source_target_pairs={{0,3},{1,0},{2,1},{3,2},{4,7},{5,4},{6,5},{7,6},{8,11},{9,8},{10,9... | collective-permute-start | bytes 3145736 | tf_op jit(solution)/shard_map/ppermute | solution.py:1041
  (45 other events, 172.8 us)
Sparse Core Ops, SparseCore 0:
  11.5 55.7 all-gather.6
  82.6 28.2 all-gather.8
  113.4 93.9 all-gather.12
  209.6 112.7 all-gather.10
  579.0 68.7 reduce-scatter.10
  651.6 115.9 reduce-scatter.8
  897.2 48.3 reduce-scatter.6
  949.4 59.0 reduce-scatter.4
  1010.2 9.8 all-gather.16
  1021.5 14.1 all-gather.14

commit v4 on v3

--- a/solution.py
+++ b/solution.py
@@ -35,10 +35,6 @@
         self.own = 2 * self.cw
 
 
-def block_of(plan, s_ref, r):
-    return lax.rem(s_ref[3] + r, plan.wide)
-
-
 def near_of(plan, z, p):
     side = jnp.minimum(z, plan.wide - 1 - z)
     both = jnp.where(lax.rem(p, 2) == 1, z + (p + 1) // 2, z - p // 2)
@@ -57,110 +53,330 @@
     return jnp.concatenate([table] * (width // 128), axis=1) if width > 128 else table
 
 
-def qkv_kernel(plan, qw, s_ref, x_ref, gain_ref, w_ref, cos_ref, sin_ref, h_ref, q_ref, kv_ref, own_ref, x_scr):
-    narrow = plan.group // 2
+MESH = pl.DeviceIdType.MESH
+
+
+def greet(partners):
+    barrier = pltpu.get_barrier_semaphore()
+    for partner in partners:
+        pl.semaphore_signal(barrier, inc=1, device_id=partner, device_id_type=MESH)
+    pl.semaphore_wait(barrier, len(partners))
+
+
+def along_wide(plan, r):
+    return {"wide": lax.rem(lax.axis_index("wide") + r + plan.wide, plan.wide)}
+
+
+def push(src, dst, send, recv, device):
+    return pltpu.make_async_remote_copy(
+        src_ref=src, dst_ref=dst, send_sem=send, recv_sem=recv, device_id=device, device_id_type=MESH
+    )
+
+
+class Chain:
+    def __init__(self, plan, buf, sems):
+        self.wide, self.buf, self.sems = plan.wide, buf, sems
+        self.z = lax.axis_index("wide")
+
+    def copy(self, slot, h, way):
+        send, recv = (self.sems[0], self.sems[1]) if way > 0 else (self.sems[2], self.sems[3])
+        return push(self.buf.at[slot], self.buf.at[slot], send.at[h], recv.at[h], {"wide": self.z + way})
+
+    def sends(self, h, way):
+        z, last = self.z, self.wide - 1
+        return (z >= h - 1) & (z < last) if way > 0 else (z + h - 1 <= last) & (z > 0)
+
+    def go(self, h):
+        for way in (1, -1):
+            @pl.when(self.sends(h, way))
+            def _():
+                self.copy(self.z - way * (h - 1), h, way).start()
+
+    def arrive(self, h):
+        for way in (1, -1):
+            @pl.when(self.z >= h if way > 0 else self.z + h <= self.wide - 1)
+            def _():
+                slot = self.z - way * h
+                send, recv = (self.sems[0], self.sems[1]) if way > 0 else (self.sems[2], self.sems[3])
+                push(self.buf.at[slot], self.buf.at[slot], send.at[h], recv.at[h], {"wide": slot}).wait_recv()
+
+    def finish(self):
+        for h in range(1, self.wide):
+            for way in (1, -1):
+                @pl.when(self.sends(h, way))
+                def _():
+                    self.copy(self.z - way * (h - 1), h, way).wait_send()
+
+
+class Group:
+    def __init__(self, plan):
+        self.size, self.narrow = plan.group, plan.group // 2
+        self.seq, self.me = lax.axis_index("seq"), lax.axis_index("narrow")
+        self.index = self.seq * self.narrow + self.me
+        self.sibling = {"seq": 1 - self.seq}
+
+    def device(self, k):
+        return lax.rem(self.index + k + self.size, self.size)
+
+    def member(self, k):
+        return {"seq": self.device(k) // self.narrow, "narrow": lax.rem(self.device(k), self.narrow)}
+
+    def beside(self, k):
+        return lax.rem(self.me + k + self.narrow, self.narrow)
+
+
+def head_kernel(
+    plan, kv_heads, qw, x_ref, g_ref, w_ref, gains_ref, cos_ref, sin_ref, kf_ref,
+    h_out, q_out, own_out, kx, vx, w_out, gains_out, g_out, side_out,
+    x_buf, side_buf, side_send, side_recv, w_buf, kv_buf, g_buf, gain_buf,
+    x_send, x_recv, x_stay, w_send, w_recv, w_on_send, w_on_recv, gain_send, gain_recv,
+    g_send, g_recv, kv_send, kv_recv, kv_on_send, kv_on_recv, keep_sem, *chain_sems
+):
+    group, wide, chunk, cw, own = plan.group, plan.wide, plan.chunk, plan.cw, plan.own
+    team = Group(plan)
+    narrow, seq, me = team.narrow, team.seq, team.me
+    z = lax.axis_index("wide")
     part = x_ref.shape[3]
-    for half in range(2):
-        for n in range(narrow):
-            x_scr[half * plan.cw : (half + 1) * plan.cw, n * part : (n + 1) * part] = x_ref[
-                s_ref[0] ^ (half * narrow + n), 0
-            ]
-    low = x_scr[...]
-
-    @pl.when(pl.program_id(0) == 0)
-    def _():
-        own_ref[...] = low
-
-    x = low.astype(F32)
-    mean = jnp.mean(x * x, axis=1, keepdims=True)
-    h = (x * lax.rsqrt(mean + EPS) * gain_ref[...]).astype(BF)
-    h_ref[...] = h
-    t = jnp.dot(h, w_ref[...], preferred_element_type=F32)
-    width = t.shape[1]
-    lane = lax.broadcasted_iota(jnp.int32, t.shape, 1)
-    plain = (lane >= qw) & (lane % 128 >= HD)
-    out = jnp.where(plain, t, t * widen(cos_ref[...], width) + turn(t, 1.0) * widen(sin_ref[...], width))
-    q_ref[...] = (out[:, :qw] * (HD ** -0.5)).astype(BF)
-    kv_ref[...] = out[:, qw:].astype(BF)
-
-
-def qkv_call(plan, scalars, x, gain, w, cos, sin, qw):
-    part = x.shape[3]
-    d = part * plan.group // 2
-    width = w.shape[1]
-    rows, bm = plan.rows, plan.own
-    return pl.pallas_call(
-        functools.partial(qkv_kernel, plan, qw),
-        grid_spec=pltpu.PrefetchScalarGridSpec(
-            num_scalar_prefetch=1,
-            grid=(plan.wide,),
-            in_specs=[
-                pl.BlockSpec((plan.group, 1, plan.cw, part), lambda r, s: (0, block_of(plan, s, r), 0, 0)),
-                pl.BlockSpec((1, d), lambda r, s: (0, 0)),
-                pl.BlockSpec((d, width), lambda r, s: (0, 0)),
-                pl.BlockSpec((bm, 128), lambda r, s: (r, 0)),
-                pl.BlockSpec((bm, 128), lambda r, s: (r, 0)),
-            ],
-            out_specs=[
-                pl.BlockSpec((bm, d), lambda r, s: (r, 0)),
-                pl.BlockSpec((bm, qw), lambda r, s: (r, 0)),
-                pl.BlockSpec((bm, width - qw), lambda r, s: (r, 0)),
-                pl.BlockSpec((bm, d), lambda r, s: (0, 0)),
-            ],
-            scratch_shapes=[pltpu.VMEM((bm, d), BF)],
-        ),
-        out_shape=[
-            jax.ShapeDtypeStruct((rows, d), BF),
-            jax.ShapeDtypeStruct((rows, qw), BF),
-            jax.ShapeDtypeStruct((rows, width - qw), BF),
-            jax.ShapeDtypeStruct((bm, d), BF),
-        ],
-        cost_estimate=pl.CostEstimate(
-            flops=2 * rows * d * width, bytes_accessed=4 * rows * d + 2 * d * width, transcendentals=rows
-        ),
-        compiler_params=pltpu.CompilerParams(vmem_limit_bytes=40 << 20),
-        name="norm_qkv",
-    )(scalars, x, gain, w, cos, sin)
-
-
-def keys_kernel(plan, s_ref, kv_ref, kf_ref, kx_ref, vx_ref):
-    cw, group = plan.cw, plan.group
-    lane = lax.broadcasted_iota(jnp.int32, (cw, 128), 1)
-    ones = jnp.where(lane < 3, 1.0, 0.0).astype(BF)
+    d = part * narrow
+    width = w_ref.shape[1]
+    fold = part // 2
+    chain = Chain(plan, g_buf, chain_sems)
+    greet([team.member(k) for k in range(1, group)] + [along_wide(plan, r) for r in range(1, wide)])
+
+    def spot(ref, slot, source):
+        rows = pl.ds(pl.multiple_of((source // narrow) * cw, cw), cw)
+        return ref.at[slot, rows, pl.ds(pl.multiple_of(lax.rem(source, narrow) * part, part), part)]
+
+    def chunk_for(device):
+        return jnp.where(seq == 0, device, group - 1 - device)
+
+    def x_to(r, k):
+        src = x_ref.at[chunk_for(team.device(k)), lax.rem(z + r, wide)]
+        return push(src, spot(x_buf, r, team.index), x_send.at[r, k], x_recv.at[r, k], team.member(k))
+
+    def x_from(r, k):
+        src = x_ref.at[0, 0]
+        return push(src, spot(x_buf, r, team.device(-k)), x_send.at[r, k], x_recv.at[r, k], team.member(k))
+
+    def x_own(r):
+        src = x_ref.at[chunk_for(team.index), lax.rem(z + r, wide)]
+        return pltpu.make_async_copy(src, spot(x_buf, r, team.index), x_stay.at[r])
+
+    def x_start(r):
+        for k in range(1, group):
+            x_to(r, k).start()
+        x_own(r).start()
+
+    def g_to(k):
+        src = g_ref.at[chunk_for(team.device(k))]
+        return push(src, spot(g_buf, z, team.index), g_send.at[k], g_recv.at[k], team.member(k))
+
+    def w_rows(n, core):
+        return w_buf.at[pl.ds(pl.multiple_of(n * part + core * fold, fold), fold)]
+
+    def w_to(k):
+        src = w_ref.at[pl.ds(pl.multiple_of(seq * fold, fold), fold)]
+        return push(src, w_rows(me, seq), w_send.at[k], w_recv.at[k], {"narrow": team.beside(k)})
+
+    def w_from(k):
+        n = team.beside(-k)
+        return push(w_rows(n, seq), w_rows(n, seq), w_send.at[k], w_recv.at[k], {"narrow": n})
+
+    def w_on(k, core):
+        n = team.beside(-k)
+        return push(w_rows(n, core), w_rows(n, core), w_on_send.at[k], w_on_recv.at[k], team.sibling)
+
+    def side_to(r, slot):
+        mine = w_ref.at[:, qw:]
+        return push(mine, side_buf.at[slot], side_send.at[r], side_recv.at[r], along_wide(plan, r))
+
+    def gain_to(k, slot):
+        return push(gains_ref, gain_buf.at[slot], gain_send.at[k], gain_recv.at[k], {"narrow": team.beside(k)})
+
+    for k in range(1, group):
+        g_to(k).start()
+    g_stay = pltpu.make_async_copy(g_ref.at[chunk_for(team.index)], spot(g_buf, z, team.index), keep_sem.at[0])
+    g_stay.start()
+    for k in range(1, narrow):
+        w_to(k).start()
+        gain_to(k, me).start()
+    x_start(0)
+    if wide > 1:
+        x_start(1)
+    for r in range(1, wide):
+        side_to(r, z).start()
+    side_buf[z] = w_ref[:, qw:]
+    w_buf[pl.ds(pl.multiple_of(me * part, part), part), :] = w_ref[...]
+    gain_buf[me] = gains_ref[...]
+    for k in range(1, narrow):
+        w_from(k).wait_recv()
+        w_on(k, seq).start()
+    g_stay.wait()
+    for k in range(1, group):
+        push(
+            g_ref.at[0], spot(g_buf, z, team.device(-k)), g_send.at[k], g_recv.at[k], team.member(k)
+        ).wait_recv()
+    chain.go(1)
+    for k in range(1, narrow):
+        gain_to(k, team.beside(-k)).wait_recv()
+        w_on(k, 1 - seq).wait_recv()
+    gain_one = jnp.concatenate([gain_buf[n, 0:1] for n in range(narrow)], axis=1)
+    gains_out[...] = gain_buf[...]
+    w_keep = pltpu.make_async_copy(w_buf, w_out, keep_sem.at[1])
+    w_keep.start()
+
+    def kv_rows(core, n, r):
+        return kv_buf.at[core, n, pl.ds(pl.multiple_of(r * own, own), own)]
+
+    def kv_to(r, k):
+        mine = kv_rows(seq, me, r)
+        return push(mine, mine, kv_send.at[r, k], kv_recv.at[r, k], {"narrow": team.beside(k)})
+
+    def kv_from(r, k):
+        theirs = kv_rows(seq, team.beside(-k), r)
+        return push(theirs, theirs, kv_send.at[r, k], kv_recv.at[r, k], {"narrow": team.beside(k)})
+
+    def kv_on(k, core):
+        slot = kv_buf.at[core, team.beside(-k)]
+        return push(slot, slot, kv_on_send.at[k], kv_on_recv.at[k], team.sibling)
+
+    @pl.loop(0, wide)
+    def _(r):
+        x_own(r).wait()
+        for k in range(1, group):
+            x_from(r, k).wait_recv()
+        for later in range(2, wide):
+            @pl.when(r == later - 2)
+            def _():
+                x_start(later)
+        at = pl.ds(pl.multiple_of(r * own, own), own)
+        low = x_buf[r]
+        x = low.astype(F32)
+        mean = jnp.mean(x * x, axis=1, keepdims=True)
+        h = (x * lax.rsqrt(mean + EPS) * gain_one).astype(BF)
+        h_out[at, :] = h
+        t = jnp.dot(h, w_buf[...], preferred_element_type=F32)
+        lane = lax.broadcasted_iota(jnp.int32, t.shape, 1)
+        plain = (lane >= qw) & (lane % 128 >= HD)
+        out = t * widen(cos_ref[at, :], width) + turn(t, 1.0) * widen(sin_ref[at, :], width)
+        out = jnp.where(plain, t, out)
+        q_out[at, :] = (out[:, :qw] * (HD ** -0.5)).astype(BF)
+        kv_buf[seq, me, at, :] = out[:, qw:].astype(BF)
+        for k in range(1, narrow):
+            kv_to(r, k).start()
+
+        @pl.when(r == min(1, wide - 1))
+        def _():
+            chain.arrive(1)
+            if wide > 2:
+                chain.go(2)
+
+    kv_on(0, seq).start()
+    own_out[...] = x_buf[0]
+    if wide > 2:
+        chain.arrive(2)
+    if wide > 3:
+        chain.go(3)
+    for k in range(1, narrow):
+        for r in range(wide):
+            kv_from(r, k).wait_recv()
+        kv_on(k, seq).start()
+    for k in range(narrow):
+        kv_on(k, 1 - seq).wait_recv()
+
+    feature = lax.broadcasted_iota(jnp.int32, (cw, 128), 1)
+    ones = jnp.where(feature < 3, 1.0, 0.0).astype(BF)
 
     @pl.loop(0, 2 * group)
     def _(c):
         late = c >= group
         owner = jnp.where(late, 2 * group - 1 - c, c)
-        for r in range(plan.wide):
-            at = pl.ds(pl.multiple_of(c * plan.chunk + block_of(plan, s_ref, r) * cw, cw), cw)
-            kv = kv_ref[s_ref[0] ^ owner, r, jnp.where(late, 1, 0)]
-            kx_ref[0, at, :] = jnp.where(lane < HD, kv, kf_ref[at, :])
-            vx_ref[0, at, :] = jnp.where(lane < HD, ones, kv)
-
-
-def keys_call(plan, scalars, kv, kf, kv_heads):
-    group, total = plan.group, plan.total
-    kv = kv.reshape(group, plan.wide, 2, plan.cw, kv_heads * 128)
-    out = pl.BlockSpec((1, total, 128), lambda g, s: (g, 0, 0))
+        for r in range(wide):
+            at = pl.ds(pl.multiple_of(c * chunk + lax.rem(z + r, wide) * cw, cw), cw)
+            source = pl.ds(pl.multiple_of(r * own + jnp.where(late, cw, 0), cw), cw)
+            for g in range(kv_heads):
+                kv = kv_buf[owner // narrow, lax.rem(owner, narrow), source, g * 128 : (g + 1) * 128]
+                kx[g, at, :] = jnp.where(feature < HD, kv, kf_ref[at, :])
+                vx[g, at, :] = jnp.where(feature < HD, ones, kv)
+
+    for h in range(3, wide):
+        chain.arrive(h)
+        if h + 1 < wide:
+            chain.go(h + 1)
+    for r in range(1, wide):
+        side_to(r, lax.rem(z - r + wide, wide)).wait_recv()
+        side_to(r, z).wait_send()
+    side_out[...] = side_buf[...]
+    keep = [
+        pltpu.make_async_copy(g_buf.at[near_of(plan, z, p)], g_out.at[p], keep_sem.at[2 + p]) for p in range(wide)
+    ]
+    for copy in keep:
+        copy.start()
+    chain.finish()
+    for k in range(1, narrow):
+        w_to(k).wait_send()
+        w_on(k, seq).wait_send()
+        gain_to(k, me).wait_send()
+        for r in range(wide):
+            kv_to(r, k).wait_send()
+    for k in range(narrow):
+        kv_on(k, seq).wait_send()
+    for k in range(1, group):
+        g_to(k).wait_send()
+        for r in range(wide):
+            x_to(r, k).wait_send()
+    w_keep.wait()
+    for copy in keep:
+        copy.wait()
+
+
+def head_call(plan, x, g, w, gains, cos, sin, kf, qw, kv_heads):
+    group, wide, cw, part = x.shape
+    narrow = group // 2
+    d = part * narrow
+    width = w.shape[1]
+    rows, own, total = plan.rows, plan.own, plan.total
+    dma = pltpu.SemaphoreType.DMA
+    whole = pl.BlockSpec(memory_space=pltpu.VMEM)
+    hbm = pl.BlockSpec(memory_space=pl.ANY)
+    keys = jax.ShapeDtypeStruct((kv_heads, total, 128), BF)
     return pl.pallas_call(
-        functools.partial(keys_kernel, plan),
-        grid_spec=pltpu.PrefetchScalarGridSpec(
-            num_scalar_prefetch=1,
-            grid=(kv_heads,),
-            in_specs=[
-                pl.BlockSpec((group, plan.wide, 2, plan.cw, 128), lambda g, s: (0, 0, 0, 0, g)),
-                pl.BlockSpec((total, 128), lambda g, s: (0, 0)),
-            ],
-            out_specs=[out, out],
+        functools.partial(head_kernel, plan, kv_heads, qw),
+        in_specs=[hbm, hbm] + [whole] * 5,
+        out_specs=[whole] * 5 + [hbm, whole, hbm, whole],
+        out_shape=[
+            jax.ShapeDtypeStruct((rows, d), BF),
+            jax.ShapeDtypeStruct((rows, qw), BF),
+            jax.ShapeDtypeStruct((own, d), BF),
+            keys,
+            keys,
+            jax.ShapeDtypeStruct((d, width), BF),
+            jax.ShapeDtypeStruct((narrow, 2, part), F32),
+            jax.ShapeDtypeStruct((wide, own, d), BF),
+            jax.ShapeDtypeStruct((wide, part, width - qw), BF),
+        ],
+        scratch_shapes=[
+            pltpu.VMEM((wide, own, d), BF),
+            pltpu.VMEM((wide, part, width - qw), BF),
+            dma((wide,)), dma((wide,)),
+            pltpu.VMEM((d, width), BF),
+            pltpu.VMEM((2, narrow, rows, width - qw), BF),
+            pltpu.VMEM((wide, own, d), BF),
+            pltpu.VMEM((narrow, 2, part), F32),
+            dma((wide, group)), dma((wide, group)), dma((wide,)),
+            dma((narrow,)), dma((narrow,)), dma((narrow,)), dma((narrow,)), dma((narrow,)), dma((narrow,)),
+            dma((group,)), dma((group,)),
+            dma((wide, narrow)), dma((wide, narrow)), dma((narrow,)), dma((narrow,)),
+            dma((2 + wide,)),
+        ] + [dma((wide,))] * 4,
+        cost_estimate=pl.CostEstimate(
+            flops=60 * rows * d * width, bytes_accessed=8 * rows * d + 2 * d * width, transcendentals=rows
         ),
-        out_shape=[jax.ShapeDtypeStruct((kv_heads, total, 128), BF)] * 2,
-        cost_estimate=pl.CostEstimate(
-            flops=kv_heads * total * 128, bytes_accessed=8 * kv_heads * total * 128, transcendentals=0
+        compiler_params=pltpu.CompilerParams(
+            vmem_limit_bytes=60 << 20, collective_id=4, has_side_effects=True
         ),
-        compiler_params=pltpu.CompilerParams(vmem_limit_bytes=40 << 20),
-        name="keys",
-    )(scalars, kv, kf)
+        name="head",
+    )(x, g, w, gains, cos, sin, kf)
 
 
 def split_heads(block, heads, low):
@@ -187,33 +403,50 @@
     return jnp.concatenate(pairs, axis=1)
 
 
-def chunk_of(plan, s_ref, half):
-    return jnp.where(half == 1, 2 * plan.group - 1 - s_ref[0], s_ref[0])
-
-
-def forward_kernel(plan, heads, r, s_ref, q_ref, kx, vx, o_ref, qe_ref):
-    cw, chunk = plan.cw, plan.chunk
-    w, c = block_of(plan, s_ref, r), chunk_of(plan, s_ref, pl.program_id(1))
+def forward_kernel(
+    plan, kv_heads, heads, s_ref, q_ref, kx, vx, wo_ref, x_ref, o_ref, qe_ref, x2_ref,
+    in_buf, out_buf, term_acc, rs_send, rs_recv,
+):
+    wide, cw, chunk, own = plan.wide, plan.cw, plan.chunk, plan.own
+    rows, width = heads * cw, heads * HD
+    z = lax.axis_index("wide")
+    index = lax.axis_index("seq") * lax.axis_size("narrow") + lax.axis_index("narrow")
+    unit, g = pl.program_id(0), pl.program_id(1)
+    last_g = kv_heads - 1
+    piece, half = wide - 1 - unit // 2, lax.rem(unit, 2)
+    w = near_of(plan, z, piece)
+    r = lax.rem(w - z + wide, wide)
+    c = jnp.where(half == 1, 2 * plan.group - 1 - index, index)
+    low_rows = pl.ds(pl.multiple_of(half * cw, cw), cw)
+    columns = pl.ds(pl.multiple_of(g * width, width), width)
+
+    def give(device):
+        return push(out_buf.at[device], in_buf.at[z], rs_send.at[device], rs_recv.at[z], {"wide": device})
+
+    @pl.when((unit == 0) & (g == 0))
+    def _():
+        greet([along_wide(plan, k) for k in range(1, wide)])
+
     lane = lax.broadcasted_iota(jnp.int32, (cw, 128), 1)
     token = c * chunk + w * cw + lax.broadcasted_iota(jnp.int32, (cw, 128), 0)
-    segment = (token >= s_ref[1]).astype(jnp.int32) + (token >= s_ref[2]).astype(jnp.int32)
+    segment = (token >= s_ref[0]).astype(jnp.int32) + (token >= s_ref[1]).astype(jnp.int32)
     mark = jnp.where(lane == HD + segment, 1.0, 0.0)
-    tiles = split_heads(q_ref[...].astype(F32), heads, True)
+    block = q_ref[pl.ds(pl.multiple_of(r * own + half * cw, cw), cw), columns]
+    tiles = split_heads(block.astype(F32), heads, True)
     q32 = jnp.concatenate([jnp.where(lane < HD, t, mark) for t in tiles], axis=0)
     q = q32.astype(BF)
-    rows = heads * cw
 
     def step(j, carry, diagonal=False):
         top, acc = carry
         at = pl.ds(pl.multiple_of(j * chunk, chunk), chunk)
-        s = lax.dot_general(q, kx[0, at, :], NT, preferred_element_type=F32)
+        s = lax.dot_general(q, kx[g, at, :], NT, preferred_element_type=F32)
         if diagonal:
             row = lax.broadcasted_iota(jnp.int32, (rows, chunk), 0) % cw + w * cw
             col = lax.broadcasted_iota(jnp.int32, (rows, chunk), 1)
             s = jnp.where(col <= row, s, NEG)
         new = jnp.maximum(top, jnp.max(s, axis=1, keepdims=True))
         p = jnp.exp(s - new).astype(BF)
-        acc = acc * jnp.exp(top - new) + jnp.dot(p, vx[0, at, :], preferred_element_type=F32)
+        acc = acc * jnp.exp(top - new) + jnp.dot(p, vx[g, at, :], preferred_element_type=F32)
         return new, acc
 
     start = (jnp.full((rows, 1), NEG, F32), jnp.zeros((rows, 128), F32))
@@ -221,125 +454,86 @@
     top, acc = step(c, carry, True)
     total = acc[:, 0:1]
     out = acc / total
-    o_ref[...] = join_heads([out[h * cw : (h + 1) * cw] for h in range(heads)], False).astype(BF)
+    out = join_heads([out[h * cw : (h + 1) * cw] for h in range(heads)], False).astype(BF)
+    o_ref[w, low_rows, columns] = out
     first, second, third = pieces_of(-(top + jnp.log(total)))
     wide_lane = lax.broadcasted_iota(jnp.int32, (rows, 128), 1)
     qe = jnp.where(wide_lane == HD + 3, first, q32)
     qe = jnp.where(wide_lane == HD + 4, second, qe)
     qe = jnp.where(wide_lane == HD + 5, third, qe)
-    qe_ref[0, 0] = qe.astype(BF)
-
-
-def forward_call(plan, scalars, q, kx, vx, kv_heads, heads, r):
-    total, cw = plan.total, plan.cw
-    pairs = kv_heads * heads * total * plan.own // 2
-    keys = pl.BlockSpec((1, total, 128), lambda g, b, s: (g, 0, 0))
+    qe_ref[r, g, half] = qe.astype(BF)
+
+    term = jnp.dot(out, wo_ref[g], preferred_element_type=F32)
+
+    @pl.when(g == 0)
+    def _():
+        term_acc[...] = term
+
+    @pl.when(g > 0)
+    def _():
+        term_acc[...] += term
+
+    @pl.when((g == last_g) & (piece == 0))
+    def _():
+        x2_ref[low_rows, :] = x_ref[low_rows, :].astype(F32) + term_acc[...]
+
+    @pl.when((g == last_g) & (piece > 0))
+    def _():
+        out_buf[w, low_rows, :] = term_acc[...].astype(BF)
+
+    @pl.when((g == last_g) & (piece > 0) & (half == 1))
+    def _():
+        give(w).start()
+
+    @pl.when((unit == 2 * wide - 1) & (g == last_g))
+    def _():
+        for p in range(1, wide):
+            other = near_of(plan, z, p)
+            push(out_buf.at[z], in_buf.at[other], rs_send.at[z], rs_recv.at[other], {"wide": other}).wait_recv()
+        tall = min(32, own)
+
+        @pl.loop(0, own // tall)
+        def _(b):
+            at = pl.ds(pl.multiple_of(b * tall, tall), tall)
+            total = x2_ref[at, :]
+            for p in range(1, wide):
+                total = total + in_buf[near_of(plan, z, p), at, :].astype(F32)
+            x2_ref[at, :] = total
+
+        for p in range(1, wide):
+            give(near_of(plan, z, p)).wait_send()
+
+
+def forward_call(plan, starts, q, kx, vx, w_o, x, heads):
+    kv_heads, total, _ = kx.shape
+    own, d = x.shape
+    wide, rows, cw = plan.wide, plan.rows, plan.cw
+    qw = q.shape[1]
+    pairs = kv_heads * heads * total * rows // 2
+    fixed = lambda a: pl.BlockSpec(a.shape, lambda u, g: (0,) * a.ndim, pipeline_mode=pl.Buffered(1))
+    given = [q, kx, vx, w_o, x]
+    outs = [
+        jax.ShapeDtypeStruct((wide, own, qw), BF),
+        jax.ShapeDtypeStruct((wide, kv_heads, 2, heads * cw, 128), BF),
+        jax.ShapeDtypeStruct((own, d), F32),
+    ]
+    buffer = pltpu.VMEM((wide, own, d), BF)
+    sems = pltpu.SemaphoreType.DMA((wide,))
     return pl.pallas_call(
-        functools.partial(forward_kernel, plan, heads, r),
-        grid_spec=pltpu.PrefetchScalarGridSpec(
-            num_scalar_prefetch=1,
-            grid=(kv_heads, 2),
-            in_specs=[pl.BlockSpec((cw, heads * HD), lambda g, b, s: (2 * r + b, g)), keys, keys],
-            out_specs=[
-                pl.BlockSpec((cw, heads * HD), lambda g, b, s: (b, g)),
-                pl.BlockSpec((1, 1, heads * cw, 128), lambda g, b, s: (g, b, 0, 0)),
-            ],
+        functools.partial(forward_kernel, plan, kv_heads, heads),
+        grid=(2 * wide, kv_heads),
+        in_specs=[pl.BlockSpec(memory_space=pltpu.SMEM)] + [fixed(a) for a in given],
+        out_specs=[fixed(a) for a in outs],
+        out_shape=outs,
+        scratch_shapes=[buffer, buffer, pltpu.VMEM((cw, d), F32), sems, sems],
+        cost_estimate=pl.CostEstimate(
+            flops=16 * pairs * HD, bytes_accessed=8 * kv_heads * total * 128, transcendentals=pairs
         ),
-        out_shape=[
-            jax.ShapeDtypeStruct((plan.own, q.shape[1]), BF),
-            jax.ShapeDtypeStruct((kv_heads, 2, heads * cw, 128), BF),
-        ],
-        cost_estimate=pl.CostEstimate(
-            flops=16 * pairs * HD, bytes_accessed=8 * total * 128, transcendentals=pairs
+        compiler_params=pltpu.CompilerParams(
+            vmem_limit_bytes=56 << 20, collective_id=5, has_side_effects=True
         ),
-        compiler_params=pltpu.CompilerParams(vmem_limit_bytes=48 << 20),
         name="attention_forward",
-    )(scalars, q, kx, vx)
-
-
-def rows_kernel(plan, s_ref, x_ref, out_ref):
-    narrow = plan.group // 2
-    part = x_ref.shape[3]
-    for half in range(2):
-        for n in range(narrow):
-            out_ref[half * plan.cw : (half + 1) * plan.cw, n * part : (n + 1) * part] = x_ref[
-                s_ref[0] ^ (half * narrow + n), 0
-            ]
-
-
-def rows_call(plan, scalars, x):
-    part = x.shape[3]
-    d = part * plan.group // 2
-    return pl.pallas_call(
-        functools.partial(rows_kernel, plan),
-        grid_spec=pltpu.PrefetchScalarGridSpec(
-            num_scalar_prefetch=1,
-            grid=(plan.wide,),
-            in_specs=[
-                pl.BlockSpec((plan.group, 1, plan.cw, part), lambda p, s: (0, near_of(plan, s[3], p), 0, 0))
-            ],
-            out_specs=pl.BlockSpec((plan.own, d), lambda p, s: (p, 0)),
-        ),
-        out_shape=jax.ShapeDtypeStruct((plan.rows, d), x.dtype),
-        cost_estimate=pl.CostEstimate(flops=x.size, bytes_accessed=4 * x.size, transcendentals=0),
-        compiler_params=pltpu.CompilerParams(vmem_limit_bytes=40 << 20),
-        name="rows",
-    )(scalars, x)
-
-
-MESH = pl.DeviceIdType.MESH
-
-
-def greet(partners):
-    barrier = pltpu.get_barrier_semaphore()
-    for partner in partners:
-        pl.semaphore_signal(barrier, inc=1, device_id=partner, device_id_type=MESH)
-    pl.semaphore_wait(barrier, len(partners))
-
-
-def along_wide(plan, r):
-    return {"wide": lax.rem(lax.axis_index("wide") + r + plan.wide, plan.wide)}
-
-
-def push(src, dst, send, recv, device):
-    return pltpu.make_async_remote_copy(
-        src_ref=src, dst_ref=dst, send_sem=send, recv_sem=recv, device_id=device, device_id_type=MESH
-    )
-
-
-class Chain:
-    def __init__(self, plan, buf, sems):
-        self.wide, self.buf, self.sems = plan.wide, buf, sems
-        self.z = lax.axis_index("wide")
-
-    def copy(self, slot, h, way):
-        send, recv = (self.sems[0], self.sems[1]) if way > 0 else (self.sems[2], self.sems[3])
-        return push(self.buf.at[slot], self.buf.at[slot], send.at[h], recv.at[h], {"wide": self.z + way})
-
-    def sends(self, h, way):
-        z, last = self.z, self.wide - 1
-        return (z >= h - 1) & (z < last) if way > 0 else (z + h - 1 <= last) & (z > 0)
-
-    def go(self, h):
-        for way in (1, -1):
-            @pl.when(self.sends(h, way))
-            def _():
-                self.copy(self.z - way * (h - 1), h, way).start()
-
-    def arrive(self, h):
-        for way in (1, -1):
-            @pl.when(self.z >= h if way > 0 else self.z + h <= self.wide - 1)
-            def _():
-                slot = self.z - way * h
-                send, recv = (self.sems[0], self.sems[1]) if way > 0 else (self.sems[2], self.sems[3])
-                push(self.buf.at[slot], self.buf.at[slot], send.at[h], recv.at[h], {"wide": slot}).wait_recv()
-
-    def finish(self):
-        for h in range(1, self.wide):
-            for way in (1, -1):
-                @pl.when(self.sends(h, way))
-                def _():
-                    self.copy(self.z - way * (h - 1), h, way).wait_send()
+    )(starts, *given)
 
 
 def ffn_kernel(
@@ -519,10 +713,100 @@
     )(x2, gain, g_rows, w_gu, w_gu, w_dn)
 
 
+def weights_kernel(
+    plan, tiles, dx2_ref, act_ref, h_ref, g_ref, dg_ref, du_ref, dn_out, gate_out, up_out, db_out,
+    db_buf, keep_sem, *chain_sems
+):
+    wide = plan.wide
+    step = pl.program_id(0)
+    last = pl.num_programs(0) - 1
+    chain = Chain(plan, db_buf, chain_sems)
+    keep = pltpu.make_async_copy(db_buf, db_out, keep_sem)
+
+    @pl.when(step == 0)
+    def _():
+        db_buf[lax.axis_index("wide")] = dx2_ref[...].astype(BF)
+        greet([along_wide(plan, k) for k in range(1, wide)])
+        chain.go(1)
+
+    @pl.when(step < tiles)
+    def _():
+        narrow, _, part = dn_out.shape
+        for n in range(narrow):
+            dn_out[n] = lax.dot_general(
+                act_ref[...], g_ref[:, n * part : (n + 1) * part], TN, preferred_element_type=F32
+            ).astype(BF)
+
+    @pl.when((step >= tiles) & (step < 2 * tiles))
+    def _():
+        gate_out[...] = lax.dot_general(h_ref[...], dg_ref[...], TN, preferred_element_type=F32).astype(BF)
+
+    @pl.when(step >= 2 * tiles)
+    def _():
+        up_out[...] = lax.dot_general(h_ref[...], du_ref[...], TN, preferred_element_type=F32).astype(BF)
+
+    for h in range(1, wide):
+        @pl.when(step == min(last, (2 * h - 1) * tiles + tiles // 2))
+        def _():
+            chain.arrive(h)
+            if h + 1 < wide:
+                chain.go(h + 1)
+
+    @pl.when(step == last)
+    def _():
+        keep.start()
+        chain.finish()
+        keep.wait()
+
+
+def weights_call(plan, dx2, act, h, g, d_gate, d_up):
+    own, d = dx2.shape
+    rows, ff = act.shape
+    wide, narrow = plan.wide, plan.group // 2
+    part = d // narrow
+    tiles = 4
+    ff_tile, d_tile = ff // tiles, d // tiles
+    fixed = lambda a: pl.BlockSpec(a.shape, lambda s: (0,) * a.ndim, pipeline_mode=pl.Buffered(1))
+    first = lambda s: jnp.minimum(s, tiles - 1)
+    second = lambda s: jnp.clip(s - tiles, 0, tiles - 1)
+    third = lambda s: jnp.clip(s - 2 * tiles, 0, tiles - 1)
+    both = lambda s: jnp.where(s < 2 * tiles, second(s), third(s))
+    sems = pltpu.SemaphoreType.DMA((wide,))
+    return pl.pallas_call(
+        functools.partial(weights_kernel, plan, tiles),
+        grid=(3 * tiles,),
+        in_specs=[
+            fixed(dx2),
+            pl.BlockSpec((rows, ff_tile), lambda s: (0, first(s))),
+            pl.BlockSpec((rows, d_tile), lambda s: (0, both(s))),
+            fixed(g), fixed(d_gate), fixed(d_up),
+        ],
+        out_specs=[
+            pl.BlockSpec((narrow, ff_tile, part), lambda s: (0, first(s), 0)),
+            pl.BlockSpec((d_tile, ff), lambda s: (second(s), 0)),
+            pl.BlockSpec((d_tile, ff), lambda s: (third(s), 0)),
+            pl.BlockSpec(memory_space=pl.ANY),
+        ],
+        out_shape=[
+            jax.ShapeDtypeStruct((narrow, ff, part), BF),
+            jax.ShapeDtypeStruct((d, ff), BF),
+            jax.ShapeDtypeStruct((d, ff), BF),
+            jax.ShapeDtypeStruct((wide, own, d), BF),
+        ],
+        scratch_shapes=[pltpu.VMEM((wide, own, d), BF), pltpu.SemaphoreType.DMA] + [sems] * 4,
+        cost_estimate=pl.CostEstimate(
+            flops=10 * rows * d * ff, bytes_accessed=20 * rows * d, transcendentals=0
+        ),
+        compiler_params=pltpu.CompilerParams(
+            vmem_limit_bytes=56 << 20, collective_id=6, has_side_effects=True
+        ),
+        name="weight_gradients",
+    )(dx2, act, h, g, d_gate, d_up)
+
+
 def backward_kernel(
-    plan, kv_heads, heads, dx2_ref, qe_ref, kx, vx, o_ref, wo_ref, wq_ref, cos_ref, sin_ref, dn_ref,
-    dq_ref, sums, dh_ref, db_out, dn_got,
-    db_buf, in_buf, out_buf, term_acc, rs_send, rs_recv, dn_send, dn_recv, out_sem, *chain_sems
+    plan, kv_heads, heads, db_ref, qe_ref, kx, vx, o_ref, wo_ref, wq_ref, cos_ref, sin_ref, dn_ref,
+    dq_ref, sums, dh_ref, dn_got, in_buf, out_buf, term_acc, rs_send, rs_recv, dn_send, dn_recv
 ):
     wide, cw, chunk, own = plan.wide, plan.cw, plan.chunk, plan.own
     rows = heads * cw
@@ -531,12 +815,10 @@
     index = lax.axis_index("seq") * lax.axis_size("narrow") + lax.axis_index("narrow")
     unit, g = pl.program_id(0), pl.program_id(1)
     last_unit, last_g = 2 * wide - 1, kv_heads - 1
-    place = jnp.where(unit == 0, 0, jnp.where(unit == last_unit, 1, unit + 1))
-    piece, half = place // 2, lax.rem(place, 2)
+    piece, half = wide - 1 - unit // 2, lax.rem(unit, 2)
     w = near_of(plan, z, piece)
     r = lax.rem(w - z + wide, wide)
     c = jnp.where(half == 1, 2 * plan.group - 1 - index, index)
-    chain = Chain(plan, db_buf, chain_sems)
     low_rows = pl.ds(pl.multiple_of(half * cw, cw), cw)
 
     def give(device):
@@ -547,43 +829,25 @@
         slot = lax.rem(z - device + wide, wide)
         return push(dn_ref.at[p], dn_got.at[slot], dn_send.at[p], dn_recv.at[slot], {"wide": device})
 
-    def keep(p):
-        device = near_of(plan, z, p)
-        slot = lax.rem(device - z + wide, wide)
-        return pltpu.make_async_copy(db_buf.at[device], db_out.at[slot], out_sem.at[p])
-
     @pl.when((unit == 0) & (g == 0))
     def _():
-        db_buf[z] = dx2_ref[...].astype(BF)
         greet([along_wide(plan, k) for k in range(1, wide)])
-        chain.go(1)
-        keep(0).start()
 
         @pl.loop(0, kv_heads * plan.total // chunk)
         def _(b):
             at = pl.ds(pl.multiple_of(lax.rem(b, plan.total // chunk) * chunk, chunk), chunk)
             sums[b // (plan.total // chunk), at, :] = jnp.zeros((chunk, 128), F32)
 
-    for h in range(1, wide):
-        @pl.when((unit == 2 * h - 1) & (g == 0))
+    for p in range(1, wide):
+        @pl.when((unit == wide - 1 - p) & (g == last_g))
         def _():
-            chain.arrive(h)
-            if h + 1 < wide:
-                chain.go(h + 1)
-
-        @pl.when((unit == 2 * h - 2) & (g == last_g))
-        def _():
-            give_down(h).start()
-
-        @pl.when((unit == 2 * h - 1) & (g == last_g))
-        def _():
-            keep(h).start()
+            give_down(p).start()
 
     lane = lax.broadcasted_iota(jnp.int32, (cw, 128), 1)
     columns = pl.ds(pl.multiple_of(g * width, width), width)
-    grad = lax.dot_general(db_buf[w, low_rows, :], wo_ref[g], NT, preferred_element_type=F32)
+    grad = lax.dot_general(db_ref[w, low_rows, :], wo_ref[g], NT, preferred_element_type=F32)
     do = split_heads(grad.astype(BF).astype(F32), heads, False)
-    o = split_heads(o_ref[r, low_rows, columns].astype(F32), heads, False)
+    o = split_heads(o_ref[w, low_rows, columns].astype(F32), heads, False)
     marked = []
     for one, other in zip(o, do):
         clean = jnp.where(lane >= HD, other, 0.0)
@@ -659,9 +923,6 @@
                 total = total + in_buf[near_of(plan, z, p), at, :].astype(F32)
             dh_ref[at, :] = total
 
-        chain.finish()
-        for p in range(wide):
-            keep(p).wait()
         for p in range(1, wide):
             other = near_of(plan, z, p)
             slot = lax.rem(other - z + wide, wide)
@@ -670,15 +931,15 @@
             give_down(p).wait_send()
 
 
-def backward_call(plan, dx2, qe, kx, vx, o, w_o, w_q, cos, sin, down, heads):
+def backward_call(plan, db, qe, kx, vx, o, w_o, w_qkv, cos, sin, down, heads):
     kv_heads, total, _ = kx.shape
-    own, d = dx2.shape
+    _, own, d = db.shape
     wide, rows, cw = plan.wide, plan.rows, plan.cw
-    qw = w_q.shape[1]
+    qw = o.shape[2]
     pairs = kv_heads * heads * total * rows // 2
     fixed = lambda a: pl.BlockSpec(a.shape, lambda u, g: (0,) * a.ndim, pipeline_mode=pl.Buffered(1))
     hbm = pl.BlockSpec(memory_space=pl.ANY)
-    given = [dx2, qe, kx, vx, o, w_o.reshape(kv_heads, heads * HD, d), w_q, cos, sin]
+    given = [db, qe, kx, vx, o, w_o, w_qkv, cos, sin]
     outs = [
         jax.ShapeDtypeStruct((rows, qw), BF),
         jax.ShapeDtypeStruct((kv_heads, total, 128), F32),
@@ -690,10 +951,11 @@
     return pl.pallas_call(
         functools.partial(backward_kernel, plan, kv_heads, heads),
         grid=(2 * wide, kv_heads),
-        in_specs=[fixed(a) for a in given] + [hbm],
-        out_specs=[fixed(a) for a in outs] + [hbm, hbm],
-        out_shape=outs + [pieces, pieces],
-        scratch_shapes=[buffer, buffer, buffer, pltpu.VMEM((cw, d), F32)] + [sems] * 9,
+        in_specs=[fixed(a) for a in given[:6]]
+        + [pl.BlockSpec((d, qw), lambda u, g: (0, 0), pipeline_mode=pl.Buffered(1)), fixed(cos), fixed(sin), hbm],
+        out_specs=[fixed(a) for a in outs] + [hbm],
+        out_shape=outs + [pieces],
+        scratch_shapes=[buffer, buffer, pltpu.VMEM((cw, d), F32)] + [sems] * 4,
         cost_estimate=pl.CostEstimate(
             flops=36 * pairs * HD, bytes_accessed=12 * kv_heads * total * 128, transcendentals=pairs
         ),
@@ -835,7 +1097,7 @@
         @pl.loop(0, dh_acc.shape[1] // tile)
         def _(b):
             at = pl.ds(pl.multiple_of(b * tile, tile), tile)
-            more = lax.dot_general(mine, wkv_ref[r, at, :], NT, preferred_element_type=F32)
+            more = lax.dot_general(mine, wkv_ref[lax.rem(z - r + wide, wide), at, :], NT, preferred_element_type=F32)
             dh_acc[:, at] = (dh_ref[:, at] if r == 0 else dh_acc[:, at]) + more
 
     gain_part[0:1, :] = jnp.zeros_like(gain2_ref[...])
@@ -1020,31 +1282,11 @@
     kv_heads = kw // HD
     heads = qw // kw
     ff = w_gate.shape[1]
-    pieces = range(wide)
 
     start_one = jnp.sum((segment_ids < 1).astype(jnp.int32))
     start_two = jnp.sum((segment_ids < 2).astype(jnp.int32))
-    scalars = jnp.stack([index, start_one, start_two, wide_index]).astype(jnp.int32)
-
-    def swap(values, axes, k, size):
-        return values if k == 0 else lax.ppermute(values, axes, [(a, a ^ k) for a in range(size)])
-
-    def exchange(parts):
-        sent = [lax.dynamic_index_in_dim(parts, index ^ k, 0, keepdims=False) for k in range(group)]
-        return jnp.stack([swap(part, SN, k, group) for k, part in enumerate(sent)])
-
-    def to_rows(values):
-        parts = values.reshape(group, wide, cw, d_part)
-        return exchange(jnp.where(seq_index == 1, parts[::-1], parts))
-
-    def send(values, r):
-        return values if r == 0 else lax.ppermute(values, "wide", [(a, (a + r) % wide) for a in pieces])
-
-    def wide_total(parts):
-        out = parts[0]
-        for r in range(1, len(parts)):
-            out = out + send(parts[r].astype(BF), r).astype(F32)
-        return out
+    starts = jnp.stack([start_one, start_two])
+    scalars = jnp.reshape(index, (1,)).astype(jnp.int32)
 
     def gather_weight(weight):
         return lax.all_gather(half_of(weight, seq_index, seq_count), NS, axis=0, tiled=True)
@@ -1056,17 +1298,9 @@
     def after(values, *others):
         return lax.optimization_barrier((values, *others))[0]
 
-    x_parts = to_rows(tokens)
     w_kv = jnp.concatenate(
         [w_key.reshape(d_part, kv_heads, 1, HD), w_value.reshape(d_part, kv_heads, 1, HD)], axis=2
     ).reshape(d_part, 2 * kw)
-    w_qkv = gather_weight(jnp.concatenate([w_query, w_kv], axis=1))
-    gains = jnp.stack([attn_gain, ffn_gain])
-    gains = jnp.stack([swap(gains, "narrow", k, narrow) for k in range(narrow)])
-    order = narrow_index ^ jnp.arange(narrow)
-    gains = jnp.sum(jnp.where((order[:, None] == jnp.arange(narrow)[None, :])[:, :, None, None], gains[None], 0.0), axis=1)
-    gains = jnp.transpose(gains, (1, 0, 2)).reshape(2, d)
-    gain_one, gain_two = gains[0:1], gains[1:2]
 
     row = jnp.arange(rows, dtype=jnp.int32)
     row_chunk = jnp.where((row // cw) % 2 == 1, 2 * group - 1 - index, index)
@@ -1078,45 +1312,46 @@
     angles = row_pos[:, None] * jnp.tile(frequency, 4)[None, :]
     cos, sin = jnp.cos(angles), jnp.sin(angles)
 
-    h_one, q, kv, x_low = qkv_call(plan, scalars, x_parts, gain_one, w_qkv, cos, sin, qw)
-    near = [swap(kv, "narrow", k, narrow) for k in range(narrow)]
-    far = [swap(part, "seq", 1, seq_count) for part in near]
-    kv_all = jnp.concatenate(near + far, axis=0)
-
     lane = jnp.arange(128, dtype=jnp.int32)[None, :]
     closed = (segment_ids[:, None] != lane - HD) | (token_mask[:, None] != 1)
     kf = jnp.where((lane >= HD) & (lane < HD + 3) & closed, NEG, 0.0)
     kf = jnp.where((lane >= HD + 3) & (lane < HD + 6), 1.0, kf).astype(BF)
-    kx, vx = keys_call(plan, scalars, kv_all, kf, kv_heads)
-
-    w_o = jnp.transpose(gather_weight(after(w_out, x_parts)).reshape(narrow, qw, d_part), (1, 0, 2)).reshape(qw, d)
-    w_gu = gather_weight(after(jnp.concatenate([w_gate, w_up], axis=1), x_parts))
-    w_dn = gather_weight(after(w_down, x_parts)).reshape(narrow, ff, d_part)
-    row_valid = lax.dynamic_slice_in_dim(token_mask, seq_index * (group * chunk), group * chunk, 0)
-    g_low = jnp.where(row_valid[:, None] == 1, out_grad, jnp.zeros_like(out_grad))
-    g_parts = to_rows(after(g_low, kv_all))
-    g_rows = rows_call(plan, scalars, g_parts)
-
-    far_first = sorted(pieces, key=lambda r: (r == 0, -min(r, wide - r)))
-    o, qe, attn = [None] * wide, [None] * wide, [None] * wide
-    for r in far_first:
-        o[r], qe[r] = forward_call(plan, scalars, q, kx, vx, kv_heads, heads, r)
-        attn[r] = jnp.dot(o[r], w_o, preferred_element_type=F32)
-    x_own = x_low.astype(F32)
-    x2 = x_own + wide_total(attn)
+
+    mask = lax.dynamic_slice_in_dim(token_mask, seq_index * (group * chunk), group * chunk, 0)
+    g_part = lax.dynamic_index_in_dim(out_grad.reshape(group, wide, cw, d_part), wide_index, 1, keepdims=False)
+    mask = lax.dynamic_index_in_dim(mask.reshape(group, wide, cw), wide_index, 1, keepdims=False)
+    g_part = jnp.where(mask[:, :, None] == 1, g_part, jnp.zeros_like(g_part))
+
+    w_o = jnp.transpose(gather_weight(w_out).reshape(narrow, kv_heads, heads * HD, d_part), (1, 2, 0, 3))
+    w_o = w_o.reshape(kv_heads, heads * HD, d)
+    h_one, q, x_low, kx, vx, w_qkv, gains, g_rows, w_kv = head_call(
+        plan, tokens.reshape(group, wide, cw, d_part), g_part, jnp.concatenate([w_query, w_kv], axis=1),
+        jnp.stack([attn_gain, ffn_gain]), cos, sin, kf, qw, kv_heads
+    )
+    gains = jnp.transpose(gains, (1, 0, 2)).reshape(2, d)
+    gain_one, gain_two = gains[0:1], gains[1:2]
+    g_rows = g_rows.reshape(rows, d)
+
+    w_gu = gather_weight(after(jnp.concatenate([w_gate, w_up], axis=1), q))
+    w_dn = gather_weight(after(w_down, q)).reshape(narrow, ff, d_part)
+    o, qe, x2 = forward_call(plan, starts, q, kx, vx, w_o, x_low, heads)
+    w_kv = jnp.transpose(w_kv.reshape(wide, seq_count, d_part // seq_count, 2 * kw), (1, 0, 2, 3))
+    w_kv = lax.dynamic_index_in_dim(w_kv, seq_index, 0, keepdims=False).reshape(-1, 2 * kw)
+    w_kv = lax.all_gather(after(w_kv, o), NS, axis=0, tiled=True)
+    w_kv = w_kv.reshape(group, wide, d_part // seq_count, 2 * kw)
+    w_kv = jnp.transpose(w_kv, (1, 0, 2, 3)).reshape(wide, d, 2 * kw)
 
     act, d_gate, d_up, h_all, down, dx2, grad_gain_two = ffn_call(plan, x2, gain_two, g_rows, w_gu, w_dn)
 
-    o = jnp.stack(o)
-    w_q, w_kv = w_qkv[:, :qw], w_qkv[:, qw:]
-    dq, sums, dh1, db, down_in = backward_call(
-        plan, dx2, jnp.stack(qe), kx, vx, o, w_o, w_q, cos, sin, down, heads
+    act = after(act, w_kv)
+    grad_dn, grad_gate, grad_up, db = weights_call(plan, dx2, act, h_all, g_rows, d_gate, d_up)
+    dq, sums, dh1, down_in = backward_call(
+        plan, db, qe, kx, vx, o, w_o, w_qkv, cos, sin, down, heads
     )
     result = x2 + down[0].astype(F32)
     for r in range(1, wide):
         result = result + down_in[r].astype(F32)
 
-    w_kv = jnp.stack([send(w_kv, r) for r in pieces])
     result, input_grad, gain_grads, grad_kv = tail_call(
         plan, sums, h_one, result.astype(BF), dh1, grad_gain_two, dx2, x_low, gain_one, w_kv, cos, sin
     )
@@ -1129,8 +1364,9 @@
     def tn_split(left, right):
         return jnp.concatenate([tn(left, right[:, n * d_part : (n + 1) * d_part]) for n in range(narrow)], axis=0)
 
-    grad_gu = scatter_grad(jnp.concatenate([tn(h_all, d_gate), tn(h_all, d_up)], axis=1))
-    grad_dn = scatter_grad(tn_split(act, g_rows))
+    grad_dn = scatter_grad(grad_dn.reshape(narrow * ff, d_part))
+    grad_gate = scatter_grad(grad_gate)
+    grad_up = scatter_grad(grad_up)
     grad_o = scatter_grad(tn_split(o.reshape(rows, qw), db.reshape(rows, d)))
     grad_q = scatter_grad(tn(h_one, dq))
     grad_kv = jnp.transpose(grad_kv.reshape(kv_heads, 2, HD, d_part), (3, 0, 1, 2))
@@ -1143,8 +1379,8 @@
         grad_kv[:, :, 1].reshape(d_part, kw),
         grad_o,
         gain_grads[1],
-        grad_gu[:, :ff],
-        grad_gu[:, ff:],
+        grad_gate,
+        grad_up,
         grad_dn,
     )
 

time: 1200 us -> 1180 us (0.983)
  Pallas kernels: 785 us -> 856 us
  local copies, waits for them, and re-layouts: 79.6 us -> 30.4 us
  waiting for transfers between devices: 172 us -> 215 us
  matrix products: 51.4 us -> 12.1 us
  starting transfers between devices: 38.7 us -> 1.15 us
    pallas_call x7 -> x3, Pallas kernels: 112 us -> 312 us  [the longest x1 125 us: head_call(): pl.pallas_call(functools.partial(head_kernel, plan, kv_heads, qw), in_spe...]
    ppermute x30 -> x0, waiting for transfers between devices: 171 us -> none  [the longest x24 101 us: swap(): lax.ppermute(values, axes, [(a, a ^ k) for a in range(size)])]
    all_gather x4 -> x3, waiting for transfers between devices: 0.01 us -> 144 us  [gather_weight(): lax.all_gather(half_of(weight, seq_index, seq_count), NS, axis=0, tiled=T...]
    pallas_call x1, Pallas kernels: 271 us -> 180 us  [backward_call(): pl.pallas_call(functools.partial(backward_kernel, plan, kv_heads, heads),...]
    all_gather x0 -> x1, waiting for transfers between devices: none -> 49.5 us  [body(): w_kv = lax.all_gather(after(w_kv, o), NS, axis=0, tiled=True)]
    unnamed x132 -> x25, local copies, waits for them, and re-layouts: 54.4 us -> 7.21 us
    ppermute x30 -> x0, starting transfers between devices: 38.1 us -> none  [the longest x24 20.4 us: swap(): lax.ppermute(values, axes, [(a, a ^ k) for a in range(size)])]
    dot_general x11 -> x5, matrix products: 46.7 us -> 12.1 us  [tn(): lax.dot_general(left, right, TN, preferred_element_type=F32).astype(BF)]
  transfers between devices with their start and end apart: 40 -> 12, of which waited for: 12 -> 4; matrix products, arithmetic and copies ran while one was open for 10% -> 6% of each run, Pallas kernels for 48% -> 42%
where the time goes in v4:
time: 1180 us
  Pallas kernels  856 us (73%)
  waiting for transfers between devices  215 us (18%)
  other arithmetic  41.7 us (4%)
  local copies, waits for them, and re-layouts  30.4 us (3%)
  between operations  14.5 us (1%)
  matrix products  12.1 us (1%)
    pallas_call x1, Pallas kernels, tail_call(): pl.pallas_call(functools.partial(tail_kernel, plan, kv_heads), in_specs=[...  186 us
    pallas_call x1, Pallas kernels, backward_call(): pl.pallas_call(functools.partial(backward_kernel, plan, kv_heads, heads),...  180 us
    pallas_call x1, Pallas kernels, ffn_call(): pl.pallas_call(functools.partial(ffn_kernel, plan), grid=(wide, tiles), i...  171 us
    all_gather x3, waiting for transfers between devices, gather_weight(): lax.all_gather(half_of(weight, seq_index, seq_count), NS, axis=0, tiled=T...  144 us
    pallas_call x1, Pallas kernels, head_call(): pl.pallas_call(functools.partial(head_kernel, plan, kv_heads, qw), in_spe...  125 us
    pallas_call x1, Pallas kernels, forward_call(): pl.pallas_call(functools.partial(forward_kernel, plan, kv_heads, heads),...  103 us
    pallas_call x1, Pallas kernels, weights_call(): pl.pallas_call(functools.partial(weights_kernel, plan, tiles), grid=(3 *...  83.3 us
    all_gather x1, waiting for transfers between devices, body(): w_kv = lax.all_gather(after(w_kv, o), NS, axis=0, tiled=True)  49.5 us
  transfers between devices with their start and end apart: 12, of which 4 were waited for; matrix products, arithmetic and copies ran while one was open for 6% of the time, Pallas kernels for 42%

profile of v4, /device:TPU:0, one launch (start us, length us, event | category | flops | bytes accessed | tf_op | source)
XLA Modules:
  0.0 1175.1 jit_solution(12243297293591090286)
XLA Ops:
  7.3 1.8 constant_dynamic-slice_fusion.3
  9.2 1.4 convert_reduce_fusion.1
  10.7 0.8 broadcast_compare_fusion
  12.2 1.0 copy.41
  13.2 1.0 copy.42
  14.4 1.3 pad_maximum_fusion.4.gains_ref
  15.7 2.0 pad_maximum_fusion.2.w_ref
  17.7 1.3 subtract_convert_fusion
  19.0 3.1 multiply_sine_fusion
  22.1 2.4 bitcast_select_fusion.g_ref
  24.5 4.5 select_convert_fusion.kf_ref
  29.0 125.1 %head.1 = (bf16[1024,2048]{1,0:T(8,128)(2,1)}, bf16[1024,512]{1,0:T(8,128)(2,1)}, bf16[256,2048]{1,0:T(8,128)(2,1)}, bf16[2,8192,128]{2,1,0:T(8,128)(2,1)}, bf16...) custom-call(bf16[8,4,128,512]{3,2,1,0:T(8,128)(2,1)} %bitcast.91, ...), custom_call_target="tpu_custom_call" | custom-call | flops 96636764160 | bytes 19922944 | tf_op jit(solution)/shard_map/head/pallas_call | solution.py:343
  154.1 1.9 pad_add_fusion.s_ref
  155.9 1.9 constant_dynamic-slice_fusion
  157.8 4.5 copy.55
  162.3 4.4 reshape.216.wo_ref
  166.8 103.5 %attention_forward.1 = (bf16[4,256,512]{2,1,0:T(8,128)(2,1)}, bf16[4,2,2,512,128]{4,3,2,1,0:T(8,128)(2,1)}, f32[256,2048]{1,0:T(8,128)}) custom-call(s32[2]{0:T(128)} %pad_add_fusion.s_ref, bf16[1024,512]{1,0:T(8,128)(2,1)} %get-tuple-element.46.q_ref, bf16[2,8192,128]{2,1,0:T(8,128)(2,1)} %get-tuple-element.47.kx, ...), custom_call_target="tpu_custom_call" | custom-call | flops 34359738368 | bytes 16777216 | tf_op jit(solution)/shard_map/attention_forward/pallas_call | solution.py:522
  270.3 1.0 constant_dynamic-slice_fusion.1
  271.5 2.7 pad_maximum_fusion
  274.2 1.5 constant_dynamic-slice_fusion.2
  276.6 49.5 %all-gather.14.cloned.1.call-done = bf16[8192,256]{1,0:T(8,128)(2,1)} async-done(((bf16[1024,256]{1,0:T(8,128)(2,1)}), bf16[8192,256]{1,0:T(8,128)(2,1)}) %all-gather.14.cloned.1.call-update) | async-done | bytes 4194320 | tf_op jit(solution)/shard_map/all_gather | solution.py:1340
  326.2 4.6 copy.46
  330.8 52.3 %all-gather.12.cloned.1.call-done = bf16[8192,512]{1,0:T(8,128)(2,1)} async-done(((bf16[1024,512]{1,0:T(8,128)(2,1)}), bf16[8192,512]{1,0:T(8,128)(2,1)}) %all-gather.12.cloned.1.call-update) | async-done | bytes 8388624 | tf_op jit(solution)/shard_map/all_gather | solution.py:1292
  383.0 92.2 %all-gather.10.cloned.1.call-done.wg_ref.wu_ref = bf16[2048,4096]{1,0:T(8,128)(2,1)} async-done(((bf16[256,4096]{1,0:T(8,128)(2,1)}), bf16[2048,4096]{1,0:T(8,128)(2,1)}) %all-gather.10.cloned.1.call-update) | async-done | bytes 16777232 | tf_op jit(solution)/shard_map/all_gather | solution.py:1292
  475.3 171.4 %feed_forward.1 = (bf16[1024,2048]{1,0:T(8,128)(2,1)}, bf16[1024,2048]{1,0:T(8,128)(2,1)}, bf16[1024,2048]{1,0:T(8,128)(2,1)}, bf16[1024,2048]{1,0:T(8,128)(2,1)...) custom-call(f32[256,2048]{1,0:T(8,128)} %get-tuple-element.50.x2_ref, ...), custom_call_target="tpu_custom_call" | custom-call | flops 68719476736 | bytes 50331648 | tf_op jit(solution)/shard_map/feed_forward/pallas_call | solution.py:675
  646.6 83.3 %weight_gradients.1 = (bf16[4,2048,512]{2,1,0:T(8,128)(2,1)}, bf16[2048,2048]{1,0:T(8,128)(2,1)}, bf16[2048,2048]{1,0:T(8,128)(2,1)}, bf16[4,256,2048]{2,1,0:T(8,128)(2,1)}) custom-call(f32[256,2048]{1,0:T(8,128)} %get-tuple-element.55.dx2_ref, bf16[1024,2048]{1,0:T(8,128)(2,1)} %get-tuple-element.60.act_ref, bf16[1024,2048]{1,0:T(8,128)(2,1)} %get-tuple-element.61.h_ref, ...), custom_call_target="tpu_custom_call" | custom-call | flops 42949672960 | bytes 41943040 | tf_op jit(solution)/shard_map/weight_gradients/pallas_call | solution.py:775
  731.6 180.1 %attention_backward.1 = (bf16[1024,512]{1,0:T(8,128)(2,1)}, f32[2,8192,128]{2,1,0:T(8,128)}, f32[256,2048]{1,0:T(8,128)}, bf16[4,256,2048]{2,1,0:T(8,128)(2,1)}) custom-call(bf16[4,256,2048]{2,1,0:T(8,128)(2,1)} %get-tuple-element.64.db_ref, bf16[4,2,2,512,128]{4,3,2,1,0:T(8,128)(2,1)} %get-tuple-element.65.qe_ref, ...), custom_call_target="tpu_custom_call" | custom-call | flops 77309411328 | bytes 25165824 | tf_op jit(solution)/shard_map/attention_backward/pallas_call | solution.py:951
  911.7 6.5 convolution_convert_fusion
  918.3 2.1 convolution_convert_fusion.1
  920.5 2.0 convolution_convert_fusion.2
  924.0 1.5 pad_maximum_fusion.1
  927.1 4.0 fusion.res_ref
  931.1 18.4 %reduce-scatter.10.cloned.1.call-done = bf16[256,2048]{1,0:T(8,128)(2,1)} async-done(((bf16[2048,2048]{1,0:T(8,128)(2,1)}), bf16[256,2048]{1,0:T(8,128)(2,1)}) %reduce-scatter.10.cloned.1.call-update) | async-done | bytes 1048592 | tf_op jit(solution)/shard_map/reduce_scatter | solution.py:1295
  949.5 186.3 %input_gradient.1 = (bf16[4,8,128,512]{3,2,1,0:T(8,128)(2,1)}, bf16[4,8,128,512]{3,2,1,0:T(8,128)(2,1)}, f32[2,512]{1,0:T(2,128)}, f32[256,512]{1,0:T(8,128)}) custom-call(f32[2,8192,128]{2,1,0:T(8,128)} %get-tuple-element.68.sums_ref, bf16[1024,2048]{1,0:T(8,128)(2,1)} %get-tuple-element.69.h_ref, bf16[256,2048]{1,0:T(8,128)(2,1)} %fusion.res_ref, ...), custom_call_target="tpu_custom_call" | custom-call | flops 107374182400 | bytes 8388608 | tf_op jit(solution)/shard_map/input_gradient/pallas_call | solution.py:1195
  1135.8 1.1 copy.56
  1136.9 0.8 copy.49
  1137.7 0.8 copy.48
  1138.6 2.2 copy-done.3
  1140.8 2.4 assemble.2
  1143.2 1.3 copy-done.2
  1144.5 3.6 assemble.3
  1148.7 2.4 all_gather.31
  1151.0 1.1 convert_element_type.87
  1152.2 2.4 all_gather.32
  1154.5 1.1 convert_element_type.92
  1155.6 4.2 convert_element_type.95
  1159.8 4.3 convert_element_type.94
  1164.1 4.1 convert_element_type.93
  (66 shorter events, 7.5 us)
Async XLA Ops:
  7.2 263.1 %copy-start = (bf16[2048,512]{1,0:T(8,128)(2,1)S(1)}, bf16[2048,512]{1,0:T(8,128)(2,1)}, u32[]{:S(2)}) copy-start(bf16[2048,512]{1,0:T(8,128)(2,1)} %param.22) | copy-start | bytes 6291460
  7.2 17.3 %copy-start.5 = (s32[8192]{0:T(1024)S(1)}, s32[8192]{0:T(1024)}, u32[]{:S(2)}) copy-start(s32[8192]{0:T(1024)} %param.23) | copy-start | bytes 98308
  7.2 150.6 %all-gather.8.cloned.1.call-start = ((), (), s32[]{:S(2)}) async-start(), calls=%async_computation.5 | async-start | bytes 2359296 | tf_op jit(solution)/shard_map/all_gather | solution.py:1292
  9.1 317.1 %all-gather.14.cloned.1.call-start = ((), (), s32[]{:S(2)}) async-start(), calls=%async_computation.8 | async-start | bytes 4718592 | tf_op jit(solution)/shard_map/all_gather | solution.py:1340
  270.3 112.8 %all-gather.12.cloned.1.call-start = ((), (), s32[]{:S(2)}) async-start(), calls=%async_computation.7 | async-start | bytes 9437184 | tf_op jit(solution)/shard_map/all_gather | solution.py:1292
  271.4 203.9 %all-gather.10.cloned.1.call-start = ((), (), s32[]{:S(2)}) async-start(), calls=%async_computation.6 | async-start | bytes 18874368 | tf_op jit(solution)/shard_map/all_gather | solution.py:1292
  274.2 1.8 copy-start.6
  275.8 649.8 %reduce-scatter.14.cloned.1.call-start = ((), (), s32[]{:S(2)}) async-start(), calls=%async_computation.15 | async-start | bytes 9437184 | tf_op jit(solution)/shard_map/reduce_scatter | solution.py:1295
  730.0 196.1 %reduce-scatter.12.cloned.1.call-start = ((), (), s32[]{:S(2)}) async-start(), calls=%async_computation.13 | async-start | bytes 9437184 | tf_op jit(solution)/shard_map/reduce_scatter | solution.py:1295
  730.6 218.9 %reduce-scatter.10.cloned.1.call-start = ((), (), s32[]{:S(2)}) async-start(), calls=%async_computation.11 | async-start | bytes 9437184 | tf_op jit(solution)/shard_map/reduce_scatter | solution.py:1295
  731.4 417.3 %reduce-scatter.6.cloned.1.call-start = ((), (), s32[]{:S(2)}) async-start(), calls=%async_computation.9 | async-start | bytes 2359296 | tf_op jit(solution)/shard_map/reduce_scatter | solution.py:1295
  911.7 6.6 copy-start.9
  918.3 233.9 %reduce-scatter.8.cloned.1.call-start = ((), (), s32[]{:S(2)}) async-start(), calls=%async_computation.10 | async-start | bytes 2359296 | tf_op jit(solution)/shard_map/reduce_scatter | solution.py:1295
  918.3 4.1 copy-start.8
  923.9 3.1 copy-start.4
  925.4 230.2 %all-gather.20.cloned.1.call-start = ((), (), s32[]{:S(2)}) async-start(), calls=%async_computation.16 | async-start | bytes 3145728 | tf_op jit(solution)/shard_map/all_gather | solution.py:1296
  926.0 233.8 %all-gather.18.cloned.1.call-start = ((), (), s32[]{:S(2)}) async-start(), calls=%async_computation.14 | async-start | bytes 3145728 | tf_op jit(solution)/shard_map/all_gather | solution.py:1296
  926.8 237.4 %all-gather.16.cloned.1.call-start = ((), (), s32[]{:S(2)}) async-start(), calls=%async_computation.12 | async-start | bytes 3145728 | tf_op jit(solution)/shard_map/all_gather | solution.py:1296
  1138.6 2.2 copy-start.3
  1140.8 3.7 copy-start.2
  1144.5 3.6 copy-start.7
  1159.8 8.4 copy-start.1
Sparse Core Ops, SparseCore 0:
  10.5 31.8 all-gather.7
  270.4 55.7 all-gather.13
  328.6 54.3 all-gather.11
  385.4 89.8 all-gather.9
  730.1 69.4 reduce-scatter.13
  803.4 71.3 reduce-scatter.11
  878.2 71.2 reduce-scatter.9
  953.7 64.5 reduce-scatter.5
  1022.1 42.7 reduce-scatter.7
  1066.3 10.5 all-gather.19
  1078.6 11.7 all-gather.17
  1091.8 11.7 all-gather.15

commit v5 on v4

--- a/solution.py
+++ b/solution.py
@@ -123,6 +123,109 @@
 
     def beside(self, k):
         return lax.rem(self.me + k + self.narrow, self.narrow)
+
+
+class Parts:
+    def __init__(self, plan, team, ref, slots, send, recv, stay):
+        self.plan, self.team, self.ref, self.send, self.recv = plan, team, ref, send, recv
+        self.slots = slots.at[lax.axis_index("wide")]
+        self.part = ref.shape[1] // team.narrow
+        self.stay = pltpu.make_async_copy(self.slab(team.index), self.slots.at[team.index], stay)
+
+    def slab(self, other):
+        cw, narrow, part = self.plan.cw, self.team.narrow, self.part
+        rows = pl.ds(pl.multiple_of((other // narrow) * cw, cw), cw)
+        return self.ref.at[rows, pl.ds(pl.multiple_of(lax.rem(other, narrow) * part, part), part)]
+
+    def to(self, k):
+        team = self.team
+        src = self.slab(team.device(k))
+        return push(src, self.slots.at[team.index], self.send.at[k], self.recv.at[k], team.member(k))
+
+    def start(self):
+        for k in range(1, self.team.size):
+            self.to(k).start()
+        self.stay.start()
+
+    def wait(self):
+        team = self.team
+        self.stay.wait()
+        for k in range(1, team.size):
+            src = self.slab(team.index)
+            push(src, self.slots.at[team.device(-k)], self.send.at[k], self.recv.at[k], team.member(k)).wait_recv()
+
+    def sent(self):
+        for k in range(1, self.team.size):
+            self.to(k).wait_send()
+
+
+class Sums:
+    def __init__(self, plan, terms, right, left, sems):
+        self.wide, self.terms, self.sums, self.sems = plan.wide, terms, (right, left), sems
+        self.z = lax.axis_index("wide")
+        self.side = jnp.minimum(self.z, plan.wide - 1 - self.z)
+
+    def term(self, h, way):
+        return jnp.where(h <= self.side, 2 * h - 1 if way > 0 else 2 * h, self.side + h)
+
+    def sends(self, t, way):
+        h = self.wide - t
+        return self.z + h <= self.wide - 1 if way > 0 else self.z >= h
+
+    def first(self, way):
+        return self.z == (0 if way > 0 else self.wide - 1)
+
+    def copy(self, src, t, way):
+        buf = self.sums[0 if way > 0 else 1]
+        send, recv = self.sems[:2] if way > 0 else self.sems[2:]
+        return push(src, buf.at[t], send.at[t], recv.at[t], {"wide": self.z + way})
+
+    def came(self, t, way):
+        buf = self.sums[0 if way > 0 else 1]
+        send, recv = self.sems[:2] if way > 0 else self.sems[2:]
+        push(buf.at[t], buf.at[t], send.at[t], recv.at[t], {"wide": self.z - way}).wait_recv()
+
+    def go(self, t):
+        for way in (1, -1):
+            term = self.term(self.wide - t, way)
+
+            @pl.when(self.sends(t, way) & self.first(way))
+            def _():
+                self.copy(self.terms.at[term], t, way).start()
+
+            if t > 1:
+                @pl.when(self.sends(t, way) & jnp.logical_not(self.first(way)))
+                def _():
+                    self.came(t - 1, way)
+                    buf = self.sums[0 if way > 0 else 1]
+                    tall = min(32, buf.shape[1])
+
+                    @pl.loop(0, buf.shape[1] // tall)
+                    def _(b):
+                        at = pl.ds(pl.multiple_of(b * tall, tall), tall)
+                        total = buf[t - 1, at, :].astype(F32) + self.terms[term, at, :].astype(F32)
+                        buf[t - 1, at, :] = total.astype(BF)
+
+                    self.copy(buf.at[t - 1], t, way).start()
+
+    def finish(self):
+        for way in (1, -1):
+            @pl.when(jnp.logical_not(self.first(way)))
+            def _():
+                self.came(self.wide - 1, way)
+
+        for t in range(1, self.wide):
+            for way in (1, -1):
+                @pl.when(self.sends(t, way))
+                def _():
+                    self.copy(self.terms.at[0], t, way).wait_send()
+
+    def total(self, own, at):
+        out = own
+        for way in (1, -1):
+            sums = self.sums[0 if way > 0 else 1][self.wide - 1, at, :].astype(F32)
+            out = out + jnp.where(self.first(way), 0.0, sums)
+        return out
 
 
 def head_kernel(
@@ -405,7 +508,7 @@
 
 def forward_kernel(
     plan, kv_heads, heads, s_ref, q_ref, kx, vx, wo_ref, x_ref, o_ref, qe_ref, x2_ref,
-    in_buf, out_buf, term_acc, rs_send, rs_recv,
+    terms, right, left, term_acc, *sems
 ):
     wide, cw, chunk, own = plan.wide, plan.cw, plan.chunk, plan.own
     rows, width = heads * cw, heads * HD
@@ -420,8 +523,7 @@
     low_rows = pl.ds(pl.multiple_of(half * cw, cw), cw)
     columns = pl.ds(pl.multiple_of(g * width, width), width)
 
-    def give(device):
-        return push(out_buf.at[device], in_buf.at[z], rs_send.at[device], rs_recv.at[z], {"wide": device})
+    attn = Sums(plan, terms, right, left, sems)
 
     @pl.when((unit == 0) & (g == 0))
     def _():
@@ -479,29 +581,22 @@
 
     @pl.when((g == last_g) & (piece > 0))
     def _():
-        out_buf[w, low_rows, :] = term_acc[...].astype(BF)
-
-    @pl.when((g == last_g) & (piece > 0) & (half == 1))
-    def _():
-        give(w).start()
+        terms[piece, low_rows, :] = term_acc[...].astype(BF)
+
+    for t in range(1, wide):
+        @pl.when((g == last_g) & (unit == 2 * t - 1))
+        def _():
+            attn.go(t)
 
     @pl.when((unit == 2 * wide - 1) & (g == last_g))
     def _():
-        for p in range(1, wide):
-            other = near_of(plan, z, p)
-            push(out_buf.at[z], in_buf.at[other], rs_send.at[z], rs_recv.at[other], {"wide": other}).wait_recv()
+        attn.finish()
         tall = min(32, own)
 
         @pl.loop(0, own // tall)
         def _(b):
             at = pl.ds(pl.multiple_of(b * tall, tall), tall)
-            total = x2_ref[at, :]
-            for p in range(1, wide):
-                total = total + in_buf[near_of(plan, z, p), at, :].astype(F32)
-            x2_ref[at, :] = total
-
-        for p in range(1, wide):
-            give(near_of(plan, z, p)).wait_send()
+            x2_ref[at, :] = attn.total(x2_ref[at, :], at)
 
 
 def forward_call(plan, starts, q, kx, vx, w_o, x, heads):
@@ -525,7 +620,7 @@
         in_specs=[pl.BlockSpec(memory_space=pltpu.SMEM)] + [fixed(a) for a in given],
         out_specs=[fixed(a) for a in outs],
         out_shape=outs,
-        scratch_shapes=[buffer, buffer, pltpu.VMEM((cw, d), F32), sems, sems],
+        scratch_shapes=[buffer] * 3 + [pltpu.VMEM((cw, d), F32)] + [sems] * 4,
         cost_estimate=pl.CostEstimate(
             flops=16 * pairs * HD, bytes_accessed=8 * kv_heads * total * 128, transcendentals=pairs
         ),
@@ -714,13 +809,15 @@
 
 
 def weights_kernel(
-    plan, tiles, dx2_ref, act_ref, h_ref, g_ref, dg_ref, du_ref, dn_out, gate_out, up_out, db_out,
-    db_buf, keep_sem, *chain_sems
+    plan, tiles, dx2_ref, act_ref, h_ref, g_ref, dg_ref, du_ref, down_ref, x2_ref,
+    dn_out, gate_out, up_out, db_out, res_out,
+    db_buf, right, left, keep_sem, *sems
 ):
     wide = plan.wide
     step = pl.program_id(0)
     last = pl.num_programs(0) - 1
-    chain = Chain(plan, db_buf, chain_sems)
+    chain = Chain(plan, db_buf, sems[:4])
+    down = Sums(plan, down_ref, right, left, sems[4:])
     keep = pltpu.make_async_copy(db_buf, db_out, keep_sem)
 
     @pl.when(step == 0)
@@ -751,15 +848,24 @@
             chain.arrive(h)
             if h + 1 < wide:
                 chain.go(h + 1)
+            down.go(h)
 
     @pl.when(step == last)
     def _():
         keep.start()
+        down.finish()
+        tall = min(32, x2_ref.shape[0])
+
+        @pl.loop(0, x2_ref.shape[0] // tall)
+        def _(b):
+            at = pl.ds(pl.multiple_of(b * tall, tall), tall)
+            res_out[at, :] = down.total(x2_ref[at, :] + down_ref[0, at, :].astype(F32), at).astype(BF)
+
         chain.finish()
         keep.wait()
 
 
-def weights_call(plan, dx2, act, h, g, d_gate, d_up):
+def weights_call(plan, dx2, act, h, g, d_gate, d_up, down, x2):
     own, d = dx2.shape
     rows, ff = act.shape
     wide, narrow = plan.wide, plan.group // 2
@@ -779,40 +885,47 @@
             fixed(dx2),
             pl.BlockSpec((rows, ff_tile), lambda s: (0, first(s))),
             pl.BlockSpec((rows, d_tile), lambda s: (0, both(s))),
-            fixed(g), fixed(d_gate), fixed(d_up),
+            fixed(g), fixed(d_gate), fixed(d_up), fixed(down), fixed(x2),
         ],
         out_specs=[
             pl.BlockSpec((narrow, ff_tile, part), lambda s: (0, first(s), 0)),
             pl.BlockSpec((d_tile, ff), lambda s: (second(s), 0)),
             pl.BlockSpec((d_tile, ff), lambda s: (third(s), 0)),
             pl.BlockSpec(memory_space=pl.ANY),
+            pl.BlockSpec((own, d), lambda s: (0, 0), pipeline_mode=pl.Buffered(1)),
         ],
         out_shape=[
             jax.ShapeDtypeStruct((narrow, ff, part), BF),
             jax.ShapeDtypeStruct((d, ff), BF),
             jax.ShapeDtypeStruct((d, ff), BF),
             jax.ShapeDtypeStruct((wide, own, d), BF),
+            jax.ShapeDtypeStruct((own, d), BF),
         ],
-        scratch_shapes=[pltpu.VMEM((wide, own, d), BF), pltpu.SemaphoreType.DMA] + [sems] * 4,
+        scratch_shapes=[pltpu.VMEM((wide, own, d), BF)] * 3 + [pltpu.SemaphoreType.DMA] + [sems] * 8,
         cost_estimate=pl.CostEstimate(
             flops=10 * rows * d * ff, bytes_accessed=20 * rows * d, transcendentals=0
         ),
         compiler_params=pltpu.CompilerParams(
-            vmem_limit_bytes=56 << 20, collective_id=6, has_side_effects=True
+            vmem_limit_bytes=60 << 20, collective_id=6, has_side_effects=True
         ),
         name="weight_gradients",
-    )(dx2, act, h, g, d_gate, d_up)
+    )(dx2, act, h, g, d_gate, d_up, down, x2)
 
 
 def backward_kernel(
-    plan, kv_heads, heads, db_ref, qe_ref, kx, vx, o_ref, wo_ref, wq_ref, cos_ref, sin_ref, dn_ref,
-    dq_ref, sums, dh_ref, dn_got, in_buf, out_buf, term_acc, rs_send, rs_recv, dn_send, dn_recv
+    plan, kv_heads, heads, db_ref, qe_ref, kx, vx, o_ref, wo_ref, wq_ref, cos_ref, sin_ref, res_ref,
+    dq_ref, sums, dh_ref, res_out, terms, right, left, term_acc, results,
+    part_send, part_recv, keep_sem, *sems
 ):
     wide, cw, chunk, own = plan.wide, plan.cw, plan.chunk, plan.own
     rows = heads * cw
     width = heads * HD
     z = lax.axis_index("wide")
-    index = lax.axis_index("seq") * lax.axis_size("narrow") + lax.axis_index("narrow")
+    team = Group(plan)
+    index = team.index
+    chain = Chain(plan, results, sems[:4])
+    back = Sums(plan, terms, right, left, sems[4:])
+    parts = Parts(plan, team, res_ref, results, part_send, part_recv, keep_sem.at[0])
     unit, g = pl.program_id(0), pl.program_id(1)
     last_unit, last_g = 2 * wide - 1, kv_heads - 1
     piece, half = wide - 1 - unit // 2, lax.rem(unit, 2)
@@ -821,27 +934,30 @@
     c = jnp.where(half == 1, 2 * plan.group - 1 - index, index)
     low_rows = pl.ds(pl.multiple_of(half * cw, cw), cw)
 
-    def give(device):
-        return push(out_buf.at[device], in_buf.at[z], rs_send.at[device], rs_recv.at[z], {"wide": device})
-
-    def give_down(p):
-        device = near_of(plan, z, p)
-        slot = lax.rem(z - device + wide, wide)
-        return push(dn_ref.at[p], dn_got.at[slot], dn_send.at[p], dn_recv.at[slot], {"wide": device})
-
     @pl.when((unit == 0) & (g == 0))
     def _():
-        greet([along_wide(plan, k) for k in range(1, wide)])
+        others = [team.member(k) for k in range(1, plan.group)]
+        greet(others + [along_wide(plan, k) for k in range(1, wide)])
+        parts.start()
 
         @pl.loop(0, kv_heads * plan.total // chunk)
         def _(b):
             at = pl.ds(pl.multiple_of(lax.rem(b, plan.total // chunk) * chunk, chunk), chunk)
             sums[b // (plan.total // chunk), at, :] = jnp.zeros((chunk, 128), F32)
 
-    for p in range(1, wide):
-        @pl.when((unit == wide - 1 - p) & (g == last_g))
+    @pl.when((unit == 1) & (g == last_g))
+    def _():
+        parts.wait()
+        chain.go(1)
+
+    for h in range(1, wide):
+        late = {1: (3, 0), 2: (4, last_g), 3: (6, 0)}.get(h, (min(h + 3, last_unit), last_g))
+
+        @pl.when((unit == late[0]) & (g == late[1]))
         def _():
-            give_down(p).start()
+            chain.arrive(h)
+            if h + 1 < wide:
+                chain.go(h + 1)
 
     lane = lax.broadcasted_iota(jnp.int32, (cw, 128), 1)
     columns = pl.ds(pl.multiple_of(g * width, width), width)
@@ -902,36 +1018,31 @@
 
     @pl.when((g == last_g) & (piece > 0))
     def _():
-        out_buf[w, low_rows, :] = term_acc[...].astype(BF)
-
-    @pl.when((g == last_g) & (piece > 0) & (half == 1))
-    def _():
-        give(w).start()
+        terms[piece, low_rows, :] = term_acc[...].astype(BF)
+
+    for t in range(1, wide):
+        @pl.when((g == last_g) & (unit == 2 * t - 1))
+        def _():
+            back.go(t)
 
     @pl.when((unit == last_unit) & (g == last_g))
     def _():
-        for p in range(1, wide):
-            other = near_of(plan, z, p)
-            push(out_buf.at[z], in_buf.at[other], rs_send.at[z], rs_recv.at[other], {"wide": other}).wait_recv()
+        keep = pltpu.make_async_copy(results, res_out, keep_sem.at[1])
+        keep.start()
+        back.finish()
         tall = min(32, own)
 
         @pl.loop(0, own // tall)
         def _(b):
             at = pl.ds(pl.multiple_of(b * tall, tall), tall)
-            total = dh_ref[at, :]
-            for p in range(1, wide):
-                total = total + in_buf[near_of(plan, z, p), at, :].astype(F32)
-            dh_ref[at, :] = total
-
-        for p in range(1, wide):
-            other = near_of(plan, z, p)
-            slot = lax.rem(other - z + wide, wide)
-            push(dn_ref.at[p], dn_got.at[slot], dn_send.at[p], dn_recv.at[slot], {"wide": other}).wait_recv()
-            give(other).wait_send()
-            give_down(p).wait_send()
-
-
-def backward_call(plan, db, qe, kx, vx, o, w_o, w_qkv, cos, sin, down, heads):
+            dh_ref[at, :] = back.total(dh_ref[at, :], at)
+
+        chain.finish()
+        parts.sent()
+        keep.wait()
+
+
+def backward_call(plan, db, qe, kx, vx, o, w_o, w_qkv, cos, sin, res, heads):
     kv_heads, total, _ = kx.shape
     _, own, d = db.shape
     wide, rows, cw = plan.wide, plan.rows, plan.cw
@@ -945,17 +1056,18 @@
         jax.ShapeDtypeStruct((kv_heads, total, 128), F32),
         jax.ShapeDtypeStruct((own, d), F32),
     ]
-    pieces = jax.ShapeDtypeStruct((wide, own, d), BF)
+    slots = (wide, plan.group, cw, d // (plan.group // 2))
     buffer = pltpu.VMEM((wide, own, d), BF)
     sems = pltpu.SemaphoreType.DMA((wide,))
     return pl.pallas_call(
         functools.partial(backward_kernel, plan, kv_heads, heads),
         grid=(2 * wide, kv_heads),
         in_specs=[fixed(a) for a in given[:6]]
-        + [pl.BlockSpec((d, qw), lambda u, g: (0, 0), pipeline_mode=pl.Buffered(1)), fixed(cos), fixed(sin), hbm],
+        + [pl.BlockSpec((d, qw), lambda u, g: (0, 0), pipeline_mode=pl.Buffered(1)), fixed(cos), fixed(sin), fixed(res)],
         out_specs=[fixed(a) for a in outs] + [hbm],
-        out_shape=outs + [pieces],
-        scratch_shapes=[buffer, buffer, pltpu.VMEM((cw, d), F32)] + [sems] * 4,
+        out_shape=outs + [jax.ShapeDtypeStruct(slots, BF)],
+        scratch_shapes=[buffer] * 3 + [pltpu.VMEM((cw, d), F32), pltpu.VMEM(slots, BF)]
+        + [pltpu.SemaphoreType.DMA((plan.group,))] * 2 + [pltpu.SemaphoreType.DMA((2,))] + [sems] * 8,
         cost_estimate=pl.CostEstimate(
             flops=36 * pairs * HD, bytes_accessed=12 * kv_heads * total * 128, transcendentals=pairs
         ),
@@ -963,61 +1075,26 @@
             vmem_limit_bytes=60 << 20, collective_id=3, has_side_effects=True
         ),
         name="attention_backward",
-    )(*given, down)
+    )(*given, res)
 
 
 def tail_kernel(
-    plan, kv_heads, sums_ref, h_ref, res_ref, dh_ref, gain2_ref, dx2_ref, x_ref, gain_ref, wkv_ref,
-    cos_ref, sin_ref, res_out, got_out, gain_out, kv_out,
-    swap_out, swap_in, low, near_in, dkv, head_in, dh_acc, dx_low, every, results,
+    plan, kv_heads, sums_ref, h_ref, dh_ref, gain2_ref, dx2_ref, x_ref, gain_ref, wkv_ref,
+    cos_ref, sin_ref, got_out, gain_out, kv_out,
+    swap_out, swap_in, low, near_in, dkv, head_in, dh_acc, dx_low, every,
     gain_part, gain_in, gain_sum, gain_all, kv_part, kv_in,
     swap_sem, near_send, near_recv, head_send, head_recv, part_send, part_recv,
-    res_send, res_recv, gain_send, gain_recv, gain2_send, gain2_recv, kv_send, kv_recv, own_sem, *chain_sems
+    gain_send, gain_recv, gain2_send, gain2_recv, kv_send, kv_recv, own_sem, *chain_sems
 ):
     group, wide, chunk, cw, own = plan.group, plan.wide, plan.chunk, plan.cw, plan.own
     narrow = group // 2
     part = dx_low.shape[1] // narrow
-    seq, me, z = lax.axis_index("seq"), lax.axis_index("narrow"), lax.axis_index("wide")
-    index = seq * narrow + me
-    res_chain = Chain(plan, results, chain_sems[:4])
-    dx_chain = Chain(plan, every, chain_sems[4:])
-
-    def device(k):
-        return lax.rem(index + k + group, group)
-
-    def member(k):
-        return {"seq": device(k) // narrow, "narrow": lax.rem(device(k), narrow)}
+    team = Group(plan)
+    seq, me, z = team.seq, team.me, lax.axis_index("wide")
+    device, member = team.device, team.member
+    dx_chain = Chain(plan, every, chain_sems)
 
     greet([member(k) for k in range(1, group)] + [along_wide(plan, r) for r in range(1, wide)])
-
-    def slab(ref, other):
-        rows = pl.ds(pl.multiple_of((other // narrow) * cw, cw), cw)
-        return ref.at[rows, pl.ds(pl.multiple_of(lax.rem(other, narrow) * part, part), part)]
-
-    class Parts:
-        def __init__(self, ref, slots, send, recv, stay):
-            self.ref, self.slots, self.send, self.recv = ref, slots, send, recv
-            self.stay = pltpu.make_async_copy(slab(ref, index), slots.at[z, index], stay)
-
-        def to(self, k):
-            return push(slab(self.ref, device(k)), self.slots.at[z, index], self.send.at[k], self.recv.at[k], member(k))
-
-        def start(self):
-            for k in range(1, group):
-                self.to(k).start()
-            self.stay.start()
-
-        def wait(self):
-            self.stay.wait()
-            for k in range(1, group):
-                other = device(-k)
-                push(
-                    slab(self.ref, index), self.slots.at[z, other], self.send.at[k], self.recv.at[k], member(k)
-                ).wait_recv()
-
-        def sent(self):
-            for k in range(1, group):
-                self.to(k).wait_send()
 
     def place(owner_seq, half, n):
         quarter = owner_seq if half == 0 else 3 - owner_seq
@@ -1033,8 +1110,6 @@
 
     swap = push(swap_out, swap_in, swap_sem.at[0], swap_sem.at[1], {"seq": 1 - seq})
     swap.start()
-    res_parts = Parts(res_ref, results, res_send, res_recv, own_sem.at[0])
-    res_parts.start()
     swap.wait_recv()
 
     @pl.loop(0, narrow)
@@ -1050,8 +1125,6 @@
 
     for k in range(1, narrow):
         near(k).start()
-    res_parts.wait()
-    res_chain.go(1)
     for k in range(1, narrow):
         near(k).wait_recv()
 
@@ -1083,10 +1156,6 @@
 
     for k in range(1, group):
         kv_to(k).start()
-    if wide > 1:
-        res_chain.arrive(1)
-    if wide > 2:
-        res_chain.go(2)
 
     tile = min(512, part)
     for r in range(wide):
@@ -1116,7 +1185,7 @@
         inner = jnp.mean(dz1 * z1, axis=1, keepdims=True)
         dx_low[at, :] = (dx2_ref[at, :] + scale * (dz1 - z1 * inner)).astype(BF)
 
-    dx_parts = Parts(dx_low, every, part_send, part_recv, own_sem.at[1])
+    dx_parts = Parts(plan, team, dx_low, every, part_send, part_recv, own_sem.at[0])
     dx_parts.start()
 
     def gain_to(k):
@@ -1125,10 +1194,6 @@
 
     for k in range(1, group):
         gain_to(k).start()
-    for h in range(2, wide):
-        res_chain.arrive(h)
-        if h + 1 < wide:
-            res_chain.go(h + 1)
     dx_parts.wait()
     dx_chain.go(1)
 
@@ -1145,8 +1210,6 @@
         gain_on(r).start()
     for k in range(1, group):
         kv_to(k).wait_recv()
-    res_keep = pltpu.make_async_copy(results, res_out, own_sem.at[2])
-    res_keep.start()
     kv_out[...] = kv_part[me].astype(F32)
     for k in range(1, group):
         kv_out[...] += kv_in[k].astype(F32)
@@ -1159,10 +1222,9 @@
         dx_chain.arrive(h)
         if h + 1 < wide:
             dx_chain.go(h + 1)
-    got_keep = pltpu.make_async_copy(every, got_out, own_sem.at[3])
+    got_keep = pltpu.make_async_copy(every, got_out, own_sem.at[1])
     got_keep.start()
 
-    res_chain.finish()
     dx_chain.finish()
     swap.wait_send()
     for k in range(1, narrow):
@@ -1170,16 +1232,14 @@
     for r in range(1, wide):
         heads_to(r).wait_send()
         gain_on(r).wait_send()
-    res_parts.sent()
     dx_parts.sent()
     for k in range(1, group):
         gain_to(k).wait_send()
         kv_to(k).wait_send()
-    res_keep.wait()
     got_keep.wait()
 
 
-def tail_call(plan, sums, h, res, dh, gain2, dx2, x, gain, w_kv, cos, sin):
+def tail_call(plan, sums, h, dh, gain2, dx2, x, gain, w_kv, cos, sin):
     kv_heads = sums.shape[0]
     own, d = dh.shape
     group, wide, chunk, cw = plan.group, plan.wide, plan.chunk, plan.cw
@@ -1189,15 +1249,14 @@
     dma = pltpu.SemaphoreType.DMA
     quarter = pltpu.VMEM((narrow, kv_heads, 2, chunk, 128), BF)
     slots = (wide, group, cw, part)
-    given = [sums, h, res, dh, gain2, dx2, x, gain, w_kv, cos, sin]
+    given = [sums, h, dh, gain2, dx2, x, gain, w_kv, cos, sin]
     whole = pl.BlockSpec(memory_space=pltpu.VMEM)
     hbm = pl.BlockSpec(memory_space=pl.ANY)
     return pl.pallas_call(
         functools.partial(tail_kernel, plan, kv_heads),
         in_specs=[whole] * len(given),
-        out_specs=[hbm, hbm, whole, whole],
+        out_specs=[hbm, whole, whole],
         out_shape=[
-            jax.ShapeDtypeStruct(slots, BF),
             jax.ShapeDtypeStruct(slots, BF),
             jax.ShapeDtypeStruct((2, part), F32),
             jax.ShapeDtypeStruct((kv_width, part), F32),
@@ -1209,7 +1268,6 @@
             pltpu.VMEM((own, d), F32),
             pltpu.VMEM((own, d), BF),
             pltpu.VMEM(slots, BF),
-            pltpu.VMEM(slots, BF),
             pltpu.VMEM((2, d), F32),
             pltpu.VMEM((group, 2, part), F32),
             pltpu.VMEM((2, part), F32),
@@ -1217,9 +1275,9 @@
             pltpu.VMEM((narrow, kv_width, part), BF),
             pltpu.VMEM((group, kv_width, part), BF),
             dma((2,)), dma((narrow,)), dma((narrow,)), dma((wide,)), dma((wide,)), dma((group,)), dma((group,)),
-            dma((group,)), dma((group,)), dma((group,)), dma((group,)), dma((wide,)), dma((wide,)),
-            dma((group,)), dma((group,)), dma((4,)),
-        ] + [dma((wide,))] * 8,
+            dma((group,)), dma((group,)), dma((wide,)), dma((wide,)),
+            dma((group,)), dma((group,)), dma((2,)),
+        ] + [dma((wide,))] * 4,
         cost_estimate=pl.CostEstimate(
             flops=200 * own * d * wide * kv_width, bytes_accessed=4 * sums.size, transcendentals=0
         ),
@@ -1337,23 +1395,20 @@
     o, qe, x2 = forward_call(plan, starts, q, kx, vx, w_o, x_low, heads)
     w_kv = jnp.transpose(w_kv.reshape(wide, seq_count, d_part // seq_count, 2 * kw), (1, 0, 2, 3))
     w_kv = lax.dynamic_index_in_dim(w_kv, seq_index, 0, keepdims=False).reshape(-1, 2 * kw)
-    w_kv = lax.all_gather(after(w_kv, o), NS, axis=0, tiled=True)
+    w_kv = lax.all_gather(after(w_kv, o, w_dn, w_gu), NS, axis=0, tiled=True)
     w_kv = w_kv.reshape(group, wide, d_part // seq_count, 2 * kw)
     w_kv = jnp.transpose(w_kv, (1, 0, 2, 3)).reshape(wide, d, 2 * kw)
 
     act, d_gate, d_up, h_all, down, dx2, grad_gain_two = ffn_call(plan, x2, gain_two, g_rows, w_gu, w_dn)
 
     act = after(act, w_kv)
-    grad_dn, grad_gate, grad_up, db = weights_call(plan, dx2, act, h_all, g_rows, d_gate, d_up)
-    dq, sums, dh1, down_in = backward_call(
-        plan, db, qe, kx, vx, o, w_o, w_qkv, cos, sin, down, heads
+    grad_dn, grad_gate, grad_up, db, result = weights_call(
+        plan, dx2, act, h_all, g_rows, d_gate, d_up, down, x2
     )
-    result = x2 + down[0].astype(F32)
-    for r in range(1, wide):
-        result = result + down_in[r].astype(F32)
-
-    result, input_grad, gain_grads, grad_kv = tail_call(
-        plan, sums, h_one, result.astype(BF), dh1, grad_gain_two, dx2, x_low, gain_one, w_kv, cos, sin
+    dq, sums, dh1, result = backward_call(plan, db, qe, kx, vx, o, w_o, w_qkv, cos, sin, result, heads)
+
+    input_grad, gain_grads, grad_kv = tail_call(
+        plan, sums, h_one, dh1, grad_gain_two, dx2, x_low, gain_one, w_kv, cos, sin
     )
     result = assemble_call(plan, scalars, result, BF)
     input_grad = assemble_call(plan, scalars, input_grad, F32)

time: 1180 us -> 1010 us (0.86)
  waiting for transfers between devices: 215 us -> 69.1 us
  Pallas kernels: 856 us -> 841 us
    all_gather x3, waiting for transfers between devices: 144 us -> 28.6 us  [gather_weight(): lax.all_gather(half_of(weight, seq_index, seq_count), NS, axis=0, tiled=T...]
    all_gather x1, waiting for transfers between devices: 49.5 us -> 0.02 us  [body(): w_kv = lax.all_gather(after(w_kv, o, w_dn, w_gu), NS, axis=0, tiled=True)]
    pallas_call x1, Pallas kernels: 186 us -> 162 us  [tail_call(): pl.pallas_call(functools.partial(tail_kernel, plan, kv_heads), in_specs=[...]
    pallas_call x1, Pallas kernels: 83.3 us -> 107 us  [weights_call(): pl.pallas_call(functools.partial(weights_kernel, plan, tiles), grid=(3 *...]
    reduce_scatter x5, waiting for transfers between devices: 18.4 us -> 37.9 us  [scatter_grad(): lax.psum_scatter(grad.astype(BF), NS, scatter_dimension=0, tiled=True)]
    pallas_call x1, Pallas kernels: 180 us -> 165 us  [backward_call(): pl.pallas_call(functools.partial(backward_kernel, plan, kv_heads, heads),...]
  transfers between devices with their start and end apart: 12 -> 12, of which waited for: 4 -> 2; matrix products, arithmetic and copies ran while one was open for 6% -> 6% of each run, Pallas kernels for 42% -> 73%
where the time goes in v5:
time: 1010 us
  Pallas kernels  841 us (83%)
  waiting for transfers between devices  69.1 us (7%)
  other arithmetic  37.7 us (4%)
  local copies, waits for them, and re-layouts  26.5 us (3%)
  between operations  14.5 us (1%)
  matrix products  12.1 us (1%)
    pallas_call x1, Pallas kernels, ffn_call(): pl.pallas_call(functools.partial(ffn_kernel, plan), grid=(wide, tiles), i...  172 us
    pallas_call x1, Pallas kernels, backward_call(): pl.pallas_call(functools.partial(backward_kernel, plan, kv_heads, heads),...  165 us
    pallas_call x1, Pallas kernels, tail_call(): pl.pallas_call(functools.partial(tail_kernel, plan, kv_heads), in_specs=[...  162 us
    pallas_call x1, Pallas kernels, head_call(): pl.pallas_call(functools.partial(head_kernel, plan, kv_heads, qw), in_spe...  125 us
    pallas_call x1, Pallas kernels, weights_call(): pl.pallas_call(functools.partial(weights_kernel, plan, tiles), grid=(3 *...  107 us
    pallas_call x1, Pallas kernels, forward_call(): pl.pallas_call(functools.partial(forward_kernel, plan, kv_heads, heads),...  104 us
    reduce_scatter x5, waiting for transfers between devices, scatter_grad(): lax.psum_scatter(grad.astype(BF), NS, scatter_dimension=0, tiled=True)  37.9 us
    all_gather x3, waiting for transfers between devices, gather_weight(): lax.all_gather(half_of(weight, seq_index, seq_count), NS, axis=0, tiled=T...  28.6 us
  transfers between devices with their start and end apart: 12, of which 2 were waited for; matrix products, arithmetic and copies ran while one was open for 6% of the time, Pallas kernels for 73%

profile of v5, /device:TPU:0, one launch (start us, length us, event | category | flops | bytes accessed | tf_op | source)
XLA Modules:
  0.0 1006.3 jit_solution(1372099765535318144)
XLA Ops:
  7.3 1.8 constant_dynamic-slice_fusion.3
  9.2 1.4 convert_reduce_fusion.1
  10.7 0.8 broadcast_compare_fusion
  11.5 0.7 dynamic_slice.22
  12.2 1.0 copy.41
  13.2 1.0 copy.42
  14.4 1.3 pad_maximum_fusion.4.gains_ref
  15.7 2.0 pad_maximum_fusion.2.w_ref
  17.7 1.3 subtract_convert_fusion
  19.0 3.1 multiply_sine_fusion
  22.1 2.4 bitcast_select_fusion.g_ref
  24.5 4.5 select_convert_fusion.kf_ref
  29.0 125.1 %head.1 = (bf16[1024,2048]{1,0:T(8,128)(2,1)}, bf16[1024,512]{1,0:T(8,128)(2,1)}, bf16[256,2048]{1,0:T(8,128)(2,1)}, bf16[2,8192,128]{2,1,0:T(8,128)(2,1)}, bf16...) custom-call(bf16[8,4,128,512]{3,2,1,0:T(8,128)(2,1)} %bitcast.79, ...), custom_call_target="tpu_custom_call" | custom-call | flops 96636764160 | bytes 19922944 | tf_op jit(solution)/shard_map/head/pallas_call | solution.py:446
  154.2 1.0 constant_dynamic-slice_fusion.1
  155.3 2.7 pad_maximum_fusion
  158.0 1.5 constant_dynamic-slice_fusion.2
  159.6 1.9 pad_add_fusion.s_ref
  161.5 0.8 constant_dynamic-slice_fusion
  162.3 3.4 copy.55
  165.7 2.8 reshape.208.wo_ref
  168.5 104.5 %attention_forward.1 = (bf16[4,256,512]{2,1,0:T(8,128)(2,1)}, bf16[4,2,2,512,128]{4,3,2,1,0:T(8,128)(2,1)}, f32[256,2048]{1,0:T(8,128)}) custom-call(s32[2]{0:T(128)} %pad_add_fusion.s_ref, bf16[1024,512]{1,0:T(8,128)(2,1)} %get-tuple-element.46.q_ref, bf16[2,8192,128]{2,1,0:T(8,128)(2,1)} %get-tuple-element.47.kx, ...), custom_call_target="tpu_custom_call" | custom-call | flops 34359738368 | bytes 16777216 | tf_op jit(solution)/shard_map/attention_forward/pallas_call | solution.py:617
  273.0 28.6 %all-gather.10.cloned.1.call-done.wg_ref.wu_ref = bf16[2048,4096]{1,0:T(8,128)(2,1)} async-done(((bf16[256,4096]{1,0:T(8,128)(2,1)}), bf16[2048,4096]{1,0:T(8,128)(2,1)}) %all-gather.10.cloned.1.call-update) | async-done | bytes 16777232 | tf_op jit(solution)/shard_map/all_gather | solution.py:1350
  302.4 171.6 %feed_forward.1 = (bf16[1024,2048]{1,0:T(8,128)(2,1)}, bf16[1024,2048]{1,0:T(8,128)(2,1)}, bf16[1024,2048]{1,0:T(8,128)(2,1)}, bf16[1024,2048]{1,0:T(8,128)(2,1)...) custom-call(f32[256,2048]{1,0:T(8,128)} %get-tuple-element.50.x2_ref, ...), custom_call_target="tpu_custom_call" | custom-call | flops 68719476736 | bytes 50331648 | tf_op jit(solution)/shard_map/feed_forward/pallas_call | solution.py:770
  474.1 4.6 copy.46
  478.7 106.6 %weight_gradients.1 = (bf16[4,2048,512]{2,1,0:T(8,128)(2,1)}, bf16[2048,2048]{1,0:T(8,128)(2,1)}, bf16[2048,2048]{1,0:T(8,128)(2,1)}, bf16[4,256,2048]{2,1,0:T(8,128)(2,1)}, bf16[256,2048]{1,0:T(8,128)(2,1)}) custom-call(f32[256,2048]{1,0:T(8,128)} %get-tuple-element.55.dx2_ref, bf16[1024,2048]{1,0:T(8,128)(2,1)} %get-tuple-element.60.act_ref, ...), custom_call_target="tpu_custom_call" | custom-call | flops 42949672960 | bytes 41943040 | tf_op jit(solution)/shard_map/weight_gradients/pallas_call | solution.py:881
  587.0 165.2 %attention_backward.1 = (bf16[1024,512]{1,0:T(8,128)(2,1)}, f32[2,8192,128]{2,1,0:T(8,128)}, f32[256,2048]{1,0:T(8,128)}, bf16[4,8,128,512]{3,2,1,0:T(8,128)(2,1)}) custom-call(bf16[4,256,2048]{2,1,0:T(8,128)(2,1)} %get-tuple-element.65.db_ref, bf16[4,2,2,512,128]{4,3,2,1,0:T(8,128)(2,1)} %get-tuple-element.66.qe_ref, ...), custom_call_target="tpu_custom_call" | custom-call | flops 77309411328 | bytes 25165824 | tf_op jit(solution)/shard_map/attention_backward/pallas_call | solution.py:1062
  752.2 6.3 convolution_convert_fusion
  758.5 2.4 convolution_convert_fusion.1
  761.0 2.0 convolution_convert_fusion.2
  762.9 0.7 convolution_convert_fusion.3
  763.7 0.7 convolution_convert_fusion.4
  764.4 1.5 pad_maximum_fusion.1
  767.5 37.9 %reduce-scatter.10.cloned.1.call-done = bf16[256,2048]{1,0:T(8,128)(2,1)} async-done(((bf16[2048,2048]{1,0:T(8,128)(2,1)}), bf16[256,2048]{1,0:T(8,128)(2,1)}) %reduce-scatter.10.cloned.1.call-update) | async-done | bytes 1048592 | tf_op jit(solution)/shard_map/reduce_scatter | solution.py:1353
  805.4 161.5 %input_gradient.1 = (bf16[4,8,128,512]{3,2,1,0:T(8,128)(2,1)}, f32[2,512]{1,0:T(2,128)}, f32[256,512]{1,0:T(8,128)}) custom-call(f32[2,8192,128]{2,1,0:T(8,128)} %get-tuple-element.70.sums_ref, bf16[1024,2048]{1,0:T(8,128)(2,1)} %get-tuple-element.71.h_ref, f32[256,2048]{1,0:T(8,128)} %get-tuple-element.72.dh_ref, f32[1,2048]{1,0:T(1,128)} %get-tuple-element.73.gain2_ref, ...), custom_call_target="tpu_custom_call" | custom-call | flops 107374182400 | bytes 8388608 | tf_op jit(solution)/shard_map/input_gradient/pallas_call | solution.py:1255
  967.0 1.1 copy.56
  968.1 0.8 copy.49
  968.9 0.8 copy.48
  969.8 2.2 copy-done.2
  972.0 2.4 assemble.2
  974.4 1.3 copy-done.3
  975.7 3.6 assemble.3
  979.8 2.4 all_gather.31
  982.2 1.1 convert_element_type.51
  983.3 2.4 all_gather.32
  985.7 1.1 convert_element_type.56
  986.8 4.2 convert_element_type.59
  991.0 4.3 convert_element_type.58
  995.3 4.1 convert_element_type.57
  (65 shorter events, 5.3 us)
Async XLA Ops:
  7.2 147.0 %copy-start = (bf16[2048,512]{1,0:T(8,128)(2,1)S(1)}, bf16[2048,512]{1,0:T(8,128)(2,1)}, u32[]{:S(2)}) copy-start(bf16[2048,512]{1,0:T(8,128)(2,1)} %param.22) | copy-start | bytes 6291460
  7.2 17.3 %copy-start.5 = (s32[8192]{0:T(1024)S(1)}, s32[8192]{0:T(1024)}, u32[]{:S(2)}) copy-start(s32[8192]{0:T(1024)} %param.23) | copy-start | bytes 98308
  7.2 155.1 %all-gather.8.cloned.1.call-start = ((), (), s32[]{:S(2)}) async-start(), calls=%async_computation.5 | async-start | bytes 2359296 | tf_op jit(solution)/shard_map/all_gather | solution.py:1350
  9.1 263.9 %all-gather.12.cloned.1.call-start = ((), (), s32[]{:S(2)}) async-start(), calls=%async_computation.7 | async-start | bytes 9437184 | tf_op jit(solution)/shard_map/all_gather | solution.py:1350
  155.2 146.3 %all-gather.10.cloned.1.call-start = ((), (), s32[]{:S(2)}) async-start(), calls=%async_computation.6 | async-start | bytes 18874368 | tf_op jit(solution)/shard_map/all_gather | solution.py:1350
  158.0 3.5 copy-start.4
  159.6 314.5 %all-gather.14.cloned.1.call-start = ((), (), s32[]{:S(2)}) async-start(), calls=%async_computation.8 | async-start | bytes 4718592 | tf_op jit(solution)/shard_map/all_gather | solution.py:1398
  168.5 133.3 %copy-start.6 = (f32[4,2,512]{2,1,0:T(2,128)S(1)}, f32[4,2,512]{2,1,0:T(2,128)}, u32[]{:S(2)}) copy-start(f32[4,2,512]{2,1,0:T(2,128)} %get-tuple-element.51) | copy-start | bytes 49156
  301.6 464.4 %reduce-scatter.14.cloned.1.call-start = ((), (), s32[]{:S(2)}) async-start(), calls=%async_computation.15 | async-start | bytes 9437184 | tf_op jit(solution)/shard_map/reduce_scatter | solution.py:1353
  585.4 181.2 %reduce-scatter.12.cloned.1.call-start = ((), (), s32[]{:S(2)}) async-start(), calls=%async_computation.13 | async-start | bytes 9437184 | tf_op jit(solution)/shard_map/reduce_scatter | solution.py:1353
  585.9 219.5 %reduce-scatter.10.cloned.1.call-start = ((), (), s32[]{:S(2)}) async-start(), calls=%async_computation.11 | async-start | bytes 9437184 | tf_op jit(solution)/shard_map/reduce_scatter | solution.py:1353
  586.7 393.2 %reduce-scatter.6.cloned.1.call-start = ((), (), s32[]{:S(2)}) async-start(), calls=%async_computation.9 | async-start | bytes 2359296 | tf_op jit(solution)/shard_map/reduce_scatter | solution.py:1353
  752.1 6.4 copy-start.9
  758.5 224.9 %reduce-scatter.8.cloned.1.call-start = ((), (), s32[]{:S(2)}) async-start(), calls=%async_computation.10 | async-start | bytes 2359296 | tf_op jit(solution)/shard_map/reduce_scatter | solution.py:1353
  758.5 4.4 copy-start.8
  765.9 220.9 %all-gather.20.cloned.1.call-start = ((), (), s32[]{:S(2)}) async-start(), calls=%async_computation.16 | async-start | bytes 3145728 | tf_op jit(solution)/shard_map/all_gather | solution.py:1354
  766.5 224.6 %all-gather.18.cloned.1.call-start = ((), (), s32[]{:S(2)}) async-start(), calls=%async_computation.14 | async-start | bytes 3145728 | tf_op jit(solution)/shard_map/all_gather | solution.py:1354
  767.2 228.1 %all-gather.16.cloned.1.call-start = ((), (), s32[]{:S(2)}) async-start(), calls=%async_computation.12 | async-start | bytes 3145728 | tf_op jit(solution)/shard_map/all_gather | solution.py:1354
  969.8 2.2 copy-start.2
  972.0 3.7 copy-start.3
  975.7 3.6 copy-start.7
  991.0 8.4 copy-start.1
Sparse Core Ops, SparseCore 0:
  10.5 31.8 all-gather.7
  155.3 53.8 all-gather.11
  211.7 89.8 all-gather.9
  303.9 36.7 all-gather.13
  585.5 70.0 reduce-scatter.13
  659.3 71.2 reduce-scatter.11
  734.1 71.2 reduce-scatter.9
  809.6 57.7 reduce-scatter.5
  871.2 40.2 reduce-scatter.7
  913.0 10.5 all-gather.19
  925.2 11.7 all-gather.17
  938.5 11.7 all-gather.15

commit v6 on v5

--- a/solution.py
+++ b/solution.py
@@ -228,10 +228,62 @@
         return out
 
 
+class WeightSum:
+    def __init__(self, team, part, came, mine, near, last, out, send, recv):
+        self.team, self.part, self.came, self.mine, self.near = team, part, came, mine, near
+        self.last, self.out, self.send, self.recv = last, out, send, recv
+        self.size = part.shape[1] // 2
+
+    def half(self, core):
+        return pl.ds(pl.multiple_of(core * self.size, self.size), self.size)
+
+    def swap(self):
+        other = self.part.at[:, self.half(1 - self.team.seq)]
+        return push(other, self.came, self.send.at[0], self.recv.at[0], self.team.sibling)
+
+    def give(self, k):
+        other = self.team.beside(k)
+        return push(self.mine.at[other], self.near.at[k], self.send.at[k], self.recv.at[k], {"narrow": other})
+
+    def back(self):
+        at = self.team.narrow
+        return push(self.last.at[0], self.last.at[1], self.send.at[at], self.recv.at[at], self.team.sibling)
+
+    def first(self):
+        self.swap().start()
+
+    def second(self):
+        self.swap().wait_recv()
+        for n in range(self.team.narrow):
+            own = self.part[n, self.half(self.team.seq), :].astype(F32)
+            self.mine[n] = (own + self.came[n].astype(F32)).astype(BF)
+        for k in range(1, self.team.narrow):
+            self.give(k).start()
+
+    def third(self):
+        total = self.mine[self.team.me].astype(F32)
+        for k in range(1, self.team.narrow):
+            self.give(k).wait_recv()
+            total = total + self.near[k].astype(F32)
+        self.last[0] = total.astype(BF)
+        self.back().start()
+        self.out[self.half(self.team.seq), :] = self.last[0].astype(F32)
+
+    def fourth(self):
+        self.back().wait_recv()
+        self.out[self.half(1 - self.team.seq), :] = self.last[1].astype(F32)
+
+    def sent(self):
+        self.swap().wait_send()
+        self.back().wait_send()
+        for k in range(1, self.team.narrow):
+            self.give(k).wait_send()
+
+
 def head_kernel(
-    plan, kv_heads, qw, x_ref, g_ref, w_ref, gains_ref, cos_ref, sin_ref, kf_ref,
+    plan, kv_heads, qw, x_ref, g_ref, w_ref, gains_ref, cos_ref, sin_ref, marks_ref,
     h_out, q_out, own_out, kx, vx, w_out, gains_out, g_out, side_out,
-    x_buf, side_buf, side_send, side_recv, w_buf, kv_buf, g_buf, gain_buf,
+    x_buf, marks, side_buf, side_send, side_recv, w_buf, kv_buf, g_buf, gain_buf,
     x_send, x_recv, x_stay, w_send, w_recv, w_on_send, w_on_recv, gain_send, gain_recv,
     g_send, g_recv, kv_send, kv_recv, kv_on_send, kv_on_recv, keep_sem, *chain_sems
 ):
@@ -389,17 +441,23 @@
 
     feature = lax.broadcasted_iota(jnp.int32, (cw, 128), 1)
     ones = jnp.where(feature < 3, 1.0, 0.0).astype(BF)
+    spread = lax.broadcasted_iota(jnp.int32, (marks_ref.shape[0], 128), 0) + HD
+    target = lax.broadcasted_iota(jnp.int32, (marks_ref.shape[0], 128), 1)
+    spread = jnp.where(spread == target, 1.0, 0.0).astype(BF)
 
     @pl.loop(0, 2 * group)
     def _(c):
+        columns = pl.ds(pl.multiple_of(c * chunk, chunk), chunk)
+        marks[...] = lax.dot_general(marks_ref[:, columns], spread, TN, preferred_element_type=F32).astype(BF)
         late = c >= group
         owner = jnp.where(late, 2 * group - 1 - c, c)
         for r in range(wide):
+            block = pl.ds(pl.multiple_of(lax.rem(z + r, wide) * cw, cw), cw)
             at = pl.ds(pl.multiple_of(c * chunk + lax.rem(z + r, wide) * cw, cw), cw)
             source = pl.ds(pl.multiple_of(r * own + jnp.where(late, cw, 0), cw), cw)
             for g in range(kv_heads):
                 kv = kv_buf[owner // narrow, lax.rem(owner, narrow), source, g * 128 : (g + 1) * 128]
-                kx[g, at, :] = jnp.where(feature < HD, kv, kf_ref[at, :])
+                kx[g, at, :] = jnp.where(feature < HD, kv, marks[block, :])
                 vx[g, at, :] = jnp.where(feature < HD, ones, kv)
 
     for h in range(3, wide):
@@ -433,7 +491,7 @@
         copy.wait()
 
 
-def head_call(plan, x, g, w, gains, cos, sin, kf, qw, kv_heads):
+def head_call(plan, x, g, w, gains, cos, sin, marks, qw, kv_heads):
     group, wide, cw, part = x.shape
     narrow = group // 2
     d = part * narrow
@@ -460,6 +518,7 @@
         ],
         scratch_shapes=[
             pltpu.VMEM((wide, own, d), BF),
+            pltpu.VMEM((plan.chunk, 128), BF),
             pltpu.VMEM((wide, part, width - qw), BF),
             dma((wide,)), dma((wide,)),
             pltpu.VMEM((d, width), BF),
@@ -479,7 +538,7 @@
             vmem_limit_bytes=60 << 20, collective_id=4, has_side_effects=True
         ),
         name="head",
-    )(x, g, w, gains, cos, sin, kf)
+    )(x, g, w, gains, cos, sin, marks)
 
 
 def split_heads(block, heads, low):
@@ -507,13 +566,14 @@
 
 
 def forward_kernel(
-    plan, kv_heads, heads, s_ref, q_ref, kx, vx, wo_ref, x_ref, o_ref, qe_ref, x2_ref,
-    terms, right, left, term_acc, *sems
+    plan, kv_heads, heads, s_ref, q_ref, kx, vx, wo_ref, x_ref, wd_ref, o_ref, qe_ref, x2_ref, wd_out,
+    terms, right, left, term_acc, wd_send, wd_recv, wd_on_send, wd_on_recv, wd_keep, *sems
 ):
     wide, cw, chunk, own = plan.wide, plan.cw, plan.chunk, plan.own
     rows, width = heads * cw, heads * HD
     z = lax.axis_index("wide")
-    index = lax.axis_index("seq") * lax.axis_size("narrow") + lax.axis_index("narrow")
+    team = Group(plan)
+    index = team.index
     unit, g = pl.program_id(0), pl.program_id(1)
     last_g = kv_heads - 1
     piece, half = wide - 1 - unit // 2, lax.rem(unit, 2)
@@ -525,9 +585,41 @@
 
     attn = Sums(plan, terms, right, left, sems)
 
+    def out_rows(n):
+        return pl.ds(pl.multiple_of((n * kv_heads + g) * width, width), width)
+
+    fold = wd_ref.shape[0] // 2
+
+    def wd_rows(n, core):
+        return wd_out.at[n, pl.ds(pl.multiple_of(core * fold, fold), fold)]
+
+    def wd_to(k):
+        mine = wd_ref.at[pl.ds(pl.multiple_of(team.seq * fold, fold), fold)]
+        return push(mine, wd_rows(team.me, team.seq), wd_send.at[k], wd_recv.at[k], {"narrow": team.beside(k)})
+
+    def wd_from(k):
+        theirs = wd_rows(team.beside(-k), team.seq)
+        return push(theirs, theirs, wd_send.at[k], wd_recv.at[k], {"narrow": team.beside(k)})
+
+    def wd_on(k, core):
+        rows_of = wd_rows(team.beside(-k), core)
+        return push(rows_of, rows_of, wd_on_send.at[k], wd_on_recv.at[k], team.sibling)
+
+    wd_own = pltpu.make_async_copy(wd_ref, wd_out.at[team.me], wd_keep)
+
     @pl.when((unit == 0) & (g == 0))
     def _():
-        greet([along_wide(plan, k) for k in range(1, wide)])
+        others = [team.member(k) for k in range(1, plan.group)]
+        greet(others + [along_wide(plan, k) for k in range(1, wide)])
+        for k in range(1, team.narrow):
+            wd_to(k).start()
+        wd_own.start()
+
+    for k in range(1, team.narrow):
+        @pl.when((unit == 2 * wide - (3 if k == 1 else 2)) & (g == 0))
+        def _():
+            wd_from(k).wait_recv()
+            wd_on(k, team.seq).start()
 
     lane = lax.broadcasted_iota(jnp.int32, (cw, 128), 1)
     token = c * chunk + w * cw + lax.broadcasted_iota(jnp.int32, (cw, 128), 0)
@@ -565,7 +657,9 @@
     qe = jnp.where(wide_lane == HD + 5, third, qe)
     qe_ref[r, g, half] = qe.astype(BF)
 
-    term = jnp.dot(out, wo_ref[g], preferred_element_type=F32)
+    term = jnp.concatenate(
+        [jnp.dot(out, wo_ref[out_rows(n), :], preferred_element_type=F32) for n in range(plan.group // 2)], axis=1
+    )
 
     @pl.when(g == 0)
     def _():
@@ -598,8 +692,14 @@
             at = pl.ds(pl.multiple_of(b * tall, tall), tall)
             x2_ref[at, :] = attn.total(x2_ref[at, :], at)
 
-
-def forward_call(plan, starts, q, kx, vx, w_o, x, heads):
+        wd_own.wait()
+        for k in range(1, team.narrow):
+            wd_on(k, 1 - team.seq).wait_recv()
+            wd_to(k).wait_send()
+            wd_on(k, team.seq).wait_send()
+
+
+def forward_call(plan, starts, q, kx, vx, w_o, x, w_down, heads):
     kv_heads, total, _ = kx.shape
     own, d = x.shape
     wide, rows, cw = plan.wide, plan.rows, plan.cw
@@ -617,10 +717,12 @@
     return pl.pallas_call(
         functools.partial(forward_kernel, plan, kv_heads, heads),
         grid=(2 * wide, kv_heads),
-        in_specs=[pl.BlockSpec(memory_space=pltpu.SMEM)] + [fixed(a) for a in given],
-        out_specs=[fixed(a) for a in outs],
-        out_shape=outs,
-        scratch_shapes=[buffer] * 3 + [pltpu.VMEM((cw, d), F32)] + [sems] * 4,
+        in_specs=[pl.BlockSpec(memory_space=pltpu.SMEM)] + [fixed(a) for a in given]
+        + [pl.BlockSpec(memory_space=pl.ANY)],
+        out_specs=[fixed(a) for a in outs] + [pl.BlockSpec(memory_space=pl.ANY)],
+        out_shape=outs + [jax.ShapeDtypeStruct((plan.group // 2, *w_down.shape), BF)],
+        scratch_shapes=[buffer] * 3 + [pltpu.VMEM((cw, d), F32)]
+        + [pltpu.SemaphoreType.DMA((plan.group // 2,))] * 4 + [pltpu.SemaphoreType.DMA] + [sems] * 4,
         cost_estimate=pl.CostEstimate(
             flops=16 * pairs * HD, bytes_accessed=8 * kv_heads * total * 128, transcendentals=pairs
         ),
@@ -628,13 +730,13 @@
             vmem_limit_bytes=56 << 20, collective_id=5, has_side_effects=True
         ),
         name="attention_forward",
-    )(starts, *given)
+    )(starts, *given, w_down)
 
 
 def ffn_kernel(
     plan, x2_ref, gain_ref, g_ref, wg_ref, wu_ref, wd_ref,
-    act_ref, dg_ref, du_ref, h_out, dn_ref, dx_ref, gain_out,
-    h_buf, in_buf, out_buf, dn_acc, dh_acc, own_dh, own_g, rs_send, rs_recv, *chain_sems
+    dg_ref, du_ref, h_out, dn_ref, dx_ref, gain_out, grad_out,
+    h_buf, in_buf, out_buf, dn_acc, dh_acc, own_dh, act_buf, g_buf, grad_buf, rs_send, rs_recv, grad_sem, *chain_sems
 ):
     wide, narrow = plan.wide, plan.group // 2
     own, d = x2_ref.shape
@@ -663,7 +765,6 @@
             h_buf[z, at, :] = (x2 * scale * gain_ref[...]).astype(BF)
 
         chain.go(1)
-        own_g[...] = g_ref[...]
 
     for h in range(1, wide):
         @pl.when((piece == h) & (step == 0))
@@ -675,6 +776,7 @@
     @pl.when(step == 0)
     def _():
         h_out[...] = h_buf[owner]
+        g_buf[pl.ds(pl.multiple_of(piece * own, own), own), :] = g_ref[...]
 
     h = h_buf[owner]
     wg, wu = wg_ref[...], wu_ref[...]
@@ -690,7 +792,8 @@
     act = (silu * up).astype(BF)
     dg = (d_act * up * sig * (1.0 + gate * (1.0 - sig))).astype(BF)
     du = (d_act * silu).astype(BF)
-    act_ref[...] = act
+    tile = act.shape[1]
+    act_buf[pl.ds(pl.multiple_of(piece * own, own), own), pl.ds(pl.multiple_of(step * tile, tile), tile)] = act
     dg_ref[...] = dg
     du_ref[...] = du
     dh = lax.dot_general(dg, wg, NT, preferred_element_type=F32) + lax.dot_general(
@@ -732,6 +835,21 @@
 
     @pl.when((step == last) & (piece == wide - 1))
     def _():
+        @pl.loop(0, last + 1)
+        def _(t):
+            at = pl.ds(pl.multiple_of(t * tile, tile), tile)
+            keep = pltpu.make_async_copy(grad_buf, grad_out.at[:, at, :], grad_sem)
+
+            @pl.when(t > 0)
+            def _():
+                keep.wait()
+
+            for n in range(narrow):
+                grad_buf[n] = lax.dot_general(
+                    act_buf[:, at], g_buf[:, n * part : (n + 1) * part], TN, preferred_element_type=F32
+                ).astype(BF)
+            keep.start()
+
         for p in range(1, wide):
             other = near_of(plan, z, p)
             push(out_buf.at[z], in_buf.at[other], rs_send.at[z], rs_recv.at[other], {"wide": other}).wait_recv()
@@ -749,11 +867,12 @@
             gain_out[...] += jnp.sum(dh2 * z2, axis=0, keepdims=True)
             dz2 = dh2 * gain_ref[...]
             inner = jnp.mean(dz2 * z2, axis=1, keepdims=True)
-            dx_ref[at, :] = own_g[at, :].astype(F32) + scale * (dz2 - z2 * inner)
+            dx_ref[at, :] = g_buf[at, :].astype(F32) + scale * (dz2 - z2 * inner)
 
         chain.finish()
         for p in range(1, wide):
             give(near_of(plan, z, p)).wait_send()
+        pltpu.make_async_copy(grad_buf, grad_out.at[:, pl.ds(0, tile), :], grad_sem).wait()
 
 
 def ffn_call(plan, x2, gain, g_rows, w_gu, w_dn):
@@ -779,38 +898,40 @@
             pl.BlockSpec((narrow, tile, part), lambda p, f: (0, f, 0)),
         ],
         out_specs=[
-            tall, tall, tall,
+            tall, tall,
             pl.BlockSpec((own, d), lambda p, f: (p, 0)),
             pl.BlockSpec((1, own, d), lambda p, f: (p, 0, 0)),
             fixed((own, d)),
             fixed((1, d)),
+            pl.BlockSpec(memory_space=pl.ANY),
         ],
         out_shape=[
-            hidden, hidden, hidden,
+            hidden, hidden,
             jax.ShapeDtypeStruct((rows, d), BF),
             jax.ShapeDtypeStruct((wide, own, d), BF),
             jax.ShapeDtypeStruct((own, d), F32),
             jax.ShapeDtypeStruct((1, d), F32),
+            jax.ShapeDtypeStruct((narrow, ff, part), BF),
         ],
         scratch_shapes=[
             buffer, buffer, buffer,
             pltpu.VMEM((own, d), F32), pltpu.VMEM((own, d), F32), pltpu.VMEM((own, d), F32),
-            pltpu.VMEM((own, d), BF),
-            sems, sems, sems, sems, sems, sems,
+            pltpu.VMEM((rows, ff), BF), pltpu.VMEM((rows, d), BF), pltpu.VMEM((narrow, tile, part), BF),
+            sems, sems, pltpu.SemaphoreType.DMA, sems, sems, sems, sems,
         ],
         cost_estimate=pl.CostEstimate(
             flops=16 * rows * d * ff, bytes_accessed=6 * d * ff + 12 * rows * d, transcendentals=rows * ff
         ),
         compiler_params=pltpu.CompilerParams(
-            vmem_limit_bytes=58 << 20, collective_id=1, has_side_effects=True
+            vmem_limit_bytes=60 << 20, collective_id=1, has_side_effects=True
         ),
         name="feed_forward",
     )(x2, gain, g_rows, w_gu, w_gu, w_dn)
 
 
 def weights_kernel(
-    plan, tiles, dx2_ref, act_ref, h_ref, g_ref, dg_ref, du_ref, down_ref, x2_ref,
-    dn_out, gate_out, up_out, db_out, res_out,
+    plan, tiles, dx2_ref, h_ref, dg_ref, du_ref, down_ref, x2_ref,
+    gate_out, up_out, db_out, res_out,
     db_buf, right, left, keep_sem, *sems
 ):
     wide = plan.wide
@@ -828,22 +949,14 @@
 
     @pl.when(step < tiles)
     def _():
-        narrow, _, part = dn_out.shape
-        for n in range(narrow):
-            dn_out[n] = lax.dot_general(
-                act_ref[...], g_ref[:, n * part : (n + 1) * part], TN, preferred_element_type=F32
-            ).astype(BF)
-
-    @pl.when((step >= tiles) & (step < 2 * tiles))
-    def _():
         gate_out[...] = lax.dot_general(h_ref[...], dg_ref[...], TN, preferred_element_type=F32).astype(BF)
 
-    @pl.when(step >= 2 * tiles)
+    @pl.when(step >= tiles)
     def _():
         up_out[...] = lax.dot_general(h_ref[...], du_ref[...], TN, preferred_element_type=F32).astype(BF)
 
     for h in range(1, wide):
-        @pl.when(step == min(last, (2 * h - 1) * tiles + tiles // 2))
+        @pl.when(step == min(last, h * (tiles + 1) - 1))
         def _():
             chain.arrive(h)
             if h + 1 < wide:
@@ -865,37 +978,31 @@
         keep.wait()
 
 
-def weights_call(plan, dx2, act, h, g, d_gate, d_up, down, x2):
+def weights_call(plan, dx2, h, d_gate, d_up, down, x2):
     own, d = dx2.shape
-    rows, ff = act.shape
-    wide, narrow = plan.wide, plan.group // 2
-    part = d // narrow
+    rows, ff = d_gate.shape
+    wide = plan.wide
     tiles = 4
-    ff_tile, d_tile = ff // tiles, d // tiles
+    d_tile = d // tiles
     fixed = lambda a: pl.BlockSpec(a.shape, lambda s: (0,) * a.ndim, pipeline_mode=pl.Buffered(1))
     first = lambda s: jnp.minimum(s, tiles - 1)
     second = lambda s: jnp.clip(s - tiles, 0, tiles - 1)
-    third = lambda s: jnp.clip(s - 2 * tiles, 0, tiles - 1)
-    both = lambda s: jnp.where(s < 2 * tiles, second(s), third(s))
     sems = pltpu.SemaphoreType.DMA((wide,))
     return pl.pallas_call(
         functools.partial(weights_kernel, plan, tiles),
-        grid=(3 * tiles,),
+        grid=(2 * tiles,),
         in_specs=[
             fixed(dx2),
-            pl.BlockSpec((rows, ff_tile), lambda s: (0, first(s))),
-            pl.BlockSpec((rows, d_tile), lambda s: (0, both(s))),
-            fixed(g), fixed(d_gate), fixed(d_up), fixed(down), fixed(x2),
+            pl.BlockSpec((rows, d_tile), lambda s: (0, lax.rem(s, tiles))),
+            fixed(d_gate), fixed(d_up), fixed(down), fixed(x2),
         ],
         out_specs=[
-            pl.BlockSpec((narrow, ff_tile, part), lambda s: (0, first(s), 0)),
+            pl.BlockSpec((d_tile, ff), lambda s: (first(s), 0)),
             pl.BlockSpec((d_tile, ff), lambda s: (second(s), 0)),
-            pl.BlockSpec((d_tile, ff), lambda s: (third(s), 0)),
             pl.BlockSpec(memory_space=pl.ANY),
             pl.BlockSpec((own, d), lambda s: (0, 0), pipeline_mode=pl.Buffered(1)),
         ],
         out_shape=[
-            jax.ShapeDtypeStruct((narrow, ff, part), BF),
             jax.ShapeDtypeStruct((d, ff), BF),
             jax.ShapeDtypeStruct((d, ff), BF),
             jax.ShapeDtypeStruct((wide, own, d), BF),
@@ -903,13 +1010,13 @@
         ],
         scratch_shapes=[pltpu.VMEM((wide, own, d), BF)] * 3 + [pltpu.SemaphoreType.DMA] + [sems] * 8,
         cost_estimate=pl.CostEstimate(
-            flops=10 * rows * d * ff, bytes_accessed=20 * rows * d, transcendentals=0
+            flops=8 * rows * d * ff, bytes_accessed=20 * rows * d, transcendentals=0
         ),
         compiler_params=pltpu.CompilerParams(
             vmem_limit_bytes=60 << 20, collective_id=6, has_side_effects=True
         ),
         name="weight_gradients",
-    )(dx2, act, h, g, d_gate, d_up, down, x2)
+    )(dx2, h, d_gate, d_up, down, x2)
 
 
 def backward_kernel(
@@ -961,7 +1068,13 @@
 
     lane = lax.broadcasted_iota(jnp.int32, (cw, 128), 1)
     columns = pl.ds(pl.multiple_of(g * width, width), width)
-    grad = lax.dot_general(db_ref[w, low_rows, :], wo_ref[g], NT, preferred_element_type=F32)
+    part = wo_ref.shape[1]
+    grad = jnp.zeros((cw, width), F32)
+    for n in range(team.narrow):
+        out_rows = pl.ds(pl.multiple_of((n * kv_heads + g) * width, width), width)
+        grad += lax.dot_general(
+            db_ref[w, low_rows, n * part : (n + 1) * part], wo_ref[out_rows, :], NT, preferred_element_type=F32
+        )
     do = split_heads(grad.astype(BF).astype(F32), heads, False)
     o = split_heads(o_ref[w, low_rows, columns].astype(F32), heads, False)
     marked = []
@@ -1079,12 +1192,12 @@
 
 
 def tail_kernel(
-    plan, kv_heads, sums_ref, h_ref, dh_ref, gain2_ref, dx2_ref, x_ref, gain_ref, wkv_ref,
-    cos_ref, sin_ref, got_out, gain_out, kv_out,
-    swap_out, swap_in, low, near_in, dkv, head_in, dh_acc, dx_low, every,
-    gain_part, gain_in, gain_sum, gain_all, kv_part, kv_in,
+    plan, kv_heads, sums_ref, h_hbm, dh_ref, gain2_ref, dx2_ref, x_ref, gain_ref, wkv_hbm,
+    cos_ref, sin_ref, dq_ref, o_ref, db_hbm, got_out, gain_out, kv_out, q_out, o_out,
+    h_ref, wkv_ref, db_buf, swap_out, swap_in, low, near_in, dkv, head_in, dh_acc, dx_low, every,
+    gain_part, gain_in, gain_sum, gain_all,
     swap_sem, near_send, near_recv, head_send, head_recv, part_send, part_recv,
-    gain_send, gain_recv, gain2_send, gain2_recv, kv_send, kv_recv, own_sem, *chain_sems
+    gain_send, gain_recv, gain2_send, gain2_recv, own_sem, *more
 ):
     group, wide, chunk, cw, own = plan.group, plan.wide, plan.chunk, plan.cw, plan.own
     narrow = group // 2
@@ -1092,7 +1205,11 @@
     team = Group(plan)
     seq, me, z = team.seq, team.me, lax.axis_index("wide")
     device, member = team.device, team.member
-    dx_chain = Chain(plan, every, chain_sems)
+    dx_chain = Chain(plan, every, more[:4])
+    q_sum = WeightSum(team, *more[4:9], q_out, *more[9:11])
+    kv_sum = WeightSum(team, *more[11:16], kv_out, *more[16:18])
+    o_sum = WeightSum(team, *more[18:23], o_out, *more[23:25])
+    q_part, kv_part, o_part = q_sum.part, kv_sum.part, o_sum.part
 
     greet([member(k) for k in range(1, group)] + [along_wide(plan, r) for r in range(1, wide)])
 
@@ -1102,71 +1219,84 @@
             pl.multiple_of((quarter * narrow + (n if half == 0 else narrow - 1 - n)) * chunk, chunk), chunk
         )
 
-    @pl.loop(0, narrow)
-    def _(n):
-        for g in range(kv_heads):
+    load_h = pltpu.make_async_copy(h_hbm, h_ref, own_sem.at[2])
+    load_w = pltpu.make_async_copy(wkv_hbm, wkv_ref, own_sem.at[3])
+    load_h.start()
+    load_w.start()
+
+    def swap(g):
+        return push(swap_out.at[g], swap_in.at[g], swap_sem.at[0, g], swap_sem.at[1, g], team.sibling)
+
+    def near(k, g):
+        other = team.beside(k)
+        return push(low.at[g, other], near_in.at[g, k], near_send.at[g, k], near_recv.at[g, k], {"narrow": other})
+
+    def heads_to(r, g):
+        columns = slice(g * 128, (g + 1) * 128)
+        mine = dkv.at[r * own : (r + 1) * own, columns]
+        return push(mine, head_in.at[r, :, columns], head_send.at[r, g], head_recv.at[r, g], along_wide(plan, r))
+
+    for g in range(kv_heads):
+        @pl.loop(0, narrow)
+        def _(n):
             for half in range(2):
-                swap_out[n, g, half] = sums_ref[g, place(1 - seq, half, n), :].astype(BF)
-
-    swap = push(swap_out, swap_in, swap_sem.at[0], swap_sem.at[1], {"seq": 1 - seq})
-    swap.start()
-    swap.wait_recv()
-
-    @pl.loop(0, narrow)
-    def _(n):
-        for g in range(kv_heads):
+                swap_out[g, n, half] = sums_ref[g, place(1 - seq, half, n), :].astype(BF)
+
+        swap(g).start()
+
+    load_h.wait()
+    for n in range(narrow):
+        columns = slice(n * part, (n + 1) * part)
+        q_part[n] = lax.dot_general(h_ref[:, columns], dq_ref[...], TN, preferred_element_type=F32).astype(BF)
+    q_sum.first()
+
+    for g in range(kv_heads):
+        swap(g).wait_recv()
+
+        @pl.loop(0, narrow)
+        def _(n):
             for half in range(2):
-                total = sums_ref[g, place(seq, half, n), :] + swap_in[n, g, half].astype(F32)
-                low[n, g, half] = total.astype(BF)
-
-    def near(k):
-        other = lax.rem(me + k, narrow)
-        return push(low.at[other], near_in.at[k], near_send.at[k], near_recv.at[k], {"narrow": other})
-
-    for k in range(1, narrow):
-        near(k).start()
-    for k in range(1, narrow):
-        near(k).wait_recv()
+                total = sums_ref[g, place(seq, half, n), :] + swap_in[g, n, half].astype(F32)
+                low[g, n, half] = total.astype(BF)
+
+        for k in range(1, narrow):
+            near(k, g).start()
 
     lane = lax.broadcasted_iota(jnp.int32, (cw, 128), 1)
-    for r in range(wide):
-        at = pl.ds(pl.multiple_of(lax.rem(z + r, wide) * cw, cw), cw)
-        for half in range(2):
-            rows = slice((2 * r + half) * cw, (2 * r + half + 1) * cw)
-            for g in range(kv_heads):
-                total = low[me, g, half, at, :].astype(F32)
+    for g in range(kv_heads):
+        for k in range(1, narrow):
+            near(k, g).wait_recv()
+        for r in range(wide):
+            at = pl.ds(pl.multiple_of(lax.rem(z + r, wide) * cw, cw), cw)
+            for half in range(2):
+                rows = slice((2 * r + half) * cw, (2 * r + half + 1) * cw)
+                total = low[g, me, half, at, :].astype(F32)
                 for k in range(1, narrow):
-                    total = total + near_in[k, g, half, at, :].astype(F32)
+                    total = total + near_in[g, k, half, at, :].astype(F32)
                 back = total * cos_ref[rows, :] + turn(total, -1.0) * sin_ref[rows, :]
                 dkv[rows, g * 128 : (g + 1) * 128] = jnp.where(lane < HD, back, total).astype(BF)
-
-    def heads_to(r):
-        mine = dkv.at[pl.ds(r * own, own)]
-        return push(mine, head_in.at[r], head_send.at[r], head_recv.at[r], along_wide(plan, r))
-
-    for r in range(1, wide):
-        heads_to(r).start()
+        for r in range(1, wide):
+            heads_to(r, g).start()
+
+    q_sum.second()
 
     for n in range(narrow):
         columns = slice(n * part, (n + 1) * part)
         kv_part[n] = lax.dot_general(dkv[...], h_ref[:, columns], TN, preferred_element_type=F32).astype(BF)
-
-    def kv_to(k):
-        return push(kv_part.at[lax.rem(device(k), narrow)], kv_in.at[k], kv_send.at[k], kv_recv.at[k], member(k))
-
-    for k in range(1, group):
-        kv_to(k).start()
-
-    tile = min(512, part)
+    kv_sum.first()
+
+    tile = part // 2
+    load_w.wait()
     for r in range(wide):
         if r > 0:
-            heads_to(r).wait_recv()
+            for g in range(kv_heads):
+                heads_to(r, g).wait_recv()
         mine = dkv[0:own] if r == 0 else head_in[r]
-
-        @pl.loop(0, dh_acc.shape[1] // tile)
-        def _(b):
-            at = pl.ds(pl.multiple_of(b * tile, tile), tile)
-            more = lax.dot_general(mine, wkv_ref[lax.rem(z - r + wide, wide), at, :], NT, preferred_element_type=F32)
+        source = lax.rem(z - r + wide, wide)
+
+        for b in range(group):
+            at = slice(b * tile, (b + 1) * tile)
+            more = lax.dot_general(mine, wkv_ref[b, source], NT, preferred_element_type=F32)
             dh_acc[:, at] = (dh_ref[:, at] if r == 0 else dh_acc[:, at]) + more
 
     gain_part[0:1, :] = jnp.zeros_like(gain2_ref[...])
@@ -1196,6 +1326,18 @@
         gain_to(k).start()
     dx_parts.wait()
     dx_chain.go(1)
+    kv_sum.second()
+
+    rows = o_ref.shape[0] * o_ref.shape[1]
+    for n in range(narrow):
+        load = pltpu.make_async_copy(db_hbm.at[:, :, n * part : (n + 1) * part], db_buf, own_sem.at[4])
+        load.start()
+        load.wait()
+        o_part[n] = lax.dot_general(
+            o_ref[...].reshape(rows, -1), db_buf[...].reshape(rows, part), TN, preferred_element_type=F32
+        ).astype(BF)
+    o_sum.first()
+    q_sum.third()
 
     gain = gain_part[:, pl.ds(pl.multiple_of(me * part, part), part)]
     for k in range(1, group):
@@ -1208,38 +1350,46 @@
 
     for r in range(1, wide):
         gain_on(r).start()
-    for k in range(1, group):
-        kv_to(k).wait_recv()
-    kv_out[...] = kv_part[me].astype(F32)
-    for k in range(1, group):
-        kv_out[...] += kv_in[k].astype(F32)
+    dx_chain.arrive(1)
+    if wide > 2:
+        dx_chain.go(2)
+    o_sum.second()
+    kv_sum.third()
+    q_sum.fourth()
     gain = gain_sum[...]
     for r in range(1, wide):
         gain_on(r).wait_recv()
         gain = gain + gain_all[r]
     gain_out[...] = gain
-    for h in range(1, wide):
+    for h in range(2, wide):
         dx_chain.arrive(h)
         if h + 1 < wide:
             dx_chain.go(h + 1)
+        if h == 2:
+            o_sum.third()
+            kv_sum.fourth()
+    o_sum.fourth()
     got_keep = pltpu.make_async_copy(every, got_out, own_sem.at[1])
     got_keep.start()
 
     dx_chain.finish()
-    swap.wait_send()
-    for k in range(1, narrow):
-        near(k).wait_send()
+    for g in range(kv_heads):
+        swap(g).wait_send()
+        for k in range(1, narrow):
+            near(k, g).wait_send()
+        for r in range(1, wide):
+            heads_to(r, g).wait_send()
     for r in range(1, wide):
-        heads_to(r).wait_send()
         gain_on(r).wait_send()
     dx_parts.sent()
     for k in range(1, group):
         gain_to(k).wait_send()
-        kv_to(k).wait_send()
+    for one in (q_sum, kv_sum, o_sum):
+        one.sent()
     got_keep.wait()
 
 
-def tail_call(plan, sums, h, dh, gain2, dx2, x, gain, w_kv, cos, sin):
+def tail_call(plan, sums, h, dh, gain2, dx2, x, gain, w_kv, cos, sin, dq, o, db):
     kv_heads = sums.shape[0]
     own, d = dh.shape
     group, wide, chunk, cw = plan.group, plan.wide, plan.chunk, plan.cw
@@ -1247,21 +1397,31 @@
     part = d // narrow
     kv_width = kv_heads * 128
     dma = pltpu.SemaphoreType.DMA
-    quarter = pltpu.VMEM((narrow, kv_heads, 2, chunk, 128), BF)
+    quarter = pltpu.VMEM((kv_heads, narrow, 2, chunk, 128), BF)
     slots = (wide, group, cw, part)
-    given = [sums, h, dh, gain2, dx2, x, gain, w_kv, cos, sin]
+
+    def weight(height, across):
+        half = pltpu.VMEM((narrow, height // 2, across), BF)
+        ends = pltpu.VMEM((2, height // 2, across), BF)
+        return [pltpu.VMEM((narrow, height, across), BF), half, half, half, ends] + [dma((narrow + 1,))] * 2
+
+    given = [sums, h, dh, gain2, dx2, x, gain, w_kv, cos, sin, dq, o, db]
+    qw = dq.shape[1]
     whole = pl.BlockSpec(memory_space=pltpu.VMEM)
     hbm = pl.BlockSpec(memory_space=pl.ANY)
     return pl.pallas_call(
         functools.partial(tail_kernel, plan, kv_heads),
-        in_specs=[whole] * len(given),
-        out_specs=[hbm, whole, whole],
+        in_specs=[hbm if i in (1, 7, 12) else whole for i in range(len(given))],
+        out_specs=[hbm] + [whole] * 4,
         out_shape=[
             jax.ShapeDtypeStruct(slots, BF),
             jax.ShapeDtypeStruct((2, part), F32),
             jax.ShapeDtypeStruct((kv_width, part), F32),
+            jax.ShapeDtypeStruct((part, qw), F32),
+            jax.ShapeDtypeStruct((qw, part), F32),
         ],
         scratch_shapes=[
+            pltpu.VMEM(h.shape, BF), pltpu.VMEM(w_kv.shape, BF), pltpu.VMEM((wide, own, part), BF),
             quarter, quarter, quarter, quarter,
             pltpu.VMEM((plan.rows, kv_width), BF),
             pltpu.VMEM((wide, own, kv_width), BF),
@@ -1272,12 +1432,11 @@
             pltpu.VMEM((group, 2, part), F32),
             pltpu.VMEM((2, part), F32),
             pltpu.VMEM((wide, 2, part), F32),
-            pltpu.VMEM((narrow, kv_width, part), BF),
-            pltpu.VMEM((group, kv_width, part), BF),
-            dma((2,)), dma((narrow,)), dma((narrow,)), dma((wide,)), dma((wide,)), dma((group,)), dma((group,)),
+            dma((2, kv_heads)), dma((kv_heads, narrow)), dma((kv_heads, narrow)),
+            dma((wide, kv_heads)), dma((wide, kv_heads)), dma((group,)), dma((group,)),
             dma((group,)), dma((group,)), dma((wide,)), dma((wide,)),
-            dma((group,)), dma((group,)), dma((2,)),
-        ] + [dma((wide,))] * 4,
+            dma((5,)),
+        ] + [dma((wide,))] * 4 + weight(part, qw) + weight(kv_width, part) + weight(qw, part),
         cost_estimate=pl.CostEstimate(
             flops=200 * own * d * wide * kv_width, bytes_accessed=4 * sums.size, transcendentals=0
         ),
@@ -1349,8 +1508,8 @@
     def gather_weight(weight):
         return lax.all_gather(half_of(weight, seq_index, seq_count), NS, axis=0, tiled=True)
 
-    def scatter_grad(grad):
-        mine = lax.psum_scatter(grad.astype(BF), NS, scatter_dimension=0, tiled=True)
+    def scatter_grad(grad, *others):
+        mine = after(lax.psum_scatter(grad.astype(BF), NS, scatter_dimension=0, tiled=True), *others)
         return lax.all_gather(mine, "seq", axis=0, tiled=True).astype(F32)
 
     def after(values, *others):
@@ -1370,60 +1529,46 @@
     angles = row_pos[:, None] * jnp.tile(frequency, 4)[None, :]
     cos, sin = jnp.cos(angles), jnp.sin(angles)
 
-    lane = jnp.arange(128, dtype=jnp.int32)[None, :]
-    closed = (segment_ids[:, None] != lane - HD) | (token_mask[:, None] != 1)
-    kf = jnp.where((lane >= HD) & (lane < HD + 3) & closed, NEG, 0.0)
-    kf = jnp.where((lane >= HD + 3) & (lane < HD + 6), 1.0, kf).astype(BF)
+    feature = jnp.arange(16, dtype=jnp.int32)[:, None]
+    closed = (segment_ids[None, :] != feature) | (token_mask[None, :] != 1)
+    marks = jnp.where((feature < 3) & closed, NEG, jnp.where((feature >= 3) & (feature < 6), 1.0, 0.0)).astype(BF)
 
     mask = lax.dynamic_slice_in_dim(token_mask, seq_index * (group * chunk), group * chunk, 0)
     g_part = lax.dynamic_index_in_dim(out_grad.reshape(group, wide, cw, d_part), wide_index, 1, keepdims=False)
     mask = lax.dynamic_index_in_dim(mask.reshape(group, wide, cw), wide_index, 1, keepdims=False)
     g_part = jnp.where(mask[:, :, None] == 1, g_part, jnp.zeros_like(g_part))
 
-    w_o = jnp.transpose(gather_weight(w_out).reshape(narrow, kv_heads, heads * HD, d_part), (1, 2, 0, 3))
-    w_o = w_o.reshape(kv_heads, heads * HD, d)
+    w_o = gather_weight(w_out)
     h_one, q, x_low, kx, vx, w_qkv, gains, g_rows, w_kv = head_call(
         plan, tokens.reshape(group, wide, cw, d_part), g_part, jnp.concatenate([w_query, w_kv], axis=1),
-        jnp.stack([attn_gain, ffn_gain]), cos, sin, kf, qw, kv_heads
+        jnp.stack([attn_gain, ffn_gain]), cos, sin, marks, qw, kv_heads
     )
     gains = jnp.transpose(gains, (1, 0, 2)).reshape(2, d)
     gain_one, gain_two = gains[0:1], gains[1:2]
     g_rows = g_rows.reshape(rows, d)
 
     w_gu = gather_weight(after(jnp.concatenate([w_gate, w_up], axis=1), q))
-    w_dn = gather_weight(after(w_down, q)).reshape(narrow, ff, d_part)
-    o, qe, x2 = forward_call(plan, starts, q, kx, vx, w_o, x_low, heads)
+    o, qe, x2, w_dn = forward_call(plan, starts, q, kx, vx, w_o, x_low, w_down, heads)
     w_kv = jnp.transpose(w_kv.reshape(wide, seq_count, d_part // seq_count, 2 * kw), (1, 0, 2, 3))
     w_kv = lax.dynamic_index_in_dim(w_kv, seq_index, 0, keepdims=False).reshape(-1, 2 * kw)
-    w_kv = lax.all_gather(after(w_kv, o, w_dn, w_gu), NS, axis=0, tiled=True)
+    w_kv = lax.all_gather(after(w_kv, o, w_gu), NS, axis=0, tiled=True)
     w_kv = w_kv.reshape(group, wide, d_part // seq_count, 2 * kw)
-    w_kv = jnp.transpose(w_kv, (1, 0, 2, 3)).reshape(wide, d, 2 * kw)
-
-    act, d_gate, d_up, h_all, down, dx2, grad_gain_two = ffn_call(plan, x2, gain_two, g_rows, w_gu, w_dn)
-
-    act = after(act, w_kv)
-    grad_dn, grad_gate, grad_up, db, result = weights_call(
-        plan, dx2, act, h_all, g_rows, d_gate, d_up, down, x2
-    )
+
+    d_gate, d_up, h_all, down, dx2, grad_gain_two, grad_dn = ffn_call(plan, x2, gain_two, g_rows, w_gu, w_dn)
+
+    h_all = after(h_all, w_kv)
+    grad_gate, grad_up, db, result = weights_call(plan, dx2, h_all, d_gate, d_up, down, x2)
     dq, sums, dh1, result = backward_call(plan, db, qe, kx, vx, o, w_o, w_qkv, cos, sin, result, heads)
 
-    input_grad, gain_grads, grad_kv = tail_call(
-        plan, sums, h_one, dh1, grad_gain_two, dx2, x_low, gain_one, w_kv, cos, sin
+    input_grad, gain_grads, grad_kv, grad_q, grad_o = tail_call(
+        plan, sums, h_one, dh1, grad_gain_two, dx2, x_low, gain_one, w_kv, cos, sin, dq, o, db
     )
     result = assemble_call(plan, scalars, result, BF)
     input_grad = assemble_call(plan, scalars, input_grad, F32)
 
-    def tn(left, right):
-        return lax.dot_general(left, right, TN, preferred_element_type=F32).astype(BF)
-
-    def tn_split(left, right):
-        return jnp.concatenate([tn(left, right[:, n * d_part : (n + 1) * d_part]) for n in range(narrow)], axis=0)
-
-    grad_dn = scatter_grad(grad_dn.reshape(narrow * ff, d_part))
-    grad_gate = scatter_grad(grad_gate)
-    grad_up = scatter_grad(grad_up)
-    grad_o = scatter_grad(tn_split(o.reshape(rows, qw), db.reshape(rows, d)))
-    grad_q = scatter_grad(tn(h_one, dq))
+    grad_dn = scatter_grad(grad_dn.reshape(narrow * ff, d_part), dq)
+    grad_gate = scatter_grad(grad_gate, dq)
+    grad_up = scatter_grad(grad_up, dq)
     grad_kv = jnp.transpose(grad_kv.reshape(kv_heads, 2, HD, d_part), (3, 0, 1, 2))
     return (
         result,

time: 1010 us -> 909 us (0.900)
  waiting for transfers between devices: 69.1 us -> 23.7 us
  Pallas kernels: 841 us -> 825 us
  matrix products: 12.1 us -> 0 us
    reduce_scatter x5 -> x3, waiting for transfers between devices: 37.9 us -> 0.06 us  [scatter_grad(): lax.psum_scatter(grad.astype(BF), NS, scatter_dimension=0, tiled=True)]
    pallas_call x1, Pallas kernels: 162 us -> 142 us  [tail_call(): pl.pallas_call(functools.partial(tail_kernel, plan, kv_heads), in_specs=[...]
    dot_general x5 -> x0, matrix products: 12.1 us -> none  [tn(): lax.dot_general(left, right, TN, preferred_element_type=F32).astype(BF)]
    all_gather x3 -> x2, waiting for transfers between devices: 28.6 us -> 21.9 us  [gather_weight(): lax.all_gather(half_of(weight, seq_index, seq_count), NS, axis=0, tiled=T...]
  transfers between devices with their start and end apart: 12 -> 9, of which waited for: 2 -> 1; matrix products, arithmetic and copies ran while one was open for 6% -> 4% of each run, Pallas kernels for 73% -> 91%
where the time goes in v6:
time: 909 us; the launch traced here: 908 us
  Pallas kernels  825 us (91%)
  other arithmetic  28 us (3%)
  waiting for transfers between devices  23.7 us (3%)
  local copies, waits for them, and re-layouts  16.6 us (2%)
  between operations  14.1 us (2%)
    pallas_call x1, Pallas kernels, ffn_call(): pl.pallas_call(functools.partial(ffn_kernel, plan), grid=(wide, tiles), i...  172 us
    pallas_call x1, Pallas kernels, backward_call(): pl.pallas_call(functools.partial(backward_kernel, plan, kv_heads, heads),...  163 us
    pallas_call x1, Pallas kernels, tail_call(): pl.pallas_call(functools.partial(tail_kernel, plan, kv_heads), in_specs=[...  142 us
    pallas_call x1, Pallas kernels, head_call(): pl.pallas_call(functools.partial(head_kernel, plan, kv_heads, qw), in_spe...  127 us
    pallas_call x1, Pallas kernels, forward_call(): pl.pallas_call(functools.partial(forward_kernel, plan, kv_heads, heads),...  109 us
    pallas_call x1, Pallas kernels, weights_call(): pl.pallas_call(functools.partial(weights_kernel, plan, tiles), grid=(2 *...  106 us
    all_gather x2, waiting for transfers between devices, gather_weight(): lax.all_gather(half_of(weight, seq_index, seq_count), NS, axis=0, tiled=T...  21.9 us
  transfers between devices with their start and end apart: 9, of which 1 were waited for; matrix products, arithmetic and copies ran while one was open for 4% of the time, Pallas kernels for 91%

profile of v6, /device:TPU:0, one launch (start us, length us, event | category | flops | bytes accessed | tf_op | source)
XLA Modules:
  0.0 908.4 jit_solution(1973403775615696307)
XLA Ops:
  7.3 1.1 copy-done
  8.4 0.7 constant_dynamic-slice_fusion.2
  9.2 0.0 all-gather.9.cloned.1.call-start
  9.3 1.4 convert_reduce_fusion.1
  10.7 0.8 broadcast_compare_fusion
  11.4 0.7 dynamic_slice.19
  12.2 1.0 copy.39
  13.2 1.0 copy.38
  14.3 0.1 copy.41
  14.4 0.1 mul.52
  14.5 2.4 bitcast_select_fusion.g_ref
  16.9 0.9 pad_maximum_fusion.1.w_ref
  17.8 0.6 pad_maximum_fusion.3.gains_ref
  18.4 1.3 subtract_convert_fusion
  19.8 3.1 multiply_sine_fusion
  22.8 0.8 select_convert_fusion.marks_ref
  23.7 127.1 %head.1 = (bf16[1024,2048]{1,0:T(8,128)(2,1)}, bf16[1024,512]{1,0:T(8,128)(2,1)}, bf16[256,2048]{1,0:T(8,128)(2,1)}, bf16[2,8192,128]{2,1,0:T(8,128)(2,1)}, bf16...) custom-call(bf16[8,4,128,512]{3,2,1,0:T(8,128)(2,1)} %bitcast.58, ...), custom_call_target="tpu_custom_call" | custom-call | flops 96636764160 | bytes 19922944 | tf_op jit(solution)/shard_map/head/pallas_call | solution.py:504
  150.7 2.1 pad_maximum_fusion
  152.8 1.5 constant_dynamic-slice_fusion.1
  154.4 0.0 all-gather.11.cloned.1.call-start
  154.4 1.9 pad_add_fusion.s_ref
  156.3 0.8 constant_dynamic-slice_fusion
  157.2 109.4 %attention_forward.1 = (bf16[4,256,512]{2,1,0:T(8,128)(2,1)}, bf16[4,2,2,512,128]{4,3,2,1,0:T(8,128)(2,1)}, f32[256,2048]{1,0:T(8,128)}, bf16[4,2048,512]{2,1,0:T(8,128)(2,1)}) custom-call(s32[2]{0:T(128)} %pad_add_fusion.s_ref, bf16[1024,512]{1,0:T(8,128)(2,1)} %get-tuple-element.50.q_ref, bf16[2,8192,128]{2,1,0:T(8,128)(2,1)} %get-tuple-element.51.kx, ...), custom_call_target="tpu_custom_call" | custom-call | flops 34359738368 | bytes 16777216 | tf_op jit(solution)/shard_map/attention_forward/pallas_call | solution.py:717
  266.6 21.9 %all-gather.9.cloned.1.call-done.wg_ref.wu_ref = bf16[2048,4096]{1,0:T(8,128)(2,1)} async-done(((bf16[256,4096]{1,0:T(8,128)(2,1)}), bf16[2048,4096]{1,0:T(8,128)(2,1)}) %all-gather.9.cloned.1.call-update) | async-done | bytes 16777232 | tf_op jit(solution)/shard_map/all_gather | solution.py:1509
  288.6 0.2 reduce-scatter.8.cloned.1.call-start
  288.8 0.6 fusion.19
  289.4 171.6 %feed_forward.1 = (bf16[1024,2048]{1,0:T(8,128)(2,1)}, bf16[1024,2048]{1,0:T(8,128)(2,1)}, bf16[1024,2048]{1,0:T(8,128)(2,1)}, bf16[4,256,2048]{2,1,0:T(8,128)(2...) custom-call(f32[256,2048]{1,0:T(8,128)} %get-tuple-element.54.x2_ref, ...), custom_call_target="tpu_custom_call" | custom-call | flops 68719476736 | bytes 50331648 | tf_op jit(solution)/shard_map/feed_forward/pallas_call | solution.py:889
  461.0 0.0 reduce-scatter.4.cloned.1.call-start
  461.1 106.0 %weight_gradients.1 = (bf16[2048,2048]{1,0:T(8,128)(2,1)}, bf16[2048,2048]{1,0:T(8,128)(2,1)}, bf16[4,256,2048]{2,1,0:T(8,128)(2,1)}, bf16[256,2048]{1,0:T(8,128)(2,1)}) custom-call(f32[256,2048]{1,0:T(8,128)} %get-tuple-element.59.dx2_ref, bf16[1024,2048]{1,0:T(8,128)(2,1)} %get-tuple-element.64.h_ref, bf16[1024,2048]{1,0:T(8,128)(2,1)} %get-tuple-element.65.dg_ref, ...), custom_call_target="tpu_custom_call" | custom-call | flops 34359738368 | bytes 41943040 | tf_op jit(solution)/shard_map/weight_gradients/pallas_call | solution.py:991
  567.2 0.5 reduce-scatter.6.cloned.1.call-update
  567.8 163.0 %attention_backward.1 = (bf16[1024,512]{1,0:T(8,128)(2,1)}, f32[2,8192,128]{2,1,0:T(8,128)}, f32[256,2048]{1,0:T(8,128)}, bf16[4,8,128,512]{3,2,1,0:T(8,128)(2,1)}) custom-call(bf16[4,256,2048]{2,1,0:T(8,128)(2,1)} %get-tuple-element.68.db_ref.db_hbm, bf16[4,2,2,512,128]{4,3,2,1,0:T(8,128)(2,1)} %get-tuple-element.69.qe_ref, ...), custom_call_target="tpu_custom_call" | custom-call | flops 77309411328 | bytes 25165824 | tf_op jit(solution)/shard_map/attention_backward/pallas_call | solution.py:1175
  730.9 0.7 all-gather.13.cloned.1.call-update
  731.6 0.3 all-gather.15.cloned.1.call-start
  731.9 0.4 all-gather.15.cloned.1.call-update
  732.3 142.0 %input_gradient.1 = (bf16[4,8,128,512]{3,2,1,0:T(8,128)(2,1)}, f32[2,512]{1,0:T(2,128)}, f32[256,512]{1,0:T(8,128)}, f32[512,512]{1,0:T(8,128)}, f32[512,512]{1,0:T(8,128)}) custom-call(f32[2,8192,128]{2,1,0:T(8,128)} %get-tuple-element.73.sums_ref, bf16[1024,2048]{1,0:T(8,128)(2,1)} %get-tuple-element.74.h_hbm, f32[256,2048]{1,0:T(8,128)} %get-tuple-element.75.dh_ref, ...), custom_call_target="tpu_custom_call" | custom-call | flops 107374182400 | bytes 8388608 | tf_op jit(solution)/shard_map/input_gradient/pallas_call | solution.py:1412
  874.4 1.1 copy.49
  875.5 0.8 copy.43
  876.3 0.8 copy.44
  877.2 2.2 copy-done.2
  879.4 2.4 assemble.2
  881.8 1.3 copy-done.3
  883.1 3.6 assemble.3
  886.7 0.6 fusion.20
  887.3 4.2 convert_element_type.31
  891.5 4.2 convert_element_type.29
  895.7 4.3 convert_element_type.30
  899.9 1.0 copy.53
  900.9 1.0 copy.54
  (52 shorter events, 0.5 us)
Async XLA Ops:
  7.2 1.2 copy-start
  7.2 15.6 %copy-start.9 = (s32[8192]{0:T(1024)S(1)}, s32[8192]{0:T(1024)}, u32[]{:S(2)}) copy-start(s32[8192]{0:T(1024)} %param.23) | copy-start | bytes 98308
  7.2 9.7 %copy-start.7 = (bf16[512,512]{1,0:T(8,128)(2,1)S(1)}, bf16[512,512]{1,0:T(8,128)(2,1)}, u32[]{:S(2)}) copy-start(bf16[512,512]{1,0:T(8,128)(2,1)} %param.15) | copy-start | bytes 1572868
  7.2 10.6 %copy-start.12 = (f32[512]{0:T(512)S(1)}, f32[512]{0:T(512)}, u32[]{:S(2)}) copy-start(f32[512]{0:T(512)} %param.19) | copy-start | bytes 6148
  7.2 10.6 %copy-start.13 = (f32[512]{0:T(512)S(1)}, f32[512]{0:T(512)}, u32[]{:S(2)}) copy-start(f32[512]{0:T(512)} %param.14) | copy-start | bytes 6148
  7.2 149.9 %all-gather.7.cloned.1.call-start = ((), (), s32[]{:S(2)}) async-start(), calls=%async_computation.3 | async-start | bytes 2359296 | tf_op jit(solution)/shard_map/all_gather | solution.py:1509
  9.2 279.4 %all-gather.9.cloned.1.call-start = ((), (), s32[]{:S(2)}) async-start(), calls=%async_computation.4 | async-start | bytes 18874368 | tf_op jit(solution)/shard_map/all_gather | solution.py:1509
  23.7 127.1 %copy-start.4 = (bf16[512,2048]{1,0:T(8,128)(2,1)S(1)}, bf16[512,2048]{1,0:T(8,128)(2,1)}, u32[]{:S(2)}) copy-start(bf16[512,2048]{1,0:T(8,128)(2,1)} %param.21) | copy-start | bytes 6291460
  152.8 3.5 copy-start.8
  154.4 306.7 %all-gather.11.cloned.1.call-start = ((), (), s32[]{:S(2)}) async-start(), calls=%async_computation.5 | async-start | bytes 4718592 | tf_op jit(solution)/shard_map/all_gather | solution.py:1554
  157.2 131.6 %copy-start.10 = (f32[4,2,512]{2,1,0:T(2,128)S(1)}, f32[4,2,512]{2,1,0:T(2,128)}, u32[]{:S(2)}) copy-start(f32[4,2,512]{2,1,0:T(2,128)} %get-tuple-element.55) | copy-start | bytes 49156
  288.6 442.2 %reduce-scatter.8.cloned.1.call-start = ((), (), s32[]{:S(2)}) async-start(), calls=%async_computation.10 | async-start | bytes 9437184 | tf_op jit(solution)/shard_map/reduce_scatter | solution.py:1512
  461.0 269.9 %reduce-scatter.4.cloned.1.call-start = ((), (), s32[]{:S(2)}) async-start(), calls=%async_computation.6 | async-start | bytes 9437184 | tf_op jit(solution)/shard_map/reduce_scatter | solution.py:1512
  567.2 164.7 %reduce-scatter.6.cloned.1.call-start = ((), (), s32[]{:S(2)}) async-start(), calls=%async_computation.8 | async-start | bytes 9437184 | tf_op jit(solution)/shard_map/reduce_scatter | solution.py:1512
  567.8 319.5 %all-gather.17.cloned.1.call-start = ((), (), s32[]{:S(2)}) async-start(), calls=%async_computation.11 | async-start | bytes 3145728 | tf_op jit(solution)/shard_map/all_gather | solution.py:1513
  730.8 160.6 %all-gather.13.cloned.1.call-start = ((), (), s32[]{:S(2)}) async-start(), calls=%async_computation.7 | async-start | bytes 3145728 | tf_op jit(solution)/shard_map/all_gather | solution.py:1513
  731.6 164.1 %all-gather.15.cloned.1.call-start = ((), (), s32[]{:S(2)}) async-start(), calls=%async_computation.9 | async-start | bytes 3145728 | tf_op jit(solution)/shard_map/all_gather | solution.py:1513
  877.2 2.2 copy-start.2
  879.4 3.7 copy-start.3
  883.1 3.6 copy-start.11
  891.5 10.4 %copy-start.1 = (bf16[512,512]{1,0:T(8,128)(2,1)S(1)}, bf16[512,512]{1,0:T(8,128)(2,1)}, u32[]{:S(2)}) copy-start(bf16[512,512]{1,0:T(8,128)(2,1)} %param.18) | copy-start | bytes 1572868
  895.6 4.3 copy-start.6
  895.7 5.3 copy-start.5
Sparse Core Ops, SparseCore 0:
  10.5 42.5 all-gather.6
  154.5 133.9 all-gather.8
  291.0 36.7 all-gather.10
  461.2 68.4 reduce-scatter.7
  567.3 69.5 reduce-scatter.3
  640.2 71.3 reduce-scatter.5
  731.0 13.3 all-gather.16
  745.9 11.4 all-gather.12
  759.0 11.7 all-gather.14

commit v7 on v6

--- a/solution.py
+++ b/solution.py
@@ -281,11 +281,11 @@
 
 
 def head_kernel(
-    plan, kv_heads, qw, x_ref, g_ref, w_ref, gains_ref, cos_ref, sin_ref, marks_ref,
-    h_out, q_out, own_out, kx, vx, w_out, gains_out, g_out, side_out,
+    plan, kv_heads, qw, x_ref, g_ref, w_ref, gains_ref, cos_ref, sin_ref, marks_ref, wg_ref, wu_ref,
+    h_out, q_out, own_out, kx, vx, w_out, gains_out, g_out, side_out, gu_out,
     x_buf, marks, side_buf, side_send, side_recv, w_buf, kv_buf, g_buf, gain_buf,
     x_send, x_recv, x_stay, w_send, w_recv, w_on_send, w_on_recv, gain_send, gain_recv,
-    g_send, g_recv, kv_send, kv_recv, kv_on_send, kv_on_recv, keep_sem, *chain_sems
+    g_send, g_recv, kv_send, kv_recv, kv_on_send, kv_on_recv, keep_sem, cut_sem, *chain_sems
 ):
     group, wide, chunk, cw, own = plan.group, plan.wide, plan.chunk, plan.cw, plan.own
     team = Group(plan)
@@ -379,6 +379,14 @@
     gains_out[...] = gain_buf[...]
     w_keep = pltpu.make_async_copy(w_buf, w_out, keep_sem.at[1])
     w_keep.start()
+    ff = wg_ref.shape[1]
+    half = pl.ds(pl.multiple_of(seq * fold, fold), fold)
+    cuts = [
+        pltpu.make_async_copy(wg_ref.at[half], gu_out.at[:, 0:ff], cut_sem.at[0]),
+        pltpu.make_async_copy(wu_ref.at[half], gu_out.at[:, ff : 2 * ff], cut_sem.at[1]),
+    ]
+    for copy in cuts:
+        copy.start()
 
     def kv_rows(core, n, r):
         return kv_buf.at[core, n, pl.ds(pl.multiple_of(r * own, own), own)]
@@ -487,11 +495,11 @@
         for r in range(wide):
             x_to(r, k).wait_send()
     w_keep.wait()
-    for copy in keep:
+    for copy in keep + cuts:
         copy.wait()
 
 
-def head_call(plan, x, g, w, gains, cos, sin, marks, qw, kv_heads):
+def head_call(plan, x, g, w, gains, cos, sin, marks, w_gate, w_up, qw, kv_heads):
     group, wide, cw, part = x.shape
     narrow = group // 2
     d = part * narrow
@@ -503,8 +511,8 @@
     keys = jax.ShapeDtypeStruct((kv_heads, total, 128), BF)
     return pl.pallas_call(
         functools.partial(head_kernel, plan, kv_heads, qw),
-        in_specs=[hbm, hbm] + [whole] * 5,
-        out_specs=[whole] * 5 + [hbm, whole, hbm, whole],
+        in_specs=[hbm, hbm] + [whole] * 5 + [hbm, hbm],
+        out_specs=[whole] * 5 + [hbm, whole, hbm, whole, hbm],
         out_shape=[
             jax.ShapeDtypeStruct((rows, d), BF),
             jax.ShapeDtypeStruct((rows, qw), BF),
@@ -515,6 +523,7 @@
             jax.ShapeDtypeStruct((narrow, 2, part), F32),
             jax.ShapeDtypeStruct((wide, own, d), BF),
             jax.ShapeDtypeStruct((wide, part, width - qw), BF),
+            jax.ShapeDtypeStruct((part // 2, 2 * w_gate.shape[1]), BF),
         ],
         scratch_shapes=[
             pltpu.VMEM((wide, own, d), BF),
@@ -529,7 +538,7 @@
             dma((narrow,)), dma((narrow,)), dma((narrow,)), dma((narrow,)), dma((narrow,)), dma((narrow,)),
             dma((group,)), dma((group,)),
             dma((wide, narrow)), dma((wide, narrow)), dma((narrow,)), dma((narrow,)),
-            dma((2 + wide,)),
+            dma((2 + wide,)), dma((2,)),
         ] + [dma((wide,))] * 4,
         cost_estimate=pl.CostEstimate(
             flops=60 * rows * d * width, bytes_accessed=8 * rows * d + 2 * d * width, transcendentals=rows
@@ -538,7 +547,7 @@
             vmem_limit_bytes=60 << 20, collective_id=4, has_side_effects=True
         ),
         name="head",
-    )(x, g, w, gains, cos, sin, marks)
+    )(x, g, w, gains, cos, sin, marks, w_gate, w_up)
 
 
 def split_heads(block, heads, low):
@@ -1447,29 +1456,42 @@
     )(*given)
 
 
-def assemble_kernel(plan, s_ref, in_ref, out_ref):
-    group = plan.group
+def finish_kernel(plan, s_ref, res_ref, dx_ref, *refs):
+    group, weights = plan.group, len(refs) // 2 - 1
+    res_out, dx_out = refs[weights : weights + 2]
     for l in range(group):
         owner = jnp.where(s_ref[0] >= group // 2, group - 1 - l, l)
-        out_ref[l, 0] = in_ref[0, owner].astype(out_ref.dtype)
-
-
-def assemble_call(plan, scalars, values, dtype):
-    wide, group, cw, part = values.shape
+        res_out[l, 0] = res_ref[0, owner]
+        dx_out[l, 0] = dx_ref[0, owner].astype(F32)
+    for low, out in zip(refs[:weights], refs[weights + 2 :]):
+        out[...] = low[...].astype(F32)
+
+
+def finish_call(plan, scalars, result, dx, weights):
+    wide, group, cw, part = result.shape
+    cuts = 2 if cw % 64 == 0 else 1
+    steps = wide * cuts
+    slots = pl.BlockSpec((1, group, cw // cuts, part), lambda w, c, s: (w, 0, c, 0))
+    tokens = pl.BlockSpec((group, 1, cw // cuts, part), lambda w, c, s: (0, w, c, 0))
+    rows = [pl.BlockSpec((a.shape[0] // steps, a.shape[1]), lambda w, c, s: (w * cuts + c, 0)) for a in weights]
+    shape = (group, wide, cw, part)
+    size = result.size + sum(a.size for a in weights)
     out = pl.pallas_call(
-        functools.partial(assemble_kernel, plan),
+        functools.partial(finish_kernel, plan),
         grid_spec=pltpu.PrefetchScalarGridSpec(
             num_scalar_prefetch=1,
-            grid=(wide,),
-            in_specs=[pl.BlockSpec((1, group, cw, part), lambda w, s: (w, 0, 0, 0))],
-            out_specs=[pl.BlockSpec((group, 1, cw, part), lambda w, s: (0, w, 0, 0))],
+            grid=(wide, cuts),
+            in_specs=[slots, slots] + rows,
+            out_specs=[tokens, tokens] + rows,
         ),
-        out_shape=[jax.ShapeDtypeStruct((group, wide, cw, part), dtype)],
-        cost_estimate=pl.CostEstimate(flops=values.size, bytes_accessed=6 * values.size, transcendentals=0),
-        compiler_params=pltpu.CompilerParams(vmem_limit_bytes=40 << 20),
-        name="assemble",
-    )(scalars, values)[0]
-    return out.reshape(group * wide * cw, part)
+        out_shape=[jax.ShapeDtypeStruct(shape, BF), jax.ShapeDtypeStruct(shape, F32)]
+        + [jax.ShapeDtypeStruct(a.shape, F32) for a in weights],
+        cost_estimate=pl.CostEstimate(flops=2 * size, bytes_accessed=8 * size, transcendentals=0),
+        compiler_params=pltpu.CompilerParams(vmem_limit_bytes=48 << 20),
+        name="finish",
+    )(scalars, result, dx, *weights)
+    flat = (group * wide * cw, part)
+    return [out[0].reshape(flat), out[1].reshape(flat)] + list(out[2:])
 
 
 def half_of(weight, seq_index, seq_count):
@@ -1500,9 +1522,8 @@
     heads = qw // kw
     ff = w_gate.shape[1]
 
-    start_one = jnp.sum((segment_ids < 1).astype(jnp.int32))
-    start_two = jnp.sum((segment_ids < 2).astype(jnp.int32))
-    starts = jnp.stack([start_one, start_two])
+    starts = jnp.sum((segment_ids[None, :] < jnp.arange(1, 3)[:, None]).astype(jnp.int32), axis=1)
+    start_one, start_two = starts[0], starts[1]
     scalars = jnp.reshape(index, (1,)).astype(jnp.int32)
 
     def gather_weight(weight):
@@ -1510,7 +1531,7 @@
 
     def scatter_grad(grad, *others):
         mine = after(lax.psum_scatter(grad.astype(BF), NS, scatter_dimension=0, tiled=True), *others)
-        return lax.all_gather(mine, "seq", axis=0, tiled=True).astype(F32)
+        return lax.all_gather(mine, "seq", axis=0, tiled=True)
 
     def after(values, *others):
         return lax.optimization_barrier((values, *others))[0]
@@ -1539,15 +1560,15 @@
     g_part = jnp.where(mask[:, :, None] == 1, g_part, jnp.zeros_like(g_part))
 
     w_o = gather_weight(w_out)
-    h_one, q, x_low, kx, vx, w_qkv, gains, g_rows, w_kv = head_call(
+    h_one, q, x_low, kx, vx, w_qkv, gains, g_rows, w_kv, w_gu = head_call(
         plan, tokens.reshape(group, wide, cw, d_part), g_part, jnp.concatenate([w_query, w_kv], axis=1),
-        jnp.stack([attn_gain, ffn_gain]), cos, sin, marks, qw, kv_heads
+        jnp.stack([attn_gain, ffn_gain]), cos, sin, marks, w_gate, w_up, qw, kv_heads
     )
     gains = jnp.transpose(gains, (1, 0, 2)).reshape(2, d)
     gain_one, gain_two = gains[0:1], gains[1:2]
     g_rows = g_rows.reshape(rows, d)
 
-    w_gu = gather_weight(after(jnp.concatenate([w_gate, w_up], axis=1), q))
+    w_gu = lax.all_gather(w_gu, NS, axis=0, tiled=True)
     o, qe, x2, w_dn = forward_call(plan, starts, q, kx, vx, w_o, x_low, w_down, heads)
     w_kv = jnp.transpose(w_kv.reshape(wide, seq_count, d_part // seq_count, 2 * kw), (1, 0, 2, 3))
     w_kv = lax.dynamic_index_in_dim(w_kv, seq_index, 0, keepdims=False).reshape(-1, 2 * kw)
@@ -1563,12 +1584,13 @@
     input_grad, gain_grads, grad_kv, grad_q, grad_o = tail_call(
         plan, sums, h_one, dh1, grad_gain_two, dx2, x_low, gain_one, w_kv, cos, sin, dq, o, db
     )
-    result = assemble_call(plan, scalars, result, BF)
-    input_grad = assemble_call(plan, scalars, input_grad, F32)
 
     grad_dn = scatter_grad(grad_dn.reshape(narrow * ff, d_part), dq)
     grad_gate = scatter_grad(grad_gate, dq)
     grad_up = scatter_grad(grad_up, dq)
+    result, input_grad, grad_dn, grad_gate, grad_up = finish_call(
+        plan, scalars, result, input_grad, [grad_dn, grad_gate, grad_up]
+    )
     grad_kv = jnp.transpose(grad_kv.reshape(kv_heads, 2, HD, d_part), (3, 0, 1, 2))
     return (
         result,

time: 909 us -> 900 us (0.990)
  other arithmetic: 28 us -> 11 us
    all_gather x3 -> x4, waiting for transfers between devices: 0.01 us -> 22.5 us  [the longest x1 22.5 us: body(): w_gu = lax.all_gather(w_gu, NS, axis=0, tiled=True)]
    all_gather x2 -> x1, waiting for transfers between devices: 21.9 us -> 0.01 us  [gather_weight(): lax.all_gather(half_of(weight, seq_index, seq_count), NS, axis=0, tiled=T...]
    convert_element_type x3 -> x0, other arithmetic: 12.7 us -> none  [scatter_grad(): return lax.all_gather(mine, 'seq', axis=0, tiled=True).astype(F32)]
  transfers between devices with their start and end apart: 9 -> 9, of which waited for: 1 -> 1; matrix products, arithmetic and copies ran while one was open for 4% -> 2% of each run, Pallas kernels for 91% -> 91%
where the time goes in v7:
time: 900 us; the launch traced here: 899 us
  Pallas kernels  831 us (92%)
  waiting for transfers between devices  24.5 us (3%)
  local copies, waits for them, and re-layouts  17.2 us (2%)
  between operations  14.1 us (2%)
  other arithmetic  11 us (1%)
    pallas_call x1, Pallas kernels, ffn_call(): pl.pallas_call(functools.partial(ffn_kernel, plan), grid=(wide, tiles), i...  172 us
    pallas_call x1, Pallas kernels, backward_call(): pl.pallas_call(functools.partial(backward_kernel, plan, kv_heads, heads),...  163 us
    pallas_call x1, Pallas kernels, tail_call(): pl.pallas_call(functools.partial(tail_kernel, plan, kv_heads), in_specs=[...  142 us
    pallas_call x1, Pallas kernels, head_call(): pl.pallas_call(functools.partial(head_kernel, plan, kv_heads, qw), in_spe...  127 us
    pallas_call x1, Pallas kernels, forward_call(): pl.pallas_call(functools.partial(forward_kernel, plan, kv_heads, heads),...  109 us
    pallas_call x1, Pallas kernels, weights_call(): pl.pallas_call(functools.partial(weights_kernel, plan, tiles), grid=(2 *...  106 us
    all_gather x1, waiting for transfers between devices, body(): w_gu = lax.all_gather(w_gu, NS, axis=0, tiled=True)  22.5 us
  transfers between devices with their start and end apart: 9, of which 1 were waited for; matrix products, arithmetic and copies ran while one was open for 2% of the time, Pallas kernels for 91%

profile of v7, /device:TPU:0, one launch (start us, length us, event | category | flops | bytes accessed | tf_op | source)
XLA Modules:
  0.0 898.9 jit_solution(5813835842808794535)
XLA Ops:
  7.2 0.0 all-gather.7.cloned.1.call-start
  7.3 1.1 copy-done
  8.4 0.7 constant_dynamic-slice_fusion.1
  9.2 0.0 all-gather.9.cloned.1.call-start
  9.3 0.8 broadcast_compare_fusion
  10.0 0.7 dynamic_slice.16
  10.8 1.0 copy.47
  11.8 1.0 copy.46
  12.9 0.1 copy.49
  13.0 0.1 mul.51
  13.1 1.0 fusion.2.s_ref
  14.1 0.6 fusion.22
  14.7 2.4 bitcast_select_fusion.g_ref
  17.1 0.9 pad_maximum_fusion.w_ref
  18.0 0.6 pad_maximum_fusion.2.gains_ref
  18.6 1.3 subtract_convert_fusion
  20.0 3.1 multiply_sine_fusion
  23.0 0.8 select_convert_fusion.marks_ref
  23.9 126.9 %head.1 = (bf16[1024,2048]{1,0:T(8,128)(2,1)}, bf16[1024,512]{1,0:T(8,128)(2,1)}, bf16[256,2048]{1,0:T(8,128)(2,1)}, bf16[2,8192,128]{2,1,0:T(8,128)(2,1)}, bf16...) custom-call(bf16[8,4,128,512]{3,2,1,0:T(8,128)(2,1)} %bitcast.57, ...), custom_call_target="tpu_custom_call" | custom-call | flops 96636764160 | bytes 19922944 | tf_op jit(solution)/shard_map/head/pallas_call | solution.py:512
  150.8 0.0 all-gather.11.cloned.1.call-start
  150.8 1.9 constant_dynamic-slice_fusion
  152.7 108.9 %attention_forward.1 = (bf16[4,256,512]{2,1,0:T(8,128)(2,1)}, bf16[4,2,2,512,128]{4,3,2,1,0:T(8,128)(2,1)}, f32[256,2048]{1,0:T(8,128)}, bf16[4,2048,512]{2,1,0:T(8,128)(2,1)}) custom-call(s32[2]{0:T(128)} %copy-done.9, bf16[1024,512]{1,0:T(8,128)(2,1)} %get-tuple-element.55.q_ref, bf16[2,8192,128]{2,1,0:T(8,128)(2,1)} %get-tuple-element.56.kx, ...), custom_call_target="tpu_custom_call" | custom-call | flops 34359738368 | bytes 16777216 | tf_op jit(solution)/shard_map/attention_forward/pallas_call | solution.py:726
  261.6 22.5 %all-gather.9.cloned.1.call-done.wg_ref.wu_ref = bf16[2048,4096]{1,0:T(8,128)(2,1)} async-done(((bf16[256,4096]{1,0:T(8,128)(2,1)}), bf16[2048,4096]{1,0:T(8,128)(2,1)}) %all-gather.9.cloned.1.call-update) | async-done | bytes 16777232 | tf_op jit(solution)/shard_map/all_gather | solution.py:1571
  284.1 0.2 reduce-scatter.4.cloned.1.call-start
  284.4 0.6 fusion.20
  285.0 171.6 %feed_forward.1 = (bf16[1024,2048]{1,0:T(8,128)(2,1)}, bf16[1024,2048]{1,0:T(8,128)(2,1)}, bf16[1024,2048]{1,0:T(8,128)(2,1)}, bf16[4,256,2048]{2,1,0:T(8,128)(2...) custom-call(f32[256,2048]{1,0:T(8,128)} %get-tuple-element.59.x2_ref, ...), custom_call_target="tpu_custom_call" | custom-call | flops 68719476736 | bytes 50331648 | tf_op jit(solution)/shard_map/feed_forward/pallas_call | solution.py:898
  456.7 0.0 reduce-scatter.6.cloned.1.call-start
  456.7 106.1 %weight_gradients.1 = (bf16[2048,2048]{1,0:T(8,128)(2,1)}, bf16[2048,2048]{1,0:T(8,128)(2,1)}, bf16[4,256,2048]{2,1,0:T(8,128)(2,1)}, bf16[256,2048]{1,0:T(8,128)(2,1)}) custom-call(f32[256,2048]{1,0:T(8,128)} %get-tuple-element.64.dx2_ref, bf16[1024,2048]{1,0:T(8,128)(2,1)} %get-tuple-element.69.h_ref, bf16[1024,2048]{1,0:T(8,128)(2,1)} %get-tuple-element.70.dg_ref, ...), custom_call_target="tpu_custom_call" | custom-call | flops 34359738368 | bytes 41943040 | tf_op jit(solution)/shard_map/weight_gradients/pallas_call | solution.py:1000
  562.8 0.0 reduce-scatter.8.cloned.1.call-start
  562.9 0.5 reduce-scatter.8.cloned.1.call-update
  563.4 0.3 all-gather.13.cloned.1.call-start
  563.7 163.3 %attention_backward.1 = (bf16[1024,512]{1,0:T(8,128)(2,1)}, f32[2,8192,128]{2,1,0:T(8,128)}, f32[256,2048]{1,0:T(8,128)}, bf16[4,8,128,512]{3,2,1,0:T(8,128)(2,1)}) custom-call(bf16[4,256,2048]{2,1,0:T(8,128)(2,1)} %get-tuple-element.73.db_ref.db_hbm, bf16[4,2,2,512,128]{4,3,2,1,0:T(8,128)(2,1)} %get-tuple-element.74.qe_ref, ...), custom_call_target="tpu_custom_call" | custom-call | flops 77309411328 | bytes 25165824 | tf_op jit(solution)/shard_map/attention_backward/pallas_call | solution.py:1184
  726.9 0.0 reduce-scatter.4.cloned.1.call-done
  727.0 0.0 all-gather.15.cloned.1.call-start
  727.1 0.7 all-gather.15.cloned.1.call-update
  727.7 0.0 all-gather.17.cloned.1.call-start
  727.8 0.0 reduce-scatter.8.cloned.1.call-done
  727.8 0.7 all-gather.17.cloned.1.call-update
  728.5 141.5 %input_gradient.1 = (bf16[4,8,128,512]{3,2,1,0:T(8,128)(2,1)}, f32[2,512]{1,0:T(2,128)}, f32[256,512]{1,0:T(8,128)}, f32[512,512]{1,0:T(8,128)}, f32[512,512]{1,0:T(8,128)}) custom-call(f32[2,8192,128]{2,1,0:T(8,128)} %get-tuple-element.78.sums_ref, bf16[1024,2048]{1,0:T(8,128)(2,1)} %get-tuple-element.79.h_hbm, f32[256,2048]{1,0:T(8,128)} %get-tuple-element.80.dh_ref, ...), custom_call_target="tpu_custom_call" | custom-call | flops 107374182400 | bytes 8388608 | tf_op jit(solution)/shard_map/input_gradient/pallas_call | solution.py:1421
  870.0 1.1 copy.57
  871.1 0.8 copy.51
  871.9 0.8 copy.52
  872.8 1.3 fusion.21
  874.2 1.6 copy-done.2
  875.7 1.6 copy-done.3
  877.3 13.1 %finish.1 = (bf16[8,4,128,512]{3,2,1,0:T(8,128)(2,1)}, f32[8,4,128,512]{3,2,1,0:T(8,128)}, f32[2048,512]{1,0:T(8,128)}, f32[512,2048]{1,0:T(8,128)}, f32[512,2048]{1,0:T(8,128)}) custom-call(s32[1]{0:T(128)} %bitcast.s_ref, bf16[4,8,128,512]{3,2,1,0:T(8,128)(2,1)} %get-tuple-element.77.res_ref, bf16[4,8,128,512]{3,2,1,0:T(8,128)(2,1)} %get-tuple-element.83.dx_ref, ...), custom_call_target="tpu_custom_call" | custom-call | flops 10485760 | bytes 41943040 | tf_op jit(solution)/shard_map/finish/pallas_call | solution.py:1479
  890.5 1.0 copy.61
  891.4 1.0 copy.62
  (43 shorter events, 0.3 us)
Async XLA Ops:
  7.2 1.2 copy-start
  7.2 15.8 %copy-start.7 = (s32[8192]{0:T(1024)S(1)}, s32[8192]{0:T(1024)}, u32[]{:S(2)}) copy-start(s32[8192]{0:T(1024)} %param.23) | copy-start | bytes 98308
  7.2 9.9 %copy-start.6 = (bf16[512,512]{1,0:T(8,128)(2,1)S(1)}, bf16[512,512]{1,0:T(8,128)(2,1)}, u32[]{:S(2)}) copy-start(bf16[512,512]{1,0:T(8,128)(2,1)} %param.15) | copy-start | bytes 1572868
  7.2 10.8 %copy-start.10 = (f32[512]{0:T(512)S(1)}, f32[512]{0:T(512)}, u32[]{:S(2)}) copy-start(f32[512]{0:T(512)} %param.19) | copy-start | bytes 6148
  7.2 10.8 %copy-start.11 = (f32[512]{0:T(512)S(1)}, f32[512]{0:T(512)}, u32[]{:S(2)}) copy-start(f32[512]{0:T(512)} %param.14) | copy-start | bytes 6148
  7.2 145.5 %all-gather.7.cloned.1.call-start = ((), (), s32[]{:S(2)}) async-start(), calls=%async_computation.3 | async-start | bytes 2359296 | tf_op jit(solution)/shard_map/all_gather | solution.py:1530
  9.2 275.0 %all-gather.9.cloned.1.call-start = ((), (), s32[]{:S(2)}) async-start(), calls=%async_computation.4 | async-start | bytes 18874368 | tf_op jit(solution)/shard_map/all_gather | solution.py:1571
  14.1 136.6 %copy-start.9 = (s32[2]{0:T(128)}, s32[2]{0:T(128)S(1)}, u32[]{:S(2)}) copy-start(s32[2]{0:T(128)S(1)} %fusion.2.s_ref) | copy-start | bytes 28
  150.8 305.9 %all-gather.11.cloned.1.call-start = ((), (), s32[]{:S(2)}) async-start(), calls=%async_computation.5 | async-start | bytes 4718592 | tf_op jit(solution)/shard_map/all_gather | solution.py:1575
  152.7 131.7 %copy-start.8 = (f32[4,2,512]{2,1,0:T(2,128)S(1)}, f32[4,2,512]{2,1,0:T(2,128)}, u32[]{:S(2)}) copy-start(f32[4,2,512]{2,1,0:T(2,128)} %get-tuple-element.60) | copy-start | bytes 49156
  284.1 442.8 %reduce-scatter.4.cloned.1.call-start = ((), (), s32[]{:S(2)}) async-start(), calls=%async_computation.6 | async-start | bytes 9437184 | tf_op jit(solution)/shard_map/reduce_scatter | solution.py:1533
  456.7 270.4 %reduce-scatter.6.cloned.1.call-start = ((), (), s32[]{:S(2)}) async-start(), calls=%async_computation.8 | async-start | bytes 9437184 | tf_op jit(solution)/shard_map/reduce_scatter | solution.py:1533
  562.8 165.0 %reduce-scatter.8.cloned.1.call-start = ((), (), s32[]{:S(2)}) async-start(), calls=%async_computation.10 | async-start | bytes 9437184 | tf_op jit(solution)/shard_map/reduce_scatter | solution.py:1533
  563.4 310.7 %all-gather.13.cloned.1.call-start = ((), (), s32[]{:S(2)}) async-start(), calls=%async_computation.7 | async-start | bytes 3145728 | tf_op jit(solution)/shard_map/all_gather | solution.py:1534
  727.0 147.1 %all-gather.15.cloned.1.call-start = ((), (), s32[]{:S(2)}) async-start(), calls=%async_computation.9 | async-start | bytes 3145728 | tf_op jit(solution)/shard_map/all_gather | solution.py:1534
  727.7 146.4 %all-gather.17.cloned.1.call-start = ((), (), s32[]{:S(2)}) async-start(), calls=%async_computation.11 | async-start | bytes 3145728 | tf_op jit(solution)/shard_map/all_gather | solution.py:1534
  874.1 1.6 copy-start.2
  875.7 1.6 copy-start.3
  877.3 13.1 %copy-start.5 = (f32[512,512]{1,0:T(8,128)S(1)}, f32[512,512]{1,0:T(8,128)}, u32[]{:S(2)}) copy-start(f32[512,512]{1,0:T(8,128)} %get-tuple-element.156) | copy-start | bytes 3145732
  877.3 14.1 %copy-start.4 = (f32[512,512]{1,0:T(8,128)S(1)}, f32[512,512]{1,0:T(8,128)}, u32[]{:S(2)}) copy-start(f32[512,512]{1,0:T(8,128)} %get-tuple-element.159) | copy-start | bytes 3145732
  877.3 15.1 %copy-start.1 = (bf16[512,512]{1,0:T(8,128)(2,1)S(1)}, bf16[512,512]{1,0:T(8,128)(2,1)}, u32[]{:S(2)}) copy-start(bf16[512,512]{1,0:T(8,128)(2,1)} %param.18) | copy-start | bytes 1572868
Sparse Core Ops, SparseCore 0:
  10.5 42.6 all-gather.6
  150.9 133.1 all-gather.8
  286.6 36.7 all-gather.10
  456.8 68.4 reduce-scatter.3
  562.9 69.6 reduce-scatter.5
  635.9 71.2 reduce-scatter.7
  727.1 13.2 all-gather.12
  742.1 11.2 all-gather.14
  755.0 11.7 all-gather.16

commit v8 on v7

--- a/solution.py
+++ b/solution.py
@@ -36,10 +36,11 @@
 
 
 def near_of(plan, z, p):
-    side = jnp.minimum(z, plan.wide - 1 - z)
-    both = jnp.where(lax.rem(p, 2) == 1, z + (p + 1) // 2, z - p // 2)
-    one = jnp.where(z <= plan.wide - 1 - z, z + p - side, z - p + side)
-    return jnp.where(p <= 2 * side, both, one)
+    flip = z > plan.wide - 1 - z
+    side = jnp.where(flip, plan.wide - 1 - z, z)
+    both = jnp.where(lax.rem(p, 2) == 1, side + (p + 1) // 2, side - p // 2)
+    place = jnp.where(p <= 2 * side, both, p)
+    return jnp.where(flip, plan.wide - 1 - place, place)
 
 
 def turn(values, sign):
@@ -166,7 +167,9 @@
         self.side = jnp.minimum(self.z, plan.wide - 1 - self.z)
 
     def term(self, h, way):
-        return jnp.where(h <= self.side, 2 * h - 1 if way > 0 else 2 * h, self.side + h)
+        lower = self.z <= self.wide - 1 - self.z
+        ahead = lower if way > 0 else jnp.logical_not(lower)
+        return jnp.where(h <= self.side, jnp.where(ahead, 2 * h - 1, 2 * h), self.side + h)
 
     def sends(self, t, way):
         h = self.wide - t
@@ -475,7 +478,7 @@
     for r in range(1, wide):
         side_to(r, lax.rem(z - r + wide, wide)).wait_recv()
         side_to(r, z).wait_send()
-    side_out[...] = side_buf[...]
+    side_out[...] = side_buf[:, half, :]
     keep = [
         pltpu.make_async_copy(g_buf.at[near_of(plan, z, p)], g_out.at[p], keep_sem.at[2 + p]) for p in range(wide)
     ]
@@ -522,7 +525,7 @@
             jax.ShapeDtypeStruct((d, width), BF),
             jax.ShapeDtypeStruct((narrow, 2, part), F32),
             jax.ShapeDtypeStruct((wide, own, d), BF),
-            jax.ShapeDtypeStruct((wide, part, width - qw), BF),
+            jax.ShapeDtypeStruct((wide, part // 2, width - qw), BF),
             jax.ShapeDtypeStruct((part // 2, 2 * w_gate.shape[1]), BF),
         ],
         scratch_shapes=[
@@ -1570,8 +1573,7 @@
 
     w_gu = lax.all_gather(w_gu, NS, axis=0, tiled=True)
     o, qe, x2, w_dn = forward_call(plan, starts, q, kx, vx, w_o, x_low, w_down, heads)
-    w_kv = jnp.transpose(w_kv.reshape(wide, seq_count, d_part // seq_count, 2 * kw), (1, 0, 2, 3))
-    w_kv = lax.dynamic_index_in_dim(w_kv, seq_index, 0, keepdims=False).reshape(-1, 2 * kw)
+    w_kv = w_kv.reshape(-1, 2 * kw)
     w_kv = lax.all_gather(after(w_kv, o, w_gu), NS, axis=0, tiled=True)
     w_kv = w_kv.reshape(group, wide, d_part // seq_count, 2 * kw)
 

time: 900 us -> 873 us (0.970)
  Pallas kernels: 831 us -> 806 us
    pallas_call x1, Pallas kernels: 172 us -> 151 us  [ffn_call(): pl.pallas_call(functools.partial(ffn_kernel, plan), grid=(wide, tiles), i...]
where the time goes in v8:
time: 873 us; the launch traced here: 872 us
  Pallas kernels  806 us (92%)
  waiting for transfers between devices  25 us (3%)
  local copies, waits for them, and re-layouts  15.3 us (2%)
  between operations  14.1 us (2%)
  other arithmetic  11 us (1%)
    pallas_call x1, Pallas kernels, backward_call(): pl.pallas_call(functools.partial(backward_kernel, plan, kv_heads, heads),...  164 us
    pallas_call x1, Pallas kernels, ffn_call(): pl.pallas_call(functools.partial(ffn_kernel, plan), grid=(wide, tiles), i...  151 us
    pallas_call x1, Pallas kernels, tail_call(): pl.pallas_call(functools.partial(tail_kernel, plan, kv_heads), in_specs=[...  141 us
    pallas_call x1, Pallas kernels, head_call(): pl.pallas_call(functools.partial(head_kernel, plan, kv_heads, qw), in_spe...  127 us
    pallas_call x1, Pallas kernels, forward_call(): pl.pallas_call(functools.partial(forward_kernel, plan, kv_heads, heads),...  108 us
    pallas_call x1, Pallas kernels, weights_call(): pl.pallas_call(functools.partial(weights_kernel, plan, tiles), grid=(2 *...  102 us
    all_gather x1, waiting for transfers between devices, body(): w_gu = lax.all_gather(w_gu, NS, axis=0, tiled=True)  23 us
  transfers between devices with their start and end apart: 9, of which 1 were waited for; matrix products, arithmetic and copies ran while one was open for 2% of the time, Pallas kernels for 91%

profile of v8, /device:TPU:0, one launch (start us, length us, event | category | flops | bytes accessed | tf_op | source)
XLA Modules:
  0.0 871.8 jit_solution(2492702891584708934)
XLA Ops:
  7.2 0.0 all-gather.7.cloned.1.call-start
  7.3 1.1 copy-done
  8.4 0.7 constant_dynamic-slice_fusion
  9.2 0.0 all-gather.9.cloned.1.call-start
  9.3 0.8 broadcast_compare_fusion
  10.0 0.7 dynamic_slice.14
  10.8 1.0 copy.47
  11.8 1.0 copy.46
  12.9 0.1 copy.49
  13.0 0.1 mul.51
  13.1 1.0 fusion.2.s_ref
  14.1 0.6 fusion.22
  14.7 2.4 bitcast_select_fusion.g_ref
  17.1 0.9 pad_maximum_fusion.w_ref
  18.0 0.6 pad_maximum_fusion.2.gains_ref
  18.6 1.3 subtract_convert_fusion
  20.0 3.1 multiply_sine_fusion
  23.0 0.8 select_convert_fusion.marks_ref
  23.9 126.8 %head.1 = (bf16[1024,2048]{1,0:T(8,128)(2,1)}, bf16[1024,512]{1,0:T(8,128)(2,1)}, bf16[256,2048]{1,0:T(8,128)(2,1)}, bf16[2,8192,128]{2,1,0:T(8,128)(2,1)}, bf16...) custom-call(bf16[8,4,128,512]{3,2,1,0:T(8,128)(2,1)} %bitcast.55, ...), custom_call_target="tpu_custom_call" | custom-call | flops 96636764160 | bytes 19922944 | tf_op jit(solution)/shard_map/head/pallas_call | solution.py:515
  150.7 0.0 all-gather.11.cloned.1.call-start
  150.7 0.0 all-gather.7.cloned.1.call-done.wo_ref
  150.8 108.4 %attention_forward.1 = (bf16[4,256,512]{2,1,0:T(8,128)(2,1)}, bf16[4,2,2,512,128]{4,3,2,1,0:T(8,128)(2,1)}, f32[256,2048]{1,0:T(8,128)}, bf16[4,2048,512]{2,1,0:T(8,128)(2,1)}) custom-call(s32[2]{0:T(128)} %copy-done.9, bf16[1024,512]{1,0:T(8,128)(2,1)} %get-tuple-element.55.q_ref, bf16[2,8192,128]{2,1,0:T(8,128)(2,1)} %get-tuple-element.56.kx, ...), custom_call_target="tpu_custom_call" | custom-call | flops 34359738368 | bytes 16777216 | tf_op jit(solution)/shard_map/attention_forward/pallas_call | solution.py:729
  259.2 23.0 %all-gather.9.cloned.1.call-done.wg_ref.wu_ref = bf16[2048,4096]{1,0:T(8,128)(2,1)} async-done(((bf16[256,4096]{1,0:T(8,128)(2,1)}), bf16[2048,4096]{1,0:T(8,128)(2,1)}) %all-gather.9.cloned.1.call-update) | async-done | bytes 16777232 | tf_op jit(solution)/shard_map/all_gather | solution.py:1574
  282.2 0.2 reduce-scatter.4.cloned.1.call-start
  282.5 0.6 fusion.20
  283.1 151.2 %feed_forward.1 = (bf16[1024,2048]{1,0:T(8,128)(2,1)}, bf16[1024,2048]{1,0:T(8,128)(2,1)}, bf16[1024,2048]{1,0:T(8,128)(2,1)}, bf16[4,256,2048]{2,1,0:T(8,128)(2...) custom-call(f32[256,2048]{1,0:T(8,128)} %get-tuple-element.59.x2_ref, ...), custom_call_target="tpu_custom_call" | custom-call | flops 68719476736 | bytes 50331648 | tf_op jit(solution)/shard_map/feed_forward/pallas_call | solution.py:901
  434.3 0.0 reduce-scatter.6.cloned.1.call-start
  434.3 0.0 all-gather.11.cloned.1.call-done
  434.4 101.5 %weight_gradients.1 = (bf16[2048,2048]{1,0:T(8,128)(2,1)}, bf16[2048,2048]{1,0:T(8,128)(2,1)}, bf16[4,256,2048]{2,1,0:T(8,128)(2,1)}, bf16[256,2048]{1,0:T(8,128)(2,1)}) custom-call(f32[256,2048]{1,0:T(8,128)} %get-tuple-element.64.dx2_ref, bf16[1024,2048]{1,0:T(8,128)(2,1)} %get-tuple-element.69.h_ref, bf16[1024,2048]{1,0:T(8,128)(2,1)} %get-tuple-element.70.dg_ref, ...), custom_call_target="tpu_custom_call" | custom-call | flops 34359738368 | bytes 41943040 | tf_op jit(solution)/shard_map/weight_gradients/pallas_call | solution.py:1003
  535.9 0.0 reduce-scatter.8.cloned.1.call-start
  536.0 0.5 reduce-scatter.8.cloned.1.call-update
  536.5 0.3 all-gather.13.cloned.1.call-start
  536.8 163.7 %attention_backward.1 = (bf16[1024,512]{1,0:T(8,128)(2,1)}, f32[2,8192,128]{2,1,0:T(8,128)}, f32[256,2048]{1,0:T(8,128)}, bf16[4,8,128,512]{3,2,1,0:T(8,128)(2,1)}) custom-call(bf16[4,256,2048]{2,1,0:T(8,128)(2,1)} %get-tuple-element.73.db_ref.db_hbm, bf16[4,2,2,512,128]{4,3,2,1,0:T(8,128)(2,1)} %get-tuple-element.74.qe_ref, ...), custom_call_target="tpu_custom_call" | custom-call | flops 77309411328 | bytes 25165824 | tf_op jit(solution)/shard_map/attention_backward/pallas_call | solution.py:1187
  700.5 0.0 reduce-scatter.4.cloned.1.call-done
  700.5 0.0 all-gather.15.cloned.1.call-start
  700.6 0.7 all-gather.15.cloned.1.call-update
  701.3 0.0 all-gather.17.cloned.1.call-start
  701.3 0.7 all-gather.17.cloned.1.call-update
  702.0 140.9 %input_gradient.1 = (bf16[4,8,128,512]{3,2,1,0:T(8,128)(2,1)}, f32[2,512]{1,0:T(2,128)}, f32[256,512]{1,0:T(8,128)}, f32[512,512]{1,0:T(8,128)}, f32[512,512]{1,0:T(8,128)}) custom-call(f32[2,8192,128]{2,1,0:T(8,128)} %get-tuple-element.78.sums_ref, bf16[1024,2048]{1,0:T(8,128)(2,1)} %get-tuple-element.79.h_hbm, f32[256,2048]{1,0:T(8,128)} %get-tuple-element.80.dh_ref, ...), custom_call_target="tpu_custom_call" | custom-call | flops 107374182400 | bytes 8388608 | tf_op jit(solution)/shard_map/input_gradient/pallas_call | solution.py:1424
  842.9 1.1 copy.57
  844.0 0.8 copy.51
  844.8 0.8 copy.52
  845.7 1.3 fusion.21
  847.1 1.6 copy-done.2
  848.6 1.6 copy-done.3
  850.2 13.1 %finish.1 = (bf16[8,4,128,512]{3,2,1,0:T(8,128)(2,1)}, f32[8,4,128,512]{3,2,1,0:T(8,128)}, f32[2048,512]{1,0:T(8,128)}, f32[512,2048]{1,0:T(8,128)}, f32[512,2048]{1,0:T(8,128)}) custom-call(s32[1]{0:T(128)} %bitcast.s_ref, bf16[4,8,128,512]{3,2,1,0:T(8,128)(2,1)} %get-tuple-element.77.res_ref, bf16[4,8,128,512]{3,2,1,0:T(8,128)(2,1)} %get-tuple-element.83.dx_ref, ...), custom_call_target="tpu_custom_call" | custom-call | flops 10485760 | bytes 41943040 | tf_op jit(solution)/shard_map/finish/pallas_call | solution.py:1482
  863.4 1.0 copy.61
  864.3 1.0 copy.62
  (42 shorter events, 0.3 us)
Async XLA Ops:
  7.2 1.2 copy-start
  7.2 15.8 %copy-start.7 = (s32[8192]{0:T(1024)S(1)}, s32[8192]{0:T(1024)}, u32[]{:S(2)}) copy-start(s32[8192]{0:T(1024)} %param.23) | copy-start | bytes 98308
  7.2 9.9 %copy-start.6 = (bf16[512,512]{1,0:T(8,128)(2,1)S(1)}, bf16[512,512]{1,0:T(8,128)(2,1)}, u32[]{:S(2)}) copy-start(bf16[512,512]{1,0:T(8,128)(2,1)} %param.15) | copy-start | bytes 1572868
  7.2 10.8 %copy-start.10 = (f32[512]{0:T(512)S(1)}, f32[512]{0:T(512)}, u32[]{:S(2)}) copy-start(f32[512]{0:T(512)} %param.19) | copy-start | bytes 6148
  7.2 10.8 %copy-start.11 = (f32[512]{0:T(512)S(1)}, f32[512]{0:T(512)}, u32[]{:S(2)}) copy-start(f32[512]{0:T(512)} %param.14) | copy-start | bytes 6148
  7.2 143.5 %all-gather.7.cloned.1.call-start = ((), (), s32[]{:S(2)}) async-start(), calls=%async_computation.3 | async-start | bytes 2359296 | tf_op jit(solution)/shard_map/all_gather | solution.py:1533
  9.2 273.0 %all-gather.9.cloned.1.call-start = ((), (), s32[]{:S(2)}) async-start(), calls=%async_computation.4 | async-start | bytes 18874368 | tf_op jit(solution)/shard_map/all_gather | solution.py:1574
  14.1 136.5 %copy-start.9 = (s32[2]{0:T(128)}, s32[2]{0:T(128)S(1)}, u32[]{:S(2)}) copy-start(s32[2]{0:T(128)S(1)} %fusion.2.s_ref) | copy-start | bytes 28
  150.7 283.7 %all-gather.11.cloned.1.call-start = ((), (), s32[]{:S(2)}) async-start(), calls=%async_computation.5 | async-start | bytes 4718592 | tf_op jit(solution)/shard_map/all_gather | solution.py:1577
  150.8 131.7 %copy-start.8 = (f32[4,2,512]{2,1,0:T(2,128)S(1)}, f32[4,2,512]{2,1,0:T(2,128)}, u32[]{:S(2)}) copy-start(f32[4,2,512]{2,1,0:T(2,128)} %get-tuple-element.60) | copy-start | bytes 49156
  282.2 418.3 %reduce-scatter.4.cloned.1.call-start = ((), (), s32[]{:S(2)}) async-start(), calls=%async_computation.6 | async-start | bytes 9437184 | tf_op jit(solution)/shard_map/reduce_scatter | solution.py:1536
  434.3 266.3 %reduce-scatter.6.cloned.1.call-start = ((), (), s32[]{:S(2)}) async-start(), calls=%async_computation.8 | async-start | bytes 9437184 | tf_op jit(solution)/shard_map/reduce_scatter | solution.py:1536
  535.9 165.4 %reduce-scatter.8.cloned.1.call-start = ((), (), s32[]{:S(2)}) async-start(), calls=%async_computation.10 | async-start | bytes 9437184 | tf_op jit(solution)/shard_map/reduce_scatter | solution.py:1536
  536.5 310.5 %all-gather.13.cloned.1.call-start = ((), (), s32[]{:S(2)}) async-start(), calls=%async_computation.7 | async-start | bytes 3145728 | tf_op jit(solution)/shard_map/all_gather | solution.py:1537
  700.5 146.5 %all-gather.15.cloned.1.call-start = ((), (), s32[]{:S(2)}) async-start(), calls=%async_computation.9 | async-start | bytes 3145728 | tf_op jit(solution)/shard_map/all_gather | solution.py:1537
  701.3 145.8 %all-gather.17.cloned.1.call-start = ((), (), s32[]{:S(2)}) async-start(), calls=%async_computation.11 | async-start | bytes 3145728 | tf_op jit(solution)/shard_map/all_gather | solution.py:1537
  847.0 1.6 copy-start.2
  848.6 1.6 copy-start.3
  850.2 13.1 %copy-start.5 = (f32[512,512]{1,0:T(8,128)S(1)}, f32[512,512]{1,0:T(8,128)}, u32[]{:S(2)}) copy-start(f32[512,512]{1,0:T(8,128)} %get-tuple-element.156) | copy-start | bytes 3145732
  850.2 14.1 %copy-start.4 = (f32[512,512]{1,0:T(8,128)S(1)}, f32[512,512]{1,0:T(8,128)}, u32[]{:S(2)}) copy-start(f32[512,512]{1,0:T(8,128)} %get-tuple-element.159) | copy-start | bytes 3145732
  850.2 15.1 %copy-start.1 = (bf16[512,512]{1,0:T(8,128)(2,1)S(1)}, bf16[512,512]{1,0:T(8,128)(2,1)}, u32[]{:S(2)}) copy-start(bf16[512,512]{1,0:T(8,128)(2,1)} %param.18) | copy-start | bytes 1572868
Sparse Core Ops, SparseCore 0:
  10.5 42.6 all-gather.6
  150.8 131.3 all-gather.8
  284.1 36.7 all-gather.10
  434.4 70.3 reduce-scatter.3
  536.0 69.9 reduce-scatter.5
  609.3 71.2 reduce-scatter.7
  700.6 13.1 all-gather.12
  715.5 10.2 all-gather.14
  727.4 11.7 all-gather.16

commit v9 on v8

--- a/solution.py
+++ b/solution.py
@@ -358,9 +358,8 @@
     for k in range(1, narrow):
         w_to(k).start()
         gain_to(k, me).start()
-    x_start(0)
-    if wide > 1:
-        x_start(1)
+    for r in range(wide):
+        x_start(r)
     for r in range(1, wide):
         side_to(r, z).start()
     side_buf[z] = w_ref[:, qw:]
@@ -411,10 +410,6 @@
         x_own(r).wait()
         for k in range(1, group):
             x_from(r, k).wait_recv()
-        for later in range(2, wide):
-            @pl.when(r == later - 2)
-            def _():
-                x_start(later)
         at = pl.ds(pl.multiple_of(r * own, own), own)
         low = x_buf[r]
         x = low.astype(F32)

time: 873 us -> 871 us (level)
  no operation moved by 1% of the time
where the time goes in v9:
time: 871 us; the launch traced here: 870 us
  Pallas kernels  804 us (92%)
  waiting for transfers between devices  25 us (3%)
  local copies, waits for them, and re-layouts  15.3 us (2%)
  between operations  14.1 us (2%)
  other arithmetic  11 us (1%)
    pallas_call x1, Pallas kernels, backward_call(): pl.pallas_call(functools.partial(backward_kernel, plan, kv_heads, heads),...  164 us
    pallas_call x1, Pallas kernels, ffn_call(): pl.pallas_call(functools.partial(ffn_kernel, plan), grid=(wide, tiles), i...  151 us
    pallas_call x1, Pallas kernels, tail_call(): pl.pallas_call(functools.partial(tail_kernel, plan, kv_heads), in_specs=[...  141 us
    pallas_call x1, Pallas kernels, head_call(): pl.pallas_call(functools.partial(head_kernel, plan, kv_heads, qw), in_spe...  125 us
    pallas_call x1, Pallas kernels, forward_call(): pl.pallas_call(functools.partial(forward_kernel, plan, kv_heads, heads),...  109 us
    pallas_call x1, Pallas kernels, weights_call(): pl.pallas_call(functools.partial(weights_kernel, plan, tiles), grid=(2 *...  102 us
    all_gather x1, waiting for transfers between devices, body(): w_gu = lax.all_gather(w_gu, NS, axis=0, tiled=True)  22.9 us
  transfers between devices with their start and end apart: 9, of which 1 were waited for; matrix products, arithmetic and copies ran while one was open for 2% of the time, Pallas kernels for 91%

profile of v9, /device:TPU:0, one launch (start us, length us, event | category | flops | bytes accessed | tf_op | source)
XLA Modules:
  0.0 870.1 jit_solution(5106990095272844465)
XLA Ops:
  7.2 0.0 all-gather.7.cloned.1.call-start
  7.3 1.1 copy-done
  8.4 0.7 constant_dynamic-slice_fusion
  9.2 0.0 all-gather.9.cloned.1.call-start
  9.3 0.8 broadcast_compare_fusion
  10.0 0.7 dynamic_slice.14
  10.8 1.0 copy.47
  11.8 1.0 copy.46
  12.9 0.1 copy.49
  13.0 0.1 mul.51
  13.1 1.0 fusion.2.s_ref
  14.1 0.6 fusion.22
  14.7 2.4 bitcast_select_fusion.g_ref
  17.1 0.9 pad_maximum_fusion.w_ref
  18.0 0.6 pad_maximum_fusion.2.gains_ref
  18.6 1.3 subtract_convert_fusion
  20.0 3.1 multiply_sine_fusion
  23.0 0.8 select_convert_fusion.marks_ref
  23.9 124.6 %head.1 = (bf16[1024,2048]{1,0:T(8,128)(2,1)}, bf16[1024,512]{1,0:T(8,128)(2,1)}, bf16[256,2048]{1,0:T(8,128)(2,1)}, bf16[2,8192,128]{2,1,0:T(8,128)(2,1)}, bf16...) custom-call(bf16[8,4,128,512]{3,2,1,0:T(8,128)(2,1)} %bitcast.55, ...), custom_call_target="tpu_custom_call" | custom-call | flops 96636764160 | bytes 19922944 | tf_op jit(solution)/shard_map/head/pallas_call | solution.py:510
  148.5 0.0 all-gather.11.cloned.1.call-start
  148.5 0.0 all-gather.7.cloned.1.call-done.wo_ref
  148.6 108.5 %attention_forward.1 = (bf16[4,256,512]{2,1,0:T(8,128)(2,1)}, bf16[4,2,2,512,128]{4,3,2,1,0:T(8,128)(2,1)}, f32[256,2048]{1,0:T(8,128)}, bf16[4,2048,512]{2,1,0:T(8,128)(2,1)}) custom-call(s32[2]{0:T(128)} %copy-done.9, bf16[1024,512]{1,0:T(8,128)(2,1)} %get-tuple-element.55.q_ref, bf16[2,8192,128]{2,1,0:T(8,128)(2,1)} %get-tuple-element.56.kx, ...), custom_call_target="tpu_custom_call" | custom-call | flops 34359738368 | bytes 16777216 | tf_op jit(solution)/shard_map/attention_forward/pallas_call | solution.py:724
  257.1 22.9 %all-gather.9.cloned.1.call-done.wg_ref.wu_ref = bf16[2048,4096]{1,0:T(8,128)(2,1)} async-done(((bf16[256,4096]{1,0:T(8,128)(2,1)}), bf16[2048,4096]{1,0:T(8,128)(2,1)}) %all-gather.9.cloned.1.call-update) | async-done | bytes 16777232 | tf_op jit(solution)/shard_map/all_gather | solution.py:1569
  280.0 0.2 reduce-scatter.4.cloned.1.call-start
  280.3 0.6 fusion.20
  280.9 151.2 %feed_forward.1 = (bf16[1024,2048]{1,0:T(8,128)(2,1)}, bf16[1024,2048]{1,0:T(8,128)(2,1)}, bf16[1024,2048]{1,0:T(8,128)(2,1)}, bf16[4,256,2048]{2,1,0:T(8,128)(2...) custom-call(f32[256,2048]{1,0:T(8,128)} %get-tuple-element.59.x2_ref, ...), custom_call_target="tpu_custom_call" | custom-call | flops 68719476736 | bytes 50331648 | tf_op jit(solution)/shard_map/feed_forward/pallas_call | solution.py:896
  432.1 0.0 reduce-scatter.6.cloned.1.call-start
  432.2 0.0 all-gather.11.cloned.1.call-done
  432.2 101.5 %weight_gradients.1 = (bf16[2048,2048]{1,0:T(8,128)(2,1)}, bf16[2048,2048]{1,0:T(8,128)(2,1)}, bf16[4,256,2048]{2,1,0:T(8,128)(2,1)}, bf16[256,2048]{1,0:T(8,128)(2,1)}) custom-call(f32[256,2048]{1,0:T(8,128)} %get-tuple-element.64.dx2_ref, bf16[1024,2048]{1,0:T(8,128)(2,1)} %get-tuple-element.69.h_ref, bf16[1024,2048]{1,0:T(8,128)(2,1)} %get-tuple-element.70.dg_ref, ...), custom_call_target="tpu_custom_call" | custom-call | flops 34359738368 | bytes 41943040 | tf_op jit(solution)/shard_map/weight_gradients/pallas_call | solution.py:998
  533.8 0.0 reduce-scatter.8.cloned.1.call-start
  533.8 0.5 reduce-scatter.8.cloned.1.call-update
  534.4 0.3 all-gather.13.cloned.1.call-start
  534.6 163.6 %attention_backward.1 = (bf16[1024,512]{1,0:T(8,128)(2,1)}, f32[2,8192,128]{2,1,0:T(8,128)}, f32[256,2048]{1,0:T(8,128)}, bf16[4,8,128,512]{3,2,1,0:T(8,128)(2,1)}) custom-call(bf16[4,256,2048]{2,1,0:T(8,128)(2,1)} %get-tuple-element.73.db_ref.db_hbm, bf16[4,2,2,512,128]{4,3,2,1,0:T(8,128)(2,1)} %get-tuple-element.74.qe_ref, ...), custom_call_target="tpu_custom_call" | custom-call | flops 77309411328 | bytes 25165824 | tf_op jit(solution)/shard_map/attention_backward/pallas_call | solution.py:1182
  698.2 0.0 reduce-scatter.4.cloned.1.call-done
  698.3 0.0 all-gather.15.cloned.1.call-start
  698.4 0.7 all-gather.15.cloned.1.call-update
  699.0 0.0 all-gather.17.cloned.1.call-start
  699.1 0.7 all-gather.17.cloned.1.call-update
  699.8 141.3 %input_gradient.1 = (bf16[4,8,128,512]{3,2,1,0:T(8,128)(2,1)}, f32[2,512]{1,0:T(2,128)}, f32[256,512]{1,0:T(8,128)}, f32[512,512]{1,0:T(8,128)}, f32[512,512]{1,0:T(8,128)}) custom-call(f32[2,8192,128]{2,1,0:T(8,128)} %get-tuple-element.78.sums_ref, bf16[1024,2048]{1,0:T(8,128)(2,1)} %get-tuple-element.79.h_hbm, f32[256,2048]{1,0:T(8,128)} %get-tuple-element.80.dh_ref, ...), custom_call_target="tpu_custom_call" | custom-call | flops 107374182400 | bytes 8388608 | tf_op jit(solution)/shard_map/input_gradient/pallas_call | solution.py:1419
  841.1 1.1 copy.57
  842.3 0.8 copy.51
  843.1 0.8 copy.52
  843.9 1.3 fusion.21
  845.3 1.6 copy-done.2
  846.9 1.6 copy-done.3
  848.5 13.1 %finish.1 = (bf16[8,4,128,512]{3,2,1,0:T(8,128)(2,1)}, f32[8,4,128,512]{3,2,1,0:T(8,128)}, f32[2048,512]{1,0:T(8,128)}, f32[512,2048]{1,0:T(8,128)}, f32[512,2048]{1,0:T(8,128)}) custom-call(s32[1]{0:T(128)} %bitcast.s_ref, bf16[4,8,128,512]{3,2,1,0:T(8,128)(2,1)} %get-tuple-element.77.res_ref, bf16[4,8,128,512]{3,2,1,0:T(8,128)(2,1)} %get-tuple-element.83.dx_ref, ...), custom_call_target="tpu_custom_call" | custom-call | flops 10485760 | bytes 41943040 | tf_op jit(solution)/shard_map/finish/pallas_call | solution.py:1477
  861.6 1.0 copy.61
  862.6 1.0 copy.62
  (42 shorter events, 0.3 us)
Async XLA Ops:
  7.2 1.2 copy-start
  7.2 15.8 %copy-start.7 = (s32[8192]{0:T(1024)S(1)}, s32[8192]{0:T(1024)}, u32[]{:S(2)}) copy-start(s32[8192]{0:T(1024)} %param.23) | copy-start | bytes 98308
  7.2 9.9 %copy-start.6 = (bf16[512,512]{1,0:T(8,128)(2,1)S(1)}, bf16[512,512]{1,0:T(8,128)(2,1)}, u32[]{:S(2)}) copy-start(bf16[512,512]{1,0:T(8,128)(2,1)} %param.15) | copy-start | bytes 1572868
  7.2 10.8 %copy-start.10 = (f32[512]{0:T(512)S(1)}, f32[512]{0:T(512)}, u32[]{:S(2)}) copy-start(f32[512]{0:T(512)} %param.19) | copy-start | bytes 6148
  7.2 10.8 %copy-start.11 = (f32[512]{0:T(512)S(1)}, f32[512]{0:T(512)}, u32[]{:S(2)}) copy-start(f32[512]{0:T(512)} %param.14) | copy-start | bytes 6148
  7.2 141.3 %all-gather.7.cloned.1.call-start = ((), (), s32[]{:S(2)}) async-start(), calls=%async_computation.3 | async-start | bytes 2359296 | tf_op jit(solution)/shard_map/all_gather | solution.py:1528
  9.2 270.9 %all-gather.9.cloned.1.call-start = ((), (), s32[]{:S(2)}) async-start(), calls=%async_computation.4 | async-start | bytes 18874368 | tf_op jit(solution)/shard_map/all_gather | solution.py:1569
  14.1 134.3 %copy-start.9 = (s32[2]{0:T(128)}, s32[2]{0:T(128)S(1)}, u32[]{:S(2)}) copy-start(s32[2]{0:T(128)S(1)} %fusion.2.s_ref) | copy-start | bytes 28
  148.5 283.7 %all-gather.11.cloned.1.call-start = ((), (), s32[]{:S(2)}) async-start(), calls=%async_computation.5 | async-start | bytes 4718592 | tf_op jit(solution)/shard_map/all_gather | solution.py:1572
  148.5 131.7 %copy-start.8 = (f32[4,2,512]{2,1,0:T(2,128)S(1)}, f32[4,2,512]{2,1,0:T(2,128)}, u32[]{:S(2)}) copy-start(f32[4,2,512]{2,1,0:T(2,128)} %get-tuple-element.60) | copy-start | bytes 49156
  280.0 418.2 %reduce-scatter.4.cloned.1.call-start = ((), (), s32[]{:S(2)}) async-start(), calls=%async_computation.6 | async-start | bytes 9437184 | tf_op jit(solution)/shard_map/reduce_scatter | solution.py:1531
  432.1 266.2 %reduce-scatter.6.cloned.1.call-start = ((), (), s32[]{:S(2)}) async-start(), calls=%async_computation.8 | async-start | bytes 9437184 | tf_op jit(solution)/shard_map/reduce_scatter | solution.py:1531
  533.8 165.3 %reduce-scatter.8.cloned.1.call-start = ((), (), s32[]{:S(2)}) async-start(), calls=%async_computation.10 | async-start | bytes 9437184 | tf_op jit(solution)/shard_map/reduce_scatter | solution.py:1531
  534.4 310.9 %all-gather.13.cloned.1.call-start = ((), (), s32[]{:S(2)}) async-start(), calls=%async_computation.7 | async-start | bytes 3145728 | tf_op jit(solution)/shard_map/all_gather | solution.py:1532
  698.3 147.0 %all-gather.15.cloned.1.call-start = ((), (), s32[]{:S(2)}) async-start(), calls=%async_computation.9 | async-start | bytes 3145728 | tf_op jit(solution)/shard_map/all_gather | solution.py:1532
  699.0 146.3 %all-gather.17.cloned.1.call-start = ((), (), s32[]{:S(2)}) async-start(), calls=%async_computation.11 | async-start | bytes 3145728 | tf_op jit(solution)/shard_map/all_gather | solution.py:1532
  845.3 1.6 copy-start.2
  846.9 1.6 copy-start.3
  848.5 13.1 %copy-start.5 = (f32[512,512]{1,0:T(8,128)S(1)}, f32[512,512]{1,0:T(8,128)}, u32[]{:S(2)}) copy-start(f32[512,512]{1,0:T(8,128)} %get-tuple-element.156) | copy-start | bytes 3145732
  848.5 14.1 %copy-start.4 = (f32[512,512]{1,0:T(8,128)S(1)}, f32[512,512]{1,0:T(8,128)}, u32[]{:S(2)}) copy-start(f32[512,512]{1,0:T(8,128)} %get-tuple-element.159) | copy-start | bytes 3145732
  848.5 15.1 %copy-start.1 = (bf16[512,512]{1,0:T(8,128)(2,1)S(1)}, bf16[512,512]{1,0:T(8,128)(2,1)}, u32[]{:S(2)}) copy-start(bf16[512,512]{1,0:T(8,128)(2,1)} %param.18) | copy-start | bytes 1572868
Sparse Core Ops, SparseCore 0:
  10.5 42.6 all-gather.6
  148.6 131.3 all-gather.8
  281.9 36.7 all-gather.10
  432.3 70.2 reduce-scatter.3
  533.9 69.9 reduce-scatter.5
  607.2 71.2 reduce-scatter.7
  698.4 13.1 all-gather.12
  713.3 10.3 all-gather.14
  725.2 11.7 all-gather.16
